TPU v7x, 32 devices: a whole 2x2x4 slice. The times are simulated.
32 devices in a mesh: dp: 8 (over z, y), head: 4 (over x, core).
Axes of the slice: x: 2, y: 2, z: 4, core: 2. Of those that a mesh axis runs over, the one named last changes fastest.
Arguments:
- inputs: bfloat16 [16, 2048, 768], P('dp', 'head'), may hold values from -6 to 6
- lengths: int32 [16], P('dp'), may hold values from 1 to 2048, 24576 in all
- w_query: bfloat16 [768, 768], P('head'), may hold values from -0.21875 to 0.21875
- w_key: bfloat16 [768, 768], P('head'), may hold values from -0.21875 to 0.21875
- w_value: bfloat16 [768, 768], P('head'), may hold values from -0.21875 to 0.21875
- w_out: bfloat16 [768, 768], P('head'), may hold values from -1.75 to 1.75
- w_up: bfloat16 [768, 3072], P(None, 'head'), may hold values from -0.21875 to 0.21875
- w_down: bfloat16 [3072, 768], P('head'), may hold values from -0.109375 to 0.109375
- conv_taps: bfloat16 [3, 3, 768], P(None, None, 'head'), may hold values from -3.5 to 3.5
- gain_attn: bfloat16 [768], replicated, may hold values from 0.5 to 1.5
- gain_ff: bfloat16 [768], replicated, may hold values from 0.5 to 1.5
- cotangent: bfloat16 [16, 2048, 768], P('dp', 'head'), may hold values from -6 to 6
Outputs:
- output: float32 [16, 2048, 768], P('dp', 'head')
- grad_input: float32 [16, 2048, 768], P('dp', 'head')
- grad_query: float32 [768, 768], P('head')
- grad_key: float32 [768, 768], P('head')
- grad_value: float32 [768, 768], P('head')
- grad_out: float32 [768, 768], P('head')
- grad_up: float32 [768, 3072], P(None, 'head')
- grad_down: float32 [3072, 768], P('head')
- grad_taps: float32 [3, 3, 768], P(None, None, 'head')
- grad_gain_attn: float32 [768], P('head')
- grad_gain_ff: float32 [768], P('head')
Inputs may be any that keep to these rules, and one draw needn't show every extreme that they name: `lengths`: one sequence in every draw has all 2048 positions real.
All inputs are finite; a program needn't handle non-finite values. No bound on the sum of `lengths` on one device may be relied on, other than what follows from the above.
Results may differ from a plain program's by a relative error of at most 0.015.
The roundings to bfloat16 on the way count: a program that leaves them out, or rounds other values in their place, can miss the bound.
Values may be sent and summed in bfloat16 or wider, within the bound.
No kernel may reach another device: no remote copies, remote signals or barrier semaphores. Data moves between devices by JAX's collectives and lax.ppermute only.
A program may use at most 256 MiB of HBM per device.

v0:
```python
import functools

import jax
import jax.numpy as jnp
from jax import lax
from jax.experimental import pallas as pl
from jax.experimental.pallas import tpu as pltpu
from jax.sharding import PartitionSpec as P

HDIM = 64
EPS = 1e-06
bf16 = jnp.bfloat16
f32 = jnp.float32

NN = (((1,), (0,)), ((), ()))
NT = (((1,), (1,)), ((), ()))
TN = (((0,), (0,)), ((), ()))

CORE = [(0, 1), (1, 0), (2, 3), (3, 2)]
XNB = [(0, 2), (2, 0), (1, 3), (3, 1)]


def dot(a, b, dims=NN):
    return lax.dot_general(a, b, dims, preferred_element_type=f32)


def cost(flops, nbytes, trans=0):
    return pl.CostEstimate(flops=int(flops), bytes_accessed=int(nbytes), transcendentals=int(trans))


def sds(shape, dtype):
    return jax.ShapeDtypeStruct(shape, dtype)


def whole(shape):
    zeros = (0,) * len(shape)
    return pl.BlockSpec(shape, lambda *_: zeros, pipeline_mode=pl.Buffered(1))


def grid_spec(grid, ins, outs, scratch=()):
    return pltpu.PrefetchScalarGridSpec(
        num_scalar_prefetch=1, grid=grid, in_specs=ins, out_specs=outs, scratch_shapes=scratch
    )


def length_of(m):
    return m[m[2] // 2]


def x_of(m):
    return m[2] // 2


def core_of(m):
    return lax.rem(m[2], 2)


def slot_of(m, b):
    v = jnp.bitwise_xor(m[2], b)
    return lax.rem(v, 2) * 2 + v // 2


def norm(x, gain):
    inv = lax.rsqrt(jnp.mean(x * x, axis=-1, keepdims=True) + EPS)
    n = x * inv
    return n, inv, (n * gain).astype(bf16)


def qkv_body(meta, x0, x2, x3, wa, wb, pack, gain, h_ref, raw_ref, mix_ref, w_ref, taps, ext):
    b = pl.program_id(0)
    rows = x0.shape[0]
    part = w_ref.shape[0] // 4
    width = x0.shape[1]
    tall = wa.shape[0]
    hd = meta[2]

    @pl.when(b == 0)
    def _():
        def put(k, ref, first):
            at = jnp.bitwise_xor(hd, k) * part
            w_ref[pl.ds(pl.multiple_of(at, 64), part), 0:width] = ref[first : first + part, :]
            for n in range(2):
                row = pl.multiple_of(at + n * (part // 2), 32)
                w_ref[pl.ds(row, part // 2), width:] = ref[
                    first + part : first + part + part // 2, n * (width // 2) : (n + 1) * (width // 2)
                ]

        put(0, wa, 0)
        put(1, wb, 0)
        put(2, pack, rows)
        put(3, pack, rows + tall)
        last = lambda ref, end: ref[end - 16 : end, :].astype(f32)
        near = last(wa, tall) + last(wb, tall)
        far = last(pack, rows + tall) + last(pack, rows + 2 * tall)
        t = jnp.where(x_of(meta) == core_of(meta), near, far)
        taps[...] = jnp.zeros_like(taps)
        taps[0:3, 0:width] = t[0:3]
        taps[0:3, width:] = t[3:6, 0 : width // 2]
        ext[0:8, :] = jnp.zeros((8, ext.shape[1]), f32)

    slot = slot_of(meta, b)
    step = ext.shape[0] - 8

    def some(n, carry):
        sl = pl.ds(pl.multiple_of(n * step, step), step)
        x = x0[sl, :]
        for k, other in ((1, pack), (2, x2), (3, x3)):
            x = jnp.where(slot == k, other[sl, :], x)
        _, _, h = norm(x.astype(f32), gain[...].astype(f32))
        h_ref[sl, :] = h
        raw = dot(h, w_ref[...]).astype(bf16)
        raw_ref[sl, :] = raw
        rawf = raw.astype(f32)
        ext[8:, :] = rawf
        t = taps[...]
        mixed = t[0:1] * rawf + t[1:2] * ext[7 : 7 + step, :] + t[2:3] * ext[6 : 6 + step, :]
        mix_ref[sl, :] = mixed.astype(bf16)
        ext[0:8, :] = ext[step:, :]
        return carry

    lax.fori_loop(0, rows // step, some, 0)


def qkv_call(meta, x_own, x_core, x_cnb, w_mine, w_core, pack, gain):
    rows, width = x_own.shape
    tall = w_mine.shape[0]
    cols = width * 3 // 2
    length = 4 * rows
    blk = lambda n: pl.BlockSpec((rows, n), lambda b, m: (b, 0))
    const = lambda r: pl.BlockSpec((r, cols), lambda b, m: (0, 0))
    return pl.pallas_call(
        qkv_body,
        out_shape=[
            sds((length, width), bf16),
            sds((length, cols), bf16),
            sds((length, cols), bf16),
            sds((width, cols), bf16),
            sds((8, cols), f32),
        ],
        grid_spec=grid_spec(
            (4,),
            [whole((rows, width))] * 3
            + [whole((tall, width))] * 2
            + [whole(pack.shape), whole((1, width))],
            [
                pl.BlockSpec((rows, width), lambda b, m: (slot_of(m, b), 0)),
                blk(cols),
                blk(cols),
                const(width),
                const(8),
            ],
            [pltpu.VMEM((T + 8, cols), f32)],
        ),
        cost_estimate=cost(2 * length * width * cols, 2 * length * (width * 2 + cols * 2)),
        name="qkv",
    )(meta, x_own, x_core, x_cnb, w_mine, w_core, pack, gain)


def two_heads(v):
    lane = lax.broadcasted_iota(jnp.int32, v.shape, 1)
    z = jnp.zeros_like(v)
    return jnp.concatenate([jnp.where(lane < HDIM, v, z), jnp.where(lane < HDIM, z, v)], axis=0)


def causal(first, keys, start, queries):
    key = first + lax.broadcasted_iota(jnp.int32, (keys, queries), 0)
    ok = key <= start + lax.broadcasted_iota(jnp.int32, (keys, queries), 1)
    return jnp.concatenate([ok, ok], axis=1)


def upper(v, axis):
    B = v.shape[axis] // 2
    h = B // 2
    if axis == 0:
        return jnp.concatenate([v[h:B], v[B + h :]], axis=0)
    return jnp.concatenate([v[:, h:B], v[:, B + h :]], axis=1)


def with_bias(k_ref, ka, length):
    L = k_ref.shape[0]
    ka[:, :128] = k_ref[...]
    lane = lax.broadcasted_iota(jnp.int32, (L, 128), 1)
    row = lax.broadcasted_iota(jnp.int32, (L, 128), 0)
    pad = jnp.logical_and(lane == 0, row >= length)
    ka[:, 128:] = jnp.where(pad, -1e9, 0.0).astype(bf16)


def biased(q):
    qq = two_heads(q)
    lane = lax.broadcasted_iota(jnp.int32, qq.shape, 1)
    return jnp.concatenate([qq, jnp.where(lane == 0, 1.0, 0.0).astype(bf16)], axis=1)


def att_fwd_body(meta, q_ref, k_ref, v_ref, mine_ref, theirs_ref, lse_ref, ka, vt, sc):
    i = pl.program_id(1)
    B = q_ref.shape[0]

    @pl.when(i == 0)
    def _():
        vt[...] = v_ref[...].T
        with_bias(k_ref, ka, length_of(meta))

    qq = biased(q_ref[...] * bf16(HDIM**-0.5))
    own = lax.rem(i, 2) == core_of(meta)

    def run(ii):
        m = None
        for j in range(ii + 1):
            ks = slice(j * B, j * B + B)
            s = dot(ka[ks, :], qq, NT)
            if j == ii:
                s = jnp.where(causal(0, B, 0, B), s, -1e9)
            sc[ks, :] = s
            mj = jnp.max(s, axis=0, keepdims=True)
            m = mj if m is None else jnp.maximum(m, mj)
        l = jnp.zeros((1, 2 * B), f32)
        acc = [jnp.zeros((HDIM, B), f32)] * 2
        for j in range(ii + 1):
            ks = slice(j * B, j * B + B)
            p = jnp.exp(sc[ks, :] - m)
            l = l + jnp.sum(p, axis=0, keepdims=True)
            pb = p.astype(bf16)
            for h in range(2):
                r = slice(HDIM * h, HDIM * h + HDIM)
                acc[h] = acc[h] + dot(vt[r, ks], pb[:, h * B : h * B + B])
        inv = 1.0 / l
        out = jnp.concatenate([acc[h] * inv[:, h * B : h * B + B] for h in range(2)], axis=0)
        out = out.T.astype(bf16)

        @pl.when(own)
        def _():
            mine_ref[...] = out

        @pl.when(jnp.logical_not(own))
        def _():
            theirs_ref[...] = out

        ls = m + jnp.log(l)
        lse_ref[0] = jnp.concatenate([ls[:, :B], ls[:, B:]], axis=0)

    for ii in range(4):
        pl.when(i == ii)(functools.partial(run, ii))


def half_map(p, i, m):
    return (jnp.bitwise_xor(i // 2, x_of(m)), p)


def att_fwd_call(meta, mix):
    length, cols = mix.shape
    width = cols // 3
    pairs = width // 128
    B = length // 4
    half = pl.BlockSpec((B, 128), half_map)
    return pl.pallas_call(
        att_fwd_body,
        out_shape=[
            sds((length // 2, width), bf16),
            sds((length // 2, width), bf16),
            sds((pairs, 2, length), f32),
        ],
        grid_spec=grid_spec(
            (pairs, 4),
            [
                pl.BlockSpec((B, 128), lambda p, i, m: (i, p)),
                pl.BlockSpec((length, 128), lambda p, i, m: (0, pairs + p)),
                pl.BlockSpec((length, 128), lambda p, i, m: (0, 2 * pairs + p)),
            ],
            [half, half, pl.BlockSpec((1, 2, B), lambda p, i, m: (p, 0, i))],
            [
                pltpu.VMEM((length, 256), bf16),
                pltpu.VMEM((128, length), bf16),
                pltpu.VMEM((length, 2 * B), f32),
            ],
        ),
        cost_estimate=cost(8 * length * length * width, 8 * length * width, 2 * length * length * pairs),
        name="attn_fwd",
    )(meta, mix, mix, mix)


def att_bwd_body(
    p0, aliased, meta, q_ref, k_ref, v_ref, om, ot, dm, dt, lse_ref, rq, rk, rv, taps, *refs
):
    gm_ref, gt_ref, gt, ka, kt, dkt, dvt, dqt, dqs, ext, stage, sem = refs[2:] if aliased else refs
    i = pl.program_id(1)
    B = q_ref.shape[0]
    L = k_ref.shape[0]
    H = B // 2

    @pl.when(i == 0)
    def _():
        kt[...] = k_ref[...].T
        with_bias(k_ref, ka, length_of(meta))

    own = lax.rem(i, 2) == core_of(meta)
    q = q_ref[...] * bf16(HDIM**-0.5)
    o = jnp.where(own, om[...], ot[...])
    do = jnp.where(own, dm[...], dt[...])
    qq, dd = biased(q), two_heads(do)
    qt, dot_ = q.T, do.T
    od = (o.astype(f32) * do.astype(f32)).T
    delta = jnp.concatenate(
        [jnp.sum(od[:HDIM], axis=0, keepdims=True), jnp.sum(od[HDIM:], axis=0, keepdims=True)],
        axis=1,
    )
    ls = lse_ref[0]
    lse = jnp.concatenate([ls[0:1], ls[1:2]], axis=1)

    dqt[...] = jnp.zeros_like(dqt)

    def tile(st, n, lo, diagonal):
        w = B - lo
        ks = pl.ds(pl.multiple_of(st, H), n)
        part = upper if lo else lambda v, axis: v
        s = dot(ka[ks, :], part(qq, 0), NT)
        dp = dot(v_ref[ks, :], part(dd, 0), NT)
        p = jnp.exp(s - part(lse, 1))
        if diagonal:
            p = jnp.where(causal(lo, n, lo, w), p, 0.0)
        ds = (p * (dp - part(delta, 1))).astype(bf16)
        pb = p.astype(bf16)
        for h in range(2):
            r, c = slice(HDIM * h, HDIM * h + HDIM), slice(h * w, h * w + w)
            dqt[r, lo:] += dot(kt[r, ks], ds[:, c])
            a = dot(qt[r, lo:], ds[:, c], NT)
            b = dot(dot_[r, lo:], pb[:, c], NT)
            if diagonal:
                dkt[r, ks] = a
                dvt[r, ks] = b
            else:
                dkt[r, ks] += a
                dvt[r, ks] += b

    lax.fori_loop(0, i, lambda j, c: (tile(j * B, B, 0, False), c)[1], 0)
    tile(i * B, H, 0, True)
    tile(i * B + H, H, H, True)
    dqs[pl.ds(pl.multiple_of(i * B, B), B), :] = dqt[...].T * HDIM**-0.5

    def copies(pair):
        width = gm_ref.shape[1] // 3
        for b in range(L // B):
            to = pl.ds(pl.multiple_of(jnp.bitwise_xor(b // 2, x_of(meta)) * B, B), B)
            for k in range(3):
                col = pl.ds(pl.multiple_of(k * width + (p0 + pair) * 128, 128), 128)
                src = stage.at[k, pl.ds(b * B, B), :]
                yield b, lambda g, to=to, col=col, src=src, k=k: pltpu.make_async_copy(
                    src, g.at[to, col], sem.at[k]
                )

    def send(pair):
        for b, copy in copies(pair):
            own = core_of(meta) == b % 2

            @pl.when(own)
            def _(copy=copy):
                copy(gm_ref).start()

            @pl.when(jnp.logical_not(own))
            def _(copy=copy):
                copy(gt_ref).start()

    def finish(pair):
        for _, copy in copies(pair):
            copy(gm_ref).wait()

    @pl.when(i == pl.num_programs(1) - 1)
    def _():
        pair = pl.program_id(0)
        gt[...] = jnp.zeros_like(gt)
        ext[...] = jnp.zeros_like(ext)

        @pl.when(pair > 0)
        def _():
            finish(pair)

        def back(n, carry):
            blk = L // B - 1 - n
            sl = pl.ds(pl.multiple_of(blk * B, B), B)
            for which, raw in enumerate((rq, rk, rv)):
                col = which * (taps.shape[1] // 3) + (p0 + pl.program_id(0)) * 128
                t = taps[:, pl.ds(pl.multiple_of(col, 128), 128)]
                g = dqs[sl, :] if which == 0 else (dkt, dvt)[which - 1][:, sl].T
                ext[which, B : B + 8, :] = ext[which, 0:8, :]
                ext[which, 0:B, :] = g
                g1, g2 = ext[which, 1 : B + 1, :], ext[which, 2 : B + 2, :]
                stage[which, sl, :] = (t[0:1] * g + t[1:2] * g1 + t[2:3] * g2).astype(bf16)
                r = raw[sl, :].astype(f32)
                for k, gg in enumerate((g, g1, g2)):
                    row = slice(3 * which + k, 3 * which + k + 1)
                    gt[row, :] += jnp.sum(r * gg, axis=0, keepdims=True)
            return carry

        lax.fori_loop(0, L // B, back, 0)
        send(pair)

        @pl.when(pair == pl.num_programs(0) - 1)
        def _():
            finish(pair)


def att_bwd_call(meta, mix, raw, om, ot, dm, dt, lse, taps, p0, count, into=None):
    length, cols = mix.shape
    pairs = cols // 384
    B = length // 4
    half = pl.BlockSpec((B, 128), lambda p, i, m: (jnp.bitwise_xor(i // 2, x_of(m)), p0 + p))
    full = lambda k: pl.BlockSpec((length, 128), lambda p, i, m: (0, k * pairs + p0 + p))
    return pl.pallas_call(
        functools.partial(att_bwd_body, p0, into is not None),
        out_shape=[sds((length // 2, cols), bf16)] * 2 + [sds((16, 128 * count), f32)],
        grid_spec=grid_spec(
            (count, 4),
            [
                pl.BlockSpec((B, 128), lambda p, i, m: (i, p0 + p)),
                full(1),
                full(2),
                half,
                half,
                half,
                half,
                pl.BlockSpec((1, 2, B), lambda p, i, m: (p0 + p, 0, i)),
                full(0),
                full(1),
                full(2),
                whole((8, cols)),
            ]
            + ([] if into is None else [pl.BlockSpec(memory_space=pl.ANY)] * 2),
            [pl.BlockSpec(memory_space=pl.ANY)] * 2 + [pl.BlockSpec((16, 128), lambda p, i, m: (0, p))],
            [
                pltpu.VMEM((length, 256), bf16),
                pltpu.VMEM((128, length), bf16),
                pltpu.VMEM((128, length), f32),
                pltpu.VMEM((128, length), f32),
                pltpu.VMEM((128, B), f32),
                pltpu.VMEM((length, 128), f32),
                pltpu.VMEM((3, B + 8, 128), f32),
                pltpu.VMEM((3, length, 128), bf16),
                pltpu.SemaphoreType.DMA((3,)),
            ],
        ),
        cost_estimate=cost(
            14 * length * length * 128 * count, 20 * length * 128 * count, 2 * length * length * count
        ),
        name="attn_bwd",
        input_output_aliases={} if into is None else {13: 0, 14: 1},
    )(meta, mix, mix, mix, om, ot, dm, dt, lse, raw, raw, raw, taps, *(into or ()))


T = 256


def valid_rows(meta, i, rows):
    per = rows // T
    block = jnp.where(i < per, meta[2], jnp.bitwise_xor(meta[2], 2))
    start = block * rows + lax.rem(i, per) * T
    return start + lax.broadcasted_iota(jnp.int32, (T, 1), 0) < length_of(meta)


def ffn_body(
    meta, xo, xx, co, cx, am, at, gain, wo_o, wo_c, pack,
    u_o, d_o, f_c, n0, n1, n2, n3, c0, c1, c2, c3,
    oo, ox, dm, dt, gg, dmid, gu0, gu1, gu2, gu3, gd0, gd1, gd2, gd3,
    wo, wus, wds, mid, h_s, g_s, fo, dh, act, du, stu, std, sto, gacc, sw, so, sg, sd, st,
):
    rows, width = xo.shape
    part = wo_o.shape[0]
    half = 2 * part
    n = 2 * rows // T
    per = rows // T
    copies = []
    for k, src in ((0, wo_o), (1, wo_c), (2, pack.at[pl.ds(rows, part), :]), (3, pack.at[pl.ds(rows + part, part), :])):
        shard = jnp.bitwise_xor(meta[2], k)
        row = jnp.where(shard // 2 == core_of(meta), 0, half) + lax.rem(shard, 2) * part
        cp = pltpu.make_async_copy(src, wo.at[pl.ds(pl.multiple_of(row, 64), part), :], so.at[k])
        cp.start()
        copies.append(cp)
    for k, pair in ((0, (f_c.at[0], f_c.at[1])), (2, (u_o, d_o))):
        for n_, src in enumerate(pair):
            pltpu.make_async_copy(src, (wus, wds)[n_].at[k], sw.at[k, n_]).start()
    for k, quarters in ((1, (c0, c1, c2, c3)), (3, (n0, n1, n2, n3))):
        for q_, src in enumerate(quarters):
            count = src.shape[1]
            to = pl.ds(pl.multiple_of(jnp.bitwise_xor(meta[3], q_) * count, 64), count)
            for n_, dst in enumerate((wus, wds)):
                pltpu.make_async_copy(src.at[n_], dst.at[k, to, :], sw.at[k, n_]).start()
    for cp in copies:
        cp.wait()
    gn = gain[...].astype(f32)

    def first_rows(i, carry):
        sl = pl.ds(pl.multiple_of(i * T, T), T)
        src = pl.ds(pl.multiple_of(lax.rem(i, per) * T, T), T)
        own = i < per
        x = jnp.where(own, xo[src, :], xx[src, :]).astype(f32)
        a = jnp.concatenate([am[sl, :], at[sl, :]], axis=1)
        m = x + dot(a, wo[...])
        mid[sl, :] = m
        fo[sl, :] = m
        h_s[sl, :] = norm(m, gn)[2]
        ct = jnp.where(own, co[src, :], cx[src, :])
        g_s[sl, :] = jnp.where(valid_rows(meta, i, rows), ct, jnp.zeros_like(ct))
        dh[sl, :] = jnp.zeros((T, width), f32)
        return carry

    lax.fori_loop(0, n, first_rows, 0)

    R = 512
    C = 768

    gus, gds = (gu0, gu1, gu2, gu3), (gd0, gd1, gd2, gd3)

    def stores(n_, slot):
        return [
            pltpu.make_async_copy(stu.at[slot], gus[n_], sg.at[slot, 0]),
            pltpu.make_async_copy(std.at[slot], gds[n_].at[pl.ds(0, width), :], sg.at[slot, 1]),
        ]

    def shard(k, carry):
        for cp in (
            pltpu.make_async_copy(u_o, wus.at[k], sw.at[k, 0]),
            pltpu.make_async_copy(d_o, wds.at[k], sw.at[k, 1]),
        ):
            cp.wait()

        def rows_step(t, c2):
            sl = pl.ds(pl.multiple_of(t * R, R), R)
            h, g = h_s[sl, :], g_s[sl, :]
            r = jnp.maximum(dot(h, wus[k]), 0.0)
            a = (r * r).astype(bf16)
            d = (dot(g, wds[k], NT) * 2.0 * r).astype(bf16)
            act[sl, :] = a
            du[sl, :] = d
            fo[sl, :] += dot(a, wds[k])
            dh[sl, :] += dot(d, wus[k], NT)
            return c2

        lax.fori_loop(0, 2 * rows // R, rows_step, 0)
        slot = lax.rem(k, 2)

        @pl.when(k >= 2)
        def _():
            for cp in stores(0, slot):
                cp.wait()

        def cols_step(t, c2):
            sl = pl.ds(pl.multiple_of(t * C, C), C)
            stu[slot, :, sl] = dot(h_s[...], du[:, sl], TN).astype(bf16)
            std[slot, sl, :] = dot(act[:, sl], g_s[...], TN).astype(bf16)
            return c2

        lax.fori_loop(0, width // C, cols_step, 0)
        for n_ in range(4):

            @pl.when(k == n_)
            def _(n_=n_):
                for cp in stores(n_, n_ % 2):
                    cp.start()

        return carry

    lax.fori_loop(0, 4, shard, 0)
    gg[...] = jnp.zeros_like(gg)

    def last_rows(i, carry):
        sl = pl.ds(pl.multiple_of(i * T, T), T)
        dst = pl.ds(pl.multiple_of(lax.rem(i, per) * T, T), T)
        ok = valid_rows(meta, i, rows)
        m = mid[sl, :]
        out = jnp.where(ok, fo[sl, :], 0.0)

        fo[sl, :] = out

        @pl.when(i < per)
        def _():
            own = oo.at[meta[2] // 2, dst, :]
            pltpu.make_async_copy(fo.at[sl, :], own, sd.at[1]).start()

        @pl.when(i >= per)
        def _():
            ox[dst, :] = out.astype(bf16)

        nm, inv, _ = norm(m, gn)
        d = dh[sl, :]
        dn = d * gn
        r = g_s[sl, :].astype(f32) + inv * (dn - nm * jnp.mean(dn * nm, axis=-1, keepdims=True))
        mid[sl, :] = r
        pltpu.make_async_copy(mid.at[sl, :], dmid.at[sl, :], sd.at[0]).start()
        db = r.astype(bf16)
        du[sl, :] = db
        da = dot(db, wo[...], NT).astype(bf16)
        dm[sl, :] = da[:, :half]
        dt[sl, :] = da[:, half:]
        gg[...] += jnp.sum(d * nm, axis=0, keepdims=True)
        return carry

    lax.fori_loop(0, n, last_rows, 0)
    gacc[0:half, :] = dot(am[...], du[...], TN)
    gacc[half:, :] = dot(at[...], du[...], TN)
    outs = [
        pltpu.make_async_copy(mid, dmid, sd.at[0]),
        pltpu.make_async_copy(fo.at[pl.ds(0, rows), :], oo.at[meta[2] // 2], sd.at[1]),
    ]
    for k, k_ in enumerate((1, 3, 0, 2)):
        shard_ = jnp.bitwise_xor(meta[2], k_)
        row = jnp.where(shard_ // 2 == core_of(meta), 0, half) + lax.rem(shard_, 2) * part
        sto[k] = gacc[pl.ds(pl.multiple_of(row, 64), part), :].astype(bf16)
        cp = pltpu.make_async_copy(sto.at[k], gds[k].at[pl.ds(width, part), :], st.at[k])
        cp.start()
        outs.append(cp)
    for slot in range(2):
        outs.extend(stores(2 + slot, slot))
    for cp in outs:
        cp.wait()


def ffn_call(meta, xo, xx, co, cx, am, at, gain, wos, ffs):
    rows, width = xo.shape
    half = am.shape[1]
    part = half // 2
    hid = ffs[0].shape[1]
    hbm = pl.BlockSpec(memory_space=pl.ANY)
    vm = lambda *shape: whole(shape)
    all_rows = 2 * rows
    return pl.pallas_call(
        ffn_body,
        out_shape=[
            sds((2, rows, width), f32),
            sds((rows, width), bf16),
            sds((all_rows, half), bf16),
            sds((all_rows, half), bf16),
            sds((1, width), f32),
            sds((all_rows, width), f32),
        ]
        + [sds((width, hid), bf16)] * 4
        + [sds((hid + part, width), bf16)] * 4,
        grid_spec=grid_spec(
            (1,),
            [vm(rows, width)] * 4 + [vm(all_rows, half)] * 2 + [vm(1, width)] + [hbm] * 14,
            [
                hbm,
                vm(rows, width),
                vm(all_rows, half),
                vm(all_rows, half),
                vm(1, width),
            ]
            + [hbm] * 9,
            [
                pltpu.VMEM((width, width), bf16),
                pltpu.VMEM((4, width, hid), bf16),
                pltpu.VMEM((4, hid, width), bf16),
                pltpu.VMEM((all_rows, width), f32),
                pltpu.VMEM((all_rows, width), bf16),
                pltpu.VMEM((all_rows, width), bf16),
                pltpu.VMEM((all_rows, width), f32),
                pltpu.VMEM((all_rows, width), f32),
                pltpu.VMEM((all_rows, hid), bf16),
                pltpu.VMEM((all_rows, hid), bf16),
                pltpu.VMEM((2, width, hid), bf16),
                pltpu.VMEM((2, hid, width), bf16),
                pltpu.VMEM((4, part, width), bf16),
                pltpu.VMEM((width, width), f32),
                pltpu.SemaphoreType.DMA((4, 2)),
                pltpu.SemaphoreType.DMA((4,)),
                pltpu.SemaphoreType.DMA((2, 2)),
                pltpu.SemaphoreType.DMA((2,)),
                pltpu.SemaphoreType.DMA((4,)),
            ],
        ),
        cost_estimate=cost(
            48 * all_rows * width * hid + 6 * all_rows * width * width, 40 * all_rows * width
        ),
        compiler_params=pltpu.CompilerParams(vmem_limit_bytes=62 * 2**20),
        name="ffn",
    )(meta, xo, xx, co, cx, am, at, gain, *wos, *ffs)


def projg_body(meta, h, dm, dt, keep, far, send, acc):
    rows = dm.shape[0]
    acc[...] = dot(h[0:rows, :], dm[...], TN) + dot(h[rows:, :], dt[...], TN)
    part = keep.shape[0]
    for ref, k, row in ((keep, 0, 0), (far, 2, 0), (send, 1, 0), (send, 3, part)):
        at = jnp.bitwise_xor(meta[2], k)
        ref[row : row + part, :] = acc[pl.ds(pl.multiple_of(at * part, 64), part), :].astype(bf16)


def projg_call(meta, h, dm, dt):
    length, width = h.shape
    cols = dm.shape[1]
    step = cols // 3
    d = pl.BlockSpec((length // 2, step), lambda j, m: (0, j))
    g = lambda rows: pl.BlockSpec((rows, step), lambda j, m: (0, j))
    part = width // 4
    return pl.pallas_call(
        projg_body,
        out_shape=[sds((rows, cols), bf16) for rows in (part, part, 2 * part)],
        grid_spec=grid_spec(
            (3,),
            [whole((length, width)), d, d],
            [g(part), g(part), g(2 * part)],
            [pltpu.VMEM((width, step), f32)],
        ),
        cost_estimate=cost(length, length),
        name="projg",
    )(meta, h, dm, dt)


def last_body(meta, xo, xx, dm, dt, wm, wt, dmid, gain, go, gx, gg):
    i = pl.program_id(0)
    per = pl.num_programs(0) // 2
    first = i < per
    x = jnp.where(first, xo[...], xx[...]).astype(f32)
    gn = gain[...].astype(f32)
    n, inv, _ = norm(x, gn)
    dh = dot(dm[...], wm[...], NT) + dot(dt[...], wt[...], NT)
    dn = dh * gn
    out = dmid[...] + inv * (dn - n * jnp.mean(dn * n, axis=-1, keepdims=True))

    @pl.when(first)
    def _():
        go[0] = out

    @pl.when(jnp.logical_not(first))
    def _():
        gx[...] = out.astype(bf16)

    ps = jnp.sum(dh * n, axis=0, keepdims=True)

    @pl.when(i == 0)
    def _():
        gg[...] = ps

    @pl.when(i > 0)
    def _():
        gg[...] += ps


def own_map(per):
    return lambda i, m: (jnp.minimum(i, per - 1), 0)


def nb_map(per):
    return lambda i, m: (jnp.maximum(i - per, 0), 0)


def last_call(meta, xo, xx, dm, dt, wm, wt, dmid, gain):
    rows, width = xo.shape
    cols = dm.shape[1]
    per = rows // T
    fst, snd = pl.BlockSpec((T, width), own_map(per)), pl.BlockSpec((T, width), nb_map(per))
    blk = lambda n: pl.BlockSpec((T, n), lambda i, m: (i, 0))
    return pl.pallas_call(
        last_body,
        out_shape=[sds((2, rows, width), f32), sds((rows, width), bf16), sds((1, width), f32)],
        grid_spec=grid_spec(
            (2 * per,),
            [fst, snd, blk(cols), blk(cols)]
            + [whole((width, cols))] * 2
            + [blk(width), whole((1, width))],
            [
                pl.BlockSpec((1, T, width), lambda i, m: (x_of(m), jnp.minimum(i, per - 1), 0)),
                snd,
                pl.BlockSpec((1, width), lambda i, m: (0, 0)),
            ],
        ),
        cost_estimate=cost(rows, rows),
        name="last",
    )(meta, xo, xx, dm, dt, wm, wt, dmid, gain)


def flip(size, bit):
    return [(i, i ^ bit) for i in range(size)]


def core_swap(v):
    return lax.ppermute(v, "head", CORE)


def x_swap(v):
    return lax.ppermute(v, "head", XNB)


def after(v, *deps):
    return lax.optimization_barrier((v, *deps))[0]


def halve(terms, index, count):
    rows = terms[0].shape[0] // count
    piece = lambda t, k: lax.dynamic_slice_in_dim(t, jnp.bitwise_xor(index, k) * rows, rows, 0)
    total = lambda k: sum(piece(t, k).astype(f32) for t in terms)
    return [total(k).astype(bf16) for k in range(1, count)], total(0)


def strides(dp):
    out = [1]
    while 2 * out[-1] < dp:
        out.append(2 * out[-1])
    return out


def side(stride):
    return lax.axis_index("dp") // stride % 2


def swap(v, stride, dp):
    return lax.ppermute(v, "dp", flip(dp, stride))


def rows_as(got, vs):
    out, row = [], 0
    for v in vs:
        out.append(got[row : row + v.shape[0]])
        row += v.shape[0]
    return out


def swap_both(vs, stride, dp):
    return rows_as(swap(jnp.concatenate(vs, axis=0), stride, dp), vs)


def scatter(sums, stride, dp):
    halves = [halve(terms, side(stride), 2) for terms in sums]
    send = jnp.concatenate([h[0][0] for h in halves], axis=0)
    got = swap(send, stride, dp)
    out, row = [], 0
    for (part,), keep in halves:
        out.append([keep, got[row : row + part.shape[0]]])
        row += part.shape[0]
    return out, send


def join(mine, got, stride):
    upper = side(stride) == 1
    return jnp.concatenate([jnp.where(upper, got, mine), jnp.where(upper, mine, got)], axis=0)


def total(terms):
    return sum(t.astype(f32) for t in terms)


def local(dp, inputs, lengths, w_query, w_key, w_value, w_out, w_up, w_down, conv_taps, gain_attn, gain_ff, cotangent):
    hd = lax.axis_index("head")
    x, c, y = hd // 2, hd % 2, lax.axis_index("dp") % 2
    q = lax.axis_index("dp") % 4
    width = inputs.shape[2]
    part = w_query.shape[0]
    half = 2 * part
    pick = lambda v, k: lax.dynamic_index_in_dim(v, k, 0, keepdims=False)
    y_swap = lambda v: lax.ppermute(v, "dp", flip(dp, 1))
    order = lambda own, nb: lax.dynamic_update_slice_in_dim(own, nb[None].astype(f32), 1 - x, 0)
    meta = jnp.concatenate([lengths, jnp.stack([hd, q])]).astype(jnp.int32)
    gain1, gain2 = gain_attn.reshape(1, width), gain_ff.reshape(1, width)

    mask = (jnp.arange(2) == c)[None, None, :, None]
    tap_rows = jnp.where(mask, conv_taps.transpose(1, 0, 2)[:, :, None, :], 0).reshape(3, 3 * half)
    tap_rows = jnp.concatenate([tap_rows[:, :width], jnp.pad(tap_rows[:, width:], ((0, 0), (0, half)))], axis=0)
    tap_rows = jnp.pad(tap_rows, ((0, 10), (0, 0)))

    def packed(k):
        cut = lambda w: lax.dynamic_slice_in_dim(w, k * half, half, 1)
        fold = cut(w_value)
        return jnp.concatenate(
            [
                jnp.concatenate([cut(w_query), cut(w_key)], axis=1),
                jnp.concatenate([fold[: part // 2], fold[part // 2 :]], axis=1),
                tap_rows,
            ],
            axis=0,
        )

    w_core = core_swap(packed(1 - c))
    w_mine = packed(c)
    x_own = pick(inputs, x)
    rows = x_own.shape[0]
    pack = x_swap(jnp.concatenate([pick(inputs, 1 - x), w_mine, w_core], axis=0))
    x_core = core_swap(x_own)
    count = width // 4
    quarter = lambda w: lax.dynamic_slice_in_dim(w, q * count, count, 0)
    wo_c = core_swap(w_out)
    c_own = pick(cotangent, x)
    ff_src = jnp.stack([quarter(w_up), quarter(w_down)])
    ff_own = jnp.stack([w_up, w_down])
    pack2 = jnp.concatenate([pick(cotangent, 1 - x), w_out, wo_c], axis=0)
    pack, ff_src, ff_own, pack2, c_own, meta, x_core = lax.optimization_barrier(
        (pack, ff_src, ff_own, pack2, c_own, meta, x_core)
    )
    x_cnb = core_swap(pack[:rows])
    h1, raw, mix, w_full, taps = qkv_call(meta, x_own, x_core, x_cnb, w_mine, w_core, pack, gain1)

    ff_first, pack2 = x_swap(ff_src), x_swap(pack2)
    ff_c = core_swap(ff_own)
    src = after(ff_first, mix)
    ff_n = [swap(src, k, dp) for k in (1, 2, 3)]
    a_mine, a_send, lse = att_fwd_call(meta, after(mix, src, ff_c))
    a_got = core_swap(a_send)
    w_other = core_swap(w_full)
    *ff_n, pack2 = lax.optimization_barrier((*ff_n, pack2, a_mine))[:-1]
    ff_n = [src, *ff_n]
    ff_cn = [core_swap(v) for v in ff_n]
    out_own, out_nb, d_mine, d_send, gg2, dmid, *gw = ffn_call(
        meta, x_own, pack, c_own, pack2, a_mine, a_got, after(gain2, w_other),
        (w_out, wo_c, pack2),
        (w_up, w_down, ff_c, *ff_n, *ff_cn),
    )
    d_got = core_swap(d_send)

    _, *rest = strides(dp)
    un, dn, do, uo = [core_swap(gw[k]) for k in (1, 5, 4, 0)]
    nu = total((gw[3], un)).astype(bf16)
    xu = x_swap(nu)
    (dn_send,), dn_keep = halve((gw[7], dn), y, 2)
    (do_send,), do_keep = halve((gw[6], do), y, 2)
    yn, yo = y_swap(dn_send), y_swap(do_send)
    out_x = x_swap(after(out_nb, nu))
    pairs = width // 256
    bwd = lambda m, p, n, into: att_bwd_call(
        meta, m, raw, a_mine, a_send, d_mine, d_got, lse, taps, p, n, into
    )
    *dall, gt_a = bwd(after(mix, nu, dn_send, do_send), 0, pairs - 1, None)
    xu, yn, yo, out_x = lax.optimization_barrier((xu, yn, yo, out_x, gt_a))[:4]
    (u_send,), u_keep = halve((gw[2], uo, xu), y, 2)
    nd = total((dn_keep, yn)).astype(bf16)
    yu, xd = y_swap(u_send), x_swap(nd)
    p_mine, p_theirs, gt_b = bwd(after(mix, u_send, nd), pairs - 1, 1, dall)
    p_got = core_swap(p_theirs)
    gt = jnp.concatenate([gt_a, gt_b], axis=1)
    yu, xd = lax.optimization_barrier((yu, xd, gt_b))[:2]
    sums, sent = scatter([[u_keep, yu], [do_keep, yo, xd]], rest[0], dp)
    keep, far, send = projg_call(meta, after(h1, sent), p_mine, p_theirs)
    flat = lax.optimization_barrier((*sums[0], *sums[1], keep))[:-1]
    sums, sent = scatter([flat[:2], flat[2:]], rest[1], dp)
    got = core_swap(after(send, sent))
    far = x_swap(jnp.concatenate([far, got[part:]], axis=0))
    gi_own, gi_nb, gg1 = last_call(
        meta, x_own, pack, p_mine, p_got, w_full, w_other, after(dmid, sent), gain1
    )
    *flat, gt, gg1 = lax.optimization_barrier((*sums[0], *sums[1], gt, x_swap(core_swap(gg1))))
    sums = [flat[:2], flat[2:]]
    for stride in rest[2:]:
        sums, _ = scatter(sums, stride, dp)
    vs = [total(t).astype(bf16) for t in sums]
    far = after(far, *vs)
    far, far2 = far[:part], far[part:]
    ga, gb = keep.astype(f32) + far.astype(f32), got[:part].astype(f32) + far2.astype(f32)
    g_send, g_keep = jnp.where(y == 0, gb, ga).astype(bf16), jnp.where(y == 0, ga, gb)
    pt = [g_keep, y_swap(g_send)]
    gi_got = x_swap(after(gi_nb, g_send))
    for stride in reversed(rest[1:]):
        vs = [join(v, g, stride) for v, g in zip(vs, swap_both(vs, stride, dp))]
    (pt,), sent = scatter([pt], rest[0], dp)
    *vs, _ = lax.optimization_barrier((*vs, sent))
    packed_vs = jnp.concatenate(vs, axis=0)
    near_got = swap(packed_vs, rest[0], dp)
    across = rows_as(y_swap(packed_vs), vs)
    for stride in rest[1:]:
        (pt,), _ = scatter([pt], stride, dp)
    others, also = rows_as(near_got, vs), rows_as(y_swap(near_got), vs)
    ps = after(total(pt).astype(bf16), near_got)
    for stride in reversed(rest):
        ps = join(ps, swap(ps, stride, dp), stride)
    ps_got = y_swap(ps)
    whole_of = lambda k: join(
        join(vs[k], others[k], rest[0]), join(across[k], also[k], rest[0]), 1
    ).astype(f32)
    grad_up, gd_all = whole_of(0), whole_of(1)
    grad_down, grad_out = gd_all[: w_down.shape[0]], gd_all[w_down.shape[0] :]
    lo, hi = jnp.where(y == c, ps, ps_got), jnp.where(y == c, ps_got, ps)
    third = lambda v, w: v[:, w * half : w * half + half]
    grads = [jnp.concatenate([third(lo, w), third(hi, w)], axis=1).astype(f32) for w in range(3)]

    gt = gt[:9].reshape(9, 2, part).transpose(1, 0, 2)
    gt = jnp.where(jnp.arange(2)[:, None, None, None] == c, gt[None], 0.0).reshape(4, 9, part)
    gains = jnp.concatenate([gg1, gg2], axis=0).reshape(2, 4, part).transpose(1, 0, 2)
    small = jnp.concatenate([gt, gains, jnp.zeros((4, 5, part), f32)], axis=1)
    small = jnp.broadcast_to(small[:, None], (4, dp, 16, part)).reshape(4 * dp, 16, part)
    small = jnp.sum(lax.all_to_all(small, ("head", "dp"), 0, 0, tiled=True), axis=0)
    output = order(after(out_own, g_send), out_x)
    grad_input = order(after(gi_own, ps), gi_got)
    return (
        output,
        grad_input,
        *grads,
        grad_out,
        grad_up,
        grad_down,
        small[:9].reshape(3, 3, part),
        small[9],
        small[10],
    )


def solution(mesh):
    placed = (
        P("dp", "head", None),
        P("dp"),
        P("head", None),
        P("head", None),
        P("head", None),
        P("head", None),
        P(None, "head"),
        P("head", None),
        P(None, None, "head"),
        P(),
        P(),
        P("dp", "head", None),
    )
    return jax.shard_map(
        functools.partial(local, mesh.shape["dp"]),
        mesh=mesh,
        in_specs=placed,
        out_specs=(
            P("dp", "head", None),
            P("dp", "head", None),
            P("head", None),
            P("head", None),
            P("head", None),
            P("head", None),
            P(None, "head"),
            P("head", None),
            P(None, None, "head"),
            P("head"),
            P("head"),
        ),
        check_vma=False,
    )
```

profile of v0, /device:TPU:0, one launch (start us, length us, event | category | flops | bytes accessed | tf_op | source)
XLA Modules:
  0.0 379.1 jit_solution(12124742954488636496)
XLA Ops:
  1.8 2.1 bitcast_dynamic-update-slice_fusion
  7.4 1.5 collective-permute-done.wb
  10.4 2.9 collective-permute-start.1
  16.7 2.5 dynamic-slice_bitcast_fusion.1
  20.1 1.6 pad_maximum_fusion
  22.9 28.4 %collective-permute-done.1.pack.xx = bf16[1120,768]{1,0:T(8,128)(2,1)S(1)} collective-permute-done((bf16[1120,768]{1,0:T(8,128)(2,1)}, bf16[1120,768]{1,0:T(8,128)(2,1)S(1)}, u32[]{:S(2)}, u32[]{:S(2)}) %collective-permute-start.1) | collective-permute-done | bytes 1720352 | tf_op jit(solution)/shard_map/ppermute | solution.py:778
  52.5 1.7 collective-permute-start.4
  54.3 2.3 collective-permute-done.5.x3
  57.5 13.6 %qkv.1 = (bf16[2048,768]{1,0:T(8,128)(2,1)}, bf16[2048,1152]{1,0:T(8,128)(2,1)}, bf16[2048,1152]{1,0:T(8,128)(2,1)}, bf16[768,1152]{1,0:T(8,128)(2,1)}, f32[8,1152]{1,0:T(8,128)}) custom-call(s32[4]{0:T(128)} %pad_add_fusion.meta, bf16[512,768]{1,0:T(8,128)(2,1)} %copy-done.1, bf16[512,768]{1,0:T(8,128)(2,1)} %collective-permute-done.3.x2, ...), custom_call_target="tpu_custom_call" | custom-call | flops 3623878656 | bytes 15728640 | tf_op jit(solution)/shard_map/qkv/pallas_call | solution.py:131
  71.5 1.7 collective-permute-start.9
  73.2 1.5 collective-permute-start.6
  74.8 1.6 collective-permute-start.7
  76.7 27.3 %attn_fwd.1 = (bf16[1024,384]{1,0:T(8,128)(2,1)}, bf16[1024,384]{1,0:T(8,128)(2,1)}, f32[3,2,2048]{2,1,0:T(2,128)}) custom-call(s32[4]{0:T(128)} %pad_add_fusion.meta, bf16[2048,1152]{1,0:T(8,128)(2,1)} %get-tuple-element.127.q_ref.k_ref.v_ref, bf16[2048,1152]{1,0:T(8,128)(2,1)} %get-tuple-element.127.q_ref.k_ref.v_ref, ...), custom_call_target="tpu_custom_call" | custom-call | flops 12884901888 | bytes 6291456 | tf_op jit(solution)/shard_map/attn_fwd/pallas_call | solution.py:255
  105.9 1.6 collective-permute-done.13.c0
  110.8 49.4 %ffn.1 = (f32[2,512,768]{2,1,0:T(8,128)}, bf16[512,768]{1,0:T(8,128)(2,1)}, bf16[1024,384]{1,0:T(8,128)(2,1)}, bf16[1024,384]{1,0:T(8,128)(2,1)}, f32[1,768]{1,0...) custom-call(s32[4]{0:T(128)} %pad_add_fusion.meta, ...), custom_call_target="tpu_custom_call" | custom-call | flops 32614907904 | bytes 31457280 | tf_op jit(solution)/shard_map/ffn/pallas_call | solution.py:623
  161.4 1.9 collective-permute-done.18
  164.4 3.0 add_convert_fusion
  167.7 1.8 collective-permute-start.24
  170.5 1.5 collective-permute-start.21
  172.0 2.6 add_convert_fusion.2
  175.1 42.7 %attn_bwd.2 = (bf16[1024,1152]{1,0:T(8,128)(2,1)}, bf16[1024,1152]{1,0:T(8,128)(2,1)}, f32[16,256]{1,0:T(8,128)}) custom-call(s32[4]{0:T(128)} %pad_add_fusion.meta, bf16[2048,1152]{1,0:T(8,128)(2,1)} %get-tuple-element.127.q_ref.k_ref.v_ref, bf16[2048,1152]{1,0:T(8,128)(2,1)} %get-tuple-element.127.q_ref.k_ref.v_ref, ...), custom_call_target="tpu_custom_call" | custom-call | flops 15032385536 | bytes 10485760 | tf_op jit(solution)/shard_map/attn_bwd/pallas_call | solution.py:407
  217.9 2.6 add_convert_fusion.1
  220.8 2.9 convert_add_fusion.1
  223.7 1.7 collective-permute-start.26
  225.4 23.5 %attn_bwd.3 = (bf16[1024,1152]{1,0:T(8,128)(2,1)}, bf16[1024,1152]{1,0:T(8,128)(2,1)}, f32[16,128]{1,0:T(8,128)}) custom-call(s32[4]{0:T(128)} %pad_add_fusion.meta, bf16[2048,1152]{1,0:T(8,128)(2,1)} %get-tuple-element.127.q_ref.k_ref.v_ref, ...), custom_call_target="tpu_custom_call", output_to_operand_aliasing={{0}: (13, {}), {1}: (14, {})} | custom-call | flops 7516192768 | bytes 5242880 | tf_op jit(solution)/shard_map/attn_bwd/pallas_call | solution.py:407
  251.1 1.5 convert_add_fusion.4
  252.6 1.6 collective-permute-start.28
  254.3 9.6 %projg.1 = (bf16[192,1152]{1,0:T(8,128)(2,1)}, bf16[192,1152]{1,0:T(8,128)(2,1)}, bf16[384,1152]{1,0:T(8,128)(2,1)}) custom-call(s32[4]{0:T(128)} %pad_add_fusion.meta, bf16[2048,768]{1,0:T(8,128)(2,1)} %get-tuple-element.134.h, bf16[1024,1152]{1,0:T(8,128)(2,1)} %get-tuple-element.135.dm, bf16[1024,1152]{1,0:T(8,128)(2,1)} %get-tuple-element.136.dt), custom_call_target="tpu_custom_call" | custom-call | flops 2048 | bytes 2048 | tf_op jit(solution)/shard_map/projg/pallas_call | solution.py:692
  263.8 6.1 %collective-permute-done.28 = bf16[432,768]{1,0:T(8,128)(2,1)S(1)} collective-permute-done((bf16[432,768]{1,0:T(8,128)(2,1)S(1)}, bf16[432,768]{1,0:T(8,128)(2,1)S(1)}, u32[]{:S(2)}, u32[]{:S(2)}) %collective-permute-start.28) | collective-permute-done | bytes 663584 | tf_op jit(solution)/shard_map/ppermute | solution.py:804
  270.3 2.7 collective-permute-start.31
  273.2 11.2 %last.1 = (f32[2,512,768]{2,1,0:T(8,128)}, bf16[512,768]{1,0:T(8,128)(2,1)}, f32[1,768]{1,0:T(1,128)}) custom-call(s32[4]{0:T(128)} %pad_add_fusion.meta, bf16[512,768]{1,0:T(8,128)(2,1)} %copy-done.1, bf16[1120,768]{1,0:T(8,128)(2,1)} %copy-done, bf16[1024,1152]{1,0:T(8,128)(2,1)} %get-tuple-element.135.dm, bf16[1024,1152]{1,0:T(8,128)(2,1)} %collective-permute-done.32.dt, ...), custom_call_target="tpu_custom_call" | custom-call | flops 512 | bytes 512 | tf_op jit(solution)/shard_map/last/pallas_call | solution.py:750
  284.7 3.8 %collective-permute-done.31 = bf16[216,768]{1,0:T(8,128)(2,1)S(1)} collective-permute-done((bf16[216,768]{1,0:T(8,128)(2,1)S(1)}, bf16[216,768]{1,0:T(8,128)(2,1)S(1)}, u32[]{:S(2)}, u32[]{:S(2)}) %collective-permute-start.31) | collective-permute-done | bytes 331808 | tf_op jit(solution)/shard_map/ppermute | solution.py:804
  288.6 1.5 collective-permute-start.34
  293.7 5.3 %all-to-all-start = ((f32[32,16,192]{2,1,0:T(8,128)}), f32[32,16,192]{2,1,0:T(8,128)S(1)}, u32[]{:S(2)}, u32[]{:S(2)}) async-start(f32[32,16,192]{2,1,0:T(8,128)} %bitcast.16), calls=%async_computation | async-start | bytes 1048576 | tf_op jit(solution)/shard_map/all_to_all | solution.py:974
  299.0 16.7 %collective-permute-done.38 = bf16[216,768]{1,0:T(8,128)(2,1)S(1)} collective-permute-done((bf16[216,768]{1,0:T(8,128)(2,1)S(1)}, bf16[216,768]{1,0:T(8,128)(2,1)S(1)}, u32[]{:S(2)}, u32[]{:S(2)}) %collective-permute-start.38) | collective-permute-done | bytes 331808 | tf_op jit(solution)/shard_map/ppermute | solution.py:804
  316.2 2.2 fusion.1
  321.8 6.7 %collective-permute-done.35 = bf16[192,1152]{1,0:T(8,128)(2,1)S(1)} collective-permute-done((bf16[192,1152]{1,0:T(8,128)(2,1)}, bf16[192,1152]{1,0:T(8,128)(2,1)S(1)}, u32[]{:S(2)}, u32[]{:S(2)}) %collective-permute-start.35) | collective-permute-done | bytes 442400 | tf_op jit(solution)/shard_map/ppermute | solution.py:847
  328.6 1.8 collective-permute-start.36
  330.8 7.4 %collective-permute-done.36 = bf16[96,1152]{1,0:T(8,128)(2,1)S(1)} collective-permute-done((bf16[96,1152]{1,0:T(8,128)(2,1)S(1)}, bf16[96,1152]{1,0:T(8,128)(2,1)S(1)}, u32[]{:S(2)}, u32[]{:S(2)}) %collective-permute-start.36) | collective-permute-done | bytes 221216 | tf_op jit(solution)/shard_map/ppermute | solution.py:804
  338.2 2.3 collective-permute-start.37
  342.9 6.4 %collective-permute-done.37 = bf16[48,1152]{1,0:T(8,128)(2,1)S(1)} collective-permute-done((bf16[48,1152]{1,0:T(8,128)(2,1)S(1)}, bf16[48,1152]{1,0:T(8,128)(2,1)S(1)}, u32[]{:S(2)}, u32[]{:S(2)}) %collective-permute-start.37) | collective-permute-done | bytes 110624 | tf_op jit(solution)/shard_map/ppermute | solution.py:804
  350.6 2.3 collective-permute-start.40
  353.5 2.8 collective-permute-done.40
  356.4 3.5 collective-permute-start.41
  360.0 3.9 %collective-permute-done.41 = bf16[96,1152]{1,0:T(8,128)(2,1)S(1)} collective-permute-done((bf16[96,1152]{1,0:T(8,128)(2,1)S(1)}, bf16[96,1152]{1,0:T(8,128)(2,1)S(1)}, u32[]{:S(2)}, u32[]{:S(2)}) %collective-permute-start.41) | collective-permute-done | bytes 221216 | tf_op jit(solution)/shard_map/ppermute | solution.py:804
  365.3 5.5 %collective-permute-done.44 = bf16[432,768]{1,0:T(8,128)(2,1)S(1)} collective-permute-done((bf16[432,768]{1,0:T(8,128)(2,1)S(1)}, bf16[432,768]{1,0:T(8,128)(2,1)S(1)}, u32[]{:S(2)}, u32[]{:S(2)}) %collective-permute-start.44) | collective-permute-done | bytes 663584 | tf_op jit(solution)/shard_map/ppermute | solution.py:847
  372.3 1.6 fusion
  373.8 1.6 maximum_convert_fusion
  (220 shorter events, 45.7 us)
Async XLA Ops:
  6.9 1.9 collective-permute-start
  10.4 40.9 %collective-permute-start.1 = (bf16[1120,768]{1,0:T(8,128)(2,1)}, bf16[1120,768]{1,0:T(8,128)(2,1)S(1)}, u32[]{:S(2)}, u32[]{:S(2)}) collective-permute-start(bf16[1120,768]{1,0:T(8,128)(2,1)} %constant_dynamic-update-slice_fusion), channel_id=1, source_target_pairs={{0,2},{2,0},{1,3},{3,1},{4,6},{6,4},{5,7},{7,5},{8,10},{10,8},{9,1... | collective-permute-start | bytes 5160968 | tf_op jit(solution)/shard_map/ppermute | solution.py:778
  13.2 8.5 %collective-permute-start.2 = (bf16[192,768]{1,0:T(8,128)(2,1)S(1)}, bf16[192,768]{1,0:T(8,128)(2,1)S(1)}, u32[]{:S(2)}, u32[]{:S(2)}) collective-permute-start(bf16[192,768]{1,0:T(8,128)(2,1)S(1)} %copy-done.17), channel_id=1, source_target_pairs={{0,1},{1,0},{2,3},{3,2},{4,5},{5,4},{6,7},{7,6},{8,9},{9,8},{10,11... | collective-permute-start | bytes 884744 | tf_op jit(solution)/shard_map/ppermute | solution.py:774
  14.4 8.5 %collective-permute-start.3 = (bf16[512,768]{1,0:T(8,128)(2,1)S(1)}, bf16[512,768]{1,0:T(8,128)(2,1)}, u32[]{:S(2)}, u32[]{:S(2)}) collective-permute-start(bf16[512,768]{1,0:T(8,128)(2,1)S(1)} %dynamic-slice_bitcast_fusion.x0.xo), channel_id=1, source_target_pairs={{0,1},{1,0},{2,3},{3,2},{4,5},{5,4},{6,7},{7,6},{8,9},{9,8},{10,11... | collective-permute-start | bytes 2359304 | tf_op jit(solution)/shard_map/ppermute | solution.py:774
  51.3 25.0 %collective-permute-start.10 = (bf16[2,768,768]{2,1,0:T(8,128)(2,1)}, bf16[2,768,768]{2,1,0:T(8,128)(2,1)}, u32[]{:S(2)}, u32[]{:S(2)}) collective-permute-start(bf16[2,768,768]{2,1,0:T(8,128)(2,1)} %pad_maximum_fusion), channel_id=1, source_target_pairs={{0,1},{1,0},{2,3},{3,2},{4,5},{5,4},{6,7},{7,6},{8,9},{9,8},{10,11... | collective-permute-start | bytes 7077896 | tf_op jit(solution)/shard_map/ppermute | solution.py:774
  51.4 5.2 %collective-permute-start.5 = (bf16[512,768]{1,0:T(8,128)(2,1)S(1)}, bf16[512,768]{1,0:T(8,128)(2,1)S(1)}, u32[]{:S(2)}, u32[]{:S(2)}) collective-permute-start(bf16[512,768]{1,0:T(8,128)(2,1)S(1)} %slice.111), channel_id=1, source_target_pairs={{0,1},{1,0},{2,3},{3,2},{4,5},{5,4},{6,7},{7,6},{8,9},{9,8},{10,11... | collective-permute-start | bytes 2359304 | tf_op jit(solution)/shard_map/ppermute | solution.py:774
  52.5 20.7 %collective-permute-start.4 = (bf16[2,192,768]{2,1,0:T(8,128)(2,1)}, bf16[2,192,768]{2,1,0:T(8,128)(2,1)}, u32[]{:S(2)}, u32[]{:S(2)}) collective-permute-start(bf16[2,192,768]{2,1,0:T(8,128)(2,1)} %pad_maximum_fusion.9), channel_id=1, source_target_pairs={{0,2},{2,0},{1,3},{3,1},{4,6},{6,4},{5,7},{7,5},{8,10},{10,8},{9,1... | collective-permute-start | bytes 1769480 | tf_op jit(solution)/shard_map/ppermute | solution.py:778
  71.1 34.1 %collective-permute-start.12 = (bf16[768,1152]{1,0:T(8,128)(2,1)}, bf16[768,1152]{1,0:T(8,128)(2,1)}, u32[]{:S(2)}, u32[]{:S(2)}) collective-permute-start(bf16[768,1152]{1,0:T(8,128)(2,1)} %get-tuple-element.101.wm), channel_id=1, source_target_pairs={{0,1},{1,0},{2,3},{3,2},{4,5},{5,4},{6,7},{7,6},{8,9},{9,8},{10,11... | collective-permute-start | bytes 5308424 | tf_op jit(solution)/shard_map/ppermute | solution.py:774
  71.5 33.2 %collective-permute-start.9 = (bf16[896,768]{1,0:T(8,128)(2,1)S(1)}, bf16[896,768]{1,0:T(8,128)(2,1)S(1)}, u32[]{:S(2)}, u32[]{:S(2)}) collective-permute-start(bf16[896,768]{1,0:T(8,128)(2,1)S(1)} %copy-done.7), channel_id=1, source_target_pairs={{0,2},{2,0},{1,3},{3,1},{4,6},{6,4},{5,7},{7,5},{8,10},{10,8},{9,1... | collective-permute-start | bytes 4128776 | tf_op jit(solution)/shard_map/ppermute | solution.py:778
  73.2 32.1 %copy-start.23 = (bf16[768]{0:T(1024)(128)(2,1)S(1)}, bf16[768]{0:T(1024)(128)(2,1)}, u32[]{:S(2)}) copy-start(bf16[768]{0:T(1024)(128)(2,1)} %param.22) | copy-start | bytes 4612
  73.2 30.8 %collective-permute-start.6 = (bf16[2,192,768]{2,1,0:T(8,128)(2,1)}, bf16[2,192,768]{2,1,0:T(8,128)(2,1)}, u32[]{:S(2)}, u32[]{:S(2)}) collective-permute-start(bf16[2,192,768]{2,1,0:T(8,128)(2,1)} %collective-permute-done.4.n0), channel_id=1, source_target_pairs={{0,4},{4,0},{8,12},{12,8},{16,20},{20,16},{24,28},{28,24},{1,5},{5... | collective-permute-start | bytes 1769480 | tf_op jit(solution)/shard_map/ppermute | solution.py:804
  74.8 29.4 %collective-permute-start.7 = (bf16[2,192,768]{2,1,0:T(8,128)(2,1)}, bf16[2,192,768]{2,1,0:T(8,128)(2,1)}, u32[]{:S(2)}, u32[]{:S(2)}) collective-permute-start(bf16[2,192,768]{2,1,0:T(8,128)(2,1)} %collective-permute-done.4.n0), channel_id=1, source_target_pairs={{0,8},{4,12},{8,0},{12,4},{16,24},{20,28},{24,16},{28,20},{1,9},{5... | collective-permute-start | bytes 1769480 | tf_op jit(solution)/shard_map/ppermute | solution.py:804
  76.3 28.3 %collective-permute-start.8 = (bf16[2,192,768]{2,1,0:T(8,128)(2,1)}, bf16[2,192,768]{2,1,0:T(8,128)(2,1)}, u32[]{:S(2)}, u32[]{:S(2)}) collective-permute-start(bf16[2,192,768]{2,1,0:T(8,128)(2,1)} %collective-permute-done.4.n0), channel_id=1, source_target_pairs={{0,12},{4,8},{8,4},{12,0},{16,28},{20,24},{24,20},{28,16},{1,13},{... | collective-permute-start | bytes 1769480 | tf_op jit(solution)/shard_map/ppermute | solution.py:804
  104.1 5.9 %collective-permute-start.11 = (bf16[1024,384]{1,0:T(8,128)(2,1)}, bf16[1024,384]{1,0:T(8,128)(2,1)}, u32[]{:S(2)}, u32[]{:S(2)}) collective-permute-start(bf16[1024,384]{1,0:T(8,128)(2,1)} %get-tuple-element.100.ot), channel_id=1, source_target_pairs={{0,1},{1,0},{2,3},{3,2},{4,5},{5,4},{6,7},{7,6},{8,9},{9,8},{10,11... | collective-permute-start | bytes 2359304 | tf_op jit(solution)/shard_map/ppermute | solution.py:774
  104.2 3.3 collective-permute-start.13
  104.7 3.7 collective-permute-start.14
  104.8 4.3 %collective-permute-start.15 = (bf16[2,192,768]{2,1,0:T(8,128)(2,1)}, bf16[2,192,768]{2,1,0:T(8,128)(2,1)S(1)}, u32[]{:S(2)}, u32[]{:S(2)}) collective-permute-start(bf16[2,192,768]{2,1,0:T(8,128)(2,1)} %collective-permute-done.7.n2), channel_id=1, source_target_pairs={{0,1},{1,0},{2,3},{3,2},{4,5},{5,4},{6,7},{7,6},{8,9},{9,8},{10,11... | collective-permute-start | bytes 1769480 | tf_op jit(solution)/shard_map/ppermute | solution.py:774
  105.2 4.8 %collective-permute-start.16 = (bf16[2,192,768]{2,1,0:T(8,128)(2,1)}, bf16[2,192,768]{2,1,0:T(8,128)(2,1)S(1)}, u32[]{:S(2)}, u32[]{:S(2)}) collective-permute-start(bf16[2,192,768]{2,1,0:T(8,128)(2,1)} %collective-permute-done.8.n3), channel_id=1, source_target_pairs={{0,1},{1,0},{2,3},{3,2},{4,5},{5,4},{6,7},{7,6},{8,9},{9,8},{10,11... | collective-permute-start | bytes 1769480 | tf_op jit(solution)/shard_map/ppermute | solution.py:774
  160.2 3.1 collective-permute-start.18
  160.4 7.3 %collective-permute-start.20 = (bf16[960,768]{1,0:T(8,128)(2,1)}, bf16[960,768]{1,0:T(8,128)(2,1)S(1)}, u32[]{:S(2)}, u32[]{:S(2)}) collective-permute-start(bf16[960,768]{1,0:T(8,128)(2,1)} %get-tuple-element.113), channel_id=1, source_target_pairs={{0,1},{1,0},{2,3},{3,2},{4,5},{5,4},{6,7},{7,6},{8,9},{9,8},{10,11... | collective-permute-start | bytes 4423688 | tf_op jit(solution)/shard_map/ppermute | solution.py:774
  160.8 9.7 %collective-permute-start.22 = (bf16[960,768]{1,0:T(8,128)(2,1)}, bf16[960,768]{1,0:T(8,128)(2,1)}, u32[]{:S(2)}, u32[]{:S(2)}) collective-permute-start(bf16[960,768]{1,0:T(8,128)(2,1)} %get-tuple-element.115), channel_id=1, source_target_pairs={{0,1},{1,0},{2,3},{3,2},{4,5},{5,4},{6,7},{7,6},{8,9},{9,8},{10,11... | collective-permute-start | bytes 4423688 | tf_op jit(solution)/shard_map/ppermute | solution.py:774
  160.9 13.7 %collective-permute-start.25 = (bf16[1024,384]{1,0:T(8,128)(2,1)}, bf16[1024,384]{1,0:T(8,128)(2,1)}, u32[]{:S(2)}, u32[]{:S(2)}) collective-permute-start(bf16[1024,384]{1,0:T(8,128)(2,1)} %get-tuple-element.120), channel_id=1, source_target_pairs={{0,1},{1,0},{2,3},{3,2},{4,5},{5,4},{6,7},{7,6},{8,9},{9,8},{10,11... | collective-permute-start | bytes 2359304 | tf_op jit(solution)/shard_map/ppermute | solution.py:774
  161.3 59.5 %collective-permute-start.17 = (bf16[768,768]{1,0:T(8,128)(2,1)}, bf16[768,768]{1,0:T(8,128)(2,1)}, u32[]{:S(2)}, u32[]{:S(2)}) collective-permute-start(bf16[768,768]{1,0:T(8,128)(2,1)} %get-tuple-element.109), channel_id=1, source_target_pairs={{0,1},{1,0},{2,3},{3,2},{4,5},{5,4},{6,7},{7,6},{8,9},{9,8},{10,11... | collective-permute-start | bytes 3538952 | tf_op jit(solution)/shard_map/ppermute | solution.py:774
  167.4 50.4 %collective-permute-start.19 = (bf16[768,768]{1,0:T(8,128)(2,1)}, bf16[768,768]{1,0:T(8,128)(2,1)}, u32[]{:S(2)}, u32[]{:S(2)}) collective-permute-start(bf16[768,768]{1,0:T(8,128)(2,1)} %add_convert_fusion), channel_id=1, source_target_pairs={{0,2},{2,0},{1,3},{3,1},{4,6},{6,4},{5,7},{7,5},{8,10},{10,8},{9,1... | collective-permute-start | bytes 3538952 | tf_op jit(solution)/shard_map/ppermute | solution.py:778
  167.7 50.1 %collective-permute-start.24 = (bf16[512,768]{1,0:T(8,128)(2,1)}, bf16[512,768]{1,0:T(8,128)(2,1)}, u32[]{:S(2)}, u32[]{:S(2)}) collective-permute-start(bf16[512,768]{1,0:T(8,128)(2,1)} %get-tuple-element.117), channel_id=1, source_target_pairs={{0,2},{2,0},{1,3},{3,1},{4,6},{6,4},{5,7},{7,5},{8,10},{10,8},{9,1... | collective-permute-start | bytes 2359304 | tf_op jit(solution)/shard_map/ppermute | solution.py:778
  170.5 47.3 %collective-permute-start.21 = (bf16[480,768]{1,0:T(8,128)(2,1)}, bf16[480,768]{1,0:T(8,128)(2,1)}, u32[]{:S(2)}, u32[]{:S(2)}) collective-permute-start(bf16[480,768]{1,0:T(8,128)(2,1)} %add_convert_fusion.3), channel_id=1, source_target_pairs={{0,4},{4,0},{8,12},{12,8},{16,20},{20,16},{24,28},{28,24},{1,5},{5... | collective-permute-start | bytes 2211848 | tf_op jit(solution)/shard_map/ppermute | solution.py:847
  174.6 43.2 %collective-permute-start.23 = (bf16[480,768]{1,0:T(8,128)(2,1)}, bf16[480,768]{1,0:T(8,128)(2,1)}, u32[]{:S(2)}, u32[]{:S(2)}) collective-permute-start(bf16[480,768]{1,0:T(8,128)(2,1)} %get-tuple-element.169), channel_id=1, source_target_pairs={{0,4},{4,0},{8,12},{12,8},{16,20},{20,16},{24,28},{28,24},{1,5},{5... | collective-permute-start | bytes 2211848 | tf_op jit(solution)/shard_map/ppermute | solution.py:847
  220.4 28.6 %collective-permute-start.27 = (bf16[480,768]{1,0:T(8,128)(2,1)}, bf16[480,768]{1,0:T(8,128)(2,1)}, u32[]{:S(2)}, u32[]{:S(2)}) collective-permute-start(bf16[480,768]{1,0:T(8,128)(2,1)} %add_convert_fusion.1), channel_id=1, source_target_pairs={{0,2},{2,0},{1,3},{3,1},{4,6},{6,4},{5,7},{7,5},{8,10},{10,8},{9,1... | collective-permute-start | bytes 2211848 | tf_op jit(solution)/shard_map/ppermute | solution.py:778
  223.7 25.4 %collective-permute-start.26 = (bf16[384,768]{1,0:T(8,128)(2,1)}, bf16[384,768]{1,0:T(8,128)(2,1)S(1)}, u32[]{:S(2)}, u32[]{:S(2)}) collective-permute-start(bf16[384,768]{1,0:T(8,128)(2,1)} %get-tuple-element.166), channel_id=1, source_target_pairs={{0,4},{4,0},{8,12},{12,8},{16,20},{20,16},{24,28},{28,24},{1,5},{5... | collective-permute-start | bytes 1769480 | tf_op jit(solution)/shard_map/ppermute | solution.py:847
  248.9 24.3 %collective-permute-start.32 = (bf16[1024,1152]{1,0:T(8,128)(2,1)}, bf16[1024,1152]{1,0:T(8,128)(2,1)}, u32[]{:S(2)}, u32[]{:S(2)}) collective-permute-start(bf16[1024,1152]{1,0:T(8,128)(2,1)} %get-tuple-element.136.dt), channel_id=1, source_target_pairs={{0,1},{1,0},{2,3},{3,2},{4,5},{5,4},{6,7},{7,6},{8,9},{9,8},{10,11... | collective-permute-start | bytes 7077896 | tf_op jit(solution)/shard_map/ppermute | solution.py:774
  252.6 17.3 %collective-permute-start.28 = (bf16[432,768]{1,0:T(8,128)(2,1)S(1)}, bf16[432,768]{1,0:T(8,128)(2,1)S(1)}, u32[]{:S(2)}, u32[]{:S(2)}) collective-permute-start(bf16[432,768]{1,0:T(8,128)(2,1)S(1)} %pad_maximum_fusion.6), channel_id=1, source_target_pairs={{0,8},{4,12},{8,0},{12,4},{16,24},{20,28},{24,16},{28,20},{1,9},{5... | collective-permute-start | bytes 1990664 | tf_op jit(solution)/shard_map/ppermute | solution.py:804
  270.2 18.3 %collective-permute-start.29 = (bf16[384,1152]{1,0:T(8,128)(2,1)}, bf16[384,1152]{1,0:T(8,128)(2,1)S(1)}, u32[]{:S(2)}, u32[]{:S(2)}) collective-permute-start(bf16[384,1152]{1,0:T(8,128)(2,1)} %get-tuple-element.143), channel_id=1, source_target_pairs={{0,1},{1,0},{2,3},{3,2},{4,5},{5,4},{6,7},{7,6},{8,9},{9,8},{10,11... | collective-permute-start | bytes 2654216 | tf_op jit(solution)/shard_map/ppermute | solution.py:774
  270.3 18.2 %collective-permute-start.31 = (bf16[216,768]{1,0:T(8,128)(2,1)S(1)}, bf16[216,768]{1,0:T(8,128)(2,1)S(1)}, u32[]{:S(2)}, u32[]{:S(2)}) collective-permute-start(bf16[216,768]{1,0:T(8,128)(2,1)S(1)} %pad_maximum_fusion.14), channel_id=1, source_target_pairs={{0,16},{4,20},{8,24},{12,28},{16,0},{20,4},{24,8},{28,12},{1,17},{... | collective-permute-start | bytes 995336 | tf_op jit(solution)/shard_map/ppermute | solution.py:804
  284.5 4.2 %collective-permute-start.33 = (f32[1,768]{1,0:T(1,128)}, f32[1,768]{1,0:T(1,128)S(1)}, u32[]{:S(2)}, u32[]{:S(2)}) collective-permute-start(f32[1,768]{1,0:T(1,128)} %get-tuple-element.147), channel_id=1, source_target_pairs={{0,1},{1,0},{2,3},{3,2},{4,5},{5,4},{6,7},{7,6},{8,9},{9,8},{10,11... | collective-permute-start | bytes 9224 | tf_op jit(solution)/shard_map/ppermute | solution.py:774
  288.6 3.7 collective-permute-start.34
  291.2 25.0 %collective-permute-start.30 = (bf16[384,1152]{1,0:T(8,128)(2,1)}, bf16[384,1152]{1,0:T(8,128)(2,1)}, u32[]{:S(2)}, u32[]{:S(2)}) collective-permute-start(bf16[384,1152]{1,0:T(8,128)(2,1)} %pad_maximum_fusion.3), channel_id=1, source_target_pairs={{0,2},{2,0},{1,3},{3,1},{4,6},{6,4},{5,7},{7,5},{8,10},{10,8},{9,1... | collective-permute-start | bytes 2654216 | tf_op jit(solution)/shard_map/ppermute | solution.py:778
  292.4 23.3 %collective-permute-start.38 = (bf16[216,768]{1,0:T(8,128)(2,1)S(1)}, bf16[216,768]{1,0:T(8,128)(2,1)S(1)}, u32[]{:S(2)}, u32[]{:S(2)}) collective-permute-start(bf16[216,768]{1,0:T(8,128)(2,1)S(1)} %pad_maximum_fusion.15), channel_id=1, source_target_pairs={{0,16},{4,20},{8,24},{12,28},{16,0},{20,4},{24,8},{28,12},{1,17},{... | collective-permute-start | bytes 995336 | tf_op jit(solution)/shard_map/ppermute | solution.py:804
  293.7 25.7 %all-to-all-start = ((f32[32,16,192]{2,1,0:T(8,128)}), f32[32,16,192]{2,1,0:T(8,128)S(1)}, u32[]{:S(2)}, u32[]{:S(2)}) async-start(f32[32,16,192]{2,1,0:T(8,128)} %bitcast.16), calls=%async_computation | async-start | bytes 1048576 | tf_op jit(solution)/shard_map/all_to_all | solution.py:974
  318.3 10.2 %collective-permute-start.35 = (bf16[192,1152]{1,0:T(8,128)(2,1)}, bf16[192,1152]{1,0:T(8,128)(2,1)S(1)}, u32[]{:S(2)}, u32[]{:S(2)}) collective-permute-start(bf16[192,1152]{1,0:T(8,128)(2,1)} %get-tuple-element.172), channel_id=1, source_target_pairs={{0,4},{4,0},{8,12},{12,8},{16,20},{20,16},{24,28},{28,24},{1,5},{5... | collective-permute-start | bytes 1327112 | tf_op jit(solution)/shard_map/ppermute | solution.py:847
  320.6 44.5 %collective-permute-start.42 = (bf16[512,768]{1,0:T(8,128)(2,1)S(1)}, bf16[512,768]{1,0:T(8,128)(2,1)S(1)}, u32[]{:S(2)}, u32[]{:S(2)}) collective-permute-start(bf16[512,768]{1,0:T(8,128)(2,1)S(1)} %copy-done.30), channel_id=1, source_target_pairs={{0,2},{2,0},{1,3},{3,1},{4,6},{6,4},{5,7},{7,5},{8,10},{10,8},{9,1... | collective-permute-start | bytes 2359304 | tf_op jit(solution)/shard_map/ppermute | solution.py:778
  328.6 9.6 %collective-permute-start.36 = (bf16[96,1152]{1,0:T(8,128)(2,1)S(1)}, bf16[96,1152]{1,0:T(8,128)(2,1)S(1)}, u32[]{:S(2)}, u32[]{:S(2)}) collective-permute-start(bf16[96,1152]{1,0:T(8,128)(2,1)S(1)} %get-tuple-element.183), channel_id=1, source_target_pairs={{0,8},{4,12},{8,0},{12,4},{16,24},{20,28},{24,16},{28,20},{1,9},{5... | collective-permute-start | bytes 663560 | tf_op jit(solution)/shard_map/ppermute | solution.py:804
  330.4 20.2 %collective-permute-start.39 = (bf16[432,768]{1,0:T(8,128)(2,1)S(1)}, bf16[432,768]{1,0:T(8,128)(2,1)S(1)}, u32[]{:S(2)}, u32[]{:S(2)}) collective-permute-start(bf16[432,768]{1,0:T(8,128)(2,1)S(1)} %constant_dynamic-update-slice_fusion.2), channel_id=1, source_target_pairs={{0,8},{4,12},{8,0},{12,4},{16,24},{20,28},{24,16},{28,20},{1,9},{5... | collective-permute-start | bytes 1990664 | tf_op jit(solution)/shard_map/ppermute | solution.py:804
  338.2 11.1 %collective-permute-start.37 = (bf16[48,1152]{1,0:T(8,128)(2,1)S(1)}, bf16[48,1152]{1,0:T(8,128)(2,1)S(1)}, u32[]{:S(2)}, u32[]{:S(2)}) collective-permute-start(bf16[48,1152]{1,0:T(8,128)(2,1)S(1)} %add_convert_fusion.13), channel_id=1, source_target_pairs={{0,16},{4,20},{8,24},{12,28},{16,0},{20,4},{24,8},{28,12},{1,17},{... | collective-permute-start | bytes 331784 | tf_op jit(solution)/shard_map/ppermute | solution.py:804
  341.8 23.5 %collective-permute-start.45 = (bf16[432,768]{1,0:T(8,128)(2,1)S(1)}, bf16[432,768]{1,0:T(8,128)(2,1)S(1)}, u32[]{:S(2)}, u32[]{:S(2)}) collective-permute-start(bf16[432,768]{1,0:T(8,128)(2,1)S(1)} %constant_dynamic-update-slice_fusion.2), channel_id=1, source_target_pairs={{0,4},{4,0},{8,12},{12,8},{16,20},{20,16},{24,28},{28,24},{1,5},{5... | collective-permute-start | bytes 1990664 | tf_op jit(solution)/shard_map/ppermute | solution.py:847
  350.6 5.7 %collective-permute-start.40 = (bf16[48,1152]{1,0:T(8,128)(2,1)S(1)}, bf16[48,1152]{1,0:T(8,128)(2,1)S(1)}, u32[]{:S(2)}, u32[]{:S(2)}) collective-permute-start(bf16[48,1152]{1,0:T(8,128)(2,1)S(1)} %add_convert_fusion.12), channel_id=1, source_target_pairs={{0,16},{4,20},{8,24},{12,28},{16,0},{20,4},{24,8},{28,12},{1,17},{... | collective-permute-start | bytes 331784 | tf_op jit(solution)/shard_map/ppermute | solution.py:804
  352.9 17.8 %collective-permute-start.44 = (bf16[432,768]{1,0:T(8,128)(2,1)S(1)}, bf16[432,768]{1,0:T(8,128)(2,1)S(1)}, u32[]{:S(2)}, u32[]{:S(2)}) collective-permute-start(bf16[432,768]{1,0:T(8,128)(2,1)S(1)} %collective-permute-done.39), channel_id=1, source_target_pairs={{0,4},{4,0},{8,12},{12,8},{16,20},{20,16},{24,28},{28,24},{1,5},{5... | collective-permute-start | bytes 1990664 | tf_op jit(solution)/shard_map/ppermute | solution.py:847
  356.4 7.4 %collective-permute-start.41 = (bf16[96,1152]{1,0:T(8,128)(2,1)S(1)}, bf16[96,1152]{1,0:T(8,128)(2,1)S(1)}, u32[]{:S(2)}, u32[]{:S(2)}) collective-permute-start(bf16[96,1152]{1,0:T(8,128)(2,1)S(1)} %pad_maximum_fusion.17), channel_id=1, source_target_pairs={{0,8},{4,12},{8,0},{12,4},{16,24},{20,28},{24,16},{28,20},{1,9},{5... | collective-permute-start | bytes 663560 | tf_op jit(solution)/shard_map/ppermute | solution.py:804
  363.9 12.3 %collective-permute-start.43 = (bf16[192,1152]{1,0:T(8,128)(2,1)S(1)}, bf16[192,1152]{1,0:T(8,128)(2,1)S(1)}, u32[]{:S(2)}, u32[]{:S(2)}) collective-permute-start(bf16[192,1152]{1,0:T(8,128)(2,1)S(1)} %pad_maximum_fusion.12), channel_id=1, source_target_pairs={{0,4},{4,0},{8,12},{12,8},{16,20},{20,16},{24,28},{28,24},{1,5},{5... | collective-permute-start | bytes 1327112 | tf_op jit(solution)/shard_map/ppermute | solution.py:847
  (35 other events, 243.6 us)
where the time goes:
time: 380 us; the launch traced here: 379 us
  Pallas kernels  177 us (47%)
  waiting for transfers between devices  100 us (26%)
  starting transfers between devices  47.2 us (12%)
  other arithmetic  34.2 us (9%)
  local copies, waits for them, and re-layouts  18.6 us (5%)
    pallas_call x2, Pallas kernels, att_bwd_call(): pl.pallas_call(functools.partial(att_bwd_body, p0, into is not None), out...  66.2 us
    pallas_call x1, Pallas kernels, ffn_call(): pl.pallas_call(ffn_body, out_shape=[sds((2, rows, width), f32), sds((rows...  49.4 us
    ppermute x11, waiting for transfers between devices, swap(): return lax.ppermute(v, 'dp', flip(dp, stride))  48.4 us
    ppermute x9, waiting for transfers between devices, x_swap(): return lax.ppermute(v, 'head', XNB)  29.3 us
    pallas_call x1, Pallas kernels, att_fwd_call(): pl.pallas_call(att_fwd_body, out_shape=[sds((length // 2, width), bf16),...  27.3 us
    ppermute x11, starting transfers between devices, swap(): return lax.ppermute(v, 'dp', flip(dp, stride))  18.2 us
    pallas_call x1, Pallas kernels, qkv_call(): pl.pallas_call(qkv_body, out_shape=[sds((length, width), bf16), sds((leng...  13.6 us
    ppermute x7, waiting for transfers between devices, local(): y_swap = lambda v: lax.ppermute(v, 'dp', flip(dp, 1))  13 us
  transfers between devices with their start and end apart: 47, of which 21 were waited for; matrix products, arithmetic and copies ran while one was open for 10% of the time, Pallas kernels for 34%

commit v1 on v0

--- a/solution.py
+++ b/solution.py
@@ -66,7 +66,7 @@
     return n, inv, (n * gain).astype(bf16)
 
 
-def qkv_body(meta, x0, x2, x3, wa, wb, pack, gain, h_ref, raw_ref, mix_ref, w_ref, taps, ext):
+def qkv_body(meta, x0, x1, x2, x3, wa, wb, pack, gain, h_ref, raw_ref, mix_ref, w_ref, taps, ext):
     b = pl.program_id(0)
     rows = x0.shape[0]
     part = w_ref.shape[0] // 4
@@ -87,11 +87,11 @@
 
         put(0, wa, 0)
         put(1, wb, 0)
-        put(2, pack, rows)
-        put(3, pack, rows + tall)
+        put(2, pack, 0)
+        put(3, pack, tall)
         last = lambda ref, end: ref[end - 16 : end, :].astype(f32)
         near = last(wa, tall) + last(wb, tall)
-        far = last(pack, rows + tall) + last(pack, rows + 2 * tall)
+        far = last(pack, tall) + last(pack, 2 * tall)
         t = jnp.where(x_of(meta) == core_of(meta), near, far)
         taps[...] = jnp.zeros_like(taps)
         taps[0:3, 0:width] = t[0:3]
@@ -104,7 +104,7 @@
     def some(n, carry):
         sl = pl.ds(pl.multiple_of(n * step, step), step)
         x = x0[sl, :]
-        for k, other in ((1, pack), (2, x2), (3, x3)):
+        for k, other in ((1, x1), (2, x2), (3, x3)):
             x = jnp.where(slot == k, other[sl, :], x)
         _, _, h = norm(x.astype(f32), gain[...].astype(f32))
         h_ref[sl, :] = h
@@ -121,7 +121,7 @@
     lax.fori_loop(0, rows // step, some, 0)
 
 
-def qkv_call(meta, x_own, x_core, x_cnb, w_mine, w_core, pack, gain):
+def qkv_call(meta, x_own, x_nb, x_core, x_cnb, w_mine, w_core, pack, gain):
     rows, width = x_own.shape
     tall = w_mine.shape[0]
     cols = width * 3 // 2
@@ -139,7 +139,7 @@
         ],
         grid_spec=grid_spec(
             (4,),
-            [whole((rows, width))] * 3
+            [whole((rows, width))] * 4
             + [whole((tall, width))] * 2
             + [whole(pack.shape), whole((1, width))],
             [
@@ -153,7 +153,7 @@
         ),
         cost_estimate=cost(2 * length * width * cols, 2 * length * (width * 2 + cols * 2)),
         name="qkv",
-    )(meta, x_own, x_core, x_cnb, w_mine, w_core, pack, gain)
+    )(meta, x_own, x_nb, x_core, x_cnb, w_mine, w_core, pack, gain)
 
 
 def two_heads(v):
@@ -870,7 +870,8 @@
     w_mine = packed(c)
     x_own = pick(inputs, x)
     rows = x_own.shape[0]
-    pack = x_swap(jnp.concatenate([pick(inputs, 1 - x), w_mine, w_core], axis=0))
+    x_nb = x_swap(pick(inputs, 1 - x))
+    pack = x_swap(jnp.concatenate([w_mine, w_core], axis=0))
     x_core = core_swap(x_own)
     count = width // 4
     quarter = lambda w: lax.dynamic_slice_in_dim(w, q * count, count, 0)
@@ -879,11 +880,11 @@
     ff_src = jnp.stack([quarter(w_up), quarter(w_down)])
     ff_own = jnp.stack([w_up, w_down])
     pack2 = jnp.concatenate([pick(cotangent, 1 - x), w_out, wo_c], axis=0)
-    pack, ff_src, ff_own, pack2, c_own, meta, x_core = lax.optimization_barrier(
-        (pack, ff_src, ff_own, pack2, c_own, meta, x_core)
+    x_nb, ff_src, ff_own, pack2, c_own, meta, x_core, pack = lax.optimization_barrier(
+        (x_nb, ff_src, ff_own, pack2, c_own, meta, x_core, pack)
     )
-    x_cnb = core_swap(pack[:rows])
-    h1, raw, mix, w_full, taps = qkv_call(meta, x_own, x_core, x_cnb, w_mine, w_core, pack, gain1)
+    x_cnb = core_swap(x_nb)
+    h1, raw, mix, w_full, taps = qkv_call(meta, x_own, x_nb, x_core, x_cnb, w_mine, w_core, pack, gain1)
 
     ff_first, pack2 = x_swap(ff_src), x_swap(pack2)
     ff_c = core_swap(ff_own)
@@ -896,7 +897,7 @@
     ff_n = [src, *ff_n]
     ff_cn = [core_swap(v) for v in ff_n]
     out_own, out_nb, d_mine, d_send, gg2, dmid, *gw = ffn_call(
-        meta, x_own, pack, c_own, pack2, a_mine, a_got, after(gain2, w_other),
+        meta, x_own, x_nb, c_own, pack2, a_mine, a_got, after(gain2, w_other),
         (w_out, wo_c, pack2),
         (w_up, w_down, ff_c, *ff_n, *ff_cn),
     )
@@ -930,7 +931,7 @@
     got = core_swap(after(send, sent))
     far = x_swap(jnp.concatenate([far, got[part:]], axis=0))
     gi_own, gi_nb, gg1 = last_call(
-        meta, x_own, pack, p_mine, p_got, w_full, w_other, after(dmid, sent), gain1
+        meta, x_own, x_nb, p_mine, p_got, w_full, w_other, after(dmid, sent), gain1
     )
     *flat, gt, gg1 = lax.optimization_barrier((*sums[0], *sums[1], gt, x_swap(core_swap(gg1))))
     sums = [flat[:2], flat[2:]]
@@ -944,7 +945,8 @@
     pt = [g_keep, y_swap(g_send)]
     gi_got = x_swap(after(gi_nb, g_send))
     for stride in reversed(rest[1:]):
-        vs = [join(v, g, stride) for v, g in zip(vs, swap_both(vs, stride, dp))]
+        *got_v, pt[1] = lax.optimization_barrier((*swap_both(vs, stride, dp), pt[1]))
+        vs = [join(v, g, stride) for v, g in zip(vs, got_v)]
     (pt,), sent = scatter([pt], rest[0], dp)
     *vs, _ = lax.optimization_barrier((*vs, sent))
     packed_vs = jnp.concatenate(vs, axis=0)

time: 380 us -> 384 us (1.011)
  waiting for transfers between devices: 100 us -> 108 us
    ppermute x9 -> x10, waiting for transfers between devices: 29.3 us -> 45.4 us  [x_swap(): return lax.ppermute(v, 'head', XNB)]
    ppermute x7, waiting for transfers between devices: 13 us -> 6.41 us  [local(): y_swap = lambda v: lax.ppermute(v, 'dp', flip(dp, 1))]
    ppermute x11, starting transfers between devices: 18.2 us -> 13.6 us  [swap(): return lax.ppermute(v, 'dp', flip(dp, stride))]
    ppermute x9 -> x10, starting transfers between devices: 12 us -> 12.4 us  [x_swap(): return lax.ppermute(v, 'head', XNB)]
  transfers between devices with their start and end apart: 47 -> 48, of which waited for: 21 -> 19; matrix products, arithmetic and copies ran while one was open for 10% -> 11% of each run, Pallas kernels for 34% -> 33%
where the time goes in v1:
time: 384 us; the launch traced here: 383 us
  Pallas kernels  177 us (46%)
  waiting for transfers between devices  108 us (28%)
  starting transfers between devices  44.3 us (12%)
  other arithmetic  33.8 us (9%)
  local copies, waits for them, and re-layouts  17.8 us (5%)
    pallas_call x2, Pallas kernels, att_bwd_call(): pl.pallas_call(functools.partial(att_bwd_body, p0, into is not None), out...  66.3 us
    pallas_call x1, Pallas kernels, ffn_call(): pl.pallas_call(ffn_body, out_shape=[sds((2, rows, width), f32), sds((rows...  49.3 us
    ppermute x11, waiting for transfers between devices, swap(): return lax.ppermute(v, 'dp', flip(dp, stride))  46.3 us
    ppermute x10, waiting for transfers between devices, x_swap(): return lax.ppermute(v, 'head', XNB)  45.4 us
    pallas_call x1, Pallas kernels, att_fwd_call(): pl.pallas_call(att_fwd_body, out_shape=[sds((length // 2, width), bf16),...  27.3 us
    ppermute x11, starting transfers between devices, swap(): return lax.ppermute(v, 'dp', flip(dp, stride))  13.6 us
    pallas_call x1, Pallas kernels, qkv_call(): pl.pallas_call(qkv_body, out_shape=[sds((length, width), bf16), sds((leng...  13.5 us
    ppermute x10, starting transfers between devices, x_swap(): return lax.ppermute(v, 'head', XNB)  12.4 us
  transfers between devices with their start and end apart: 48, of which 19 were waited for; matrix products, arithmetic and copies ran while one was open for 11% of the time, Pallas kernels for 33%

profile of v1, /device:TPU:0, one launch (start us, length us, event | category | flops | bytes accessed | tf_op | source)
XLA Modules:
  0.0 383.2 jit_solution(17932098582404697859)
XLA Ops:
  6.9 3.2 collective-permute-start.4
  13.1 2.5 dynamic-slice_bitcast_fusion.1
  16.7 2.2 pad_maximum_fusion.1
  18.9 29.4 %collective-permute-done.x1.xx = bf16[512,768]{1,0:T(8,128)(2,1)} collective-permute-done((bf16[512,768]{1,0:T(8,128)(2,1)}, bf16[512,768]{1,0:T(8,128)(2,1)}, u32[]{:S(2)}, u32[]{:S(2)}) %collective-permute-start) | collective-permute-done | bytes 786464 | tf_op jit(solution)/shard_map/ppermute | solution.py:778
  49.4 1.7 collective-permute-start.5
  51.2 2.6 collective-permute-done.6.x3
  54.7 13.5 %qkv.1 = (bf16[2048,768]{1,0:T(8,128)(2,1)}, bf16[2048,1152]{1,0:T(8,128)(2,1)}, bf16[2048,1152]{1,0:T(8,128)(2,1)}, bf16[768,1152]{1,0:T(8,128)(2,1)}, f32[8,1152]{1,0:T(8,128)}) custom-call(s32[4]{0:T(128)} %pad_add_fusion.meta, bf16[512,768]{1,0:T(8,128)(2,1)} %copy-done, bf16[512,768]{1,0:T(8,128)(2,1)} %collective-permute-done.x1.xx, ...), custom_call_target="tpu_custom_call" | custom-call | flops 3623878656 | bytes 15728640 | tf_op jit(solution)/shard_map/qkv/pallas_call | solution.py:131
  68.6 1.7 collective-permute-start.10
  70.3 1.5 collective-permute-start.7
  71.8 1.6 collective-permute-start.8
  73.8 27.3 %attn_fwd.1 = (bf16[1024,384]{1,0:T(8,128)(2,1)}, bf16[1024,384]{1,0:T(8,128)(2,1)}, f32[3,2,2048]{2,1,0:T(2,128)}) custom-call(s32[4]{0:T(128)} %pad_add_fusion.meta, bf16[2048,1152]{1,0:T(8,128)(2,1)} %get-tuple-element.132.q_ref.k_ref.v_ref, bf16[2048,1152]{1,0:T(8,128)(2,1)} %get-tuple-element.132.q_ref.k_ref.v_ref, ...), custom_call_target="tpu_custom_call" | custom-call | flops 12884901888 | bytes 6291456 | tf_op jit(solution)/shard_map/attn_fwd/pallas_call | solution.py:255
  103.0 2.4 collective-permute-done.14.c0
  105.4 1.7 collective-permute-done.16.c2
  109.6 49.3 %ffn.1 = (f32[2,512,768]{2,1,0:T(8,128)}, bf16[512,768]{1,0:T(8,128)(2,1)}, bf16[1024,384]{1,0:T(8,128)(2,1)}, bf16[1024,384]{1,0:T(8,128)(2,1)}, f32[1,768]{1,0...) custom-call(s32[4]{0:T(128)} %pad_add_fusion.meta, ...), custom_call_target="tpu_custom_call" | custom-call | flops 32614907904 | bytes 31457280 | tf_op jit(solution)/shard_map/ffn/pallas_call | solution.py:623
  160.2 1.9 collective-permute-done.19
  163.1 3.1 add_convert_fusion
  166.3 1.9 collective-permute-start.25
  169.3 1.6 collective-permute-start.22
  170.8 2.6 add_convert_fusion.2
  173.9 42.8 %attn_bwd.2 = (bf16[1024,1152]{1,0:T(8,128)(2,1)}, bf16[1024,1152]{1,0:T(8,128)(2,1)}, f32[16,256]{1,0:T(8,128)}) custom-call(s32[4]{0:T(128)} %pad_add_fusion.meta, bf16[2048,1152]{1,0:T(8,128)(2,1)} %get-tuple-element.132.q_ref.k_ref.v_ref, bf16[2048,1152]{1,0:T(8,128)(2,1)} %get-tuple-element.132.q_ref.k_ref.v_ref, ...), custom_call_target="tpu_custom_call" | custom-call | flops 15032385536 | bytes 10485760 | tf_op jit(solution)/shard_map/attn_bwd/pallas_call | solution.py:407
  216.7 2.6 add_convert_fusion.1
  219.6 2.9 convert_add_fusion.1
  222.4 1.8 collective-permute-start.27
  224.2 23.5 %attn_bwd.3 = (bf16[1024,1152]{1,0:T(8,128)(2,1)}, bf16[1024,1152]{1,0:T(8,128)(2,1)}, f32[16,128]{1,0:T(8,128)}) custom-call(s32[4]{0:T(128)} %pad_add_fusion.meta, bf16[2048,1152]{1,0:T(8,128)(2,1)} %get-tuple-element.132.q_ref.k_ref.v_ref, ...), custom_call_target="tpu_custom_call", output_to_operand_aliasing={{0}: (13, {}), {1}: (14, {})} | custom-call | flops 7516192768 | bytes 5242880 | tf_op jit(solution)/shard_map/attn_bwd/pallas_call | solution.py:407
  249.9 1.5 convert_add_fusion.4
  252.9 9.5 %projg.1 = (bf16[192,1152]{1,0:T(8,128)(2,1)}, bf16[192,1152]{1,0:T(8,128)(2,1)}, bf16[384,1152]{1,0:T(8,128)(2,1)}) custom-call(s32[4]{0:T(128)} %pad_add_fusion.meta, bf16[2048,768]{1,0:T(8,128)(2,1)} %get-tuple-element.139.h, bf16[1024,1152]{1,0:T(8,128)(2,1)} %get-tuple-element.140.dm, bf16[1024,1152]{1,0:T(8,128)(2,1)} %get-tuple-element.141.dt), custom_call_target="tpu_custom_call" | custom-call | flops 2048 | bytes 2048 | tf_op jit(solution)/shard_map/projg/pallas_call | solution.py:692
  262.4 6.4 %collective-permute-done.29 = bf16[432,768]{1,0:T(8,128)(2,1)S(1)} collective-permute-done((bf16[432,768]{1,0:T(8,128)(2,1)S(1)}, bf16[432,768]{1,0:T(8,128)(2,1)S(1)}, u32[]{:S(2)}, u32[]{:S(2)}) %collective-permute-start.29) | collective-permute-done | bytes 663584 | tf_op jit(solution)/shard_map/ppermute | solution.py:804
  269.2 2.4 collective-permute-start.32
  271.8 11.4 %last.1 = (f32[2,512,768]{2,1,0:T(8,128)}, bf16[512,768]{1,0:T(8,128)(2,1)}, f32[1,768]{1,0:T(1,128)}) custom-call(s32[4]{0:T(128)} %pad_add_fusion.meta, bf16[512,768]{1,0:T(8,128)(2,1)} %copy-done, bf16[512,768]{1,0:T(8,128)(2,1)} %collective-permute-done.x1.xx, bf16[1024,1152]{1,0:T(8,128)(2,1)} %get-tuple-element.140.dm, ...), custom_call_target="tpu_custom_call" | custom-call | flops 512 | bytes 512 | tf_op jit(solution)/shard_map/last/pallas_call | solution.py:750
  283.5 3.9 %collective-permute-done.32 = bf16[216,768]{1,0:T(8,128)(2,1)S(1)} collective-permute-done((bf16[216,768]{1,0:T(8,128)(2,1)S(1)}, bf16[216,768]{1,0:T(8,128)(2,1)S(1)}, u32[]{:S(2)}, u32[]{:S(2)}) %collective-permute-start.32) | collective-permute-done | bytes 331808 | tf_op jit(solution)/shard_map/ppermute | solution.py:804
  287.4 1.6 collective-permute-start.35
  292.3 4.8 %all-to-all-start = ((f32[32,16,192]{2,1,0:T(8,128)}), f32[32,16,192]{2,1,0:T(8,128)S(1)}, u32[]{:S(2)}, u32[]{:S(2)}) async-start(f32[32,16,192]{2,1,0:T(8,128)} %bitcast.16), calls=%async_computation | async-start | bytes 1048576 | tf_op jit(solution)/shard_map/all_to_all | solution.py:976
  297.3 2.7 collective-permute-start.36
  300.0 15.5 %collective-permute-done.31 = bf16[384,1152]{1,0:T(8,128)(2,1)} collective-permute-done((bf16[384,1152]{1,0:T(8,128)(2,1)}, bf16[384,1152]{1,0:T(8,128)(2,1)}, u32[]{:S(2)}, u32[]{:S(2)}) %collective-permute-start.31) | collective-permute-done | bytes 884768 | tf_op jit(solution)/shard_map/ppermute | solution.py:778
  315.5 2.2 fusion.1
  318.4 8.1 %collective-permute-done.36 = bf16[216,768]{1,0:T(8,128)(2,1)} collective-permute-done((bf16[216,768]{1,0:T(8,128)(2,1)S(1)}, bf16[216,768]{1,0:T(8,128)(2,1)}, u32[]{:S(2)}, u32[]{:S(2)}) %collective-permute-start.36) | collective-permute-done | bytes 331808 | tf_op jit(solution)/shard_map/ppermute | solution.py:804
  331.5 2.1 collective-permute-start.40
  333.5 6.2 %collective-permute-done.38 = bf16[96,1152]{1,0:T(8,128)(2,1)S(1)} collective-permute-done((bf16[96,1152]{1,0:T(8,128)(2,1)S(1)}, bf16[96,1152]{1,0:T(8,128)(2,1)S(1)}, u32[]{:S(2)}, u32[]{:S(2)}) %collective-permute-start.38) | collective-permute-done | bytes 221216 | tf_op jit(solution)/shard_map/ppermute | solution.py:804
  341.1 1.6 collective-permute-start.46
  342.6 9.8 %collective-permute-done.39 = bf16[48,1152]{1,0:T(8,128)(2,1)S(1)} collective-permute-done((bf16[48,1152]{1,0:T(8,128)(2,1)S(1)}, bf16[48,1152]{1,0:T(8,128)(2,1)S(1)}, u32[]{:S(2)}, u32[]{:S(2)}) %collective-permute-start.39) | collective-permute-done | bytes 110624 | tf_op jit(solution)/shard_map/ppermute | solution.py:804
  352.4 2.1 collective-permute-done.40
  357.5 3.9 %collective-permute-done.41 = bf16[48,1152]{1,0:T(8,128)(2,1)S(1)} collective-permute-done((bf16[48,1152]{1,0:T(8,128)(2,1)S(1)}, bf16[48,1152]{1,0:T(8,128)(2,1)S(1)}, u32[]{:S(2)}, u32[]{:S(2)}) %collective-permute-start.41) | collective-permute-done | bytes 110624 | tf_op jit(solution)/shard_map/ppermute | solution.py:804
  361.7 5.8 %collective-permute-done.42 = bf16[96,1152]{1,0:T(8,128)(2,1)S(1)} collective-permute-done((bf16[96,1152]{1,0:T(8,128)(2,1)S(1)}, bf16[96,1152]{1,0:T(8,128)(2,1)S(1)}, u32[]{:S(2)}, u32[]{:S(2)}) %collective-permute-start.42) | collective-permute-done | bytes 221216 | tf_op jit(solution)/shard_map/ppermute | solution.py:804
  367.6 1.6 collective-permute-start.44
  369.3 4.4 %collective-permute-done.45 = bf16[432,768]{1,0:T(8,128)(2,1)S(1)} collective-permute-done((bf16[432,768]{1,0:T(8,128)(2,1)S(1)}, bf16[432,768]{1,0:T(8,128)(2,1)S(1)}, u32[]{:S(2)}, u32[]{:S(2)}) %collective-permute-start.45) | collective-permute-done | bytes 663584 | tf_op jit(solution)/shard_map/ppermute | solution.py:847
  375.2 1.6 fusion
  376.8 1.6 maximum_convert_fusion
  378.4 2.0 collective-permute-done.44
  (216 shorter events, 43.7 us)
Async XLA Ops:
  3.9 2.0 collective-permute-start.3
  4.3 12.4 %collective-permute-start.1 = (bf16[192,768]{1,0:T(8,128)(2,1)}, bf16[192,768]{1,0:T(8,128)(2,1)}, u32[]{:S(2)}, u32[]{:S(2)}) collective-permute-start(bf16[192,768]{1,0:T(8,128)(2,1)} %wo_o.1), channel_id=1, source_target_pairs={{0,1},{1,0},{2,3},{3,2},{4,5},{5,4},{6,7},{7,6},{8,9},{9,8},{10,11... | collective-permute-start | bytes 884744 | tf_op jit(solution)/shard_map/ppermute | solution.py:774
  6.9 41.4 %collective-permute-start.4 = (bf16[608,768]{1,0:T(8,128)(2,1)}, bf16[608,768]{1,0:T(8,128)(2,1)}, u32[]{:S(2)}, u32[]{:S(2)}) collective-permute-start(bf16[608,768]{1,0:T(8,128)(2,1)} %pad_maximum_fusion.3), channel_id=1, source_target_pairs={{0,2},{2,0},{1,3},{3,1},{4,6},{6,4},{5,7},{7,5},{8,10},{10,8},{9,1... | collective-permute-start | bytes 2801672 | tf_op jit(solution)/shard_map/ppermute | solution.py:778
  11.1 37.2 %collective-permute-start = (bf16[512,768]{1,0:T(8,128)(2,1)}, bf16[512,768]{1,0:T(8,128)(2,1)}, u32[]{:S(2)}, u32[]{:S(2)}) collective-permute-start(bf16[512,768]{1,0:T(8,128)(2,1)} %get-tuple-element.184), channel_id=1, source_target_pairs={{0,2},{2,0},{1,3},{3,1},{4,6},{6,4},{5,7},{7,5},{8,10},{10,8},{9,1... | collective-permute-start | bytes 2359304 | tf_op jit(solution)/shard_map/ppermute | solution.py:778
  11.1 37.2 %collective-permute-start.2 = (bf16[512,768]{1,0:T(8,128)(2,1)S(1)}, bf16[512,768]{1,0:T(8,128)(2,1)}, u32[]{:S(2)}, u32[]{:S(2)}) collective-permute-start(bf16[512,768]{1,0:T(8,128)(2,1)S(1)} %get-tuple-element.183.x0.xo), channel_id=1, source_target_pairs={{0,1},{1,0},{2,3},{3,2},{4,5},{5,4},{6,7},{7,6},{8,9},{9,8},{10,11... | collective-permute-start | bytes 2359304 | tf_op jit(solution)/shard_map/ppermute | solution.py:774
  48.3 25.1 %collective-permute-start.11 = (bf16[2,768,768]{2,1,0:T(8,128)(2,1)S(1)}, bf16[2,768,768]{2,1,0:T(8,128)(2,1)}, u32[]{:S(2)}, u32[]{:S(2)}) collective-permute-start(bf16[2,768,768]{2,1,0:T(8,128)(2,1)S(1)} %pad_maximum_fusion), channel_id=1, source_target_pairs={{0,1},{1,0},{2,3},{3,2},{4,5},{5,4},{6,7},{7,6},{8,9},{9,8},{10,11... | collective-permute-start | bytes 7077896 | tf_op jit(solution)/shard_map/ppermute | solution.py:774
  48.3 5.5 %collective-permute-start.6 = (bf16[512,768]{1,0:T(8,128)(2,1)}, bf16[512,768]{1,0:T(8,128)(2,1)S(1)}, u32[]{:S(2)}, u32[]{:S(2)}) collective-permute-start(bf16[512,768]{1,0:T(8,128)(2,1)} %collective-permute-done.x1.xx), channel_id=1, source_target_pairs={{0,1},{1,0},{2,3},{3,2},{4,5},{5,4},{6,7},{7,6},{8,9},{9,8},{10,11... | collective-permute-start | bytes 2359304 | tf_op jit(solution)/shard_map/ppermute | solution.py:774
  49.4 20.9 %collective-permute-start.5 = (bf16[2,192,768]{2,1,0:T(8,128)(2,1)}, bf16[2,192,768]{2,1,0:T(8,128)(2,1)}, u32[]{:S(2)}, u32[]{:S(2)}) collective-permute-start(bf16[2,192,768]{2,1,0:T(8,128)(2,1)} %pad_maximum_fusion.10), channel_id=1, source_target_pairs={{0,2},{2,0},{1,3},{3,1},{4,6},{6,4},{5,7},{7,5},{8,10},{10,8},{9,1... | collective-permute-start | bytes 1769480 | tf_op jit(solution)/shard_map/ppermute | solution.py:778
  68.2 34.1 %collective-permute-start.13 = (bf16[768,1152]{1,0:T(8,128)(2,1)}, bf16[768,1152]{1,0:T(8,128)(2,1)}, u32[]{:S(2)}, u32[]{:S(2)}) collective-permute-start(bf16[768,1152]{1,0:T(8,128)(2,1)} %get-tuple-element.106.wm), channel_id=1, source_target_pairs={{0,1},{1,0},{2,3},{3,2},{4,5},{5,4},{6,7},{7,6},{8,9},{9,8},{10,11... | collective-permute-start | bytes 5308424 | tf_op jit(solution)/shard_map/ppermute | solution.py:774
  68.6 33.2 %collective-permute-start.10 = (bf16[896,768]{1,0:T(8,128)(2,1)}, bf16[896,768]{1,0:T(8,128)(2,1)}, u32[]{:S(2)}, u32[]{:S(2)}) collective-permute-start(bf16[896,768]{1,0:T(8,128)(2,1)} %pad_maximum_fusion.1), channel_id=1, source_target_pairs={{0,2},{2,0},{1,3},{3,1},{4,6},{6,4},{5,7},{7,5},{8,10},{10,8},{9,1... | collective-permute-start | bytes 4128776 | tf_op jit(solution)/shard_map/ppermute | solution.py:778
  70.3 30.8 %collective-permute-start.7 = (bf16[2,192,768]{2,1,0:T(8,128)(2,1)}, bf16[2,192,768]{2,1,0:T(8,128)(2,1)S(1)}, u32[]{:S(2)}, u32[]{:S(2)}) collective-permute-start(bf16[2,192,768]{2,1,0:T(8,128)(2,1)} %collective-permute-done.5.n0), channel_id=1, source_target_pairs={{0,4},{4,0},{8,12},{12,8},{16,20},{20,16},{24,28},{28,24},{1,5},{5... | collective-permute-start | bytes 1769480 | tf_op jit(solution)/shard_map/ppermute | solution.py:804
  71.8 29.4 %collective-permute-start.8 = (bf16[2,192,768]{2,1,0:T(8,128)(2,1)}, bf16[2,192,768]{2,1,0:T(8,128)(2,1)}, u32[]{:S(2)}, u32[]{:S(2)}) collective-permute-start(bf16[2,192,768]{2,1,0:T(8,128)(2,1)} %collective-permute-done.5.n0), channel_id=1, source_target_pairs={{0,8},{4,12},{8,0},{12,4},{16,24},{20,28},{24,16},{28,20},{1,9},{5... | collective-permute-start | bytes 1769480 | tf_op jit(solution)/shard_map/ppermute | solution.py:804
  73.4 28.3 %collective-permute-start.9 = (bf16[2,192,768]{2,1,0:T(8,128)(2,1)}, bf16[2,192,768]{2,1,0:T(8,128)(2,1)S(1)}, u32[]{:S(2)}, u32[]{:S(2)}) collective-permute-start(bf16[2,192,768]{2,1,0:T(8,128)(2,1)} %collective-permute-done.5.n0), channel_id=1, source_target_pairs={{0,12},{4,8},{8,4},{12,0},{16,28},{20,24},{24,20},{28,16},{1,13},{... | collective-permute-start | bytes 1769480 | tf_op jit(solution)/shard_map/ppermute | solution.py:804
  101.2 7.6 %collective-permute-start.12 = (bf16[1024,384]{1,0:T(8,128)(2,1)}, bf16[1024,384]{1,0:T(8,128)(2,1)S(1)}, u32[]{:S(2)}, u32[]{:S(2)}) collective-permute-start(bf16[1024,384]{1,0:T(8,128)(2,1)} %get-tuple-element.105.ot), channel_id=1, source_target_pairs={{0,1},{1,0},{2,3},{3,2},{4,5},{5,4},{6,7},{7,6},{8,9},{9,8},{10,11... | collective-permute-start | bytes 2359304 | tf_op jit(solution)/shard_map/ppermute | solution.py:774
  101.2 4.2 %collective-permute-start.14 = (bf16[2,192,768]{2,1,0:T(8,128)(2,1)}, bf16[2,192,768]{2,1,0:T(8,128)(2,1)S(1)}, u32[]{:S(2)}, u32[]{:S(2)}) collective-permute-start(bf16[2,192,768]{2,1,0:T(8,128)(2,1)} %collective-permute-done.5.n0), channel_id=1, source_target_pairs={{0,1},{1,0},{2,3},{3,2},{4,5},{5,4},{6,7},{7,6},{8,9},{9,8},{10,11... | collective-permute-start | bytes 1769480 | tf_op jit(solution)/shard_map/ppermute | solution.py:774
  101.7 3.7 collective-permute-start.15
  101.9 5.2 %collective-permute-start.16 = (bf16[2,192,768]{2,1,0:T(8,128)(2,1)}, bf16[2,192,768]{2,1,0:T(8,128)(2,1)S(1)}, u32[]{:S(2)}, u32[]{:S(2)}) collective-permute-start(bf16[2,192,768]{2,1,0:T(8,128)(2,1)} %collective-permute-done.8.n2), channel_id=1, source_target_pairs={{0,1},{1,0},{2,3},{3,2},{4,5},{5,4},{6,7},{7,6},{8,9},{9,8},{10,11... | collective-permute-start | bytes 1769480 | tf_op jit(solution)/shard_map/ppermute | solution.py:774
  102.3 4.8 %collective-permute-start.17 = (bf16[2,192,768]{2,1,0:T(8,128)(2,1)S(1)}, bf16[2,192,768]{2,1,0:T(8,128)(2,1)S(1)}, u32[]{:S(2)}, u32[]{:S(2)}) collective-permute-start(bf16[2,192,768]{2,1,0:T(8,128)(2,1)S(1)} %collective-permute-done.9.n3), channel_id=1, source_target_pairs={{0,1},{1,0},{2,3},{3,2},{4,5},{5,4},{6,7},{7,6},{8,9},{9,8},{10,11... | collective-permute-start | bytes 1769480 | tf_op jit(solution)/shard_map/ppermute | solution.py:774
  159.0 3.1 collective-permute-start.19
  159.2 7.1 %collective-permute-start.21 = (bf16[960,768]{1,0:T(8,128)(2,1)}, bf16[960,768]{1,0:T(8,128)(2,1)S(1)}, u32[]{:S(2)}, u32[]{:S(2)}) collective-permute-start(bf16[960,768]{1,0:T(8,128)(2,1)} %get-tuple-element.118), channel_id=1, source_target_pairs={{0,1},{1,0},{2,3},{3,2},{4,5},{5,4},{6,7},{7,6},{8,9},{9,8},{10,11... | collective-permute-start | bytes 4423688 | tf_op jit(solution)/shard_map/ppermute | solution.py:774
  159.5 9.7 %collective-permute-start.23 = (bf16[960,768]{1,0:T(8,128)(2,1)}, bf16[960,768]{1,0:T(8,128)(2,1)}, u32[]{:S(2)}, u32[]{:S(2)}) collective-permute-start(bf16[960,768]{1,0:T(8,128)(2,1)} %get-tuple-element.120), channel_id=1, source_target_pairs={{0,1},{1,0},{2,3},{3,2},{4,5},{5,4},{6,7},{7,6},{8,9},{9,8},{10,11... | collective-permute-start | bytes 4423688 | tf_op jit(solution)/shard_map/ppermute | solution.py:774
  159.7 13.7 %collective-permute-start.26 = (bf16[1024,384]{1,0:T(8,128)(2,1)}, bf16[1024,384]{1,0:T(8,128)(2,1)}, u32[]{:S(2)}, u32[]{:S(2)}) collective-permute-start(bf16[1024,384]{1,0:T(8,128)(2,1)} %get-tuple-element.125), channel_id=1, source_target_pairs={{0,1},{1,0},{2,3},{3,2},{4,5},{5,4},{6,7},{7,6},{8,9},{9,8},{10,11... | collective-permute-start | bytes 2359304 | tf_op jit(solution)/shard_map/ppermute | solution.py:774
  160.0 59.5 %collective-permute-start.18 = (bf16[768,768]{1,0:T(8,128)(2,1)}, bf16[768,768]{1,0:T(8,128)(2,1)}, u32[]{:S(2)}, u32[]{:S(2)}) collective-permute-start(bf16[768,768]{1,0:T(8,128)(2,1)} %get-tuple-element.114), channel_id=1, source_target_pairs={{0,1},{1,0},{2,3},{3,2},{4,5},{5,4},{6,7},{7,6},{8,9},{9,8},{10,11... | collective-permute-start | bytes 3538952 | tf_op jit(solution)/shard_map/ppermute | solution.py:774
  166.2 50.5 %collective-permute-start.20 = (bf16[768,768]{1,0:T(8,128)(2,1)}, bf16[768,768]{1,0:T(8,128)(2,1)}, u32[]{:S(2)}, u32[]{:S(2)}) collective-permute-start(bf16[768,768]{1,0:T(8,128)(2,1)} %add_convert_fusion), channel_id=1, source_target_pairs={{0,2},{2,0},{1,3},{3,1},{4,6},{6,4},{5,7},{7,5},{8,10},{10,8},{9,1... | collective-permute-start | bytes 3538952 | tf_op jit(solution)/shard_map/ppermute | solution.py:778
  166.3 50.4 %collective-permute-start.25 = (bf16[512,768]{1,0:T(8,128)(2,1)}, bf16[512,768]{1,0:T(8,128)(2,1)}, u32[]{:S(2)}, u32[]{:S(2)}) collective-permute-start(bf16[512,768]{1,0:T(8,128)(2,1)} %get-tuple-element.122), channel_id=1, source_target_pairs={{0,2},{2,0},{1,3},{3,1},{4,6},{6,4},{5,7},{7,5},{8,10},{10,8},{9,1... | collective-permute-start | bytes 2359304 | tf_op jit(solution)/shard_map/ppermute | solution.py:778
  169.3 47.4 %collective-permute-start.22 = (bf16[480,768]{1,0:T(8,128)(2,1)}, bf16[480,768]{1,0:T(8,128)(2,1)}, u32[]{:S(2)}, u32[]{:S(2)}) collective-permute-start(bf16[480,768]{1,0:T(8,128)(2,1)} %add_convert_fusion.3), channel_id=1, source_target_pairs={{0,4},{4,0},{8,12},{12,8},{16,20},{20,16},{24,28},{28,24},{1,5},{5... | collective-permute-start | bytes 2211848 | tf_op jit(solution)/shard_map/ppermute | solution.py:847
  173.4 43.3 %collective-permute-start.24 = (bf16[480,768]{1,0:T(8,128)(2,1)}, bf16[480,768]{1,0:T(8,128)(2,1)}, u32[]{:S(2)}, u32[]{:S(2)}) collective-permute-start(bf16[480,768]{1,0:T(8,128)(2,1)} %get-tuple-element.177), channel_id=1, source_target_pairs={{0,4},{4,0},{8,12},{12,8},{16,20},{20,16},{24,28},{28,24},{1,5},{5... | collective-permute-start | bytes 2211848 | tf_op jit(solution)/shard_map/ppermute | solution.py:847
  219.3 28.6 %collective-permute-start.28 = (bf16[480,768]{1,0:T(8,128)(2,1)}, bf16[480,768]{1,0:T(8,128)(2,1)}, u32[]{:S(2)}, u32[]{:S(2)}) collective-permute-start(bf16[480,768]{1,0:T(8,128)(2,1)} %add_convert_fusion.1), channel_id=1, source_target_pairs={{0,2},{2,0},{1,3},{3,1},{4,6},{6,4},{5,7},{7,5},{8,10},{10,8},{9,1... | collective-permute-start | bytes 2211848 | tf_op jit(solution)/shard_map/ppermute | solution.py:778
  222.4 25.5 %collective-permute-start.27 = (bf16[384,768]{1,0:T(8,128)(2,1)}, bf16[384,768]{1,0:T(8,128)(2,1)S(1)}, u32[]{:S(2)}, u32[]{:S(2)}) collective-permute-start(bf16[384,768]{1,0:T(8,128)(2,1)} %get-tuple-element.174), channel_id=1, source_target_pairs={{0,4},{4,0},{8,12},{12,8},{16,20},{20,16},{24,28},{28,24},{1,5},{5... | collective-permute-start | bytes 1769480 | tf_op jit(solution)/shard_map/ppermute | solution.py:847
  247.8 24.1 %collective-permute-start.33 = (bf16[1024,1152]{1,0:T(8,128)(2,1)}, bf16[1024,1152]{1,0:T(8,128)(2,1)}, u32[]{:S(2)}, u32[]{:S(2)}) collective-permute-start(bf16[1024,1152]{1,0:T(8,128)(2,1)} %get-tuple-element.141.dt), channel_id=1, source_target_pairs={{0,1},{1,0},{2,3},{3,2},{4,5},{5,4},{6,7},{7,6},{8,9},{9,8},{10,11... | collective-permute-start | bytes 7077896 | tf_op jit(solution)/shard_map/ppermute | solution.py:774
  251.5 17.3 %collective-permute-start.29 = (bf16[432,768]{1,0:T(8,128)(2,1)S(1)}, bf16[432,768]{1,0:T(8,128)(2,1)S(1)}, u32[]{:S(2)}, u32[]{:S(2)}) collective-permute-start(bf16[432,768]{1,0:T(8,128)(2,1)S(1)} %pad_maximum_fusion.7), channel_id=1, source_target_pairs={{0,8},{4,12},{8,0},{12,4},{16,24},{20,28},{24,16},{28,20},{1,9},{5... | collective-permute-start | bytes 1990664 | tf_op jit(solution)/shard_map/ppermute | solution.py:804
  269.1 18.3 %collective-permute-start.30 = (bf16[384,1152]{1,0:T(8,128)(2,1)}, bf16[384,1152]{1,0:T(8,128)(2,1)S(1)}, u32[]{:S(2)}, u32[]{:S(2)}) collective-permute-start(bf16[384,1152]{1,0:T(8,128)(2,1)} %get-tuple-element.148), channel_id=1, source_target_pairs={{0,1},{1,0},{2,3},{3,2},{4,5},{5,4},{6,7},{7,6},{8,9},{9,8},{10,11... | collective-permute-start | bytes 2654216 | tf_op jit(solution)/shard_map/ppermute | solution.py:774
  269.2 18.2 %collective-permute-start.32 = (bf16[216,768]{1,0:T(8,128)(2,1)S(1)}, bf16[216,768]{1,0:T(8,128)(2,1)S(1)}, u32[]{:S(2)}, u32[]{:S(2)}) collective-permute-start(bf16[216,768]{1,0:T(8,128)(2,1)S(1)} %pad_maximum_fusion.15), channel_id=1, source_target_pairs={{0,16},{4,20},{8,24},{12,28},{16,0},{20,4},{24,8},{28,12},{1,17},{... | collective-permute-start | bytes 995336 | tf_op jit(solution)/shard_map/ppermute | solution.py:804
  283.2 4.2 %collective-permute-start.34 = (f32[1,768]{1,0:T(1,128)}, f32[1,768]{1,0:T(1,128)S(1)}, u32[]{:S(2)}, u32[]{:S(2)}) collective-permute-start(f32[1,768]{1,0:T(1,128)} %get-tuple-element.152), channel_id=1, source_target_pairs={{0,1},{1,0},{2,3},{3,2},{4,5},{5,4},{6,7},{7,6},{8,9},{9,8},{10,11... | collective-permute-start | bytes 9224 | tf_op jit(solution)/shard_map/ppermute | solution.py:774
  287.4 3.7 collective-permute-start.35
  290.0 25.5 %collective-permute-start.31 = (bf16[384,1152]{1,0:T(8,128)(2,1)}, bf16[384,1152]{1,0:T(8,128)(2,1)}, u32[]{:S(2)}, u32[]{:S(2)}) collective-permute-start(bf16[384,1152]{1,0:T(8,128)(2,1)} %pad_maximum_fusion.4), channel_id=1, source_target_pairs={{0,2},{2,0},{1,3},{3,1},{4,6},{6,4},{5,7},{7,5},{8,10},{10,8},{9,1... | collective-permute-start | bytes 2654216 | tf_op jit(solution)/shard_map/ppermute | solution.py:778
  292.3 36.0 %all-to-all-start = ((f32[32,16,192]{2,1,0:T(8,128)}), f32[32,16,192]{2,1,0:T(8,128)S(1)}, u32[]{:S(2)}, u32[]{:S(2)}) async-start(f32[32,16,192]{2,1,0:T(8,128)} %bitcast.16), calls=%async_computation | async-start | bytes 1048576 | tf_op jit(solution)/shard_map/all_to_all | solution.py:976
  297.3 29.2 %collective-permute-start.36 = (bf16[216,768]{1,0:T(8,128)(2,1)S(1)}, bf16[216,768]{1,0:T(8,128)(2,1)}, u32[]{:S(2)}, u32[]{:S(2)}) collective-permute-start(bf16[216,768]{1,0:T(8,128)(2,1)S(1)} %pad_maximum_fusion.16), channel_id=1, source_target_pairs={{0,16},{4,20},{8,24},{12,28},{16,0},{20,4},{24,8},{28,12},{1,17},{... | collective-permute-start | bytes 995336 | tf_op jit(solution)/shard_map/ppermute | solution.py:804
  317.7 13.4 %collective-permute-start.37 = (bf16[192,1152]{1,0:T(8,128)(2,1)}, bf16[192,1152]{1,0:T(8,128)(2,1)S(1)}, u32[]{:S(2)}, u32[]{:S(2)}) collective-permute-start(bf16[192,1152]{1,0:T(8,128)(2,1)} %get-tuple-element.180), channel_id=1, source_target_pairs={{0,4},{4,0},{8,12},{12,8},{16,20},{20,16},{24,28},{28,24},{1,5},{5... | collective-permute-start | bytes 1327112 | tf_op jit(solution)/shard_map/ppermute | solution.py:847
  329.6 39.6 %collective-permute-start.43 = (bf16[512,768]{1,0:T(8,128)(2,1)}, bf16[512,768]{1,0:T(8,128)(2,1)S(1)}, u32[]{:S(2)}, u32[]{:S(2)}) collective-permute-start(bf16[512,768]{1,0:T(8,128)(2,1)} %get-tuple-element.169), channel_id=1, source_target_pairs={{0,2},{2,0},{1,3},{3,1},{4,6},{6,4},{5,7},{7,5},{8,10},{10,8},{9,1... | collective-permute-start | bytes 2359304 | tf_op jit(solution)/shard_map/ppermute | solution.py:778
  331.2 8.4 %collective-permute-start.38 = (bf16[96,1152]{1,0:T(8,128)(2,1)S(1)}, bf16[96,1152]{1,0:T(8,128)(2,1)S(1)}, u32[]{:S(2)}, u32[]{:S(2)}) collective-permute-start(bf16[96,1152]{1,0:T(8,128)(2,1)S(1)} %get-tuple-element.193), channel_id=1, source_target_pairs={{0,8},{4,12},{8,0},{12,4},{16,24},{20,28},{24,16},{28,20},{1,9},{5... | collective-permute-start | bytes 663560 | tf_op jit(solution)/shard_map/ppermute | solution.py:804
  331.5 23.1 %collective-permute-start.40 = (bf16[432,768]{1,0:T(8,128)(2,1)S(1)}, bf16[432,768]{1,0:T(8,128)(2,1)S(1)}, u32[]{:S(2)}, u32[]{:S(2)}) collective-permute-start(bf16[432,768]{1,0:T(8,128)(2,1)S(1)} %constant_dynamic-update-slice_fusion), channel_id=1, source_target_pairs={{0,8},{4,12},{8,0},{12,4},{16,24},{20,28},{24,16},{28,20},{1,9},{5... | collective-permute-start | bytes 1990664 | tf_op jit(solution)/shard_map/ppermute | solution.py:804
  339.7 12.7 %collective-permute-start.39 = (bf16[48,1152]{1,0:T(8,128)(2,1)S(1)}, bf16[48,1152]{1,0:T(8,128)(2,1)S(1)}, u32[]{:S(2)}, u32[]{:S(2)}) collective-permute-start(bf16[48,1152]{1,0:T(8,128)(2,1)S(1)} %add_convert_fusion.13), channel_id=1, source_target_pairs={{0,16},{4,20},{8,24},{12,28},{16,0},{20,4},{24,8},{28,12},{1,17},{... | collective-permute-start | bytes 331784 | tf_op jit(solution)/shard_map/ppermute | solution.py:804
  341.1 28.3 %collective-permute-start.46 = (bf16[432,768]{1,0:T(8,128)(2,1)S(1)}, bf16[432,768]{1,0:T(8,128)(2,1)S(1)}, u32[]{:S(2)}, u32[]{:S(2)}) collective-permute-start(bf16[432,768]{1,0:T(8,128)(2,1)S(1)} %constant_dynamic-update-slice_fusion), channel_id=1, source_target_pairs={{0,4},{4,0},{8,12},{12,8},{16,20},{20,16},{24,28},{28,24},{1,5},{5... | collective-permute-start | bytes 1990664 | tf_op jit(solution)/shard_map/ppermute | solution.py:847
  354.6 6.8 %collective-permute-start.41 = (bf16[48,1152]{1,0:T(8,128)(2,1)S(1)}, bf16[48,1152]{1,0:T(8,128)(2,1)S(1)}, u32[]{:S(2)}, u32[]{:S(2)}) collective-permute-start(bf16[48,1152]{1,0:T(8,128)(2,1)S(1)} %add_convert_fusion.12), channel_id=1, source_target_pairs={{0,16},{4,20},{8,24},{12,28},{16,0},{20,4},{24,8},{28,12},{1,17},{... | collective-permute-start | bytes 331784 | tf_op jit(solution)/shard_map/ppermute | solution.py:804
  355.9 17.8 %collective-permute-start.45 = (bf16[432,768]{1,0:T(8,128)(2,1)S(1)}, bf16[432,768]{1,0:T(8,128)(2,1)S(1)}, u32[]{:S(2)}, u32[]{:S(2)}) collective-permute-start(bf16[432,768]{1,0:T(8,128)(2,1)S(1)} %collective-permute-done.40), channel_id=1, source_target_pairs={{0,4},{4,0},{8,12},{12,8},{16,20},{20,16},{24,28},{28,24},{1,5},{5... | collective-permute-start | bytes 1990664 | tf_op jit(solution)/shard_map/ppermute | solution.py:847
  361.5 6.0 %collective-permute-start.42 = (bf16[96,1152]{1,0:T(8,128)(2,1)S(1)}, bf16[96,1152]{1,0:T(8,128)(2,1)S(1)}, u32[]{:S(2)}, u32[]{:S(2)}) collective-permute-start(bf16[96,1152]{1,0:T(8,128)(2,1)S(1)} %pad_maximum_fusion.18), channel_id=1, source_target_pairs={{0,8},{4,12},{8,0},{12,4},{16,24},{20,28},{24,16},{28,20},{1,9},{5... | collective-permute-start | bytes 663560 | tf_op jit(solution)/shard_map/ppermute | solution.py:804
  367.6 12.7 %collective-permute-start.44 = (bf16[192,1152]{1,0:T(8,128)(2,1)S(1)}, bf16[192,1152]{1,0:T(8,128)(2,1)S(1)}, u32[]{:S(2)}, u32[]{:S(2)}) collective-permute-start(bf16[192,1152]{1,0:T(8,128)(2,1)S(1)} %pad_maximum_fusion.13), channel_id=1, source_target_pairs={{0,4},{4,0},{8,12},{12,8},{16,20},{20,16},{24,28},{28,24},{1,5},{5... | collective-permute-start | bytes 1327112 | tf_op jit(solution)/shard_map/ppermute | solution.py:847
  (35 other events, 247.0 us)

commit v2 on v1

--- a/solution.py
+++ b/solution.py
@@ -929,7 +929,7 @@
     flat = lax.optimization_barrier((*sums[0], *sums[1], keep))[:-1]
     sums, sent = scatter([flat[:2], flat[2:]], rest[1], dp)
     got = core_swap(after(send, sent))
-    far = x_swap(jnp.concatenate([far, got[part:]], axis=0))
+    far, far2 = x_swap(far), x_swap(got[part:])
     gi_own, gi_nb, gg1 = last_call(
         meta, x_own, x_nb, p_mine, p_got, w_full, w_other, after(dmid, sent), gain1
     )
@@ -938,17 +938,17 @@
     for stride in rest[2:]:
         sums, _ = scatter(sums, stride, dp)
     vs = [total(t).astype(bf16) for t in sums]
-    far = after(far, *vs)
-    far, far2 = far[:part], far[part:]
+    far, far2 = lax.optimization_barrier((far, far2, *vs))[:2]
     ga, gb = keep.astype(f32) + far.astype(f32), got[:part].astype(f32) + far2.astype(f32)
     g_send, g_keep = jnp.where(y == 0, gb, ga).astype(bf16), jnp.where(y == 0, ga, gb)
     pt = [g_keep, y_swap(g_send)]
     gi_got = x_swap(after(gi_nb, g_send))
     for stride in reversed(rest[1:]):
-        *got_v, pt[1] = lax.optimization_barrier((*swap_both(vs, stride, dp), pt[1]))
-        vs = [join(v, g, stride) for v, g in zip(vs, got_v)]
+        cat = jnp.concatenate(vs, axis=0)
+        first_cat = cat if stride == rest[-1] else first_cat
+        got_v = swap(cat, stride, dp)
+        vs = [join(v, g, stride) for v, g in zip(vs, rows_as(got_v, vs))]
     (pt,), sent = scatter([pt], rest[0], dp)
-    *vs, _ = lax.optimization_barrier((*vs, sent))
     packed_vs = jnp.concatenate(vs, axis=0)
     near_got = swap(packed_vs, rest[0], dp)
     across = rows_as(y_swap(packed_vs), vs)
@@ -972,6 +972,7 @@
     gt = jnp.where(jnp.arange(2)[:, None, None, None] == c, gt[None], 0.0).reshape(4, 9, part)
     gains = jnp.concatenate([gg1, gg2], axis=0).reshape(2, 4, part).transpose(1, 0, 2)
     small = jnp.concatenate([gt, gains, jnp.zeros((4, 5, part), f32)], axis=1)
+    small = after(small, first_cat)
     small = jnp.broadcast_to(small[:, None], (4, dp, 16, part)).reshape(4 * dp, 16, part)
     small = jnp.sum(lax.all_to_all(small, ("head", "dp"), 0, 0, tiled=True), axis=0)
     output = order(after(out_own, g_send), out_x)

time: 384 us -> 371 us (0.966)
  waiting for transfers between devices: 108 us -> 97.7 us
  starting transfers between devices: 44.3 us -> 39.4 us
    ppermute x11, waiting for transfers between devices: 46.3 us -> 28.2 us  [swap(): return lax.ppermute(v, 'dp', flip(dp, stride))]
    ppermute x7, waiting for transfers between devices: 6.41 us -> 13.1 us  [local(): y_swap = lambda v: lax.ppermute(v, 'dp', flip(dp, 1))]
    select_n x10, other arithmetic: 0.93 us -> 5.4 us  [join(): jnp.where(upper, got, mine)]
    ppermute x10 -> x11, starting transfers between devices: 12.4 us -> 12.7 us  [x_swap(): return lax.ppermute(v, 'head', XNB)]
    ppermute x10 -> x11, waiting for transfers between devices: 45.4 us -> 45.3 us  [x_swap(): return lax.ppermute(v, 'head', XNB)]
  transfers between devices with their start and end apart: 48 -> 49, of which waited for: 19 -> 19; matrix products, arithmetic and copies ran while one was open for 11% -> 12% of each run, Pallas kernels for 33% -> 35%
where the time goes in v2:
time: 371 us; the launch traced here: 370 us
  Pallas kernels  177 us (48%)
  waiting for transfers between devices  97.7 us (26%)
  starting transfers between devices  39.4 us (11%)
  other arithmetic  37.5 us (10%)
  local copies, waits for them, and re-layouts  16.7 us (5%)
    pallas_call x2, Pallas kernels, att_bwd_call(): pl.pallas_call(functools.partial(att_bwd_body, p0, into is not None), out...  66.2 us
    pallas_call x1, Pallas kernels, ffn_call(): pl.pallas_call(ffn_body, out_shape=[sds((2, rows, width), f32), sds((rows...  49.3 us
    ppermute x11, waiting for transfers between devices, x_swap(): return lax.ppermute(v, 'head', XNB)  45.3 us
    ppermute x11, waiting for transfers between devices, swap(): return lax.ppermute(v, 'dp', flip(dp, stride))  28.2 us
    pallas_call x1, Pallas kernels, att_fwd_call(): pl.pallas_call(att_fwd_body, out_shape=[sds((length // 2, width), bf16),...  27.3 us
    pallas_call x1, Pallas kernels, qkv_call(): pl.pallas_call(qkv_body, out_shape=[sds((length, width), bf16), sds((leng...  13.5 us
    ppermute x7, waiting for transfers between devices, local(): y_swap = lambda v: lax.ppermute(v, 'dp', flip(dp, 1))  13.1 us
    ppermute x11, starting transfers between devices, x_swap(): return lax.ppermute(v, 'head', XNB)  12.7 us
  transfers between devices with their start and end apart: 49, of which 19 were waited for; matrix products, arithmetic and copies ran while one was open for 12% of the time, Pallas kernels for 35%

profile of v2, /device:TPU:0, one launch (start us, length us, event | category | flops | bytes accessed | tf_op | source)
XLA Modules:
  0.0 370.1 jit_solution(1374683399259353030)
XLA Ops:
  4.4 1.5 collective-permute-done.3.wb
  6.9 3.2 collective-permute-start.4
  13.0 2.5 dynamic-slice_bitcast_fusion.1
  16.7 2.2 pad_maximum_fusion.1
  18.9 29.4 %collective-permute-done.x1.xx = bf16[512,768]{1,0:T(8,128)(2,1)} collective-permute-done((bf16[512,768]{1,0:T(8,128)(2,1)}, bf16[512,768]{1,0:T(8,128)(2,1)}, u32[]{:S(2)}, u32[]{:S(2)}) %collective-permute-start) | collective-permute-done | bytes 786464 | tf_op jit(solution)/shard_map/ppermute | solution.py:778
  49.4 1.7 collective-permute-start.5
  51.2 2.6 collective-permute-done.6.x3
  54.7 13.5 %qkv.1 = (bf16[2048,768]{1,0:T(8,128)(2,1)}, bf16[2048,1152]{1,0:T(8,128)(2,1)}, bf16[2048,1152]{1,0:T(8,128)(2,1)}, bf16[768,1152]{1,0:T(8,128)(2,1)}, f32[8,1152]{1,0:T(8,128)}) custom-call(s32[4]{0:T(128)} %pad_add_fusion.meta, bf16[512,768]{1,0:T(8,128)(2,1)} %copy-done, bf16[512,768]{1,0:T(8,128)(2,1)} %collective-permute-done.x1.xx, ...), custom_call_target="tpu_custom_call" | custom-call | flops 3623878656 | bytes 15728640 | tf_op jit(solution)/shard_map/qkv/pallas_call | solution.py:131
  68.6 1.7 collective-permute-start.10
  70.3 1.5 collective-permute-start.7
  71.8 1.6 collective-permute-start.8
  73.8 27.3 %attn_fwd.1 = (bf16[1024,384]{1,0:T(8,128)(2,1)}, bf16[1024,384]{1,0:T(8,128)(2,1)}, f32[3,2,2048]{2,1,0:T(2,128)}) custom-call(s32[4]{0:T(128)} %pad_add_fusion.meta, bf16[2048,1152]{1,0:T(8,128)(2,1)} %get-tuple-element.129.q_ref.k_ref.v_ref, bf16[2048,1152]{1,0:T(8,128)(2,1)} %get-tuple-element.129.q_ref.k_ref.v_ref, ...), custom_call_target="tpu_custom_call" | custom-call | flops 12884901888 | bytes 6291456 | tf_op jit(solution)/shard_map/attn_fwd/pallas_call | solution.py:255
  102.9 2.4 collective-permute-done.14.c0
  105.4 1.7 collective-permute-done.16.c2
  109.6 49.3 %ffn.1 = (f32[2,512,768]{2,1,0:T(8,128)}, bf16[512,768]{1,0:T(8,128)(2,1)}, bf16[1024,384]{1,0:T(8,128)(2,1)}, bf16[1024,384]{1,0:T(8,128)(2,1)}, f32[1,768]{1,0...) custom-call(s32[4]{0:T(128)} %pad_add_fusion.meta, ...), custom_call_target="tpu_custom_call" | custom-call | flops 32614907904 | bytes 31457280 | tf_op jit(solution)/shard_map/ffn/pallas_call | solution.py:623
  160.1 1.9 collective-permute-done.19
  163.0 3.1 add_convert_fusion
  166.2 2.0 collective-permute-start.25
  169.2 1.5 collective-permute-start.22
  170.8 2.6 add_convert_fusion.2
  173.8 42.7 %attn_bwd.2 = (bf16[1024,1152]{1,0:T(8,128)(2,1)}, bf16[1024,1152]{1,0:T(8,128)(2,1)}, f32[16,256]{1,0:T(8,128)}) custom-call(s32[4]{0:T(128)} %pad_add_fusion.meta, bf16[2048,1152]{1,0:T(8,128)(2,1)} %get-tuple-element.129.q_ref.k_ref.v_ref, bf16[2048,1152]{1,0:T(8,128)(2,1)} %get-tuple-element.129.q_ref.k_ref.v_ref, ...), custom_call_target="tpu_custom_call" | custom-call | flops 15032385536 | bytes 10485760 | tf_op jit(solution)/shard_map/attn_bwd/pallas_call | solution.py:407
  216.6 2.6 add_convert_fusion.1
  219.4 2.9 convert_add_fusion.1
  222.3 1.8 collective-permute-start.27
  224.1 23.6 %attn_bwd.3 = (bf16[1024,1152]{1,0:T(8,128)(2,1)}, bf16[1024,1152]{1,0:T(8,128)(2,1)}, f32[16,128]{1,0:T(8,128)}) custom-call(s32[4]{0:T(128)} %pad_add_fusion.meta, bf16[2048,1152]{1,0:T(8,128)(2,1)} %get-tuple-element.129.q_ref.k_ref.v_ref, ...), custom_call_target="tpu_custom_call", output_to_operand_aliasing={{0}: (13, {}), {1}: (14, {})} | custom-call | flops 7516192768 | bytes 5242880 | tf_op jit(solution)/shard_map/attn_bwd/pallas_call | solution.py:407
  249.8 1.5 convert_add_fusion.4
  251.4 1.6 collective-permute-start.29
  253.0 9.6 %projg.1 = (bf16[192,1152]{1,0:T(8,128)(2,1)}, bf16[192,1152]{1,0:T(8,128)(2,1)}, bf16[384,1152]{1,0:T(8,128)(2,1)}) custom-call(s32[4]{0:T(128)} %pad_add_fusion.meta, bf16[2048,768]{1,0:T(8,128)(2,1)} %get-tuple-element.136.h, bf16[1024,1152]{1,0:T(8,128)(2,1)} %get-tuple-element.137.dm, bf16[1024,1152]{1,0:T(8,128)(2,1)} %get-tuple-element.138.dt), custom_call_target="tpu_custom_call" | custom-call | flops 2048 | bytes 2048 | tf_op jit(solution)/shard_map/projg/pallas_call | solution.py:692
  262.6 6.1 %collective-permute-done.29 = bf16[432,768]{1,0:T(8,128)(2,1)S(1)} collective-permute-done((bf16[432,768]{1,0:T(8,128)(2,1)S(1)}, bf16[432,768]{1,0:T(8,128)(2,1)S(1)}, u32[]{:S(2)}, u32[]{:S(2)}) %collective-permute-start.29) | collective-permute-done | bytes 663584 | tf_op jit(solution)/shard_map/ppermute | solution.py:804
  269.1 2.7 collective-permute-start.33
  271.7 11.4 %last.1 = (f32[2,512,768]{2,1,0:T(8,128)}, bf16[512,768]{1,0:T(8,128)(2,1)}, f32[1,768]{1,0:T(1,128)}) custom-call(s32[4]{0:T(128)} %pad_add_fusion.meta, bf16[512,768]{1,0:T(8,128)(2,1)} %copy-done, bf16[512,768]{1,0:T(8,128)(2,1)} %collective-permute-done.x1.xx, bf16[1024,1152]{1,0:T(8,128)(2,1)} %get-tuple-element.137.dm, ...), custom_call_target="tpu_custom_call" | custom-call | flops 512 | bytes 512 | tf_op jit(solution)/shard_map/last/pallas_call | solution.py:750
  284.5 1.5 collective-permute-start.36
  288.1 1.5 collective-permute-start.32
  291.0 4.4 %all-to-all-start = ((f32[32,16,192]{2,1,0:T(8,128)}), f32[32,16,192]{2,1,0:T(8,128)S(1)}, u32[]{:S(2)}, u32[]{:S(2)}) async-start(f32[32,16,192]{2,1,0:T(8,128)} %bitcast.16), calls=%async_computation | async-start | bytes 1048576 | tf_op jit(solution)/shard_map/all_to_all | solution.py:977
  295.5 4.2 %collective-permute-done.31 = bf16[192,1152]{1,0:T(8,128)(2,1)S(1)} collective-permute-done((bf16[192,1152]{1,0:T(8,128)(2,1)}, bf16[192,1152]{1,0:T(8,128)(2,1)S(1)}, u32[]{:S(2)}, u32[]{:S(2)}) %collective-permute-start.31) | collective-permute-done | bytes 442400 | tf_op jit(solution)/shard_map/ppermute | solution.py:778
  299.7 11.7 %collective-permute-done.32 = bf16[192,1152]{1,0:T(8,128)(2,1)} collective-permute-done((bf16[192,1152]{1,0:T(8,128)(2,1)}, bf16[192,1152]{1,0:T(8,128)(2,1)}, u32[]{:S(2)}, u32[]{:S(2)}) %collective-permute-start.32) | collective-permute-done | bytes 442400 | tf_op jit(solution)/shard_map/ppermute | solution.py:778
  315.2 1.7 collective-permute-start.47
  317.1 9.1 %collective-permute-done.37 = bf16[192,1152]{1,0:T(8,128)(2,1)S(1)} collective-permute-done((bf16[192,1152]{1,0:T(8,128)(2,1)S(1)}, bf16[192,1152]{1,0:T(8,128)(2,1)S(1)}, u32[]{:S(2)}, u32[]{:S(2)}) %collective-permute-start.37) | collective-permute-done | bytes 442400 | tf_op jit(solution)/shard_map/ppermute | solution.py:847
  326.3 2.2 collective-permute-start.38
  328.4 2.4 convert_dynamic-update-slice_fusion.1
  330.9 4.5 %collective-permute-done.38 = bf16[96,1152]{1,0:T(8,128)(2,1)S(1)} collective-permute-done((bf16[96,1152]{1,0:T(8,128)(2,1)S(1)}, bf16[96,1152]{1,0:T(8,128)(2,1)S(1)}, u32[]{:S(2)}, u32[]{:S(2)}) %collective-permute-start.38) | collective-permute-done | bytes 221216 | tf_op jit(solution)/shard_map/ppermute | solution.py:804
  337.4 4.6 %collective-permute-done.39 = bf16[48,1152]{1,0:T(8,128)(2,1)S(1)} collective-permute-done((bf16[48,1152]{1,0:T(8,128)(2,1)S(1)}, bf16[48,1152]{1,0:T(8,128)(2,1)S(1)}, u32[]{:S(2)}, u32[]{:S(2)}) %collective-permute-start.39) | collective-permute-done | bytes 110624 | tf_op jit(solution)/shard_map/ppermute | solution.py:804
  343.2 5.5 %collective-permute-done.42 = bf16[48,1152]{1,0:T(8,128)(2,1)S(1)} collective-permute-done((bf16[48,1152]{1,0:T(8,128)(2,1)S(1)}, bf16[48,1152]{1,0:T(8,128)(2,1)S(1)}, u32[]{:S(2)}, u32[]{:S(2)}) %collective-permute-start.42) | collective-permute-done | bytes 110624 | tf_op jit(solution)/shard_map/ppermute | solution.py:804
  350.1 6.0 %collective-permute-done.43 = bf16[96,1152]{1,0:T(8,128)(2,1)S(1)} collective-permute-done((bf16[96,1152]{1,0:T(8,128)(2,1)S(1)}, bf16[96,1152]{1,0:T(8,128)(2,1)S(1)}, u32[]{:S(2)}, u32[]{:S(2)}) %collective-permute-start.43) | collective-permute-done | bytes 221216 | tf_op jit(solution)/shard_map/ppermute | solution.py:804
  356.4 1.4 broadcast_select_fusion.9
  360.2 1.6 fusion
  361.7 1.6 maximum_convert_fusion
  363.3 4.0 %collective-permute-done.45 = bf16[192,1152]{1,0:T(8,128)(2,1)S(1)} collective-permute-done((bf16[192,1152]{1,0:T(8,128)(2,1)S(1)}, bf16[192,1152]{1,0:T(8,128)(2,1)S(1)}, u32[]{:S(2)}, u32[]{:S(2)}) %collective-permute-start.45) | collective-permute-done | bytes 442400 | tf_op jit(solution)/shard_map/ppermute | solution.py:847
  (202 shorter events, 41.4 us)
Async XLA Ops:
  3.9 2.0 collective-permute-start.3
  4.3 12.3 %collective-permute-start.1 = (bf16[192,768]{1,0:T(8,128)(2,1)}, bf16[192,768]{1,0:T(8,128)(2,1)}, u32[]{:S(2)}, u32[]{:S(2)}) collective-permute-start(bf16[192,768]{1,0:T(8,128)(2,1)} %wo_o.1), channel_id=1, source_target_pairs={{0,1},{1,0},{2,3},{3,2},{4,5},{5,4},{6,7},{7,6},{8,9},{9,8},{10,11... | collective-permute-start | bytes 884744 | tf_op jit(solution)/shard_map/ppermute | solution.py:774
  6.9 41.4 %collective-permute-start.4 = (bf16[608,768]{1,0:T(8,128)(2,1)}, bf16[608,768]{1,0:T(8,128)(2,1)}, u32[]{:S(2)}, u32[]{:S(2)}) collective-permute-start(bf16[608,768]{1,0:T(8,128)(2,1)} %pad_maximum_fusion.3), channel_id=1, source_target_pairs={{0,2},{2,0},{1,3},{3,1},{4,6},{6,4},{5,7},{7,5},{8,10},{10,8},{9,1... | collective-permute-start | bytes 2801672 | tf_op jit(solution)/shard_map/ppermute | solution.py:778
  11.1 37.2 %collective-permute-start = (bf16[512,768]{1,0:T(8,128)(2,1)}, bf16[512,768]{1,0:T(8,128)(2,1)}, u32[]{:S(2)}, u32[]{:S(2)}) collective-permute-start(bf16[512,768]{1,0:T(8,128)(2,1)} %get-tuple-element.178), channel_id=1, source_target_pairs={{0,2},{2,0},{1,3},{3,1},{4,6},{6,4},{5,7},{7,5},{8,10},{10,8},{9,1... | collective-permute-start | bytes 2359304 | tf_op jit(solution)/shard_map/ppermute | solution.py:778
  11.1 37.2 %collective-permute-start.2 = (bf16[512,768]{1,0:T(8,128)(2,1)S(1)}, bf16[512,768]{1,0:T(8,128)(2,1)}, u32[]{:S(2)}, u32[]{:S(2)}) collective-permute-start(bf16[512,768]{1,0:T(8,128)(2,1)S(1)} %get-tuple-element.177.x0.xo), channel_id=1, source_target_pairs={{0,1},{1,0},{2,3},{3,2},{4,5},{5,4},{6,7},{7,6},{8,9},{9,8},{10,11... | collective-permute-start | bytes 2359304 | tf_op jit(solution)/shard_map/ppermute | solution.py:774
  48.3 25.1 %collective-permute-start.11 = (bf16[2,768,768]{2,1,0:T(8,128)(2,1)S(1)}, bf16[2,768,768]{2,1,0:T(8,128)(2,1)}, u32[]{:S(2)}, u32[]{:S(2)}) collective-permute-start(bf16[2,768,768]{2,1,0:T(8,128)(2,1)S(1)} %pad_maximum_fusion), channel_id=1, source_target_pairs={{0,1},{1,0},{2,3},{3,2},{4,5},{5,4},{6,7},{7,6},{8,9},{9,8},{10,11... | collective-permute-start | bytes 7077896 | tf_op jit(solution)/shard_map/ppermute | solution.py:774
  48.3 5.5 %collective-permute-start.6 = (bf16[512,768]{1,0:T(8,128)(2,1)}, bf16[512,768]{1,0:T(8,128)(2,1)S(1)}, u32[]{:S(2)}, u32[]{:S(2)}) collective-permute-start(bf16[512,768]{1,0:T(8,128)(2,1)} %collective-permute-done.x1.xx), channel_id=1, source_target_pairs={{0,1},{1,0},{2,3},{3,2},{4,5},{5,4},{6,7},{7,6},{8,9},{9,8},{10,11... | collective-permute-start | bytes 2359304 | tf_op jit(solution)/shard_map/ppermute | solution.py:774
  49.4 20.9 %collective-permute-start.5 = (bf16[2,192,768]{2,1,0:T(8,128)(2,1)}, bf16[2,192,768]{2,1,0:T(8,128)(2,1)}, u32[]{:S(2)}, u32[]{:S(2)}) collective-permute-start(bf16[2,192,768]{2,1,0:T(8,128)(2,1)} %pad_maximum_fusion.10), channel_id=1, source_target_pairs={{0,2},{2,0},{1,3},{3,1},{4,6},{6,4},{5,7},{7,5},{8,10},{10,8},{9,1... | collective-permute-start | bytes 1769480 | tf_op jit(solution)/shard_map/ppermute | solution.py:778
  68.2 34.1 %collective-permute-start.13 = (bf16[768,1152]{1,0:T(8,128)(2,1)}, bf16[768,1152]{1,0:T(8,128)(2,1)}, u32[]{:S(2)}, u32[]{:S(2)}) collective-permute-start(bf16[768,1152]{1,0:T(8,128)(2,1)} %get-tuple-element.103.wm), channel_id=1, source_target_pairs={{0,1},{1,0},{2,3},{3,2},{4,5},{5,4},{6,7},{7,6},{8,9},{9,8},{10,11... | collective-permute-start | bytes 5308424 | tf_op jit(solution)/shard_map/ppermute | solution.py:774
  68.6 33.1 %collective-permute-start.10 = (bf16[896,768]{1,0:T(8,128)(2,1)}, bf16[896,768]{1,0:T(8,128)(2,1)}, u32[]{:S(2)}, u32[]{:S(2)}) collective-permute-start(bf16[896,768]{1,0:T(8,128)(2,1)} %pad_maximum_fusion.1), channel_id=1, source_target_pairs={{0,2},{2,0},{1,3},{3,1},{4,6},{6,4},{5,7},{7,5},{8,10},{10,8},{9,1... | collective-permute-start | bytes 4128776 | tf_op jit(solution)/shard_map/ppermute | solution.py:778
  70.3 30.8 %collective-permute-start.7 = (bf16[2,192,768]{2,1,0:T(8,128)(2,1)}, bf16[2,192,768]{2,1,0:T(8,128)(2,1)S(1)}, u32[]{:S(2)}, u32[]{:S(2)}) collective-permute-start(bf16[2,192,768]{2,1,0:T(8,128)(2,1)} %collective-permute-done.5.n0), channel_id=1, source_target_pairs={{0,4},{4,0},{8,12},{12,8},{16,20},{20,16},{24,28},{28,24},{1,5},{5... | collective-permute-start | bytes 1769480 | tf_op jit(solution)/shard_map/ppermute | solution.py:804
  71.8 29.4 %collective-permute-start.8 = (bf16[2,192,768]{2,1,0:T(8,128)(2,1)}, bf16[2,192,768]{2,1,0:T(8,128)(2,1)}, u32[]{:S(2)}, u32[]{:S(2)}) collective-permute-start(bf16[2,192,768]{2,1,0:T(8,128)(2,1)} %collective-permute-done.5.n0), channel_id=1, source_target_pairs={{0,8},{4,12},{8,0},{12,4},{16,24},{20,28},{24,16},{28,20},{1,9},{5... | collective-permute-start | bytes 1769480 | tf_op jit(solution)/shard_map/ppermute | solution.py:804
  73.4 28.3 %collective-permute-start.9 = (bf16[2,192,768]{2,1,0:T(8,128)(2,1)}, bf16[2,192,768]{2,1,0:T(8,128)(2,1)S(1)}, u32[]{:S(2)}, u32[]{:S(2)}) collective-permute-start(bf16[2,192,768]{2,1,0:T(8,128)(2,1)} %collective-permute-done.5.n0), channel_id=1, source_target_pairs={{0,12},{4,8},{8,4},{12,0},{16,28},{20,24},{24,20},{28,16},{1,13},{... | collective-permute-start | bytes 1769480 | tf_op jit(solution)/shard_map/ppermute | solution.py:804
  101.1 7.6 %collective-permute-start.12 = (bf16[1024,384]{1,0:T(8,128)(2,1)}, bf16[1024,384]{1,0:T(8,128)(2,1)S(1)}, u32[]{:S(2)}, u32[]{:S(2)}) collective-permute-start(bf16[1024,384]{1,0:T(8,128)(2,1)} %get-tuple-element.102.ot), channel_id=1, source_target_pairs={{0,1},{1,0},{2,3},{3,2},{4,5},{5,4},{6,7},{7,6},{8,9},{9,8},{10,11... | collective-permute-start | bytes 2359304 | tf_op jit(solution)/shard_map/ppermute | solution.py:774
  101.2 4.2 %collective-permute-start.14 = (bf16[2,192,768]{2,1,0:T(8,128)(2,1)}, bf16[2,192,768]{2,1,0:T(8,128)(2,1)S(1)}, u32[]{:S(2)}, u32[]{:S(2)}) collective-permute-start(bf16[2,192,768]{2,1,0:T(8,128)(2,1)} %collective-permute-done.5.n0), channel_id=1, source_target_pairs={{0,1},{1,0},{2,3},{3,2},{4,5},{5,4},{6,7},{7,6},{8,9},{9,8},{10,11... | collective-permute-start | bytes 1769480 | tf_op jit(solution)/shard_map/ppermute | solution.py:774
  101.7 3.7 collective-permute-start.15
  101.8 5.2 %collective-permute-start.16 = (bf16[2,192,768]{2,1,0:T(8,128)(2,1)}, bf16[2,192,768]{2,1,0:T(8,128)(2,1)S(1)}, u32[]{:S(2)}, u32[]{:S(2)}) collective-permute-start(bf16[2,192,768]{2,1,0:T(8,128)(2,1)} %collective-permute-done.8.n2), channel_id=1, source_target_pairs={{0,1},{1,0},{2,3},{3,2},{4,5},{5,4},{6,7},{7,6},{8,9},{9,8},{10,11... | collective-permute-start | bytes 1769480 | tf_op jit(solution)/shard_map/ppermute | solution.py:774
  102.3 4.8 %collective-permute-start.17 = (bf16[2,192,768]{2,1,0:T(8,128)(2,1)S(1)}, bf16[2,192,768]{2,1,0:T(8,128)(2,1)S(1)}, u32[]{:S(2)}, u32[]{:S(2)}) collective-permute-start(bf16[2,192,768]{2,1,0:T(8,128)(2,1)S(1)} %collective-permute-done.9.n3), channel_id=1, source_target_pairs={{0,1},{1,0},{2,3},{3,2},{4,5},{5,4},{6,7},{7,6},{8,9},{9,8},{10,11... | collective-permute-start | bytes 1769480 | tf_op jit(solution)/shard_map/ppermute | solution.py:774
  158.9 3.1 collective-permute-start.19
  159.1 7.1 %collective-permute-start.21 = (bf16[960,768]{1,0:T(8,128)(2,1)}, bf16[960,768]{1,0:T(8,128)(2,1)S(1)}, u32[]{:S(2)}, u32[]{:S(2)}) collective-permute-start(bf16[960,768]{1,0:T(8,128)(2,1)} %get-tuple-element.115), channel_id=1, source_target_pairs={{0,1},{1,0},{2,3},{3,2},{4,5},{5,4},{6,7},{7,6},{8,9},{9,8},{10,11... | collective-permute-start | bytes 4423688 | tf_op jit(solution)/shard_map/ppermute | solution.py:774
  159.4 9.8 %collective-permute-start.23 = (bf16[960,768]{1,0:T(8,128)(2,1)}, bf16[960,768]{1,0:T(8,128)(2,1)}, u32[]{:S(2)}, u32[]{:S(2)}) collective-permute-start(bf16[960,768]{1,0:T(8,128)(2,1)} %get-tuple-element.117), channel_id=1, source_target_pairs={{0,1},{1,0},{2,3},{3,2},{4,5},{5,4},{6,7},{7,6},{8,9},{9,8},{10,11... | collective-permute-start | bytes 4423688 | tf_op jit(solution)/shard_map/ppermute | solution.py:774
  159.6 13.8 %collective-permute-start.26 = (bf16[1024,384]{1,0:T(8,128)(2,1)}, bf16[1024,384]{1,0:T(8,128)(2,1)}, u32[]{:S(2)}, u32[]{:S(2)}) collective-permute-start(bf16[1024,384]{1,0:T(8,128)(2,1)} %get-tuple-element.122), channel_id=1, source_target_pairs={{0,1},{1,0},{2,3},{3,2},{4,5},{5,4},{6,7},{7,6},{8,9},{9,8},{10,11... | collective-permute-start | bytes 2359304 | tf_op jit(solution)/shard_map/ppermute | solution.py:774
  160.0 59.5 %collective-permute-start.18 = (bf16[768,768]{1,0:T(8,128)(2,1)}, bf16[768,768]{1,0:T(8,128)(2,1)}, u32[]{:S(2)}, u32[]{:S(2)}) collective-permute-start(bf16[768,768]{1,0:T(8,128)(2,1)} %get-tuple-element.111), channel_id=1, source_target_pairs={{0,1},{1,0},{2,3},{3,2},{4,5},{5,4},{6,7},{7,6},{8,9},{9,8},{10,11... | collective-permute-start | bytes 3538952 | tf_op jit(solution)/shard_map/ppermute | solution.py:774
  166.1 50.4 %collective-permute-start.20 = (bf16[768,768]{1,0:T(8,128)(2,1)}, bf16[768,768]{1,0:T(8,128)(2,1)}, u32[]{:S(2)}, u32[]{:S(2)}) collective-permute-start(bf16[768,768]{1,0:T(8,128)(2,1)} %add_convert_fusion), channel_id=1, source_target_pairs={{0,2},{2,0},{1,3},{3,1},{4,6},{6,4},{5,7},{7,5},{8,10},{10,8},{9,1... | collective-permute-start | bytes 3538952 | tf_op jit(solution)/shard_map/ppermute | solution.py:778
  166.2 50.3 %collective-permute-start.25 = (bf16[512,768]{1,0:T(8,128)(2,1)}, bf16[512,768]{1,0:T(8,128)(2,1)}, u32[]{:S(2)}, u32[]{:S(2)}) collective-permute-start(bf16[512,768]{1,0:T(8,128)(2,1)} %get-tuple-element.119), channel_id=1, source_target_pairs={{0,2},{2,0},{1,3},{3,1},{4,6},{6,4},{5,7},{7,5},{8,10},{10,8},{9,1... | collective-permute-start | bytes 2359304 | tf_op jit(solution)/shard_map/ppermute | solution.py:778
  169.2 47.3 %collective-permute-start.22 = (bf16[480,768]{1,0:T(8,128)(2,1)}, bf16[480,768]{1,0:T(8,128)(2,1)}, u32[]{:S(2)}, u32[]{:S(2)}) collective-permute-start(bf16[480,768]{1,0:T(8,128)(2,1)} %add_convert_fusion.3), channel_id=1, source_target_pairs={{0,4},{4,0},{8,12},{12,8},{16,20},{20,16},{24,28},{28,24},{1,5},{5... | collective-permute-start | bytes 2211848 | tf_op jit(solution)/shard_map/ppermute | solution.py:847
  173.3 43.2 %collective-permute-start.24 = (bf16[480,768]{1,0:T(8,128)(2,1)}, bf16[480,768]{1,0:T(8,128)(2,1)}, u32[]{:S(2)}, u32[]{:S(2)}) collective-permute-start(bf16[480,768]{1,0:T(8,128)(2,1)} %get-tuple-element.171), channel_id=1, source_target_pairs={{0,4},{4,0},{8,12},{12,8},{16,20},{20,16},{24,28},{28,24},{1,5},{5... | collective-permute-start | bytes 2211848 | tf_op jit(solution)/shard_map/ppermute | solution.py:847
  219.2 28.7 %collective-permute-start.28 = (bf16[480,768]{1,0:T(8,128)(2,1)}, bf16[480,768]{1,0:T(8,128)(2,1)}, u32[]{:S(2)}, u32[]{:S(2)}) collective-permute-start(bf16[480,768]{1,0:T(8,128)(2,1)} %add_convert_fusion.1), channel_id=1, source_target_pairs={{0,2},{2,0},{1,3},{3,1},{4,6},{6,4},{5,7},{7,5},{8,10},{10,8},{9,1... | collective-permute-start | bytes 2211848 | tf_op jit(solution)/shard_map/ppermute | solution.py:778
  222.3 25.5 %collective-permute-start.27 = (bf16[384,768]{1,0:T(8,128)(2,1)}, bf16[384,768]{1,0:T(8,128)(2,1)S(1)}, u32[]{:S(2)}, u32[]{:S(2)}) collective-permute-start(bf16[384,768]{1,0:T(8,128)(2,1)} %get-tuple-element.168), channel_id=1, source_target_pairs={{0,4},{4,0},{8,12},{12,8},{16,20},{20,16},{24,28},{28,24},{1,5},{5... | collective-permute-start | bytes 1769480 | tf_op jit(solution)/shard_map/ppermute | solution.py:847
  247.7 24.0 %collective-permute-start.34 = (bf16[1024,1152]{1,0:T(8,128)(2,1)}, bf16[1024,1152]{1,0:T(8,128)(2,1)}, u32[]{:S(2)}, u32[]{:S(2)}) collective-permute-start(bf16[1024,1152]{1,0:T(8,128)(2,1)} %get-tuple-element.138.dt), channel_id=1, source_target_pairs={{0,1},{1,0},{2,3},{3,2},{4,5},{5,4},{6,7},{7,6},{8,9},{9,8},{10,11... | collective-permute-start | bytes 7077896 | tf_op jit(solution)/shard_map/ppermute | solution.py:774
  251.4 17.3 %collective-permute-start.29 = (bf16[432,768]{1,0:T(8,128)(2,1)S(1)}, bf16[432,768]{1,0:T(8,128)(2,1)S(1)}, u32[]{:S(2)}, u32[]{:S(2)}) collective-permute-start(bf16[432,768]{1,0:T(8,128)(2,1)S(1)} %pad_maximum_fusion.6), channel_id=1, source_target_pairs={{0,8},{4,12},{8,0},{12,4},{16,24},{20,28},{24,16},{28,20},{1,9},{5... | collective-permute-start | bytes 1990664 | tf_op jit(solution)/shard_map/ppermute | solution.py:804
  269.0 18.3 %collective-permute-start.30 = (bf16[384,1152]{1,0:T(8,128)(2,1)}, bf16[384,1152]{1,0:T(8,128)(2,1)S(1)}, u32[]{:S(2)}, u32[]{:S(2)}) collective-permute-start(bf16[384,1152]{1,0:T(8,128)(2,1)} %get-tuple-element.145), channel_id=1, source_target_pairs={{0,1},{1,0},{2,3},{3,2},{4,5},{5,4},{6,7},{7,6},{8,9},{9,8},{10,11... | collective-permute-start | bytes 2654216 | tf_op jit(solution)/shard_map/ppermute | solution.py:774
  269.1 18.2 %collective-permute-start.33 = (bf16[216,768]{1,0:T(8,128)(2,1)S(1)}, bf16[216,768]{1,0:T(8,128)(2,1)S(1)}, u32[]{:S(2)}, u32[]{:S(2)}) collective-permute-start(bf16[216,768]{1,0:T(8,128)(2,1)S(1)} %pad_maximum_fusion.15), channel_id=1, source_target_pairs={{0,16},{4,20},{8,24},{12,28},{16,0},{20,4},{24,8},{28,12},{1,17},{... | collective-permute-start | bytes 995336 | tf_op jit(solution)/shard_map/ppermute | solution.py:804
  284.5 5.1 %collective-permute-start.36 = (f32[1,768]{1,0:T(1,128)S(1)}, f32[1,768]{1,0:T(1,128)S(1)}, u32[]{:S(2)}, u32[]{:S(2)}) collective-permute-start(f32[1,768]{1,0:T(1,128)S(1)} %collective-permute-done.35), channel_id=1, source_target_pairs={{0,2},{2,0},{1,3},{3,1},{4,6},{6,4},{5,7},{7,5},{8,10},{10,8},{9,1... | collective-permute-start | bytes 9224 | tf_op jit(solution)/shard_map/ppermute | solution.py:778
  286.1 13.7 %collective-permute-start.31 = (bf16[192,1152]{1,0:T(8,128)(2,1)}, bf16[192,1152]{1,0:T(8,128)(2,1)S(1)}, u32[]{:S(2)}, u32[]{:S(2)}) collective-permute-start(bf16[192,1152]{1,0:T(8,128)(2,1)} %get-tuple-element.146), channel_id=1, source_target_pairs={{0,2},{2,0},{1,3},{3,1},{4,6},{6,4},{5,7},{7,5},{8,10},{10,8},{9,1... | collective-permute-start | bytes 1327112 | tf_op jit(solution)/shard_map/ppermute | solution.py:778
  288.1 23.3 %collective-permute-start.32 = (bf16[192,1152]{1,0:T(8,128)(2,1)}, bf16[192,1152]{1,0:T(8,128)(2,1)}, u32[]{:S(2)}, u32[]{:S(2)}) collective-permute-start(bf16[192,1152]{1,0:T(8,128)(2,1)} %slice.133), channel_id=1, source_target_pairs={{0,2},{2,0},{1,3},{3,1},{4,6},{6,4},{5,7},{7,5},{8,10},{10,8},{9,1... | collective-permute-start | bytes 1327112 | tf_op jit(solution)/shard_map/ppermute | solution.py:778
  289.9 24.2 %collective-permute-start.40 = (bf16[216,768]{1,0:T(8,128)(2,1)S(1)}, bf16[216,768]{1,0:T(8,128)(2,1)S(1)}, u32[]{:S(2)}, u32[]{:S(2)}) collective-permute-start(bf16[216,768]{1,0:T(8,128)(2,1)S(1)} %pad_maximum_fusion.16), channel_id=1, source_target_pairs={{0,16},{4,20},{8,24},{12,28},{16,0},{20,4},{24,8},{28,12},{1,17},{... | collective-permute-start | bytes 995336 | tf_op jit(solution)/shard_map/ppermute | solution.py:804
  291.0 39.8 %all-to-all-start = ((f32[32,16,192]{2,1,0:T(8,128)}), f32[32,16,192]{2,1,0:T(8,128)S(1)}, u32[]{:S(2)}, u32[]{:S(2)}) async-start(f32[32,16,192]{2,1,0:T(8,128)} %bitcast.16), calls=%async_computation | async-start | bytes 1048576 | tf_op jit(solution)/shard_map/all_to_all | solution.py:977
  312.7 13.5 %collective-permute-start.37 = (bf16[192,1152]{1,0:T(8,128)(2,1)S(1)}, bf16[192,1152]{1,0:T(8,128)(2,1)S(1)}, u32[]{:S(2)}, u32[]{:S(2)}) collective-permute-start(bf16[192,1152]{1,0:T(8,128)(2,1)S(1)} %get-tuple-element.174), channel_id=1, source_target_pairs={{0,4},{4,0},{8,12},{12,8},{16,20},{20,16},{24,28},{28,24},{1,5},{5... | collective-permute-start | bytes 1327112 | tf_op jit(solution)/shard_map/ppermute | solution.py:847
  314.3 22.4 %collective-permute-start.41 = (bf16[432,768]{1,0:T(8,128)(2,1)S(1)}, bf16[432,768]{1,0:T(8,128)(2,1)}, u32[]{:S(2)}, u32[]{:S(2)}) collective-permute-start(bf16[432,768]{1,0:T(8,128)(2,1)S(1)} %pad_maximum_fusion.7), channel_id=1, source_target_pairs={{0,8},{4,12},{8,0},{12,4},{16,24},{20,28},{24,16},{28,20},{1,9},{5... | collective-permute-start | bytes 1990664 | tf_op jit(solution)/shard_map/ppermute | solution.py:804
  315.2 41.2 %collective-permute-start.47 = (bf16[432,768]{1,0:T(8,128)(2,1)S(1)}, bf16[432,768]{1,0:T(8,128)(2,1)}, u32[]{:S(2)}, u32[]{:S(2)}) collective-permute-start(bf16[432,768]{1,0:T(8,128)(2,1)S(1)} %pad_maximum_fusion.7), channel_id=1, source_target_pairs={{0,4},{4,0},{8,12},{12,8},{16,20},{20,16},{24,28},{28,24},{1,5},{5... | collective-permute-start | bytes 1990664 | tf_op jit(solution)/shard_map/ppermute | solution.py:847
  316.9 39.3 %collective-permute-start.44 = (bf16[512,768]{1,0:T(8,128)(2,1)}, bf16[512,768]{1,0:T(8,128)(2,1)S(1)}, u32[]{:S(2)}, u32[]{:S(2)}) collective-permute-start(bf16[512,768]{1,0:T(8,128)(2,1)} %get-tuple-element.162), channel_id=1, source_target_pairs={{0,2},{2,0},{1,3},{3,1},{4,6},{6,4},{5,7},{7,5},{8,10},{10,8},{9,1... | collective-permute-start | bytes 2359304 | tf_op jit(solution)/shard_map/ppermute | solution.py:778
  326.3 9.1 %collective-permute-start.38 = (bf16[96,1152]{1,0:T(8,128)(2,1)S(1)}, bf16[96,1152]{1,0:T(8,128)(2,1)S(1)}, u32[]{:S(2)}, u32[]{:S(2)}) collective-permute-start(bf16[96,1152]{1,0:T(8,128)(2,1)S(1)} %get-tuple-element.187), channel_id=1, source_target_pairs={{0,8},{4,12},{8,0},{12,4},{16,24},{20,28},{24,16},{28,20},{1,9},{5... | collective-permute-start | bytes 663560 | tf_op jit(solution)/shard_map/ppermute | solution.py:804
  335.4 6.6 %collective-permute-start.39 = (bf16[48,1152]{1,0:T(8,128)(2,1)S(1)}, bf16[48,1152]{1,0:T(8,128)(2,1)S(1)}, u32[]{:S(2)}, u32[]{:S(2)}) collective-permute-start(bf16[48,1152]{1,0:T(8,128)(2,1)S(1)} %add_convert_fusion.13), channel_id=1, source_target_pairs={{0,16},{4,20},{8,24},{12,28},{16,0},{20,4},{24,8},{28,12},{1,17},{... | collective-permute-start | bytes 331784 | tf_op jit(solution)/shard_map/ppermute | solution.py:804
  336.7 19.7 %collective-permute-start.46 = (bf16[432,768]{1,0:T(8,128)(2,1)}, bf16[432,768]{1,0:T(8,128)(2,1)S(1)}, u32[]{:S(2)}, u32[]{:S(2)}) collective-permute-start(bf16[432,768]{1,0:T(8,128)(2,1)} %collective-permute-done.41), channel_id=1, source_target_pairs={{0,4},{4,0},{8,12},{12,8},{16,20},{20,16},{24,28},{28,24},{1,5},{5... | collective-permute-start | bytes 1990664 | tf_op jit(solution)/shard_map/ppermute | solution.py:847
  342.0 6.7 %collective-permute-start.42 = (bf16[48,1152]{1,0:T(8,128)(2,1)S(1)}, bf16[48,1152]{1,0:T(8,128)(2,1)S(1)}, u32[]{:S(2)}, u32[]{:S(2)}) collective-permute-start(bf16[48,1152]{1,0:T(8,128)(2,1)S(1)} %add_convert_fusion.12), channel_id=1, source_target_pairs={{0,16},{4,20},{8,24},{12,28},{16,0},{20,4},{24,8},{28,12},{1,17},{... | collective-permute-start | bytes 331784 | tf_op jit(solution)/shard_map/ppermute | solution.py:804
  348.8 7.3 %collective-permute-start.43 = (bf16[96,1152]{1,0:T(8,128)(2,1)S(1)}, bf16[96,1152]{1,0:T(8,128)(2,1)S(1)}, u32[]{:S(2)}, u32[]{:S(2)}) collective-permute-start(bf16[96,1152]{1,0:T(8,128)(2,1)S(1)} %pad_maximum_fusion.18), channel_id=1, source_target_pairs={{0,8},{4,12},{8,0},{12,4},{16,24},{20,28},{24,16},{28,20},{1,9},{5... | collective-permute-start | bytes 663560 | tf_op jit(solution)/shard_map/ppermute | solution.py:804
  356.1 11.1 %collective-permute-start.45 = (bf16[192,1152]{1,0:T(8,128)(2,1)S(1)}, bf16[192,1152]{1,0:T(8,128)(2,1)S(1)}, u32[]{:S(2)}, u32[]{:S(2)}) collective-permute-start(bf16[192,1152]{1,0:T(8,128)(2,1)S(1)} %pad_maximum_fusion.13), channel_id=1, source_target_pairs={{0,4},{4,0},{8,12},{12,8},{16,20},{20,16},{24,28},{28,24},{1,5},{5... | collective-permute-start | bytes 1327112 | tf_op jit(solution)/shard_map/ppermute | solution.py:847
  (30 other events, 200.6 us)

commit v3 on v2

--- a/solution.py
+++ b/solution.py
@@ -832,6 +832,24 @@
     return jnp.concatenate([jnp.where(upper, got, mine), jnp.where(upper, mine, got)], axis=0)
 
 
+def scatter4(terms, dp):
+    sends, keep = halve(terms, lax.axis_index("dp") // 2 % 4, 4)
+    return [keep] + [swap(v, 2 * k, dp) for k, v in enumerate(sends, 1)]
+
+
+def gather4(v, dp):
+    index = lax.axis_index("dp") // 2 % 4
+    parts = [v] + [swap(v, 2 * k, dp) for k in (1, 2, 3)]
+
+    def block(j):
+        out = parts[0]
+        for k in (1, 2, 3):
+            out = jnp.where(jnp.bitwise_xor(index, j) == k, parts[k], out)
+        return out
+
+    return jnp.concatenate([block(j) for j in range(4)], axis=0)
+
+
 def total(terms):
     return sum(t.astype(f32) for t in terms)
 
@@ -948,16 +966,17 @@
         first_cat = cat if stride == rest[-1] else first_cat
         got_v = swap(cat, stride, dp)
         vs = [join(v, g, stride) for v, g in zip(vs, rows_as(got_v, vs))]
-    (pt,), sent = scatter([pt], rest[0], dp)
+    pt = scatter4(pt, dp)
     packed_vs = jnp.concatenate(vs, axis=0)
     near_got = swap(packed_vs, rest[0], dp)
     across = rows_as(y_swap(packed_vs), vs)
-    for stride in rest[1:]:
+    for stride in rest[2:]:
         (pt,), _ = scatter([pt], stride, dp)
     others, also = rows_as(near_got, vs), rows_as(y_swap(near_got), vs)
-    ps = after(total(pt).astype(bf16), near_got)
-    for stride in reversed(rest):
+    ps = total(pt).astype(bf16)
+    for stride in reversed(rest[2:]):
         ps = join(ps, swap(ps, stride, dp), stride)
+    ps = gather4(ps, dp)
     ps_got = y_swap(ps)
     whole_of = lambda k: join(
         join(vs[k], others[k], rest[0]), join(across[k], also[k], rest[0]), 1

time: 371 us -> 379 us (1.022)
  starting transfers between devices: 39.4 us -> 46.9 us
    ppermute x11, waiting for transfers between devices: 45.3 us -> 29.4 us  [x_swap(): return lax.ppermute(v, 'head', XNB)]
    ppermute x7, waiting for transfers between devices: 13.1 us -> 22.1 us  [local(): y_swap = lambda v: lax.ppermute(v, 'dp', flip(dp, 1))]
    ppermute x11 -> x13, starting transfers between devices: 11.1 us -> 19.1 us  [swap(): return lax.ppermute(v, 'dp', flip(dp, stride))]
    ppermute x11 -> x13, waiting for transfers between devices: 28.2 us -> 33.1 us  [swap(): return lax.ppermute(v, 'dp', flip(dp, stride))]
  transfers between devices with their start and end apart: 49 -> 51, of which waited for: 19 -> 17; matrix products, arithmetic and copies ran while one was open for 12% -> 11% of each run, Pallas kernels for 35% -> 34%
where the time goes in v3:
time: 379 us; the launch traced here: 378 us
  Pallas kernels  177 us (47%)
  waiting for transfers between devices  95.8 us (25%)
  starting transfers between devices  46.9 us (12%)
  other arithmetic  39.6 us (10%)
  local copies, waits for them, and re-layouts  17.4 us (5%)
    pallas_call x2, Pallas kernels, att_bwd_call(): pl.pallas_call(functools.partial(att_bwd_body, p0, into is not None), out...  66.2 us
    pallas_call x1, Pallas kernels, ffn_call(): pl.pallas_call(ffn_body, out_shape=[sds((2, rows, width), f32), sds((rows...  49.3 us
    ppermute x13, waiting for transfers between devices, swap(): return lax.ppermute(v, 'dp', flip(dp, stride))  33.1 us
    ppermute x11, waiting for transfers between devices, x_swap(): return lax.ppermute(v, 'head', XNB)  29.4 us
    pallas_call x1, Pallas kernels, att_fwd_call(): pl.pallas_call(att_fwd_body, out_shape=[sds((length // 2, width), bf16),...  27.3 us
    ppermute x7, waiting for transfers between devices, local(): y_swap = lambda v: lax.ppermute(v, 'dp', flip(dp, 1))  22.1 us
    ppermute x13, starting transfers between devices, swap(): return lax.ppermute(v, 'dp', flip(dp, stride))  19.1 us
    pallas_call x1, Pallas kernels, qkv_call(): pl.pallas_call(qkv_body, out_shape=[sds((length, width), bf16), sds((leng...  13.5 us
  transfers between devices with their start and end apart: 51, of which 17 were waited for; matrix products, arithmetic and copies ran while one was open for 11% of the time, Pallas kernels for 34%

profile of v3, /device:TPU:0, one launch (start us, length us, event | category | flops | bytes accessed | tf_op | source)
XLA Modules:
  0.0 378.4 jit_solution(3671935334910697934)
XLA Ops:
  4.4 1.5 collective-permute-done.3.wb
  6.9 3.2 collective-permute-start.4
  13.1 2.5 dynamic-slice_bitcast_fusion.1
  16.7 2.2 pad_maximum_fusion.1
  18.9 29.3 %collective-permute-done.x1.xx = bf16[512,768]{1,0:T(8,128)(2,1)} collective-permute-done((bf16[512,768]{1,0:T(8,128)(2,1)}, bf16[512,768]{1,0:T(8,128)(2,1)}, u32[]{:S(2)}, u32[]{:S(2)}) %collective-permute-start) | collective-permute-done | bytes 786464 | tf_op jit(solution)/shard_map/ppermute | solution.py:778
  49.4 1.7 collective-permute-start.5
  51.1 2.7 collective-permute-done.6.x3
  54.7 13.5 %qkv.1 = (bf16[2048,768]{1,0:T(8,128)(2,1)}, bf16[2048,1152]{1,0:T(8,128)(2,1)}, bf16[2048,1152]{1,0:T(8,128)(2,1)}, bf16[768,1152]{1,0:T(8,128)(2,1)}, f32[8,1152]{1,0:T(8,128)}) custom-call(s32[4]{0:T(128)} %pad_add_fusion.meta, bf16[512,768]{1,0:T(8,128)(2,1)} %copy-done, bf16[512,768]{1,0:T(8,128)(2,1)} %collective-permute-done.x1.xx, ...), custom_call_target="tpu_custom_call" | custom-call | flops 3623878656 | bytes 15728640 | tf_op jit(solution)/shard_map/qkv/pallas_call | solution.py:131
  68.6 1.7 collective-permute-start.10
  70.3 1.5 collective-permute-start.7
  71.8 1.6 collective-permute-start.8
  73.8 27.3 %attn_fwd.1 = (bf16[1024,384]{1,0:T(8,128)(2,1)}, bf16[1024,384]{1,0:T(8,128)(2,1)}, f32[3,2,2048]{2,1,0:T(2,128)}) custom-call(s32[4]{0:T(128)} %pad_add_fusion.meta, bf16[2048,1152]{1,0:T(8,128)(2,1)} %get-tuple-element.128.q_ref.k_ref.v_ref, bf16[2048,1152]{1,0:T(8,128)(2,1)} %get-tuple-element.128.q_ref.k_ref.v_ref, ...), custom_call_target="tpu_custom_call" | custom-call | flops 12884901888 | bytes 6291456 | tf_op jit(solution)/shard_map/attn_fwd/pallas_call | solution.py:255
  102.9 2.4 collective-permute-done.14.c0
  105.4 1.7 collective-permute-done.16.c2
  109.6 49.3 %ffn.1 = (f32[2,512,768]{2,1,0:T(8,128)}, bf16[512,768]{1,0:T(8,128)(2,1)}, bf16[1024,384]{1,0:T(8,128)(2,1)}, bf16[1024,384]{1,0:T(8,128)(2,1)}, f32[1,768]{1,0...) custom-call(s32[4]{0:T(128)} %pad_add_fusion.meta, ...), custom_call_target="tpu_custom_call" | custom-call | flops 32614907904 | bytes 31457280 | tf_op jit(solution)/shard_map/ffn/pallas_call | solution.py:623
  160.1 1.9 collective-permute-done.19
  163.0 3.1 add_convert_fusion
  166.2 1.9 collective-permute-start.25
  169.2 1.5 collective-permute-start.22
  170.8 2.6 add_convert_fusion.2
  173.8 42.7 %attn_bwd.2 = (bf16[1024,1152]{1,0:T(8,128)(2,1)}, bf16[1024,1152]{1,0:T(8,128)(2,1)}, f32[16,256]{1,0:T(8,128)}) custom-call(s32[4]{0:T(128)} %pad_add_fusion.meta, bf16[2048,1152]{1,0:T(8,128)(2,1)} %get-tuple-element.128.q_ref.k_ref.v_ref, bf16[2048,1152]{1,0:T(8,128)(2,1)} %get-tuple-element.128.q_ref.k_ref.v_ref, ...), custom_call_target="tpu_custom_call" | custom-call | flops 15032385536 | bytes 10485760 | tf_op jit(solution)/shard_map/attn_bwd/pallas_call | solution.py:407
  216.6 2.6 add_convert_fusion.1
  219.5 2.9 convert_add_fusion.1
  222.3 1.8 collective-permute-start.27
  224.1 23.5 %attn_bwd.3 = (bf16[1024,1152]{1,0:T(8,128)(2,1)}, bf16[1024,1152]{1,0:T(8,128)(2,1)}, f32[16,128]{1,0:T(8,128)}) custom-call(s32[4]{0:T(128)} %pad_add_fusion.meta, bf16[2048,1152]{1,0:T(8,128)(2,1)} %get-tuple-element.128.q_ref.k_ref.v_ref, ...), custom_call_target="tpu_custom_call", output_to_operand_aliasing={{0}: (13, {}), {1}: (14, {})} | custom-call | flops 7516192768 | bytes 5242880 | tf_op jit(solution)/shard_map/attn_bwd/pallas_call | solution.py:407
  249.8 1.5 convert_add_fusion.4
  251.4 1.6 collective-permute-start.29
  253.0 9.6 %projg.1 = (bf16[192,1152]{1,0:T(8,128)(2,1)}, bf16[192,1152]{1,0:T(8,128)(2,1)}, bf16[384,1152]{1,0:T(8,128)(2,1)}) custom-call(s32[4]{0:T(128)} %pad_add_fusion.meta, bf16[2048,768]{1,0:T(8,128)(2,1)} %get-tuple-element.135.h, bf16[1024,1152]{1,0:T(8,128)(2,1)} %get-tuple-element.136.dm, bf16[1024,1152]{1,0:T(8,128)(2,1)} %get-tuple-element.137.dt), custom_call_target="tpu_custom_call" | custom-call | flops 2048 | bytes 2048 | tf_op jit(solution)/shard_map/projg/pallas_call | solution.py:692
  262.6 6.1 %collective-permute-done.29 = bf16[432,768]{1,0:T(8,128)(2,1)S(1)} collective-permute-done((bf16[432,768]{1,0:T(8,128)(2,1)S(1)}, bf16[432,768]{1,0:T(8,128)(2,1)S(1)}, u32[]{:S(2)}, u32[]{:S(2)}) %collective-permute-start.29) | collective-permute-done | bytes 663584 | tf_op jit(solution)/shard_map/ppermute | solution.py:804
  269.0 2.7 collective-permute-start.33
  271.7 11.4 %last.1 = (f32[2,512,768]{2,1,0:T(8,128)}, bf16[512,768]{1,0:T(8,128)(2,1)}, f32[1,768]{1,0:T(1,128)}) custom-call(s32[4]{0:T(128)} %pad_add_fusion.meta, bf16[512,768]{1,0:T(8,128)(2,1)} %copy-done, bf16[512,768]{1,0:T(8,128)(2,1)} %collective-permute-done.x1.xx, bf16[1024,1152]{1,0:T(8,128)(2,1)} %get-tuple-element.136.dm, ...), custom_call_target="tpu_custom_call" | custom-call | flops 512 | bytes 512 | tf_op jit(solution)/shard_map/last/pallas_call | solution.py:750
  284.5 1.5 collective-permute-start.36
  288.1 1.5 collective-permute-start.32
  291.0 4.4 %all-to-all-start = ((f32[32,16,192]{2,1,0:T(8,128)}), f32[32,16,192]{2,1,0:T(8,128)S(1)}, u32[]{:S(2)}, u32[]{:S(2)}) async-start(f32[32,16,192]{2,1,0:T(8,128)} %bitcast.16), calls=%async_computation | async-start | bytes 1048576 | tf_op jit(solution)/shard_map/all_to_all | solution.py:996
  295.5 18.5 %collective-permute-done.46 = bf16[216,768]{1,0:T(8,128)(2,1)S(1)} collective-permute-done((bf16[216,768]{1,0:T(8,128)(2,1)S(1)}, bf16[216,768]{1,0:T(8,128)(2,1)S(1)}, u32[]{:S(2)}, u32[]{:S(2)}) %collective-permute-start.46) | collective-permute-done | bytes 331808 | tf_op jit(solution)/shard_map/ppermute | solution.py:804
  314.7 2.2 fusion.1
  318.4 1.6 collective-permute-start.49
  320.0 2.4 convert_dynamic-update-slice_fusion.1
  322.5 7.8 %collective-permute-done.37 = bf16[192,1152]{1,0:T(8,128)(2,1)} collective-permute-done((bf16[192,1152]{1,0:T(8,128)(2,1)}, bf16[192,1152]{1,0:T(8,128)(2,1)}, u32[]{:S(2)}, u32[]{:S(2)}) %collective-permute-start.37) | collective-permute-done | bytes 442400 | tf_op jit(solution)/shard_map/ppermute | solution.py:865
  330.3 1.7 add_convert_fusion.14
  332.4 4.0 %collective-permute-start.40 = (bf16[48,1152]{1,0:T(8,128)(2,1)S(1)}, bf16[48,1152]{1,0:T(8,128)(2,1)S(1)}, u32[]{:S(2)}, u32[]{:S(2)}) collective-permute-start(bf16[48,1152]{1,0:T(8,128)(2,1)S(1)} %get-tuple-element.186), channel_id=1, source_target_pairs={{0,24},{4,28},{8,16},{12,20},{16,8},{20,12},{24,0},{28,4},{1,25},{... | collective-permute-start | bytes 331784 | tf_op jit(solution)/shard_map/ppermute | solution.py:804
  339.2 2.1 collective-permute-done.39
  342.3 1.7 collective-permute-start.41
  344.1 5.1 %collective-permute-start.42 = (bf16[48,1152]{1,0:T(8,128)(2,1)S(1)}, bf16[48,1152]{1,0:T(8,128)(2,1)S(1)}, u32[]{:S(2)}, u32[]{:S(2)}) collective-permute-start(bf16[48,1152]{1,0:T(8,128)(2,1)S(1)} %add_convert_fusion.11), channel_id=1, source_target_pairs={{0,16},{4,20},{8,24},{12,28},{16,0},{20,4},{24,8},{28,12},{1,17},{... | collective-permute-start | bytes 331784 | tf_op jit(solution)/shard_map/ppermute | solution.py:804
  350.5 3.8 %collective-permute-done.42 = bf16[48,1152]{1,0:T(8,128)(2,1)S(1)} collective-permute-done((bf16[48,1152]{1,0:T(8,128)(2,1)S(1)}, bf16[48,1152]{1,0:T(8,128)(2,1)S(1)}, u32[]{:S(2)}, u32[]{:S(2)}) %collective-permute-start.42) | collective-permute-done | bytes 110624 | tf_op jit(solution)/shard_map/ppermute | solution.py:804
  356.5 14.3 %collective-permute-done.45 = bf16[192,1152]{1,0:T(8,128)(2,1)S(1)} collective-permute-done((bf16[192,1152]{1,0:T(8,128)(2,1)S(1)}, bf16[192,1152]{1,0:T(8,128)(2,1)S(1)}, u32[]{:S(2)}, u32[]{:S(2)}) %collective-permute-start.45) | collective-permute-done | bytes 442400 | tf_op jit(solution)/shard_map/ppermute | solution.py:865
  374.1 1.6 fusion
  376.8 1.6 maximum_convert_fusion
  (205 shorter events, 41.5 us)
Async XLA Ops:
  4.3 12.4 %collective-permute-start.1 = (bf16[192,768]{1,0:T(8,128)(2,1)}, bf16[192,768]{1,0:T(8,128)(2,1)}, u32[]{:S(2)}, u32[]{:S(2)}) collective-permute-start(bf16[192,768]{1,0:T(8,128)(2,1)} %wo_o.1), channel_id=1, source_target_pairs={{0,1},{1,0},{2,3},{3,2},{4,5},{5,4},{6,7},{7,6},{8,9},{9,8},{10,11... | collective-permute-start | bytes 884744 | tf_op jit(solution)/shard_map/ppermute | solution.py:774
  6.9 41.4 %collective-permute-start.4 = (bf16[608,768]{1,0:T(8,128)(2,1)}, bf16[608,768]{1,0:T(8,128)(2,1)}, u32[]{:S(2)}, u32[]{:S(2)}) collective-permute-start(bf16[608,768]{1,0:T(8,128)(2,1)} %pad_maximum_fusion.3), channel_id=1, source_target_pairs={{0,2},{2,0},{1,3},{3,1},{4,6},{6,4},{5,7},{7,5},{8,10},{10,8},{9,1... | collective-permute-start | bytes 2801672 | tf_op jit(solution)/shard_map/ppermute | solution.py:778
  11.1 37.2 %collective-permute-start = (bf16[512,768]{1,0:T(8,128)(2,1)}, bf16[512,768]{1,0:T(8,128)(2,1)}, u32[]{:S(2)}, u32[]{:S(2)}) collective-permute-start(bf16[512,768]{1,0:T(8,128)(2,1)} %get-tuple-element.176), channel_id=1, source_target_pairs={{0,2},{2,0},{1,3},{3,1},{4,6},{6,4},{5,7},{7,5},{8,10},{10,8},{9,1... | collective-permute-start | bytes 2359304 | tf_op jit(solution)/shard_map/ppermute | solution.py:778
  11.1 37.2 %collective-permute-start.2 = (bf16[512,768]{1,0:T(8,128)(2,1)S(1)}, bf16[512,768]{1,0:T(8,128)(2,1)}, u32[]{:S(2)}, u32[]{:S(2)}) collective-permute-start(bf16[512,768]{1,0:T(8,128)(2,1)S(1)} %get-tuple-element.175.x0.xo), channel_id=1, source_target_pairs={{0,1},{1,0},{2,3},{3,2},{4,5},{5,4},{6,7},{7,6},{8,9},{9,8},{10,11... | collective-permute-start | bytes 2359304 | tf_op jit(solution)/shard_map/ppermute | solution.py:774
  48.3 25.1 %collective-permute-start.11 = (bf16[2,768,768]{2,1,0:T(8,128)(2,1)S(1)}, bf16[2,768,768]{2,1,0:T(8,128)(2,1)}, u32[]{:S(2)}, u32[]{:S(2)}) collective-permute-start(bf16[2,768,768]{2,1,0:T(8,128)(2,1)S(1)} %pad_maximum_fusion), channel_id=1, source_target_pairs={{0,1},{1,0},{2,3},{3,2},{4,5},{5,4},{6,7},{7,6},{8,9},{9,8},{10,11... | collective-permute-start | bytes 7077896 | tf_op jit(solution)/shard_map/ppermute | solution.py:774
  48.3 5.5 %collective-permute-start.6 = (bf16[512,768]{1,0:T(8,128)(2,1)}, bf16[512,768]{1,0:T(8,128)(2,1)S(1)}, u32[]{:S(2)}, u32[]{:S(2)}) collective-permute-start(bf16[512,768]{1,0:T(8,128)(2,1)} %collective-permute-done.x1.xx), channel_id=1, source_target_pairs={{0,1},{1,0},{2,3},{3,2},{4,5},{5,4},{6,7},{7,6},{8,9},{9,8},{10,11... | collective-permute-start | bytes 2359304 | tf_op jit(solution)/shard_map/ppermute | solution.py:774
  49.4 20.9 %collective-permute-start.5 = (bf16[2,192,768]{2,1,0:T(8,128)(2,1)}, bf16[2,192,768]{2,1,0:T(8,128)(2,1)}, u32[]{:S(2)}, u32[]{:S(2)}) collective-permute-start(bf16[2,192,768]{2,1,0:T(8,128)(2,1)} %pad_maximum_fusion.10), channel_id=1, source_target_pairs={{0,2},{2,0},{1,3},{3,1},{4,6},{6,4},{5,7},{7,5},{8,10},{10,8},{9,1... | collective-permute-start | bytes 1769480 | tf_op jit(solution)/shard_map/ppermute | solution.py:778
  68.2 34.1 %collective-permute-start.13 = (bf16[768,1152]{1,0:T(8,128)(2,1)}, bf16[768,1152]{1,0:T(8,128)(2,1)}, u32[]{:S(2)}, u32[]{:S(2)}) collective-permute-start(bf16[768,1152]{1,0:T(8,128)(2,1)} %get-tuple-element.102.wm), channel_id=1, source_target_pairs={{0,1},{1,0},{2,3},{3,2},{4,5},{5,4},{6,7},{7,6},{8,9},{9,8},{10,11... | collective-permute-start | bytes 5308424 | tf_op jit(solution)/shard_map/ppermute | solution.py:774
  68.6 33.1 %collective-permute-start.10 = (bf16[896,768]{1,0:T(8,128)(2,1)}, bf16[896,768]{1,0:T(8,128)(2,1)}, u32[]{:S(2)}, u32[]{:S(2)}) collective-permute-start(bf16[896,768]{1,0:T(8,128)(2,1)} %pad_maximum_fusion.1), channel_id=1, source_target_pairs={{0,2},{2,0},{1,3},{3,1},{4,6},{6,4},{5,7},{7,5},{8,10},{10,8},{9,1... | collective-permute-start | bytes 4128776 | tf_op jit(solution)/shard_map/ppermute | solution.py:778
  70.3 30.8 %collective-permute-start.7 = (bf16[2,192,768]{2,1,0:T(8,128)(2,1)}, bf16[2,192,768]{2,1,0:T(8,128)(2,1)S(1)}, u32[]{:S(2)}, u32[]{:S(2)}) collective-permute-start(bf16[2,192,768]{2,1,0:T(8,128)(2,1)} %collective-permute-done.5.n0), channel_id=1, source_target_pairs={{0,4},{4,0},{8,12},{12,8},{16,20},{20,16},{24,28},{28,24},{1,5},{5... | collective-permute-start | bytes 1769480 | tf_op jit(solution)/shard_map/ppermute | solution.py:804
  71.8 29.4 %collective-permute-start.8 = (bf16[2,192,768]{2,1,0:T(8,128)(2,1)}, bf16[2,192,768]{2,1,0:T(8,128)(2,1)}, u32[]{:S(2)}, u32[]{:S(2)}) collective-permute-start(bf16[2,192,768]{2,1,0:T(8,128)(2,1)} %collective-permute-done.5.n0), channel_id=1, source_target_pairs={{0,8},{4,12},{8,0},{12,4},{16,24},{20,28},{24,16},{28,20},{1,9},{5... | collective-permute-start | bytes 1769480 | tf_op jit(solution)/shard_map/ppermute | solution.py:804
  73.4 28.3 %collective-permute-start.9 = (bf16[2,192,768]{2,1,0:T(8,128)(2,1)}, bf16[2,192,768]{2,1,0:T(8,128)(2,1)S(1)}, u32[]{:S(2)}, u32[]{:S(2)}) collective-permute-start(bf16[2,192,768]{2,1,0:T(8,128)(2,1)} %collective-permute-done.5.n0), channel_id=1, source_target_pairs={{0,12},{4,8},{8,4},{12,0},{16,28},{20,24},{24,20},{28,16},{1,13},{... | collective-permute-start | bytes 1769480 | tf_op jit(solution)/shard_map/ppermute | solution.py:804
  101.1 7.6 %collective-permute-start.12 = (bf16[1024,384]{1,0:T(8,128)(2,1)}, bf16[1024,384]{1,0:T(8,128)(2,1)S(1)}, u32[]{:S(2)}, u32[]{:S(2)}) collective-permute-start(bf16[1024,384]{1,0:T(8,128)(2,1)} %get-tuple-element.101.ot), channel_id=1, source_target_pairs={{0,1},{1,0},{2,3},{3,2},{4,5},{5,4},{6,7},{7,6},{8,9},{9,8},{10,11... | collective-permute-start | bytes 2359304 | tf_op jit(solution)/shard_map/ppermute | solution.py:774
  101.2 4.2 %collective-permute-start.14 = (bf16[2,192,768]{2,1,0:T(8,128)(2,1)}, bf16[2,192,768]{2,1,0:T(8,128)(2,1)S(1)}, u32[]{:S(2)}, u32[]{:S(2)}) collective-permute-start(bf16[2,192,768]{2,1,0:T(8,128)(2,1)} %collective-permute-done.5.n0), channel_id=1, source_target_pairs={{0,1},{1,0},{2,3},{3,2},{4,5},{5,4},{6,7},{7,6},{8,9},{9,8},{10,11... | collective-permute-start | bytes 1769480 | tf_op jit(solution)/shard_map/ppermute | solution.py:774
  101.7 3.7 collective-permute-start.15
  101.8 5.2 %collective-permute-start.16 = (bf16[2,192,768]{2,1,0:T(8,128)(2,1)}, bf16[2,192,768]{2,1,0:T(8,128)(2,1)S(1)}, u32[]{:S(2)}, u32[]{:S(2)}) collective-permute-start(bf16[2,192,768]{2,1,0:T(8,128)(2,1)} %collective-permute-done.8.n2), channel_id=1, source_target_pairs={{0,1},{1,0},{2,3},{3,2},{4,5},{5,4},{6,7},{7,6},{8,9},{9,8},{10,11... | collective-permute-start | bytes 1769480 | tf_op jit(solution)/shard_map/ppermute | solution.py:774
  102.3 4.8 %collective-permute-start.17 = (bf16[2,192,768]{2,1,0:T(8,128)(2,1)S(1)}, bf16[2,192,768]{2,1,0:T(8,128)(2,1)S(1)}, u32[]{:S(2)}, u32[]{:S(2)}) collective-permute-start(bf16[2,192,768]{2,1,0:T(8,128)(2,1)S(1)} %collective-permute-done.9.n3), channel_id=1, source_target_pairs={{0,1},{1,0},{2,3},{3,2},{4,5},{5,4},{6,7},{7,6},{8,9},{9,8},{10,11... | collective-permute-start | bytes 1769480 | tf_op jit(solution)/shard_map/ppermute | solution.py:774
  159.1 7.1 %collective-permute-start.21 = (bf16[960,768]{1,0:T(8,128)(2,1)}, bf16[960,768]{1,0:T(8,128)(2,1)S(1)}, u32[]{:S(2)}, u32[]{:S(2)}) collective-permute-start(bf16[960,768]{1,0:T(8,128)(2,1)} %get-tuple-element.114), channel_id=1, source_target_pairs={{0,1},{1,0},{2,3},{3,2},{4,5},{5,4},{6,7},{7,6},{8,9},{9,8},{10,11... | collective-permute-start | bytes 4423688 | tf_op jit(solution)/shard_map/ppermute | solution.py:774
  159.5 9.8 %collective-permute-start.23 = (bf16[960,768]{1,0:T(8,128)(2,1)}, bf16[960,768]{1,0:T(8,128)(2,1)}, u32[]{:S(2)}, u32[]{:S(2)}) collective-permute-start(bf16[960,768]{1,0:T(8,128)(2,1)} %get-tuple-element.116), channel_id=1, source_target_pairs={{0,1},{1,0},{2,3},{3,2},{4,5},{5,4},{6,7},{7,6},{8,9},{9,8},{10,11... | collective-permute-start | bytes 4423688 | tf_op jit(solution)/shard_map/ppermute | solution.py:774
  159.6 13.7 %collective-permute-start.26 = (bf16[1024,384]{1,0:T(8,128)(2,1)}, bf16[1024,384]{1,0:T(8,128)(2,1)}, u32[]{:S(2)}, u32[]{:S(2)}) collective-permute-start(bf16[1024,384]{1,0:T(8,128)(2,1)} %get-tuple-element.121), channel_id=1, source_target_pairs={{0,1},{1,0},{2,3},{3,2},{4,5},{5,4},{6,7},{7,6},{8,9},{9,8},{10,11... | collective-permute-start | bytes 2359304 | tf_op jit(solution)/shard_map/ppermute | solution.py:774
  160.0 59.5 %collective-permute-start.18 = (bf16[768,768]{1,0:T(8,128)(2,1)}, bf16[768,768]{1,0:T(8,128)(2,1)}, u32[]{:S(2)}, u32[]{:S(2)}) collective-permute-start(bf16[768,768]{1,0:T(8,128)(2,1)} %get-tuple-element.110), channel_id=1, source_target_pairs={{0,1},{1,0},{2,3},{3,2},{4,5},{5,4},{6,7},{7,6},{8,9},{9,8},{10,11... | collective-permute-start | bytes 3538952 | tf_op jit(solution)/shard_map/ppermute | solution.py:774
  166.2 50.4 %collective-permute-start.20 = (bf16[768,768]{1,0:T(8,128)(2,1)}, bf16[768,768]{1,0:T(8,128)(2,1)}, u32[]{:S(2)}, u32[]{:S(2)}) collective-permute-start(bf16[768,768]{1,0:T(8,128)(2,1)} %add_convert_fusion), channel_id=1, source_target_pairs={{0,2},{2,0},{1,3},{3,1},{4,6},{6,4},{5,7},{7,5},{8,10},{10,8},{9,1... | collective-permute-start | bytes 3538952 | tf_op jit(solution)/shard_map/ppermute | solution.py:778
  166.2 50.3 %collective-permute-start.25 = (bf16[512,768]{1,0:T(8,128)(2,1)}, bf16[512,768]{1,0:T(8,128)(2,1)}, u32[]{:S(2)}, u32[]{:S(2)}) collective-permute-start(bf16[512,768]{1,0:T(8,128)(2,1)} %get-tuple-element.118), channel_id=1, source_target_pairs={{0,2},{2,0},{1,3},{3,1},{4,6},{6,4},{5,7},{7,5},{8,10},{10,8},{9,1... | collective-permute-start | bytes 2359304 | tf_op jit(solution)/shard_map/ppermute | solution.py:778
  169.2 47.3 %collective-permute-start.22 = (bf16[480,768]{1,0:T(8,128)(2,1)}, bf16[480,768]{1,0:T(8,128)(2,1)}, u32[]{:S(2)}, u32[]{:S(2)}) collective-permute-start(bf16[480,768]{1,0:T(8,128)(2,1)} %add_convert_fusion.3), channel_id=1, source_target_pairs={{0,4},{4,0},{8,12},{12,8},{16,20},{20,16},{24,28},{28,24},{1,5},{5... | collective-permute-start | bytes 2211848 | tf_op jit(solution)/shard_map/ppermute | solution.py:865
  173.3 43.2 %collective-permute-start.24 = (bf16[480,768]{1,0:T(8,128)(2,1)}, bf16[480,768]{1,0:T(8,128)(2,1)}, u32[]{:S(2)}, u32[]{:S(2)}) collective-permute-start(bf16[480,768]{1,0:T(8,128)(2,1)} %get-tuple-element.169), channel_id=1, source_target_pairs={{0,4},{4,0},{8,12},{12,8},{16,20},{20,16},{24,28},{28,24},{1,5},{5... | collective-permute-start | bytes 2211848 | tf_op jit(solution)/shard_map/ppermute | solution.py:865
  219.2 28.7 %collective-permute-start.28 = (bf16[480,768]{1,0:T(8,128)(2,1)}, bf16[480,768]{1,0:T(8,128)(2,1)}, u32[]{:S(2)}, u32[]{:S(2)}) collective-permute-start(bf16[480,768]{1,0:T(8,128)(2,1)} %add_convert_fusion.1), channel_id=1, source_target_pairs={{0,2},{2,0},{1,3},{3,1},{4,6},{6,4},{5,7},{7,5},{8,10},{10,8},{9,1... | collective-permute-start | bytes 2211848 | tf_op jit(solution)/shard_map/ppermute | solution.py:778
  222.3 25.5 %collective-permute-start.27 = (bf16[384,768]{1,0:T(8,128)(2,1)}, bf16[384,768]{1,0:T(8,128)(2,1)S(1)}, u32[]{:S(2)}, u32[]{:S(2)}) collective-permute-start(bf16[384,768]{1,0:T(8,128)(2,1)} %get-tuple-element.166), channel_id=1, source_target_pairs={{0,4},{4,0},{8,12},{12,8},{16,20},{20,16},{24,28},{28,24},{1,5},{5... | collective-permute-start | bytes 1769480 | tf_op jit(solution)/shard_map/ppermute | solution.py:865
  247.7 24.0 %collective-permute-start.34 = (bf16[1024,1152]{1,0:T(8,128)(2,1)}, bf16[1024,1152]{1,0:T(8,128)(2,1)}, u32[]{:S(2)}, u32[]{:S(2)}) collective-permute-start(bf16[1024,1152]{1,0:T(8,128)(2,1)} %get-tuple-element.137.dt), channel_id=1, source_target_pairs={{0,1},{1,0},{2,3},{3,2},{4,5},{5,4},{6,7},{7,6},{8,9},{9,8},{10,11... | collective-permute-start | bytes 7077896 | tf_op jit(solution)/shard_map/ppermute | solution.py:774
  251.4 17.3 %collective-permute-start.29 = (bf16[432,768]{1,0:T(8,128)(2,1)S(1)}, bf16[432,768]{1,0:T(8,128)(2,1)S(1)}, u32[]{:S(2)}, u32[]{:S(2)}) collective-permute-start(bf16[432,768]{1,0:T(8,128)(2,1)S(1)} %pad_maximum_fusion.6), channel_id=1, source_target_pairs={{0,8},{4,12},{8,0},{12,4},{16,24},{20,28},{24,16},{28,20},{1,9},{5... | collective-permute-start | bytes 1990664 | tf_op jit(solution)/shard_map/ppermute | solution.py:804
  269.0 18.4 %collective-permute-start.30 = (bf16[384,1152]{1,0:T(8,128)(2,1)}, bf16[384,1152]{1,0:T(8,128)(2,1)S(1)}, u32[]{:S(2)}, u32[]{:S(2)}) collective-permute-start(bf16[384,1152]{1,0:T(8,128)(2,1)} %get-tuple-element.144), channel_id=1, source_target_pairs={{0,1},{1,0},{2,3},{3,2},{4,5},{5,4},{6,7},{7,6},{8,9},{9,8},{10,11... | collective-permute-start | bytes 2654216 | tf_op jit(solution)/shard_map/ppermute | solution.py:774
  269.0 18.2 %collective-permute-start.33 = (bf16[216,768]{1,0:T(8,128)(2,1)S(1)}, bf16[216,768]{1,0:T(8,128)(2,1)S(1)}, u32[]{:S(2)}, u32[]{:S(2)}) collective-permute-start(bf16[216,768]{1,0:T(8,128)(2,1)S(1)} %pad_maximum_fusion.15), channel_id=1, source_target_pairs={{0,16},{4,20},{8,24},{12,28},{16,0},{20,4},{24,8},{28,12},{1,17},{... | collective-permute-start | bytes 995336 | tf_op jit(solution)/shard_map/ppermute | solution.py:804
  284.5 5.1 %collective-permute-start.36 = (f32[1,768]{1,0:T(1,128)S(1)}, f32[1,768]{1,0:T(1,128)S(1)}, u32[]{:S(2)}, u32[]{:S(2)}) collective-permute-start(f32[1,768]{1,0:T(1,128)S(1)} %collective-permute-done.35), channel_id=1, source_target_pairs={{0,2},{2,0},{1,3},{3,1},{4,6},{6,4},{5,7},{7,5},{8,10},{10,8},{9,1... | collective-permute-start | bytes 9224 | tf_op jit(solution)/shard_map/ppermute | solution.py:778
  286.1 27.9 %collective-permute-start.31 = (bf16[192,1152]{1,0:T(8,128)(2,1)}, bf16[192,1152]{1,0:T(8,128)(2,1)}, u32[]{:S(2)}, u32[]{:S(2)}) collective-permute-start(bf16[192,1152]{1,0:T(8,128)(2,1)} %get-tuple-element.145), channel_id=1, source_target_pairs={{0,2},{2,0},{1,3},{3,1},{4,6},{6,4},{5,7},{7,5},{8,10},{10,8},{9,1... | collective-permute-start | bytes 1327112 | tf_op jit(solution)/shard_map/ppermute | solution.py:778
  288.1 26.6 %collective-permute-start.32 = (bf16[192,1152]{1,0:T(8,128)(2,1)}, bf16[192,1152]{1,0:T(8,128)(2,1)}, u32[]{:S(2)}, u32[]{:S(2)}) collective-permute-start(bf16[192,1152]{1,0:T(8,128)(2,1)} %slice.133), channel_id=1, source_target_pairs={{0,2},{2,0},{1,3},{3,1},{4,6},{6,4},{5,7},{7,5},{8,10},{10,8},{9,1... | collective-permute-start | bytes 1327112 | tf_op jit(solution)/shard_map/ppermute | solution.py:778
  289.7 24.2 %collective-permute-start.46 = (bf16[216,768]{1,0:T(8,128)(2,1)S(1)}, bf16[216,768]{1,0:T(8,128)(2,1)S(1)}, u32[]{:S(2)}, u32[]{:S(2)}) collective-permute-start(bf16[216,768]{1,0:T(8,128)(2,1)S(1)} %pad_maximum_fusion.16), channel_id=1, source_target_pairs={{0,16},{4,20},{8,24},{12,28},{16,0},{20,4},{24,8},{28,12},{1,17},{... | collective-permute-start | bytes 995336 | tf_op jit(solution)/shard_map/ppermute | solution.py:804
  291.0 31.4 %all-to-all-start = ((f32[32,16,192]{2,1,0:T(8,128)}), f32[32,16,192]{2,1,0:T(8,128)S(1)}, u32[]{:S(2)}, u32[]{:S(2)}) async-start(f32[32,16,192]{2,1,0:T(8,128)} %bitcast.16), calls=%async_computation | async-start | bytes 1048576 | tf_op jit(solution)/shard_map/all_to_all | solution.py:996
  316.9 13.4 %collective-permute-start.37 = (bf16[192,1152]{1,0:T(8,128)(2,1)}, bf16[192,1152]{1,0:T(8,128)(2,1)}, u32[]{:S(2)}, u32[]{:S(2)}) collective-permute-start(bf16[192,1152]{1,0:T(8,128)(2,1)} %get-tuple-element.172), channel_id=1, source_target_pairs={{0,4},{4,0},{8,12},{12,8},{16,20},{20,16},{24,28},{28,24},{1,5},{5... | collective-permute-start | bytes 1327112 | tf_op jit(solution)/shard_map/ppermute | solution.py:865
  318.4 30.8 %collective-permute-start.47 = (bf16[432,768]{1,0:T(8,128)(2,1)S(1)}, bf16[432,768]{1,0:T(8,128)(2,1)}, u32[]{:S(2)}, u32[]{:S(2)}) collective-permute-start(bf16[432,768]{1,0:T(8,128)(2,1)S(1)} %pad_maximum_fusion.7), channel_id=1, source_target_pairs={{0,8},{4,12},{8,0},{12,4},{16,24},{20,28},{24,16},{28,20},{1,9},{5... | collective-permute-start | bytes 1990664 | tf_op jit(solution)/shard_map/ppermute | solution.py:804
  318.4 55.3 %collective-permute-start.49 = (bf16[432,768]{1,0:T(8,128)(2,1)S(1)}, bf16[432,768]{1,0:T(8,128)(2,1)S(1)}, u32[]{:S(2)}, u32[]{:S(2)}) collective-permute-start(bf16[432,768]{1,0:T(8,128)(2,1)S(1)} %pad_maximum_fusion.7), channel_id=1, source_target_pairs={{0,4},{4,0},{8,12},{12,8},{16,20},{20,16},{24,28},{28,24},{1,5},{5... | collective-permute-start | bytes 1990664 | tf_op jit(solution)/shard_map/ppermute | solution.py:865
  332.0 6.7 %collective-permute-start.38 = (bf16[48,1152]{1,0:T(8,128)(2,1)}, bf16[48,1152]{1,0:T(8,128)(2,1)S(1)}, u32[]{:S(2)}, u32[]{:S(2)}) collective-permute-start(bf16[48,1152]{1,0:T(8,128)(2,1)} %get-tuple-element.185), channel_id=1, source_target_pairs={{0,8},{4,12},{8,0},{12,4},{16,24},{20,28},{24,16},{28,20},{1,9},{5... | collective-permute-start | bytes 331784 | tf_op jit(solution)/shard_map/ppermute | solution.py:804
  332.0 9.4 %collective-permute-start.39 = (bf16[48,1152]{1,0:T(8,128)(2,1)S(1)}, bf16[48,1152]{1,0:T(8,128)(2,1)S(1)}, u32[]{:S(2)}, u32[]{:S(2)}) collective-permute-start(bf16[48,1152]{1,0:T(8,128)(2,1)S(1)} %get-tuple-element.187), channel_id=1, source_target_pairs={{0,16},{4,20},{8,24},{12,28},{16,0},{20,4},{24,8},{28,12},{1,17},{... | collective-permute-start | bytes 331784 | tf_op jit(solution)/shard_map/ppermute | solution.py:804
  332.4 9.0 %collective-permute-start.40 = (bf16[48,1152]{1,0:T(8,128)(2,1)S(1)}, bf16[48,1152]{1,0:T(8,128)(2,1)S(1)}, u32[]{:S(2)}, u32[]{:S(2)}) collective-permute-start(bf16[48,1152]{1,0:T(8,128)(2,1)S(1)} %get-tuple-element.186), channel_id=1, source_target_pairs={{0,24},{4,28},{8,16},{12,20},{16,8},{20,12},{24,0},{28,4},{1,25},{... | collective-permute-start | bytes 331784 | tf_op jit(solution)/shard_map/ppermute | solution.py:804
  338.7 17.7 %collective-permute-start.44 = (bf16[512,768]{1,0:T(8,128)(2,1)}, bf16[512,768]{1,0:T(8,128)(2,1)S(1)}, u32[]{:S(2)}, u32[]{:S(2)}) collective-permute-start(bf16[512,768]{1,0:T(8,128)(2,1)} %get-tuple-element.160), channel_id=1, source_target_pairs={{0,2},{2,0},{1,3},{3,1},{4,6},{6,4},{5,7},{7,5},{8,10},{10,8},{9,1... | collective-permute-start | bytes 2359304 | tf_op jit(solution)/shard_map/ppermute | solution.py:778
  342.3 8.1 %collective-permute-start.41 = (bf16[48,1152]{1,0:T(8,128)(2,1)S(1)}, bf16[48,1152]{1,0:T(8,128)(2,1)S(1)}, u32[]{:S(2)}, u32[]{:S(2)}) collective-permute-start(bf16[48,1152]{1,0:T(8,128)(2,1)S(1)} %add_convert_fusion.11), channel_id=1, source_target_pairs={{0,24},{4,28},{8,16},{12,20},{16,8},{20,12},{24,0},{28,4},{1,25},{... | collective-permute-start | bytes 331784 | tf_op jit(solution)/shard_map/ppermute | solution.py:804
  344.1 10.3 %collective-permute-start.42 = (bf16[48,1152]{1,0:T(8,128)(2,1)S(1)}, bf16[48,1152]{1,0:T(8,128)(2,1)S(1)}, u32[]{:S(2)}, u32[]{:S(2)}) collective-permute-start(bf16[48,1152]{1,0:T(8,128)(2,1)S(1)} %add_convert_fusion.11), channel_id=1, source_target_pairs={{0,16},{4,20},{8,24},{12,28},{16,0},{20,4},{24,8},{28,12},{1,17},{... | collective-permute-start | bytes 331784 | tf_op jit(solution)/shard_map/ppermute | solution.py:804
  349.2 5.9 %collective-permute-start.43 = (bf16[48,1152]{1,0:T(8,128)(2,1)S(1)}, bf16[48,1152]{1,0:T(8,128)(2,1)S(1)}, u32[]{:S(2)}, u32[]{:S(2)}) collective-permute-start(bf16[48,1152]{1,0:T(8,128)(2,1)S(1)} %add_convert_fusion.11), channel_id=1, source_target_pairs={{0,8},{4,12},{8,0},{12,4},{16,24},{20,28},{24,16},{28,20},{1,9},{5... | collective-permute-start | bytes 331784 | tf_op jit(solution)/shard_map/ppermute | solution.py:804
  350.5 23.2 %collective-permute-start.48 = (bf16[432,768]{1,0:T(8,128)(2,1)}, bf16[432,768]{1,0:T(8,128)(2,1)S(1)}, u32[]{:S(2)}, u32[]{:S(2)}) collective-permute-start(bf16[432,768]{1,0:T(8,128)(2,1)} %collective-permute-done.47), channel_id=1, source_target_pairs={{0,4},{4,0},{8,12},{12,8},{16,20},{20,16},{24,28},{28,24},{1,5},{5... | collective-permute-start | bytes 1990664 | tf_op jit(solution)/shard_map/ppermute | solution.py:865
  355.2 15.6 %collective-permute-start.45 = (bf16[192,1152]{1,0:T(8,128)(2,1)S(1)}, bf16[192,1152]{1,0:T(8,128)(2,1)S(1)}, u32[]{:S(2)}, u32[]{:S(2)}) collective-permute-start(bf16[192,1152]{1,0:T(8,128)(2,1)S(1)} %pad_maximum_fusion.13), channel_id=1, source_target_pairs={{0,4},{4,0},{8,12},{12,8},{16,20},{20,16},{24,28},{28,24},{1,5},{5... | collective-permute-start | bytes 1327112 | tf_op jit(solution)/shard_map/ppermute | solution.py:865
  (33 other events, 218.5 us)

commit v4 on v2

--- a/solution.py
+++ b/solution.py
@@ -926,12 +926,13 @@
     yu, xd = lax.optimization_barrier((yu, xd, gt_b))[:2]
     sums, sent = scatter([[u_keep, yu], [do_keep, yo, xd]], rest[0], dp)
     keep, far, send = projg_call(meta, after(h1, sent), p_mine, p_theirs)
-    flat = lax.optimization_barrier((*sums[0], *sums[1], keep))[:-1]
+    far = x_swap(far)
+    *flat, far = lax.optimization_barrier((*sums[0], *sums[1], far))
     sums, sent = scatter([flat[:2], flat[2:]], rest[1], dp)
     got = core_swap(after(send, sent))
-    far, far2 = x_swap(far), x_swap(got[part:])
+    far2 = x_swap(got[part:])
     gi_own, gi_nb, gg1 = last_call(
-        meta, x_own, x_nb, p_mine, p_got, w_full, w_other, after(dmid, sent), gain1
+        meta, x_own, x_nb, p_mine, p_got, w_full, w_other, after(dmid, sent, far), gain1
     )
     *flat, gt, gg1 = lax.optimization_barrier((*sums[0], *sums[1], gt, x_swap(core_swap(gg1))))
     sums = [flat[:2], flat[2:]]

time: 371 us -> 382 us (1.030)
  waiting for transfers between devices: 97.7 us -> 109 us
  starting transfers between devices: 39.4 us -> 35.5 us
    ppermute x11, waiting for transfers between devices: 28.2 us -> 49.1 us  [swap(): return lax.ppermute(v, 'dp', flip(dp, stride))]
    ppermute x7, waiting for transfers between devices: 13.1 us -> 3.82 us  [local(): y_swap = lambda v: lax.ppermute(v, 'dp', flip(dp, 1))]
  transfers between devices with their start and end apart: 49 -> 49, of which waited for: 19 -> 18; matrix products, arithmetic and copies ran while one was open for 12% -> 12% of each run, Pallas kernels for 35% -> 34%
where the time goes in v4:
time: 382 us; the launch traced here: 381 us
  Pallas kernels  177 us (46%)
  waiting for transfers between devices  109 us (29%)
  other arithmetic  39.7 us (10%)
  starting transfers between devices  35.5 us (9%)
  local copies, waits for them, and re-layouts  17.1 us (4%)
    pallas_call x2, Pallas kernels, att_bwd_call(): pl.pallas_call(functools.partial(att_bwd_body, p0, into is not None), out...  66.2 us
    pallas_call x1, Pallas kernels, ffn_call(): pl.pallas_call(ffn_body, out_shape=[sds((2, rows, width), f32), sds((rows...  49.3 us
    ppermute x11, waiting for transfers between devices, swap(): return lax.ppermute(v, 'dp', flip(dp, stride))  49.1 us
    ppermute x11, waiting for transfers between devices, x_swap(): return lax.ppermute(v, 'head', XNB)  44 us
    pallas_call x1, Pallas kernels, att_fwd_call(): pl.pallas_call(att_fwd_body, out_shape=[sds((length // 2, width), bf16),...  27.3 us
    pallas_call x1, Pallas kernels, qkv_call(): pl.pallas_call(qkv_body, out_shape=[sds((length, width), bf16), sds((leng...  13.6 us
    ppermute x19, waiting for transfers between devices, core_swap(): return lax.ppermute(v, 'head', CORE)  12.6 us
    ppermute x11, starting transfers between devices, x_swap(): return lax.ppermute(v, 'head', XNB)  12.4 us
  transfers between devices with their start and end apart: 49, of which 18 were waited for; matrix products, arithmetic and copies ran while one was open for 12% of the time, Pallas kernels for 34%

profile of v4, /device:TPU:0, one launch (start us, length us, event | category | flops | bytes accessed | tf_op | source)
XLA Modules:
  0.0 380.7 jit_solution(3879403069675075335)
XLA Ops:
  1.7 1.2 constant_dynamic-slice_fusion.4
  4.4 1.5 collective-permute-done.3.wb
  6.9 3.2 collective-permute-start.4
  13.0 2.5 dynamic-slice_bitcast_fusion.1
  16.7 2.2 pad_maximum_fusion.1
  18.9 29.4 %collective-permute-done.x1.xx = bf16[512,768]{1,0:T(8,128)(2,1)} collective-permute-done((bf16[512,768]{1,0:T(8,128)(2,1)}, bf16[512,768]{1,0:T(8,128)(2,1)}, u32[]{:S(2)}, u32[]{:S(2)}) %collective-permute-start) | collective-permute-done | bytes 786464 | tf_op jit(solution)/shard_map/ppermute | solution.py:778
  49.4 1.7 collective-permute-start.5
  51.2 2.6 collective-permute-done.6.x3
  54.7 13.6 %qkv.1 = (bf16[2048,768]{1,0:T(8,128)(2,1)}, bf16[2048,1152]{1,0:T(8,128)(2,1)}, bf16[2048,1152]{1,0:T(8,128)(2,1)}, bf16[768,1152]{1,0:T(8,128)(2,1)}, f32[8,1152]{1,0:T(8,128)}) custom-call(s32[4]{0:T(128)} %pad_add_fusion.meta, bf16[512,768]{1,0:T(8,128)(2,1)} %copy-done, bf16[512,768]{1,0:T(8,128)(2,1)} %collective-permute-done.x1.xx, ...), custom_call_target="tpu_custom_call" | custom-call | flops 3623878656 | bytes 15728640 | tf_op jit(solution)/shard_map/qkv/pallas_call | solution.py:131
  68.7 1.7 collective-permute-start.10
  70.4 1.5 collective-permute-start.7
  72.0 1.6 collective-permute-start.8
  73.9 27.3 %attn_fwd.1 = (bf16[1024,384]{1,0:T(8,128)(2,1)}, bf16[1024,384]{1,0:T(8,128)(2,1)}, f32[3,2,2048]{2,1,0:T(2,128)}) custom-call(s32[4]{0:T(128)} %pad_add_fusion.meta, bf16[2048,1152]{1,0:T(8,128)(2,1)} %get-tuple-element.130.q_ref.k_ref.v_ref, bf16[2048,1152]{1,0:T(8,128)(2,1)} %get-tuple-element.130.q_ref.k_ref.v_ref, ...), custom_call_target="tpu_custom_call" | custom-call | flops 12884901888 | bytes 6291456 | tf_op jit(solution)/shard_map/attn_fwd/pallas_call | solution.py:255
  103.1 2.4 collective-permute-done.14.c0
  105.5 1.7 collective-permute-done.16.c2
  109.8 49.3 %ffn.1 = (f32[2,512,768]{2,1,0:T(8,128)}, bf16[512,768]{1,0:T(8,128)(2,1)}, bf16[1024,384]{1,0:T(8,128)(2,1)}, bf16[1024,384]{1,0:T(8,128)(2,1)}, f32[1,768]{1,0...) custom-call(s32[4]{0:T(128)} %pad_add_fusion.meta, ...), custom_call_target="tpu_custom_call" | custom-call | flops 32614907904 | bytes 31457280 | tf_op jit(solution)/shard_map/ffn/pallas_call | solution.py:623
  160.3 1.9 collective-permute-done.19
  162.2 2.7 add_convert_fusion
  164.9 1.5 collective-permute-done.23
  167.6 2.7 convert_add_fusion
  170.3 1.5 collective-permute-start.24
  171.8 2.2 add_convert_fusion.3
  174.4 42.7 %attn_bwd.2 = (bf16[1024,1152]{1,0:T(8,128)(2,1)}, bf16[1024,1152]{1,0:T(8,128)(2,1)}, f32[16,256]{1,0:T(8,128)}) custom-call(s32[4]{0:T(128)} %pad_add_fusion.meta, bf16[2048,1152]{1,0:T(8,128)(2,1)} %get-tuple-element.130.q_ref.k_ref.v_ref, bf16[2048,1152]{1,0:T(8,128)(2,1)} %get-tuple-element.130.q_ref.k_ref.v_ref, ...), custom_call_target="tpu_custom_call" | custom-call | flops 15032385536 | bytes 10485760 | tf_op jit(solution)/shard_map/attn_bwd/pallas_call | solution.py:407
  217.2 2.6 add_convert_fusion.1
  220.7 2.9 add_convert_fusion.4
  223.5 1.5 collective-permute-start.27
  225.0 23.5 %attn_bwd.3 = (bf16[1024,1152]{1,0:T(8,128)(2,1)}, bf16[1024,1152]{1,0:T(8,128)(2,1)}, f32[16,128]{1,0:T(8,128)}) custom-call(s32[4]{0:T(128)} %pad_add_fusion.meta, bf16[2048,1152]{1,0:T(8,128)(2,1)} %get-tuple-element.130.q_ref.k_ref.v_ref, ...), custom_call_target="tpu_custom_call", output_to_operand_aliasing={{0}: (13, {}), {1}: (14, {})} | custom-call | flops 7516192768 | bytes 5242880 | tf_op jit(solution)/shard_map/attn_bwd/pallas_call | solution.py:407
  250.7 1.5 convert_add_fusion.4
  252.3 1.7 collective-permute-start.29
  254.0 9.6 %projg.1 = (bf16[192,1152]{1,0:T(8,128)(2,1)}, bf16[192,1152]{1,0:T(8,128)(2,1)}, bf16[384,1152]{1,0:T(8,128)(2,1)}) custom-call(s32[4]{0:T(128)} %pad_add_fusion.meta, bf16[2048,768]{1,0:T(8,128)(2,1)} %get-tuple-element.137.h, bf16[1024,1152]{1,0:T(8,128)(2,1)} %get-tuple-element.138.dm, bf16[1024,1152]{1,0:T(8,128)(2,1)} %get-tuple-element.139.dt), custom_call_target="tpu_custom_call" | custom-call | flops 2048 | bytes 2048 | tf_op jit(solution)/shard_map/projg/pallas_call | solution.py:692
  264.7 5.0 %collective-permute-done.29 = bf16[432,768]{1,0:T(8,128)(2,1)S(1)} collective-permute-done((bf16[432,768]{1,0:T(8,128)(2,1)S(1)}, bf16[432,768]{1,0:T(8,128)(2,1)S(1)}, u32[]{:S(2)}, u32[]{:S(2)}) %collective-permute-start.29) | collective-permute-done | bytes 663584 | tf_op jit(solution)/shard_map/ppermute | solution.py:804
  269.7 6.3 %collective-permute-done.30 = bf16[192,1152]{1,0:T(8,128)(2,1)S(1)} collective-permute-done((bf16[192,1152]{1,0:T(8,128)(2,1)}, bf16[192,1152]{1,0:T(8,128)(2,1)S(1)}, u32[]{:S(2)}, u32[]{:S(2)}) %collective-permute-start.30) | collective-permute-done | bytes 442400 | tf_op jit(solution)/shard_map/ppermute | solution.py:778
  277.0 2.7 collective-permute-start.33
  279.7 11.4 %last.1 = (f32[2,512,768]{2,1,0:T(8,128)}, bf16[512,768]{1,0:T(8,128)(2,1)}, f32[1,768]{1,0:T(1,128)}) custom-call(s32[4]{0:T(128)} %pad_add_fusion.meta, bf16[512,768]{1,0:T(8,128)(2,1)} %copy-done, bf16[512,768]{1,0:T(8,128)(2,1)} %collective-permute-done.x1.xx, bf16[1024,1152]{1,0:T(8,128)(2,1)} %get-tuple-element.138.dm, ...), custom_call_target="tpu_custom_call" | custom-call | flops 512 | bytes 512 | tf_op jit(solution)/shard_map/last/pallas_call | solution.py:750
  298.5 3.9 %all-to-all-start = ((f32[32,16,192]{2,1,0:T(8,128)}), f32[32,16,192]{2,1,0:T(8,128)S(1)}, u32[]{:S(2)}, u32[]{:S(2)}) async-start(f32[32,16,192]{2,1,0:T(8,128)} %bitcast.16), calls=%async_computation | async-start | bytes 1048576 | tf_op jit(solution)/shard_map/all_to_all | solution.py:978
  302.4 8.2 %collective-permute-done.32 = bf16[192,1152]{1,0:T(8,128)(2,1)S(1)} collective-permute-done((bf16[192,1152]{1,0:T(8,128)(2,1)}, bf16[192,1152]{1,0:T(8,128)(2,1)S(1)}, u32[]{:S(2)}, u32[]{:S(2)}) %collective-permute-start.32) | collective-permute-done | bytes 442400 | tf_op jit(solution)/shard_map/ppermute | solution.py:778
  311.0 9.5 %collective-permute-done.40 = bf16[216,768]{1,0:T(8,128)(2,1)} collective-permute-done((bf16[216,768]{1,0:T(8,128)(2,1)S(1)}, bf16[216,768]{1,0:T(8,128)(2,1)}, u32[]{:S(2)}, u32[]{:S(2)}) %collective-permute-start.40) | collective-permute-done | bytes 331808 | tf_op jit(solution)/shard_map/ppermute | solution.py:804
  324.1 2.0 collective-permute-start.38
  326.1 2.4 convert_dynamic-update-slice_fusion.1
  328.5 16.1 %collective-permute-done.38 = bf16[96,1152]{1,0:T(8,128)(2,1)S(1)} collective-permute-done((bf16[96,1152]{1,0:T(8,128)(2,1)S(1)}, bf16[96,1152]{1,0:T(8,128)(2,1)S(1)}, u32[]{:S(2)}, u32[]{:S(2)}) %collective-permute-start.38) | collective-permute-done | bytes 221216 | tf_op jit(solution)/shard_map/ppermute | solution.py:804
  346.1 5.6 %collective-permute-done.39 = bf16[48,1152]{1,0:T(8,128)(2,1)S(1)} collective-permute-done((bf16[48,1152]{1,0:T(8,128)(2,1)S(1)}, bf16[48,1152]{1,0:T(8,128)(2,1)S(1)}, u32[]{:S(2)}, u32[]{:S(2)}) %collective-permute-start.39) | collective-permute-done | bytes 110624 | tf_op jit(solution)/shard_map/ppermute | solution.py:804
  353.0 6.0 %collective-permute-done.42 = bf16[48,1152]{1,0:T(8,128)(2,1)S(1)} collective-permute-done((bf16[48,1152]{1,0:T(8,128)(2,1)S(1)}, bf16[48,1152]{1,0:T(8,128)(2,1)S(1)}, u32[]{:S(2)}, u32[]{:S(2)}) %collective-permute-start.42) | collective-permute-done | bytes 110624 | tf_op jit(solution)/shard_map/ppermute | solution.py:804
  359.1 1.2 broadcast_select_fusion.11
  360.3 6.1 %collective-permute-done.43 = bf16[96,1152]{1,0:T(8,128)(2,1)S(1)} collective-permute-done((bf16[96,1152]{1,0:T(8,128)(2,1)S(1)}, bf16[96,1152]{1,0:T(8,128)(2,1)S(1)}, u32[]{:S(2)}, u32[]{:S(2)}) %collective-permute-start.43) | collective-permute-done | bytes 221216 | tf_op jit(solution)/shard_map/ppermute | solution.py:804
  367.1 1.4 broadcast_select_fusion.9
  370.9 1.6 fusion
  372.5 1.6 maximum_convert_fusion
  374.0 3.8 collective-permute-done.45
  (206 shorter events, 42.7 us)
Async XLA Ops:
  3.9 2.0 collective-permute-start.3
  4.3 12.4 %collective-permute-start.1 = (bf16[192,768]{1,0:T(8,128)(2,1)}, bf16[192,768]{1,0:T(8,128)(2,1)}, u32[]{:S(2)}, u32[]{:S(2)}) collective-permute-start(bf16[192,768]{1,0:T(8,128)(2,1)} %wo_o.1), channel_id=1, source_target_pairs={{0,1},{1,0},{2,3},{3,2},{4,5},{5,4},{6,7},{7,6},{8,9},{9,8},{10,11... | collective-permute-start | bytes 884744 | tf_op jit(solution)/shard_map/ppermute | solution.py:774
  6.9 41.4 %collective-permute-start.4 = (bf16[608,768]{1,0:T(8,128)(2,1)}, bf16[608,768]{1,0:T(8,128)(2,1)}, u32[]{:S(2)}, u32[]{:S(2)}) collective-permute-start(bf16[608,768]{1,0:T(8,128)(2,1)} %pad_maximum_fusion.3), channel_id=1, source_target_pairs={{0,2},{2,0},{1,3},{3,1},{4,6},{6,4},{5,7},{7,5},{8,10},{10,8},{9,1... | collective-permute-start | bytes 2801672 | tf_op jit(solution)/shard_map/ppermute | solution.py:778
  11.1 37.2 %collective-permute-start = (bf16[512,768]{1,0:T(8,128)(2,1)}, bf16[512,768]{1,0:T(8,128)(2,1)}, u32[]{:S(2)}, u32[]{:S(2)}) collective-permute-start(bf16[512,768]{1,0:T(8,128)(2,1)} %get-tuple-element.180), channel_id=1, source_target_pairs={{0,2},{2,0},{1,3},{3,1},{4,6},{6,4},{5,7},{7,5},{8,10},{10,8},{9,1... | collective-permute-start | bytes 2359304 | tf_op jit(solution)/shard_map/ppermute | solution.py:778
  11.1 37.2 %collective-permute-start.2 = (bf16[512,768]{1,0:T(8,128)(2,1)S(1)}, bf16[512,768]{1,0:T(8,128)(2,1)}, u32[]{:S(2)}, u32[]{:S(2)}) collective-permute-start(bf16[512,768]{1,0:T(8,128)(2,1)S(1)} %get-tuple-element.179.x0.xo), channel_id=1, source_target_pairs={{0,1},{1,0},{2,3},{3,2},{4,5},{5,4},{6,7},{7,6},{8,9},{9,8},{10,11... | collective-permute-start | bytes 2359304 | tf_op jit(solution)/shard_map/ppermute | solution.py:774
  48.3 25.2 %collective-permute-start.11 = (bf16[2,768,768]{2,1,0:T(8,128)(2,1)S(1)}, bf16[2,768,768]{2,1,0:T(8,128)(2,1)}, u32[]{:S(2)}, u32[]{:S(2)}) collective-permute-start(bf16[2,768,768]{2,1,0:T(8,128)(2,1)S(1)} %pad_maximum_fusion), channel_id=1, source_target_pairs={{0,1},{1,0},{2,3},{3,2},{4,5},{5,4},{6,7},{7,6},{8,9},{9,8},{10,11... | collective-permute-start | bytes 7077896 | tf_op jit(solution)/shard_map/ppermute | solution.py:774
  48.3 5.5 %collective-permute-start.6 = (bf16[512,768]{1,0:T(8,128)(2,1)}, bf16[512,768]{1,0:T(8,128)(2,1)S(1)}, u32[]{:S(2)}, u32[]{:S(2)}) collective-permute-start(bf16[512,768]{1,0:T(8,128)(2,1)} %collective-permute-done.x1.xx), channel_id=1, source_target_pairs={{0,1},{1,0},{2,3},{3,2},{4,5},{5,4},{6,7},{7,6},{8,9},{9,8},{10,11... | collective-permute-start | bytes 2359304 | tf_op jit(solution)/shard_map/ppermute | solution.py:774
  49.4 21.0 %collective-permute-start.5 = (bf16[2,192,768]{2,1,0:T(8,128)(2,1)}, bf16[2,192,768]{2,1,0:T(8,128)(2,1)}, u32[]{:S(2)}, u32[]{:S(2)}) collective-permute-start(bf16[2,192,768]{2,1,0:T(8,128)(2,1)} %pad_maximum_fusion.10), channel_id=1, source_target_pairs={{0,2},{2,0},{1,3},{3,1},{4,6},{6,4},{5,7},{7,5},{8,10},{10,8},{9,1... | collective-permute-start | bytes 1769480 | tf_op jit(solution)/shard_map/ppermute | solution.py:778
  68.3 34.1 %collective-permute-start.13 = (bf16[768,1152]{1,0:T(8,128)(2,1)}, bf16[768,1152]{1,0:T(8,128)(2,1)}, u32[]{:S(2)}, u32[]{:S(2)}) collective-permute-start(bf16[768,1152]{1,0:T(8,128)(2,1)} %get-tuple-element.104.wm), channel_id=1, source_target_pairs={{0,1},{1,0},{2,3},{3,2},{4,5},{5,4},{6,7},{7,6},{8,9},{9,8},{10,11... | collective-permute-start | bytes 5308424 | tf_op jit(solution)/shard_map/ppermute | solution.py:774
  68.7 33.2 %collective-permute-start.10 = (bf16[896,768]{1,0:T(8,128)(2,1)}, bf16[896,768]{1,0:T(8,128)(2,1)}, u32[]{:S(2)}, u32[]{:S(2)}) collective-permute-start(bf16[896,768]{1,0:T(8,128)(2,1)} %pad_maximum_fusion.1), channel_id=1, source_target_pairs={{0,2},{2,0},{1,3},{3,1},{4,6},{6,4},{5,7},{7,5},{8,10},{10,8},{9,1... | collective-permute-start | bytes 4128776 | tf_op jit(solution)/shard_map/ppermute | solution.py:778
  70.4 30.8 %collective-permute-start.7 = (bf16[2,192,768]{2,1,0:T(8,128)(2,1)}, bf16[2,192,768]{2,1,0:T(8,128)(2,1)S(1)}, u32[]{:S(2)}, u32[]{:S(2)}) collective-permute-start(bf16[2,192,768]{2,1,0:T(8,128)(2,1)} %collective-permute-done.5.n0), channel_id=1, source_target_pairs={{0,4},{4,0},{8,12},{12,8},{16,20},{20,16},{24,28},{28,24},{1,5},{5... | collective-permute-start | bytes 1769480 | tf_op jit(solution)/shard_map/ppermute | solution.py:804
  72.0 29.4 %collective-permute-start.8 = (bf16[2,192,768]{2,1,0:T(8,128)(2,1)}, bf16[2,192,768]{2,1,0:T(8,128)(2,1)}, u32[]{:S(2)}, u32[]{:S(2)}) collective-permute-start(bf16[2,192,768]{2,1,0:T(8,128)(2,1)} %collective-permute-done.5.n0), channel_id=1, source_target_pairs={{0,8},{4,12},{8,0},{12,4},{16,24},{20,28},{24,16},{28,20},{1,9},{5... | collective-permute-start | bytes 1769480 | tf_op jit(solution)/shard_map/ppermute | solution.py:804
  73.5 28.3 %collective-permute-start.9 = (bf16[2,192,768]{2,1,0:T(8,128)(2,1)}, bf16[2,192,768]{2,1,0:T(8,128)(2,1)S(1)}, u32[]{:S(2)}, u32[]{:S(2)}) collective-permute-start(bf16[2,192,768]{2,1,0:T(8,128)(2,1)} %collective-permute-done.5.n0), channel_id=1, source_target_pairs={{0,12},{4,8},{8,4},{12,0},{16,28},{20,24},{24,20},{28,16},{1,13},{... | collective-permute-start | bytes 1769480 | tf_op jit(solution)/shard_map/ppermute | solution.py:804
  101.3 7.6 %collective-permute-start.12 = (bf16[1024,384]{1,0:T(8,128)(2,1)}, bf16[1024,384]{1,0:T(8,128)(2,1)S(1)}, u32[]{:S(2)}, u32[]{:S(2)}) collective-permute-start(bf16[1024,384]{1,0:T(8,128)(2,1)} %get-tuple-element.103.ot), channel_id=1, source_target_pairs={{0,1},{1,0},{2,3},{3,2},{4,5},{5,4},{6,7},{7,6},{8,9},{9,8},{10,11... | collective-permute-start | bytes 2359304 | tf_op jit(solution)/shard_map/ppermute | solution.py:774
  101.4 4.2 %collective-permute-start.14 = (bf16[2,192,768]{2,1,0:T(8,128)(2,1)}, bf16[2,192,768]{2,1,0:T(8,128)(2,1)S(1)}, u32[]{:S(2)}, u32[]{:S(2)}) collective-permute-start(bf16[2,192,768]{2,1,0:T(8,128)(2,1)} %collective-permute-done.5.n0), channel_id=1, source_target_pairs={{0,1},{1,0},{2,3},{3,2},{4,5},{5,4},{6,7},{7,6},{8,9},{9,8},{10,11... | collective-permute-start | bytes 1769480 | tf_op jit(solution)/shard_map/ppermute | solution.py:774
  101.9 3.7 collective-permute-start.15
  102.0 5.2 %collective-permute-start.16 = (bf16[2,192,768]{2,1,0:T(8,128)(2,1)}, bf16[2,192,768]{2,1,0:T(8,128)(2,1)S(1)}, u32[]{:S(2)}, u32[]{:S(2)}) collective-permute-start(bf16[2,192,768]{2,1,0:T(8,128)(2,1)} %collective-permute-done.8.n2), channel_id=1, source_target_pairs={{0,1},{1,0},{2,3},{3,2},{4,5},{5,4},{6,7},{7,6},{8,9},{9,8},{10,11... | collective-permute-start | bytes 1769480 | tf_op jit(solution)/shard_map/ppermute | solution.py:774
  102.5 4.8 %collective-permute-start.17 = (bf16[2,192,768]{2,1,0:T(8,128)(2,1)S(1)}, bf16[2,192,768]{2,1,0:T(8,128)(2,1)S(1)}, u32[]{:S(2)}, u32[]{:S(2)}) collective-permute-start(bf16[2,192,768]{2,1,0:T(8,128)(2,1)S(1)} %collective-permute-done.9.n3), channel_id=1, source_target_pairs={{0,1},{1,0},{2,3},{3,2},{4,5},{5,4},{6,7},{7,6},{8,9},{9,8},{10,11... | collective-permute-start | bytes 1769480 | tf_op jit(solution)/shard_map/ppermute | solution.py:774
  159.1 3.1 collective-permute-start.19
  159.3 7.1 %collective-permute-start.23 = (bf16[960,768]{1,0:T(8,128)(2,1)}, bf16[960,768]{1,0:T(8,128)(2,1)S(1)}, u32[]{:S(2)}, u32[]{:S(2)}) collective-permute-start(bf16[960,768]{1,0:T(8,128)(2,1)} %get-tuple-element.118), channel_id=1, source_target_pairs={{0,1},{1,0},{2,3},{3,2},{4,5},{5,4},{6,7},{7,6},{8,9},{9,8},{10,11... | collective-permute-start | bytes 4423688 | tf_op jit(solution)/shard_map/ppermute | solution.py:774
  159.7 10.6 %collective-permute-start.21 = (bf16[960,768]{1,0:T(8,128)(2,1)}, bf16[960,768]{1,0:T(8,128)(2,1)}, u32[]{:S(2)}, u32[]{:S(2)}) collective-permute-start(bf16[960,768]{1,0:T(8,128)(2,1)} %get-tuple-element.116), channel_id=1, source_target_pairs={{0,1},{1,0},{2,3},{3,2},{4,5},{5,4},{6,7},{7,6},{8,9},{9,8},{10,11... | collective-permute-start | bytes 4423688 | tf_op jit(solution)/shard_map/ppermute | solution.py:774
  159.8 14.1 %collective-permute-start.26 = (bf16[1024,384]{1,0:T(8,128)(2,1)}, bf16[1024,384]{1,0:T(8,128)(2,1)}, u32[]{:S(2)}, u32[]{:S(2)}) collective-permute-start(bf16[1024,384]{1,0:T(8,128)(2,1)} %get-tuple-element.123), channel_id=1, source_target_pairs={{0,1},{1,0},{2,3},{3,2},{4,5},{5,4},{6,7},{7,6},{8,9},{9,8},{10,11... | collective-permute-start | bytes 2359304 | tf_op jit(solution)/shard_map/ppermute | solution.py:774
  160.2 60.5 %collective-permute-start.18 = (bf16[768,768]{1,0:T(8,128)(2,1)}, bf16[768,768]{1,0:T(8,128)(2,1)}, u32[]{:S(2)}, u32[]{:S(2)}) collective-permute-start(bf16[768,768]{1,0:T(8,128)(2,1)} %get-tuple-element.112), channel_id=1, source_target_pairs={{0,1},{1,0},{2,3},{3,2},{4,5},{5,4},{6,7},{7,6},{8,9},{9,8},{10,11... | collective-permute-start | bytes 3538952 | tf_op jit(solution)/shard_map/ppermute | solution.py:774
  164.9 52.2 %collective-permute-start.20 = (bf16[768,768]{1,0:T(8,128)(2,1)}, bf16[768,768]{1,0:T(8,128)(2,1)}, u32[]{:S(2)}, u32[]{:S(2)}) collective-permute-start(bf16[768,768]{1,0:T(8,128)(2,1)} %add_convert_fusion), channel_id=1, source_target_pairs={{0,2},{2,0},{1,3},{3,1},{4,6},{6,4},{5,7},{7,5},{8,10},{10,8},{9,1... | collective-permute-start | bytes 3538952 | tf_op jit(solution)/shard_map/ppermute | solution.py:778
  166.5 50.7 %collective-permute-start.25 = (bf16[512,768]{1,0:T(8,128)(2,1)}, bf16[512,768]{1,0:T(8,128)(2,1)}, u32[]{:S(2)}, u32[]{:S(2)}) collective-permute-start(bf16[512,768]{1,0:T(8,128)(2,1)} %get-tuple-element.120), channel_id=1, source_target_pairs={{0,2},{2,0},{1,3},{3,1},{4,6},{6,4},{5,7},{7,5},{8,10},{10,8},{9,1... | collective-permute-start | bytes 2359304 | tf_op jit(solution)/shard_map/ppermute | solution.py:778
  170.3 46.9 %collective-permute-start.24 = (bf16[480,768]{1,0:T(8,128)(2,1)}, bf16[480,768]{1,0:T(8,128)(2,1)}, u32[]{:S(2)}, u32[]{:S(2)}) collective-permute-start(bf16[480,768]{1,0:T(8,128)(2,1)} %get-tuple-element.174), channel_id=1, source_target_pairs={{0,4},{4,0},{8,12},{12,8},{16,20},{20,16},{24,28},{28,24},{1,5},{5... | collective-permute-start | bytes 2211848 | tf_op jit(solution)/shard_map/ppermute | solution.py:847
  173.9 43.2 %collective-permute-start.22 = (bf16[480,768]{1,0:T(8,128)(2,1)}, bf16[480,768]{1,0:T(8,128)(2,1)}, u32[]{:S(2)}, u32[]{:S(2)}) collective-permute-start(bf16[480,768]{1,0:T(8,128)(2,1)} %add_convert_fusion.3), channel_id=1, source_target_pairs={{0,4},{4,0},{8,12},{12,8},{16,20},{20,16},{24,28},{28,24},{1,5},{5... | collective-permute-start | bytes 2211848 | tf_op jit(solution)/shard_map/ppermute | solution.py:847
  219.8 29.0 %collective-permute-start.28 = (bf16[480,768]{1,0:T(8,128)(2,1)}, bf16[480,768]{1,0:T(8,128)(2,1)}, u32[]{:S(2)}, u32[]{:S(2)}) collective-permute-start(bf16[480,768]{1,0:T(8,128)(2,1)} %add_convert_fusion.1), channel_id=1, source_target_pairs={{0,2},{2,0},{1,3},{3,1},{4,6},{6,4},{5,7},{7,5},{8,10},{10,8},{9,1... | collective-permute-start | bytes 2211848 | tf_op jit(solution)/shard_map/ppermute | solution.py:778
  223.5 25.2 %collective-permute-start.27 = (bf16[384,768]{1,0:T(8,128)(2,1)}, bf16[384,768]{1,0:T(8,128)(2,1)S(1)}, u32[]{:S(2)}, u32[]{:S(2)}) collective-permute-start(bf16[384,768]{1,0:T(8,128)(2,1)} %get-tuple-element.169), channel_id=1, source_target_pairs={{0,4},{4,0},{8,12},{12,8},{16,20},{20,16},{24,28},{28,24},{1,5},{5... | collective-permute-start | bytes 1769480 | tf_op jit(solution)/shard_map/ppermute | solution.py:847
  248.6 31.1 %collective-permute-start.34 = (bf16[1024,1152]{1,0:T(8,128)(2,1)}, bf16[1024,1152]{1,0:T(8,128)(2,1)}, u32[]{:S(2)}, u32[]{:S(2)}) collective-permute-start(bf16[1024,1152]{1,0:T(8,128)(2,1)} %get-tuple-element.139.dt), channel_id=1, source_target_pairs={{0,1},{1,0},{2,3},{3,2},{4,5},{5,4},{6,7},{7,6},{8,9},{9,8},{10,11... | collective-permute-start | bytes 7077896 | tf_op jit(solution)/shard_map/ppermute | solution.py:774
  252.3 17.3 %collective-permute-start.29 = (bf16[432,768]{1,0:T(8,128)(2,1)S(1)}, bf16[432,768]{1,0:T(8,128)(2,1)S(1)}, u32[]{:S(2)}, u32[]{:S(2)}) collective-permute-start(bf16[432,768]{1,0:T(8,128)(2,1)S(1)} %pad_maximum_fusion.6), channel_id=1, source_target_pairs={{0,8},{4,12},{8,0},{12,4},{16,24},{20,28},{24,16},{28,20},{1,9},{5... | collective-permute-start | bytes 1990664 | tf_op jit(solution)/shard_map/ppermute | solution.py:804
  263.6 12.4 %collective-permute-start.30 = (bf16[192,1152]{1,0:T(8,128)(2,1)}, bf16[192,1152]{1,0:T(8,128)(2,1)S(1)}, u32[]{:S(2)}, u32[]{:S(2)}) collective-permute-start(bf16[192,1152]{1,0:T(8,128)(2,1)} %get-tuple-element.141), channel_id=1, source_target_pairs={{0,2},{2,0},{1,3},{3,1},{4,6},{6,4},{5,7},{7,5},{8,10},{10,8},{9,1... | collective-permute-start | bytes 1327112 | tf_op jit(solution)/shard_map/ppermute | solution.py:778
  277.0 18.2 %collective-permute-start.31 = (bf16[384,1152]{1,0:T(8,128)(2,1)}, bf16[384,1152]{1,0:T(8,128)(2,1)S(1)}, u32[]{:S(2)}, u32[]{:S(2)}) collective-permute-start(bf16[384,1152]{1,0:T(8,128)(2,1)} %get-tuple-element.146), channel_id=1, source_target_pairs={{0,1},{1,0},{2,3},{3,2},{4,5},{5,4},{6,7},{7,6},{8,9},{9,8},{10,11... | collective-permute-start | bytes 2654216 | tf_op jit(solution)/shard_map/ppermute | solution.py:774
  277.0 18.1 %collective-permute-start.33 = (bf16[216,768]{1,0:T(8,128)(2,1)S(1)}, bf16[216,768]{1,0:T(8,128)(2,1)S(1)}, u32[]{:S(2)}, u32[]{:S(2)}) collective-permute-start(bf16[216,768]{1,0:T(8,128)(2,1)S(1)} %pad_maximum_fusion.15), channel_id=1, source_target_pairs={{0,16},{4,20},{8,24},{12,28},{16,0},{20,4},{24,8},{28,12},{1,17},{... | collective-permute-start | bytes 995336 | tf_op jit(solution)/shard_map/ppermute | solution.py:804
  292.5 4.6 %collective-permute-start.36 = (f32[1,768]{1,0:T(1,128)S(1)}, f32[1,768]{1,0:T(1,128)S(1)}, u32[]{:S(2)}, u32[]{:S(2)}) collective-permute-start(f32[1,768]{1,0:T(1,128)S(1)} %collective-permute-done.35), channel_id=1, source_target_pairs={{0,2},{2,0},{1,3},{3,1},{4,6},{6,4},{5,7},{7,5},{8,10},{10,8},{9,1... | collective-permute-start | bytes 9224 | tf_op jit(solution)/shard_map/ppermute | solution.py:778
  296.0 14.6 %collective-permute-start.32 = (bf16[192,1152]{1,0:T(8,128)(2,1)}, bf16[192,1152]{1,0:T(8,128)(2,1)S(1)}, u32[]{:S(2)}, u32[]{:S(2)}) collective-permute-start(bf16[192,1152]{1,0:T(8,128)(2,1)} %slice.133), channel_id=1, source_target_pairs={{0,2},{2,0},{1,3},{3,1},{4,6},{6,4},{5,7},{7,5},{8,10},{10,8},{9,1... | collective-permute-start | bytes 1327112 | tf_op jit(solution)/shard_map/ppermute | solution.py:778
  297.4 23.0 %collective-permute-start.40 = (bf16[216,768]{1,0:T(8,128)(2,1)S(1)}, bf16[216,768]{1,0:T(8,128)(2,1)}, u32[]{:S(2)}, u32[]{:S(2)}) collective-permute-start(bf16[216,768]{1,0:T(8,128)(2,1)S(1)} %pad_maximum_fusion.16), channel_id=1, source_target_pairs={{0,16},{4,20},{8,24},{12,28},{16,0},{20,4},{24,8},{28,12},{1,17},{... | collective-permute-start | bytes 995336 | tf_op jit(solution)/shard_map/ppermute | solution.py:804
  298.5 29.9 %all-to-all-start = ((f32[32,16,192]{2,1,0:T(8,128)}), f32[32,16,192]{2,1,0:T(8,128)S(1)}, u32[]{:S(2)}, u32[]{:S(2)}) async-start(f32[32,16,192]{2,1,0:T(8,128)} %bitcast.16), calls=%async_computation | async-start | bytes 1048576 | tf_op jit(solution)/shard_map/all_to_all | solution.py:978
  310.9 13.1 %collective-permute-start.37 = (bf16[192,1152]{1,0:T(8,128)(2,1)S(1)}, bf16[192,1152]{1,0:T(8,128)(2,1)S(1)}, u32[]{:S(2)}, u32[]{:S(2)}) collective-permute-start(bf16[192,1152]{1,0:T(8,128)(2,1)S(1)} %get-tuple-element.176), channel_id=1, source_target_pairs={{0,4},{4,0},{8,12},{12,8},{16,20},{20,16},{24,28},{28,24},{1,5},{5... | collective-permute-start | bytes 1327112 | tf_op jit(solution)/shard_map/ppermute | solution.py:847
  322.4 23.5 %collective-permute-start.41 = (bf16[432,768]{1,0:T(8,128)(2,1)S(1)}, bf16[432,768]{1,0:T(8,128)(2,1)}, u32[]{:S(2)}, u32[]{:S(2)}) collective-permute-start(bf16[432,768]{1,0:T(8,128)(2,1)S(1)} %pad_maximum_fusion.7), channel_id=1, source_target_pairs={{0,8},{4,12},{8,0},{12,4},{16,24},{20,28},{24,16},{28,20},{1,9},{5... | collective-permute-start | bytes 1990664 | tf_op jit(solution)/shard_map/ppermute | solution.py:804
  322.5 44.6 %collective-permute-start.47 = (bf16[432,768]{1,0:T(8,128)(2,1)S(1)}, bf16[432,768]{1,0:T(8,128)(2,1)}, u32[]{:S(2)}, u32[]{:S(2)}) collective-permute-start(bf16[432,768]{1,0:T(8,128)(2,1)S(1)} %pad_maximum_fusion.7), channel_id=1, source_target_pairs={{0,4},{4,0},{8,12},{12,8},{16,20},{20,16},{24,28},{28,24},{1,5},{5... | collective-permute-start | bytes 1990664 | tf_op jit(solution)/shard_map/ppermute | solution.py:847
  323.0 44.0 %collective-permute-start.44 = (bf16[512,768]{1,0:T(8,128)(2,1)}, bf16[512,768]{1,0:T(8,128)(2,1)S(1)}, u32[]{:S(2)}, u32[]{:S(2)}) collective-permute-start(bf16[512,768]{1,0:T(8,128)(2,1)} %get-tuple-element.164), channel_id=1, source_target_pairs={{0,2},{2,0},{1,3},{3,1},{4,6},{6,4},{5,7},{7,5},{8,10},{10,8},{9,1... | collective-permute-start | bytes 2359304 | tf_op jit(solution)/shard_map/ppermute | solution.py:778
  324.1 20.6 %collective-permute-start.38 = (bf16[96,1152]{1,0:T(8,128)(2,1)S(1)}, bf16[96,1152]{1,0:T(8,128)(2,1)S(1)}, u32[]{:S(2)}, u32[]{:S(2)}) collective-permute-start(bf16[96,1152]{1,0:T(8,128)(2,1)S(1)} %get-tuple-element.189), channel_id=1, source_target_pairs={{0,8},{4,12},{8,0},{12,4},{16,24},{20,28},{24,16},{28,20},{1,9},{5... | collective-permute-start | bytes 663560 | tf_op jit(solution)/shard_map/ppermute | solution.py:804
  344.7 7.0 %collective-permute-start.39 = (bf16[48,1152]{1,0:T(8,128)(2,1)S(1)}, bf16[48,1152]{1,0:T(8,128)(2,1)S(1)}, u32[]{:S(2)}, u32[]{:S(2)}) collective-permute-start(bf16[48,1152]{1,0:T(8,128)(2,1)S(1)} %add_convert_fusion.13), channel_id=1, source_target_pairs={{0,16},{4,20},{8,24},{12,28},{16,0},{20,4},{24,8},{28,12},{1,17},{... | collective-permute-start | bytes 331784 | tf_op jit(solution)/shard_map/ppermute | solution.py:804
  345.9 21.2 %collective-permute-start.46 = (bf16[432,768]{1,0:T(8,128)(2,1)}, bf16[432,768]{1,0:T(8,128)(2,1)S(1)}, u32[]{:S(2)}, u32[]{:S(2)}) collective-permute-start(bf16[432,768]{1,0:T(8,128)(2,1)} %collective-permute-done.41), channel_id=1, source_target_pairs={{0,4},{4,0},{8,12},{12,8},{16,20},{20,16},{24,28},{28,24},{1,5},{5... | collective-permute-start | bytes 1990664 | tf_op jit(solution)/shard_map/ppermute | solution.py:847
  351.7 7.2 %collective-permute-start.42 = (bf16[48,1152]{1,0:T(8,128)(2,1)S(1)}, bf16[48,1152]{1,0:T(8,128)(2,1)S(1)}, u32[]{:S(2)}, u32[]{:S(2)}) collective-permute-start(bf16[48,1152]{1,0:T(8,128)(2,1)S(1)} %add_convert_fusion.12), channel_id=1, source_target_pairs={{0,16},{4,20},{8,24},{12,28},{16,0},{20,4},{24,8},{28,12},{1,17},{... | collective-permute-start | bytes 331784 | tf_op jit(solution)/shard_map/ppermute | solution.py:804
  359.0 7.4 %collective-permute-start.43 = (bf16[96,1152]{1,0:T(8,128)(2,1)S(1)}, bf16[96,1152]{1,0:T(8,128)(2,1)S(1)}, u32[]{:S(2)}, u32[]{:S(2)}) collective-permute-start(bf16[96,1152]{1,0:T(8,128)(2,1)S(1)} %pad_maximum_fusion.18), channel_id=1, source_target_pairs={{0,8},{4,12},{8,0},{12,4},{16,24},{20,28},{24,16},{28,20},{1,9},{5... | collective-permute-start | bytes 663560 | tf_op jit(solution)/shard_map/ppermute | solution.py:804
  366.5 11.3 %collective-permute-start.45 = (bf16[192,1152]{1,0:T(8,128)(2,1)S(1)}, bf16[192,1152]{1,0:T(8,128)(2,1)S(1)}, u32[]{:S(2)}, u32[]{:S(2)}) collective-permute-start(bf16[192,1152]{1,0:T(8,128)(2,1)S(1)} %pad_maximum_fusion.13), channel_id=1, source_target_pairs={{0,4},{4,0},{8,12},{12,8},{16,20},{20,16},{24,28},{28,24},{1,5},{5... | collective-permute-start | bytes 1327112 | tf_op jit(solution)/shard_map/ppermute | solution.py:847
  (32 other events, 204.0 us)

commit v5 on v2

--- a/solution.py
+++ b/solution.py
@@ -949,6 +949,7 @@
         got_v = swap(cat, stride, dp)
         vs = [join(v, g, stride) for v, g in zip(vs, rows_as(got_v, vs))]
     (pt,), sent = scatter([pt], rest[0], dp)
+    *vs, _ = lax.optimization_barrier((*vs, sent))
     packed_vs = jnp.concatenate(vs, axis=0)
     near_got = swap(packed_vs, rest[0], dp)
     across = rows_as(y_swap(packed_vs), vs)

time: 371 us -> 380 us (1.024)
  waiting for transfers between devices: 97.7 us -> 104 us
    ppermute x11, waiting for transfers between devices: 28.2 us -> 48.7 us  [swap(): return lax.ppermute(v, 'dp', flip(dp, stride))]
    ppermute x11, waiting for transfers between devices: 45.3 us -> 29.5 us  [x_swap(): return lax.ppermute(v, 'head', XNB)]
  transfers between devices with their start and end apart: 49 -> 49, of which waited for: 19 -> 19; matrix products, arithmetic and copies ran while one was open for 12% -> 11% of each run, Pallas kernels for 35% -> 34%
where the time goes in v5:
time: 380 us
  Pallas kernels  177 us (47%)
  waiting for transfers between devices  104 us (27%)
  starting transfers between devices  42.6 us (11%)
  other arithmetic  36.4 us (10%)
  local copies, waits for them, and re-layouts  18.2 us (5%)
    pallas_call x2, Pallas kernels, att_bwd_call(): pl.pallas_call(functools.partial(att_bwd_body, p0, into is not None), out...  66.3 us
    pallas_call x1, Pallas kernels, ffn_call(): pl.pallas_call(ffn_body, out_shape=[sds((2, rows, width), f32), sds((rows...  49.3 us
    ppermute x11, waiting for transfers between devices, swap(): return lax.ppermute(v, 'dp', flip(dp, stride))  48.7 us
    ppermute x11, waiting for transfers between devices, x_swap(): return lax.ppermute(v, 'head', XNB)  29.5 us
    pallas_call x1, Pallas kernels, att_fwd_call(): pl.pallas_call(att_fwd_body, out_shape=[sds((length // 2, width), bf16),...  27.4 us
    ppermute x11, starting transfers between devices, swap(): return lax.ppermute(v, 'dp', flip(dp, stride))  14.3 us
    ppermute x7, waiting for transfers between devices, local(): y_swap = lambda v: lax.ppermute(v, 'dp', flip(dp, 1))  14.3 us
    pallas_call x1, Pallas kernels, qkv_call(): pl.pallas_call(qkv_body, out_shape=[sds((length, width), bf16), sds((leng...  13.5 us
  transfers between devices with their start and end apart: 49, of which 19 were waited for; matrix products, arithmetic and copies ran while one was open for 11% of the time, Pallas kernels for 34%

profile of v5, /device:TPU:0, one launch (start us, length us, event | category | flops | bytes accessed | tf_op | source)
XLA Modules:
  0.0 379.6 jit_solution(6809854980433919046)
XLA Ops:
  6.9 3.2 collective-permute-start.4
  13.0 2.5 dynamic-slice_bitcast_fusion.1
  16.6 2.2 pad_maximum_fusion.1
  18.9 29.4 %collective-permute-done.x1.xx = bf16[512,768]{1,0:T(8,128)(2,1)} collective-permute-done((bf16[512,768]{1,0:T(8,128)(2,1)}, bf16[512,768]{1,0:T(8,128)(2,1)}, u32[]{:S(2)}, u32[]{:S(2)}) %collective-permute-start) | collective-permute-done | bytes 786464 | tf_op jit(solution)/shard_map/ppermute | solution.py:778
  49.4 1.7 collective-permute-start.5
  51.1 2.7 collective-permute-done.6.x3
  54.7 13.5 %qkv.1 = (bf16[2048,768]{1,0:T(8,128)(2,1)}, bf16[2048,1152]{1,0:T(8,128)(2,1)}, bf16[2048,1152]{1,0:T(8,128)(2,1)}, bf16[768,1152]{1,0:T(8,128)(2,1)}, f32[8,1152]{1,0:T(8,128)}) custom-call(s32[4]{0:T(128)} %pad_add_fusion.meta, bf16[512,768]{1,0:T(8,128)(2,1)} %copy-done, bf16[512,768]{1,0:T(8,128)(2,1)} %collective-permute-done.x1.xx, ...), custom_call_target="tpu_custom_call" | custom-call | flops 3623878656 | bytes 15728640 | tf_op jit(solution)/shard_map/qkv/pallas_call | solution.py:131
  68.6 1.7 collective-permute-start.10
  70.3 1.5 collective-permute-start.7
  71.8 1.6 collective-permute-start.8
  73.8 27.4 %attn_fwd.1 = (bf16[1024,384]{1,0:T(8,128)(2,1)}, bf16[1024,384]{1,0:T(8,128)(2,1)}, f32[3,2,2048]{2,1,0:T(2,128)}) custom-call(s32[4]{0:T(128)} %pad_add_fusion.meta, bf16[2048,1152]{1,0:T(8,128)(2,1)} %get-tuple-element.131.q_ref.k_ref.v_ref, bf16[2048,1152]{1,0:T(8,128)(2,1)} %get-tuple-element.131.q_ref.k_ref.v_ref, ...), custom_call_target="tpu_custom_call" | custom-call | flops 12884901888 | bytes 6291456 | tf_op jit(solution)/shard_map/attn_fwd/pallas_call | solution.py:255
  103.0 2.4 collective-permute-done.14.c0
  105.4 1.7 collective-permute-done.16.c2
  109.7 49.3 %ffn.1 = (f32[2,512,768]{2,1,0:T(8,128)}, bf16[512,768]{1,0:T(8,128)(2,1)}, bf16[1024,384]{1,0:T(8,128)(2,1)}, bf16[1024,384]{1,0:T(8,128)(2,1)}, f32[1,768]{1,0...) custom-call(s32[4]{0:T(128)} %pad_add_fusion.meta, ...), custom_call_target="tpu_custom_call" | custom-call | flops 32614907904 | bytes 31457280 | tf_op jit(solution)/shard_map/ffn/pallas_call | solution.py:623
  160.2 1.9 collective-permute-done.19
  163.1 3.1 add_convert_fusion
  166.3 1.9 collective-permute-start.25
  169.3 1.6 collective-permute-start.22
  170.8 2.6 add_convert_fusion.2
  173.9 42.8 %attn_bwd.2 = (bf16[1024,1152]{1,0:T(8,128)(2,1)}, bf16[1024,1152]{1,0:T(8,128)(2,1)}, f32[16,256]{1,0:T(8,128)}) custom-call(s32[4]{0:T(128)} %pad_add_fusion.meta, bf16[2048,1152]{1,0:T(8,128)(2,1)} %get-tuple-element.131.q_ref.k_ref.v_ref, bf16[2048,1152]{1,0:T(8,128)(2,1)} %get-tuple-element.131.q_ref.k_ref.v_ref, ...), custom_call_target="tpu_custom_call" | custom-call | flops 15032385536 | bytes 10485760 | tf_op jit(solution)/shard_map/attn_bwd/pallas_call | solution.py:407
  216.7 2.6 add_convert_fusion.1
  219.5 2.9 convert_add_fusion.1
  222.4 1.8 collective-permute-start.27
  224.2 23.5 %attn_bwd.3 = (bf16[1024,1152]{1,0:T(8,128)(2,1)}, bf16[1024,1152]{1,0:T(8,128)(2,1)}, f32[16,128]{1,0:T(8,128)}) custom-call(s32[4]{0:T(128)} %pad_add_fusion.meta, bf16[2048,1152]{1,0:T(8,128)(2,1)} %get-tuple-element.131.q_ref.k_ref.v_ref, ...), custom_call_target="tpu_custom_call", output_to_operand_aliasing={{0}: (13, {}), {1}: (14, {})} | custom-call | flops 7516192768 | bytes 5242880 | tf_op jit(solution)/shard_map/attn_bwd/pallas_call | solution.py:407
  249.8 1.5 convert_add_fusion.4
  251.4 1.6 collective-permute-start.29
  253.1 9.6 %projg.1 = (bf16[192,1152]{1,0:T(8,128)(2,1)}, bf16[192,1152]{1,0:T(8,128)(2,1)}, bf16[384,1152]{1,0:T(8,128)(2,1)}) custom-call(s32[4]{0:T(128)} %pad_add_fusion.meta, bf16[2048,768]{1,0:T(8,128)(2,1)} %get-tuple-element.138.h, bf16[1024,1152]{1,0:T(8,128)(2,1)} %get-tuple-element.139.dm, bf16[1024,1152]{1,0:T(8,128)(2,1)} %get-tuple-element.140.dt), custom_call_target="tpu_custom_call" | custom-call | flops 2048 | bytes 2048 | tf_op jit(solution)/shard_map/projg/pallas_call | solution.py:692
  262.6 6.1 %collective-permute-done.29 = bf16[432,768]{1,0:T(8,128)(2,1)S(1)} collective-permute-done((bf16[432,768]{1,0:T(8,128)(2,1)S(1)}, bf16[432,768]{1,0:T(8,128)(2,1)S(1)}, u32[]{:S(2)}, u32[]{:S(2)}) %collective-permute-start.29) | collective-permute-done | bytes 663584 | tf_op jit(solution)/shard_map/ppermute | solution.py:804
  269.1 2.7 collective-permute-start.33
  271.7 11.4 %last.1 = (f32[2,512,768]{2,1,0:T(8,128)}, bf16[512,768]{1,0:T(8,128)(2,1)}, f32[1,768]{1,0:T(1,128)}) custom-call(s32[4]{0:T(128)} %pad_add_fusion.meta, bf16[512,768]{1,0:T(8,128)(2,1)} %copy-done, bf16[512,768]{1,0:T(8,128)(2,1)} %collective-permute-done.x1.xx, bf16[1024,1152]{1,0:T(8,128)(2,1)} %get-tuple-element.139.dm, ...), custom_call_target="tpu_custom_call" | custom-call | flops 512 | bytes 512 | tf_op jit(solution)/shard_map/last/pallas_call | solution.py:750
  284.6 1.6 collective-permute-start.36
  287.4 1.7 collective-permute-start.32
  291.1 4.4 %all-to-all-start = ((f32[32,16,192]{2,1,0:T(8,128)}), f32[32,16,192]{2,1,0:T(8,128)S(1)}, u32[]{:S(2)}, u32[]{:S(2)}) async-start(f32[32,16,192]{2,1,0:T(8,128)} %bitcast.16), calls=%async_computation | async-start | bytes 1048576 | tf_op jit(solution)/shard_map/all_to_all | solution.py:978
  295.6 18.8 %collective-permute-done.40 = bf16[216,768]{1,0:T(8,128)(2,1)} collective-permute-done((bf16[216,768]{1,0:T(8,128)(2,1)}, bf16[216,768]{1,0:T(8,128)(2,1)}, u32[]{:S(2)}, u32[]{:S(2)}) %collective-permute-start.40) | collective-permute-done | bytes 331808 | tf_op jit(solution)/shard_map/ppermute | solution.py:804
  317.0 2.2 fusion.1
  320.3 2.4 convert_dynamic-update-slice_fusion.1
  322.7 6.0 %collective-permute-done.37 = bf16[192,1152]{1,0:T(8,128)(2,1)S(1)} collective-permute-done((bf16[192,1152]{1,0:T(8,128)(2,1)}, bf16[192,1152]{1,0:T(8,128)(2,1)S(1)}, u32[]{:S(2)}, u32[]{:S(2)}) %collective-permute-start.37) | collective-permute-done | bytes 442400 | tf_op jit(solution)/shard_map/ppermute | solution.py:847
  330.4 2.0 collective-permute-start.41
  332.4 5.9 %collective-permute-done.38 = bf16[96,1152]{1,0:T(8,128)(2,1)S(1)} collective-permute-done((bf16[96,1152]{1,0:T(8,128)(2,1)S(1)}, bf16[96,1152]{1,0:T(8,128)(2,1)S(1)}, u32[]{:S(2)}, u32[]{:S(2)}) %collective-permute-start.38) | collective-permute-done | bytes 221216 | tf_op jit(solution)/shard_map/ppermute | solution.py:804
  340.3 8.8 %collective-permute-done.39 = bf16[48,1152]{1,0:T(8,128)(2,1)S(1)} collective-permute-done((bf16[48,1152]{1,0:T(8,128)(2,1)S(1)}, bf16[48,1152]{1,0:T(8,128)(2,1)S(1)}, u32[]{:S(2)}, u32[]{:S(2)}) %collective-permute-start.39) | collective-permute-done | bytes 110624 | tf_op jit(solution)/shard_map/ppermute | solution.py:804
  350.6 2.0 collective-permute-start.42
  353.8 3.1 collective-permute-done.42
  357.0 2.4 collective-permute-start.43
  359.5 3.9 %collective-permute-done.43 = bf16[96,1152]{1,0:T(8,128)(2,1)S(1)} collective-permute-done((bf16[96,1152]{1,0:T(8,128)(2,1)S(1)}, bf16[96,1152]{1,0:T(8,128)(2,1)S(1)}, u32[]{:S(2)}, u32[]{:S(2)}) %collective-permute-start.43) | collective-permute-done | bytes 221216 | tf_op jit(solution)/shard_map/ppermute | solution.py:804
  363.9 6.6 %collective-permute-done.46 = bf16[432,768]{1,0:T(8,128)(2,1)S(1)} collective-permute-done((bf16[432,768]{1,0:T(8,128)(2,1)S(1)}, bf16[432,768]{1,0:T(8,128)(2,1)S(1)}, u32[]{:S(2)}, u32[]{:S(2)}) %collective-permute-start.46) | collective-permute-done | bytes 663584 | tf_op jit(solution)/shard_map/ppermute | solution.py:847
  371.9 1.6 fusion
  373.5 1.6 maximum_convert_fusion
  375.1 1.7 collective-permute-done.45
  (207 shorter events, 43.3 us)
Async XLA Ops:
  3.9 2.0 collective-permute-start.3
  4.3 12.3 %collective-permute-start.1 = (bf16[192,768]{1,0:T(8,128)(2,1)}, bf16[192,768]{1,0:T(8,128)(2,1)}, u32[]{:S(2)}, u32[]{:S(2)}) collective-permute-start(bf16[192,768]{1,0:T(8,128)(2,1)} %wo_o.1), channel_id=1, source_target_pairs={{0,1},{1,0},{2,3},{3,2},{4,5},{5,4},{6,7},{7,6},{8,9},{9,8},{10,11... | collective-permute-start | bytes 884744 | tf_op jit(solution)/shard_map/ppermute | solution.py:774
  6.9 41.4 %collective-permute-start.4 = (bf16[608,768]{1,0:T(8,128)(2,1)}, bf16[608,768]{1,0:T(8,128)(2,1)}, u32[]{:S(2)}, u32[]{:S(2)}) collective-permute-start(bf16[608,768]{1,0:T(8,128)(2,1)} %pad_maximum_fusion.3), channel_id=1, source_target_pairs={{0,2},{2,0},{1,3},{3,1},{4,6},{6,4},{5,7},{7,5},{8,10},{10,8},{9,1... | collective-permute-start | bytes 2801672 | tf_op jit(solution)/shard_map/ppermute | solution.py:778
  11.1 37.2 %collective-permute-start = (bf16[512,768]{1,0:T(8,128)(2,1)}, bf16[512,768]{1,0:T(8,128)(2,1)}, u32[]{:S(2)}, u32[]{:S(2)}) collective-permute-start(bf16[512,768]{1,0:T(8,128)(2,1)} %get-tuple-element.182), channel_id=1, source_target_pairs={{0,2},{2,0},{1,3},{3,1},{4,6},{6,4},{5,7},{7,5},{8,10},{10,8},{9,1... | collective-permute-start | bytes 2359304 | tf_op jit(solution)/shard_map/ppermute | solution.py:778
  11.1 37.2 %collective-permute-start.2 = (bf16[512,768]{1,0:T(8,128)(2,1)S(1)}, bf16[512,768]{1,0:T(8,128)(2,1)}, u32[]{:S(2)}, u32[]{:S(2)}) collective-permute-start(bf16[512,768]{1,0:T(8,128)(2,1)S(1)} %get-tuple-element.181.x0.xo), channel_id=1, source_target_pairs={{0,1},{1,0},{2,3},{3,2},{4,5},{5,4},{6,7},{7,6},{8,9},{9,8},{10,11... | collective-permute-start | bytes 2359304 | tf_op jit(solution)/shard_map/ppermute | solution.py:774
  48.3 25.1 %collective-permute-start.11 = (bf16[2,768,768]{2,1,0:T(8,128)(2,1)S(1)}, bf16[2,768,768]{2,1,0:T(8,128)(2,1)}, u32[]{:S(2)}, u32[]{:S(2)}) collective-permute-start(bf16[2,768,768]{2,1,0:T(8,128)(2,1)S(1)} %pad_maximum_fusion), channel_id=1, source_target_pairs={{0,1},{1,0},{2,3},{3,2},{4,5},{5,4},{6,7},{7,6},{8,9},{9,8},{10,11... | collective-permute-start | bytes 7077896 | tf_op jit(solution)/shard_map/ppermute | solution.py:774
  48.3 5.5 %collective-permute-start.6 = (bf16[512,768]{1,0:T(8,128)(2,1)}, bf16[512,768]{1,0:T(8,128)(2,1)S(1)}, u32[]{:S(2)}, u32[]{:S(2)}) collective-permute-start(bf16[512,768]{1,0:T(8,128)(2,1)} %collective-permute-done.x1.xx), channel_id=1, source_target_pairs={{0,1},{1,0},{2,3},{3,2},{4,5},{5,4},{6,7},{7,6},{8,9},{9,8},{10,11... | collective-permute-start | bytes 2359304 | tf_op jit(solution)/shard_map/ppermute | solution.py:774
  49.4 20.9 %collective-permute-start.5 = (bf16[2,192,768]{2,1,0:T(8,128)(2,1)}, bf16[2,192,768]{2,1,0:T(8,128)(2,1)}, u32[]{:S(2)}, u32[]{:S(2)}) collective-permute-start(bf16[2,192,768]{2,1,0:T(8,128)(2,1)} %pad_maximum_fusion.9), channel_id=1, source_target_pairs={{0,2},{2,0},{1,3},{3,1},{4,6},{6,4},{5,7},{7,5},{8,10},{10,8},{9,1... | collective-permute-start | bytes 1769480 | tf_op jit(solution)/shard_map/ppermute | solution.py:778
  68.2 34.2 %collective-permute-start.13 = (bf16[768,1152]{1,0:T(8,128)(2,1)}, bf16[768,1152]{1,0:T(8,128)(2,1)}, u32[]{:S(2)}, u32[]{:S(2)}) collective-permute-start(bf16[768,1152]{1,0:T(8,128)(2,1)} %get-tuple-element.105.wm), channel_id=1, source_target_pairs={{0,1},{1,0},{2,3},{3,2},{4,5},{5,4},{6,7},{7,6},{8,9},{9,8},{10,11... | collective-permute-start | bytes 5308424 | tf_op jit(solution)/shard_map/ppermute | solution.py:774
  68.6 33.2 %collective-permute-start.10 = (bf16[896,768]{1,0:T(8,128)(2,1)}, bf16[896,768]{1,0:T(8,128)(2,1)}, u32[]{:S(2)}, u32[]{:S(2)}) collective-permute-start(bf16[896,768]{1,0:T(8,128)(2,1)} %pad_maximum_fusion.1), channel_id=1, source_target_pairs={{0,2},{2,0},{1,3},{3,1},{4,6},{6,4},{5,7},{7,5},{8,10},{10,8},{9,1... | collective-permute-start | bytes 4128776 | tf_op jit(solution)/shard_map/ppermute | solution.py:778
  70.3 30.8 %collective-permute-start.7 = (bf16[2,192,768]{2,1,0:T(8,128)(2,1)}, bf16[2,192,768]{2,1,0:T(8,128)(2,1)S(1)}, u32[]{:S(2)}, u32[]{:S(2)}) collective-permute-start(bf16[2,192,768]{2,1,0:T(8,128)(2,1)} %collective-permute-done.5.n0), channel_id=1, source_target_pairs={{0,4},{4,0},{8,12},{12,8},{16,20},{20,16},{24,28},{28,24},{1,5},{5... | collective-permute-start | bytes 1769480 | tf_op jit(solution)/shard_map/ppermute | solution.py:804
  71.8 29.4 %collective-permute-start.8 = (bf16[2,192,768]{2,1,0:T(8,128)(2,1)}, bf16[2,192,768]{2,1,0:T(8,128)(2,1)}, u32[]{:S(2)}, u32[]{:S(2)}) collective-permute-start(bf16[2,192,768]{2,1,0:T(8,128)(2,1)} %collective-permute-done.5.n0), channel_id=1, source_target_pairs={{0,8},{4,12},{8,0},{12,4},{16,24},{20,28},{24,16},{28,20},{1,9},{5... | collective-permute-start | bytes 1769480 | tf_op jit(solution)/shard_map/ppermute | solution.py:804
  73.4 28.3 %collective-permute-start.9 = (bf16[2,192,768]{2,1,0:T(8,128)(2,1)}, bf16[2,192,768]{2,1,0:T(8,128)(2,1)S(1)}, u32[]{:S(2)}, u32[]{:S(2)}) collective-permute-start(bf16[2,192,768]{2,1,0:T(8,128)(2,1)} %collective-permute-done.5.n0), channel_id=1, source_target_pairs={{0,12},{4,8},{8,4},{12,0},{16,28},{20,24},{24,20},{28,16},{1,13},{... | collective-permute-start | bytes 1769480 | tf_op jit(solution)/shard_map/ppermute | solution.py:804
  101.2 7.6 %collective-permute-start.12 = (bf16[1024,384]{1,0:T(8,128)(2,1)}, bf16[1024,384]{1,0:T(8,128)(2,1)S(1)}, u32[]{:S(2)}, u32[]{:S(2)}) collective-permute-start(bf16[1024,384]{1,0:T(8,128)(2,1)} %get-tuple-element.104.ot), channel_id=1, source_target_pairs={{0,1},{1,0},{2,3},{3,2},{4,5},{5,4},{6,7},{7,6},{8,9},{9,8},{10,11... | collective-permute-start | bytes 2359304 | tf_op jit(solution)/shard_map/ppermute | solution.py:774
  101.3 4.2 %collective-permute-start.14 = (bf16[2,192,768]{2,1,0:T(8,128)(2,1)}, bf16[2,192,768]{2,1,0:T(8,128)(2,1)S(1)}, u32[]{:S(2)}, u32[]{:S(2)}) collective-permute-start(bf16[2,192,768]{2,1,0:T(8,128)(2,1)} %collective-permute-done.5.n0), channel_id=1, source_target_pairs={{0,1},{1,0},{2,3},{3,2},{4,5},{5,4},{6,7},{7,6},{8,9},{9,8},{10,11... | collective-permute-start | bytes 1769480 | tf_op jit(solution)/shard_map/ppermute | solution.py:774
  101.8 3.7 collective-permute-start.15
  101.9 5.2 %collective-permute-start.16 = (bf16[2,192,768]{2,1,0:T(8,128)(2,1)}, bf16[2,192,768]{2,1,0:T(8,128)(2,1)S(1)}, u32[]{:S(2)}, u32[]{:S(2)}) collective-permute-start(bf16[2,192,768]{2,1,0:T(8,128)(2,1)} %collective-permute-done.8.n2), channel_id=1, source_target_pairs={{0,1},{1,0},{2,3},{3,2},{4,5},{5,4},{6,7},{7,6},{8,9},{9,8},{10,11... | collective-permute-start | bytes 1769480 | tf_op jit(solution)/shard_map/ppermute | solution.py:774
  102.3 4.8 %collective-permute-start.17 = (bf16[2,192,768]{2,1,0:T(8,128)(2,1)S(1)}, bf16[2,192,768]{2,1,0:T(8,128)(2,1)S(1)}, u32[]{:S(2)}, u32[]{:S(2)}) collective-permute-start(bf16[2,192,768]{2,1,0:T(8,128)(2,1)S(1)} %collective-permute-done.9.n3), channel_id=1, source_target_pairs={{0,1},{1,0},{2,3},{3,2},{4,5},{5,4},{6,7},{7,6},{8,9},{9,8},{10,11... | collective-permute-start | bytes 1769480 | tf_op jit(solution)/shard_map/ppermute | solution.py:774
  158.9 3.1 collective-permute-start.19
  159.1 7.1 %collective-permute-start.21 = (bf16[960,768]{1,0:T(8,128)(2,1)}, bf16[960,768]{1,0:T(8,128)(2,1)S(1)}, u32[]{:S(2)}, u32[]{:S(2)}) collective-permute-start(bf16[960,768]{1,0:T(8,128)(2,1)} %get-tuple-element.117), channel_id=1, source_target_pairs={{0,1},{1,0},{2,3},{3,2},{4,5},{5,4},{6,7},{7,6},{8,9},{9,8},{10,11... | collective-permute-start | bytes 4423688 | tf_op jit(solution)/shard_map/ppermute | solution.py:774
  159.5 9.8 %collective-permute-start.23 = (bf16[960,768]{1,0:T(8,128)(2,1)}, bf16[960,768]{1,0:T(8,128)(2,1)}, u32[]{:S(2)}, u32[]{:S(2)}) collective-permute-start(bf16[960,768]{1,0:T(8,128)(2,1)} %get-tuple-element.119), channel_id=1, source_target_pairs={{0,1},{1,0},{2,3},{3,2},{4,5},{5,4},{6,7},{7,6},{8,9},{9,8},{10,11... | collective-permute-start | bytes 4423688 | tf_op jit(solution)/shard_map/ppermute | solution.py:774
  159.7 13.7 %collective-permute-start.26 = (bf16[1024,384]{1,0:T(8,128)(2,1)}, bf16[1024,384]{1,0:T(8,128)(2,1)}, u32[]{:S(2)}, u32[]{:S(2)}) collective-permute-start(bf16[1024,384]{1,0:T(8,128)(2,1)} %get-tuple-element.124), channel_id=1, source_target_pairs={{0,1},{1,0},{2,3},{3,2},{4,5},{5,4},{6,7},{7,6},{8,9},{9,8},{10,11... | collective-permute-start | bytes 2359304 | tf_op jit(solution)/shard_map/ppermute | solution.py:774
  160.0 59.5 %collective-permute-start.18 = (bf16[768,768]{1,0:T(8,128)(2,1)}, bf16[768,768]{1,0:T(8,128)(2,1)}, u32[]{:S(2)}, u32[]{:S(2)}) collective-permute-start(bf16[768,768]{1,0:T(8,128)(2,1)} %get-tuple-element.113), channel_id=1, source_target_pairs={{0,1},{1,0},{2,3},{3,2},{4,5},{5,4},{6,7},{7,6},{8,9},{9,8},{10,11... | collective-permute-start | bytes 3538952 | tf_op jit(solution)/shard_map/ppermute | solution.py:774
  166.2 50.5 %collective-permute-start.20 = (bf16[768,768]{1,0:T(8,128)(2,1)}, bf16[768,768]{1,0:T(8,128)(2,1)}, u32[]{:S(2)}, u32[]{:S(2)}) collective-permute-start(bf16[768,768]{1,0:T(8,128)(2,1)} %add_convert_fusion), channel_id=1, source_target_pairs={{0,2},{2,0},{1,3},{3,1},{4,6},{6,4},{5,7},{7,5},{8,10},{10,8},{9,1... | collective-permute-start | bytes 3538952 | tf_op jit(solution)/shard_map/ppermute | solution.py:778
  166.3 50.4 %collective-permute-start.25 = (bf16[512,768]{1,0:T(8,128)(2,1)}, bf16[512,768]{1,0:T(8,128)(2,1)}, u32[]{:S(2)}, u32[]{:S(2)}) collective-permute-start(bf16[512,768]{1,0:T(8,128)(2,1)} %get-tuple-element.121), channel_id=1, source_target_pairs={{0,2},{2,0},{1,3},{3,1},{4,6},{6,4},{5,7},{7,5},{8,10},{10,8},{9,1... | collective-permute-start | bytes 2359304 | tf_op jit(solution)/shard_map/ppermute | solution.py:778
  169.3 47.4 %collective-permute-start.22 = (bf16[480,768]{1,0:T(8,128)(2,1)}, bf16[480,768]{1,0:T(8,128)(2,1)}, u32[]{:S(2)}, u32[]{:S(2)}) collective-permute-start(bf16[480,768]{1,0:T(8,128)(2,1)} %add_convert_fusion.3), channel_id=1, source_target_pairs={{0,4},{4,0},{8,12},{12,8},{16,20},{20,16},{24,28},{28,24},{1,5},{5... | collective-permute-start | bytes 2211848 | tf_op jit(solution)/shard_map/ppermute | solution.py:847
  173.4 43.3 %collective-permute-start.24 = (bf16[480,768]{1,0:T(8,128)(2,1)}, bf16[480,768]{1,0:T(8,128)(2,1)}, u32[]{:S(2)}, u32[]{:S(2)}) collective-permute-start(bf16[480,768]{1,0:T(8,128)(2,1)} %get-tuple-element.175), channel_id=1, source_target_pairs={{0,4},{4,0},{8,12},{12,8},{16,20},{20,16},{24,28},{28,24},{1,5},{5... | collective-permute-start | bytes 2211848 | tf_op jit(solution)/shard_map/ppermute | solution.py:847
  219.3 28.6 %collective-permute-start.28 = (bf16[480,768]{1,0:T(8,128)(2,1)}, bf16[480,768]{1,0:T(8,128)(2,1)}, u32[]{:S(2)}, u32[]{:S(2)}) collective-permute-start(bf16[480,768]{1,0:T(8,128)(2,1)} %add_convert_fusion.1), channel_id=1, source_target_pairs={{0,2},{2,0},{1,3},{3,1},{4,6},{6,4},{5,7},{7,5},{8,10},{10,8},{9,1... | collective-permute-start | bytes 2211848 | tf_op jit(solution)/shard_map/ppermute | solution.py:778
  222.4 25.4 %collective-permute-start.27 = (bf16[384,768]{1,0:T(8,128)(2,1)}, bf16[384,768]{1,0:T(8,128)(2,1)S(1)}, u32[]{:S(2)}, u32[]{:S(2)}) collective-permute-start(bf16[384,768]{1,0:T(8,128)(2,1)} %get-tuple-element.172), channel_id=1, source_target_pairs={{0,4},{4,0},{8,12},{12,8},{16,20},{20,16},{24,28},{28,24},{1,5},{5... | collective-permute-start | bytes 1769480 | tf_op jit(solution)/shard_map/ppermute | solution.py:847
  247.7 24.0 %collective-permute-start.34 = (bf16[1024,1152]{1,0:T(8,128)(2,1)}, bf16[1024,1152]{1,0:T(8,128)(2,1)}, u32[]{:S(2)}, u32[]{:S(2)}) collective-permute-start(bf16[1024,1152]{1,0:T(8,128)(2,1)} %get-tuple-element.140.dt), channel_id=1, source_target_pairs={{0,1},{1,0},{2,3},{3,2},{4,5},{5,4},{6,7},{7,6},{8,9},{9,8},{10,11... | collective-permute-start | bytes 7077896 | tf_op jit(solution)/shard_map/ppermute | solution.py:774
  251.4 17.3 %collective-permute-start.29 = (bf16[432,768]{1,0:T(8,128)(2,1)S(1)}, bf16[432,768]{1,0:T(8,128)(2,1)S(1)}, u32[]{:S(2)}, u32[]{:S(2)}) collective-permute-start(bf16[432,768]{1,0:T(8,128)(2,1)S(1)} %pad_maximum_fusion.6), channel_id=1, source_target_pairs={{0,8},{4,12},{8,0},{12,4},{16,24},{20,28},{24,16},{28,20},{1,9},{5... | collective-permute-start | bytes 1990664 | tf_op jit(solution)/shard_map/ppermute | solution.py:804
  269.0 18.4 %collective-permute-start.30 = (bf16[384,1152]{1,0:T(8,128)(2,1)}, bf16[384,1152]{1,0:T(8,128)(2,1)S(1)}, u32[]{:S(2)}, u32[]{:S(2)}) collective-permute-start(bf16[384,1152]{1,0:T(8,128)(2,1)} %get-tuple-element.147), channel_id=1, source_target_pairs={{0,1},{1,0},{2,3},{3,2},{4,5},{5,4},{6,7},{7,6},{8,9},{9,8},{10,11... | collective-permute-start | bytes 2654216 | tf_op jit(solution)/shard_map/ppermute | solution.py:774
  269.1 18.2 %collective-permute-start.33 = (bf16[216,768]{1,0:T(8,128)(2,1)S(1)}, bf16[216,768]{1,0:T(8,128)(2,1)S(1)}, u32[]{:S(2)}, u32[]{:S(2)}) collective-permute-start(bf16[216,768]{1,0:T(8,128)(2,1)S(1)} %pad_maximum_fusion.14), channel_id=1, source_target_pairs={{0,16},{4,20},{8,24},{12,28},{16,0},{20,4},{24,8},{28,12},{1,17},{... | collective-permute-start | bytes 995336 | tf_op jit(solution)/shard_map/ppermute | solution.py:804
  284.6 4.5 %collective-permute-start.36 = (f32[1,768]{1,0:T(1,128)S(1)}, f32[1,768]{1,0:T(1,128)S(1)}, u32[]{:S(2)}, u32[]{:S(2)}) collective-permute-start(f32[1,768]{1,0:T(1,128)S(1)} %collective-permute-done.35), channel_id=1, source_target_pairs={{0,2},{2,0},{1,3},{3,1},{4,6},{6,4},{5,7},{7,5},{8,10},{10,8},{9,1... | collective-permute-start | bytes 9224 | tf_op jit(solution)/shard_map/ppermute | solution.py:778
  286.2 30.1 %collective-permute-start.31 = (bf16[192,1152]{1,0:T(8,128)(2,1)}, bf16[192,1152]{1,0:T(8,128)(2,1)S(1)}, u32[]{:S(2)}, u32[]{:S(2)}) collective-permute-start(bf16[192,1152]{1,0:T(8,128)(2,1)} %get-tuple-element.148), channel_id=1, source_target_pairs={{0,2},{2,0},{1,3},{3,1},{4,6},{6,4},{5,7},{7,5},{8,10},{10,8},{9,1... | collective-permute-start | bytes 1327112 | tf_op jit(solution)/shard_map/ppermute | solution.py:778
  287.4 29.6 %collective-permute-start.32 = (bf16[192,1152]{1,0:T(8,128)(2,1)S(1)}, bf16[192,1152]{1,0:T(8,128)(2,1)}, u32[]{:S(2)}, u32[]{:S(2)}) collective-permute-start(bf16[192,1152]{1,0:T(8,128)(2,1)S(1)} %slice.133), channel_id=1, source_target_pairs={{0,2},{2,0},{1,3},{3,1},{4,6},{6,4},{5,7},{7,5},{8,10},{10,8},{9,1... | collective-permute-start | bytes 1327112 | tf_op jit(solution)/shard_map/ppermute | solution.py:778
  289.9 24.5 %collective-permute-start.40 = (bf16[216,768]{1,0:T(8,128)(2,1)}, bf16[216,768]{1,0:T(8,128)(2,1)}, u32[]{:S(2)}, u32[]{:S(2)}) collective-permute-start(bf16[216,768]{1,0:T(8,128)(2,1)} %pad_maximum_fusion.15), channel_id=1, source_target_pairs={{0,16},{4,20},{8,24},{12,28},{16,0},{20,4},{24,8},{28,12},{1,17},{... | collective-permute-start | bytes 995336 | tf_op jit(solution)/shard_map/ppermute | solution.py:804
  291.1 31.6 %all-to-all-start = ((f32[32,16,192]{2,1,0:T(8,128)}), f32[32,16,192]{2,1,0:T(8,128)S(1)}, u32[]{:S(2)}, u32[]{:S(2)}) async-start(f32[32,16,192]{2,1,0:T(8,128)} %bitcast.16), calls=%async_computation | async-start | bytes 1048576 | tf_op jit(solution)/shard_map/all_to_all | solution.py:978
  319.2 9.5 %collective-permute-start.37 = (bf16[192,1152]{1,0:T(8,128)(2,1)}, bf16[192,1152]{1,0:T(8,128)(2,1)S(1)}, u32[]{:S(2)}, u32[]{:S(2)}) collective-permute-start(bf16[192,1152]{1,0:T(8,128)(2,1)} %get-tuple-element.178), channel_id=1, source_target_pairs={{0,4},{4,0},{8,12},{12,8},{16,20},{20,16},{24,28},{28,24},{1,5},{5... | collective-permute-start | bytes 1327112 | tf_op jit(solution)/shard_map/ppermute | solution.py:847
  319.7 44.0 %collective-permute-start.44 = (bf16[512,768]{1,0:T(8,128)(2,1)}, bf16[512,768]{1,0:T(8,128)(2,1)S(1)}, u32[]{:S(2)}, u32[]{:S(2)}) collective-permute-start(bf16[512,768]{1,0:T(8,128)(2,1)} %get-tuple-element.166), channel_id=1, source_target_pairs={{0,2},{2,0},{1,3},{3,1},{4,6},{6,4},{5,7},{7,5},{8,10},{10,8},{9,1... | collective-permute-start | bytes 2359304 | tf_op jit(solution)/shard_map/ppermute | solution.py:778
  328.8 9.5 %collective-permute-start.38 = (bf16[96,1152]{1,0:T(8,128)(2,1)S(1)}, bf16[96,1152]{1,0:T(8,128)(2,1)S(1)}, u32[]{:S(2)}, u32[]{:S(2)}) collective-permute-start(bf16[96,1152]{1,0:T(8,128)(2,1)S(1)} %get-tuple-element.191), channel_id=1, source_target_pairs={{0,8},{4,12},{8,0},{12,4},{16,24},{20,28},{24,16},{28,20},{1,9},{5... | collective-permute-start | bytes 663560 | tf_op jit(solution)/shard_map/ppermute | solution.py:804
  330.4 20.2 %collective-permute-start.41 = (bf16[432,768]{1,0:T(8,128)(2,1)}, bf16[432,768]{1,0:T(8,128)(2,1)S(1)}, u32[]{:S(2)}, u32[]{:S(2)}) collective-permute-start(bf16[432,768]{1,0:T(8,128)(2,1)} %constant_dynamic-update-slice_fusion), channel_id=1, source_target_pairs={{0,8},{4,12},{8,0},{12,4},{16,24},{20,28},{24,16},{28,20},{1,9},{5... | collective-permute-start | bytes 1990664 | tf_op jit(solution)/shard_map/ppermute | solution.py:804
  338.4 10.7 %collective-permute-start.39 = (bf16[48,1152]{1,0:T(8,128)(2,1)S(1)}, bf16[48,1152]{1,0:T(8,128)(2,1)S(1)}, u32[]{:S(2)}, u32[]{:S(2)}) collective-permute-start(bf16[48,1152]{1,0:T(8,128)(2,1)S(1)} %add_convert_fusion.13), channel_id=1, source_target_pairs={{0,16},{4,20},{8,24},{12,28},{16,0},{20,4},{24,8},{28,12},{1,17},{... | collective-permute-start | bytes 331784 | tf_op jit(solution)/shard_map/ppermute | solution.py:804
  339.6 24.2 %collective-permute-start.47 = (bf16[432,768]{1,0:T(8,128)(2,1)}, bf16[432,768]{1,0:T(8,128)(2,1)S(1)}, u32[]{:S(2)}, u32[]{:S(2)}) collective-permute-start(bf16[432,768]{1,0:T(8,128)(2,1)} %constant_dynamic-update-slice_fusion), channel_id=1, source_target_pairs={{0,4},{4,0},{8,12},{12,8},{16,20},{20,16},{24,28},{28,24},{1,5},{5... | collective-permute-start | bytes 1990664 | tf_op jit(solution)/shard_map/ppermute | solution.py:847
  350.6 6.3 %collective-permute-start.42 = (bf16[48,1152]{1,0:T(8,128)(2,1)S(1)}, bf16[48,1152]{1,0:T(8,128)(2,1)S(1)}, u32[]{:S(2)}, u32[]{:S(2)}) collective-permute-start(bf16[48,1152]{1,0:T(8,128)(2,1)S(1)} %add_convert_fusion.12), channel_id=1, source_target_pairs={{0,16},{4,20},{8,24},{12,28},{16,0},{20,4},{24,8},{28,12},{1,17},{... | collective-permute-start | bytes 331784 | tf_op jit(solution)/shard_map/ppermute | solution.py:804
  352.6 17.8 %collective-permute-start.46 = (bf16[432,768]{1,0:T(8,128)(2,1)S(1)}, bf16[432,768]{1,0:T(8,128)(2,1)S(1)}, u32[]{:S(2)}, u32[]{:S(2)}) collective-permute-start(bf16[432,768]{1,0:T(8,128)(2,1)S(1)} %collective-permute-done.41), channel_id=1, source_target_pairs={{0,4},{4,0},{8,12},{12,8},{16,20},{20,16},{24,28},{28,24},{1,5},{5... | collective-permute-start | bytes 1990664 | tf_op jit(solution)/shard_map/ppermute | solution.py:847
  357.0 6.3 %collective-permute-start.43 = (bf16[96,1152]{1,0:T(8,128)(2,1)S(1)}, bf16[96,1152]{1,0:T(8,128)(2,1)S(1)}, u32[]{:S(2)}, u32[]{:S(2)}) collective-permute-start(bf16[96,1152]{1,0:T(8,128)(2,1)S(1)} %pad_maximum_fusion.17), channel_id=1, source_target_pairs={{0,8},{4,12},{8,0},{12,4},{16,24},{20,28},{24,16},{28,20},{1,9},{5... | collective-permute-start | bytes 663560 | tf_op jit(solution)/shard_map/ppermute | solution.py:804
  363.5 13.3 %collective-permute-start.45 = (bf16[192,1152]{1,0:T(8,128)(2,1)S(1)}, bf16[192,1152]{1,0:T(8,128)(2,1)S(1)}, u32[]{:S(2)}, u32[]{:S(2)}) collective-permute-start(bf16[192,1152]{1,0:T(8,128)(2,1)S(1)} %pad_maximum_fusion.12), channel_id=1, source_target_pairs={{0,4},{4,0},{8,12},{12,8},{16,20},{20,16},{24,28},{28,24},{1,5},{5... | collective-permute-start | bytes 1327112 | tf_op jit(solution)/shard_map/ppermute | solution.py:847
  (31 other events, 207.4 us)

commit v6 on v2

--- a/solution.py
+++ b/solution.py
@@ -972,7 +972,7 @@
     gt = jnp.where(jnp.arange(2)[:, None, None, None] == c, gt[None], 0.0).reshape(4, 9, part)
     gains = jnp.concatenate([gg1, gg2], axis=0).reshape(2, 4, part).transpose(1, 0, 2)
     small = jnp.concatenate([gt, gains, jnp.zeros((4, 5, part), f32)], axis=1)
-    small = after(small, first_cat)
+    small = after(small, near_got)
     small = jnp.broadcast_to(small[:, None], (4, dp, 16, part)).reshape(4 * dp, 16, part)
     small = jnp.sum(lax.all_to_all(small, ("head", "dp"), 0, 0, tiled=True), axis=0)
     output = order(after(out_own, g_send), out_x)

time: 371 us -> 381 us (1.027)
  starting transfers between devices: 39.4 us -> 45.2 us
  waiting for transfers between devices: 97.7 us -> 102 us
    ppermute x11, waiting for transfers between devices: 28.2 us -> 33.8 us  [swap(): return lax.ppermute(v, 'dp', flip(dp, stride))]
  transfers between devices with their start and end apart: 49 -> 49, of which waited for: 19 -> 17; matrix products, arithmetic and copies ran while one was open for 12% -> 11% of each run, Pallas kernels for 35% -> 34%
where the time goes in v6:
time: 381 us; the launch traced here: 380 us
  Pallas kernels  177 us (46%)
  waiting for transfers between devices  102 us (27%)
  starting transfers between devices  45.2 us (12%)
  other arithmetic  36.4 us (10%)
  local copies, waits for them, and re-layouts  17.9 us (5%)
    pallas_call x2, Pallas kernels, att_bwd_call(): pl.pallas_call(functools.partial(att_bwd_body, p0, into is not None), out...  66.2 us
    pallas_call x1, Pallas kernels, ffn_call(): pl.pallas_call(ffn_body, out_shape=[sds((2, rows, width), f32), sds((rows...  49.3 us
    ppermute x11, waiting for transfers between devices, x_swap(): return lax.ppermute(v, 'head', XNB)  47.1 us
    ppermute x11, waiting for transfers between devices, swap(): return lax.ppermute(v, 'dp', flip(dp, stride))  33.8 us
    pallas_call x1, Pallas kernels, att_fwd_call(): pl.pallas_call(att_fwd_body, out_shape=[sds((length // 2, width), bf16),...  27.3 us
    ppermute x11, starting transfers between devices, swap(): return lax.ppermute(v, 'dp', flip(dp, stride))  14 us
    pallas_call x1, Pallas kernels, qkv_call(): pl.pallas_call(qkv_body, out_shape=[sds((length, width), bf16), sds((leng...  13.5 us
    ppermute x11, starting transfers between devices, x_swap(): return lax.ppermute(v, 'head', XNB)  13.1 us
  transfers between devices with their start and end apart: 49, of which 17 were waited for; matrix products, arithmetic and copies ran while one was open for 11% of the time, Pallas kernels for 34%

profile of v6, /device:TPU:0, one launch (start us, length us, event | category | flops | bytes accessed | tf_op | source)
XLA Modules:
  0.0 380.2 jit_solution(16128335361553587072)
XLA Ops:
  4.4 1.5 collective-permute-done.3.wb
  6.9 3.2 collective-permute-start.4
  13.0 2.5 dynamic-slice_bitcast_fusion.1
  16.7 2.2 pad_maximum_fusion.1
  18.9 29.4 %collective-permute-done.x1.xx = bf16[512,768]{1,0:T(8,128)(2,1)} collective-permute-done((bf16[512,768]{1,0:T(8,128)(2,1)}, bf16[512,768]{1,0:T(8,128)(2,1)}, u32[]{:S(2)}, u32[]{:S(2)}) %collective-permute-start) | collective-permute-done | bytes 786464 | tf_op jit(solution)/shard_map/ppermute | solution.py:778
  49.4 1.7 collective-permute-start.5
  51.2 2.6 collective-permute-done.6.x3
  54.7 13.5 %qkv.1 = (bf16[2048,768]{1,0:T(8,128)(2,1)}, bf16[2048,1152]{1,0:T(8,128)(2,1)}, bf16[2048,1152]{1,0:T(8,128)(2,1)}, bf16[768,1152]{1,0:T(8,128)(2,1)}, f32[8,1152]{1,0:T(8,128)}) custom-call(s32[4]{0:T(128)} %pad_add_fusion.meta, bf16[512,768]{1,0:T(8,128)(2,1)} %copy-done, bf16[512,768]{1,0:T(8,128)(2,1)} %collective-permute-done.x1.xx, ...), custom_call_target="tpu_custom_call" | custom-call | flops 3623878656 | bytes 15728640 | tf_op jit(solution)/shard_map/qkv/pallas_call | solution.py:131
  68.6 1.7 collective-permute-start.10
  70.3 1.5 collective-permute-start.7
  71.8 1.6 collective-permute-start.8
  73.8 27.3 %attn_fwd.1 = (bf16[1024,384]{1,0:T(8,128)(2,1)}, bf16[1024,384]{1,0:T(8,128)(2,1)}, f32[3,2,2048]{2,1,0:T(2,128)}) custom-call(s32[4]{0:T(128)} %pad_add_fusion.meta, bf16[2048,1152]{1,0:T(8,128)(2,1)} %get-tuple-element.129.q_ref.k_ref.v_ref, bf16[2048,1152]{1,0:T(8,128)(2,1)} %get-tuple-element.129.q_ref.k_ref.v_ref, ...), custom_call_target="tpu_custom_call" | custom-call | flops 12884901888 | bytes 6291456 | tf_op jit(solution)/shard_map/attn_fwd/pallas_call | solution.py:255
  102.9 2.4 collective-permute-done.14.c0
  105.4 1.7 collective-permute-done.16.c2
  109.6 49.3 %ffn.1 = (f32[2,512,768]{2,1,0:T(8,128)}, bf16[512,768]{1,0:T(8,128)(2,1)}, bf16[1024,384]{1,0:T(8,128)(2,1)}, bf16[1024,384]{1,0:T(8,128)(2,1)}, f32[1,768]{1,0...) custom-call(s32[4]{0:T(128)} %pad_add_fusion.meta, ...), custom_call_target="tpu_custom_call" | custom-call | flops 32614907904 | bytes 31457280 | tf_op jit(solution)/shard_map/ffn/pallas_call | solution.py:623
  160.1 1.9 collective-permute-done.19
  163.0 3.1 add_convert_fusion
  166.2 1.9 collective-permute-start.25
  169.2 1.5 collective-permute-start.22
  170.8 2.6 add_convert_fusion.2
  173.8 42.7 %attn_bwd.2 = (bf16[1024,1152]{1,0:T(8,128)(2,1)}, bf16[1024,1152]{1,0:T(8,128)(2,1)}, f32[16,256]{1,0:T(8,128)}) custom-call(s32[4]{0:T(128)} %pad_add_fusion.meta, bf16[2048,1152]{1,0:T(8,128)(2,1)} %get-tuple-element.129.q_ref.k_ref.v_ref, bf16[2048,1152]{1,0:T(8,128)(2,1)} %get-tuple-element.129.q_ref.k_ref.v_ref, ...), custom_call_target="tpu_custom_call" | custom-call | flops 15032385536 | bytes 10485760 | tf_op jit(solution)/shard_map/attn_bwd/pallas_call | solution.py:407
  216.6 2.6 add_convert_fusion.1
  219.5 2.9 convert_add_fusion.1
  222.3 1.8 collective-permute-start.27
  224.1 23.5 %attn_bwd.3 = (bf16[1024,1152]{1,0:T(8,128)(2,1)}, bf16[1024,1152]{1,0:T(8,128)(2,1)}, f32[16,128]{1,0:T(8,128)}) custom-call(s32[4]{0:T(128)} %pad_add_fusion.meta, bf16[2048,1152]{1,0:T(8,128)(2,1)} %get-tuple-element.129.q_ref.k_ref.v_ref, ...), custom_call_target="tpu_custom_call", output_to_operand_aliasing={{0}: (13, {}), {1}: (14, {})} | custom-call | flops 7516192768 | bytes 5242880 | tf_op jit(solution)/shard_map/attn_bwd/pallas_call | solution.py:407
  249.8 1.5 convert_add_fusion.4
  251.4 1.6 collective-permute-start.29
  253.0 9.6 %projg.1 = (bf16[192,1152]{1,0:T(8,128)(2,1)}, bf16[192,1152]{1,0:T(8,128)(2,1)}, bf16[384,1152]{1,0:T(8,128)(2,1)}) custom-call(s32[4]{0:T(128)} %pad_add_fusion.meta, bf16[2048,768]{1,0:T(8,128)(2,1)} %get-tuple-element.136.h, bf16[1024,1152]{1,0:T(8,128)(2,1)} %get-tuple-element.137.dm, bf16[1024,1152]{1,0:T(8,128)(2,1)} %get-tuple-element.138.dt), custom_call_target="tpu_custom_call" | custom-call | flops 2048 | bytes 2048 | tf_op jit(solution)/shard_map/projg/pallas_call | solution.py:692
  262.6 6.1 %collective-permute-done.29 = bf16[432,768]{1,0:T(8,128)(2,1)S(1)} collective-permute-done((bf16[432,768]{1,0:T(8,128)(2,1)S(1)}, bf16[432,768]{1,0:T(8,128)(2,1)S(1)}, u32[]{:S(2)}, u32[]{:S(2)}) %collective-permute-start.29) | collective-permute-done | bytes 663584 | tf_op jit(solution)/shard_map/ppermute | solution.py:804
  269.0 2.7 collective-permute-start.33
  271.7 11.4 %last.1 = (f32[2,512,768]{2,1,0:T(8,128)}, bf16[512,768]{1,0:T(8,128)(2,1)}, f32[1,768]{1,0:T(1,128)}) custom-call(s32[4]{0:T(128)} %pad_add_fusion.meta, bf16[512,768]{1,0:T(8,128)(2,1)} %copy-done, bf16[512,768]{1,0:T(8,128)(2,1)} %collective-permute-done.x1.xx, bf16[1024,1152]{1,0:T(8,128)(2,1)} %get-tuple-element.137.dm, ...), custom_call_target="tpu_custom_call" | custom-call | flops 512 | bytes 512 | tf_op jit(solution)/shard_map/last/pallas_call | solution.py:750
  284.5 1.5 collective-permute-start.36
  288.1 1.5 collective-permute-start.32
  290.1 9.3 %collective-permute-done.31 = bf16[192,1152]{1,0:T(8,128)(2,1)S(1)} collective-permute-done((bf16[192,1152]{1,0:T(8,128)(2,1)}, bf16[192,1152]{1,0:T(8,128)(2,1)S(1)}, u32[]{:S(2)}, u32[]{:S(2)}) %collective-permute-start.31) | collective-permute-done | bytes 442400 | tf_op jit(solution)/shard_map/ppermute | solution.py:778
  299.4 8.4 %collective-permute-done.32 = bf16[192,1152]{1,0:T(8,128)(2,1)S(1)} collective-permute-done((bf16[192,1152]{1,0:T(8,128)(2,1)}, bf16[192,1152]{1,0:T(8,128)(2,1)S(1)}, u32[]{:S(2)}, u32[]{:S(2)}) %collective-permute-start.32) | collective-permute-done | bytes 442400 | tf_op jit(solution)/shard_map/ppermute | solution.py:778
  308.8 1.7 collective-permute-start.41
  310.4 8.8 %collective-permute-done.37 = bf16[192,1152]{1,0:T(8,128)(2,1)S(1)} collective-permute-done((bf16[192,1152]{1,0:T(8,128)(2,1)S(1)}, bf16[192,1152]{1,0:T(8,128)(2,1)S(1)}, u32[]{:S(2)}, u32[]{:S(2)}) %collective-permute-start.37) | collective-permute-done | bytes 442400 | tf_op jit(solution)/shard_map/ppermute | solution.py:847
  319.3 1.6 collective-permute-start.38
  322.1 7.0 %collective-permute-done.38 = bf16[96,1152]{1,0:T(8,128)(2,1)S(1)} collective-permute-done((bf16[96,1152]{1,0:T(8,128)(2,1)S(1)}, bf16[96,1152]{1,0:T(8,128)(2,1)S(1)}, u32[]{:S(2)}, u32[]{:S(2)}) %collective-permute-start.38) | collective-permute-done | bytes 221216 | tf_op jit(solution)/shard_map/ppermute | solution.py:804
  332.8 5.6 %all-to-all-start = ((f32[32,16,192]{2,1,0:T(8,128)}), f32[32,16,192]{2,1,0:T(8,128)S(1)}, u32[]{:S(2)}, u32[]{:S(2)}) async-start(f32[32,16,192]{2,1,0:T(8,128)} %bitcast.16), calls=%async_computation | async-start | bytes 1048576 | tf_op jit(solution)/shard_map/all_to_all | solution.py:977
  338.4 1.8 collective-permute-start.46
  340.3 2.4 collective-permute-start.42
  343.8 14.3 %collective-permute-done.42 = bf16[48,1152]{1,0:T(8,128)(2,1)S(1)} collective-permute-done((bf16[48,1152]{1,0:T(8,128)(2,1)S(1)}, bf16[48,1152]{1,0:T(8,128)(2,1)S(1)}, u32[]{:S(2)}, u32[]{:S(2)}) %collective-permute-start.42) | collective-permute-done | bytes 110624 | tf_op jit(solution)/shard_map/ppermute | solution.py:804
  359.5 5.7 %collective-permute-done.43 = bf16[96,1152]{1,0:T(8,128)(2,1)S(1)} collective-permute-done((bf16[96,1152]{1,0:T(8,128)(2,1)S(1)}, bf16[96,1152]{1,0:T(8,128)(2,1)S(1)}, u32[]{:S(2)}, u32[]{:S(2)}) %collective-permute-start.43) | collective-permute-done | bytes 221216 | tf_op jit(solution)/shard_map/ppermute | solution.py:804
  365.3 1.5 collective-permute-start.45
  367.0 1.4 broadcast_select_fusion.9
  370.0 1.6 fusion
  372.4 1.6 maximum_convert_fusion
  (208 shorter events, 43.4 us)
Async XLA Ops:
  3.9 2.0 collective-permute-start.3
  4.3 12.3 %collective-permute-start.1 = (bf16[192,768]{1,0:T(8,128)(2,1)}, bf16[192,768]{1,0:T(8,128)(2,1)}, u32[]{:S(2)}, u32[]{:S(2)}) collective-permute-start(bf16[192,768]{1,0:T(8,128)(2,1)} %wo_o.1), channel_id=1, source_target_pairs={{0,1},{1,0},{2,3},{3,2},{4,5},{5,4},{6,7},{7,6},{8,9},{9,8},{10,11... | collective-permute-start | bytes 884744 | tf_op jit(solution)/shard_map/ppermute | solution.py:774
  6.9 41.4 %collective-permute-start.4 = (bf16[608,768]{1,0:T(8,128)(2,1)}, bf16[608,768]{1,0:T(8,128)(2,1)}, u32[]{:S(2)}, u32[]{:S(2)}) collective-permute-start(bf16[608,768]{1,0:T(8,128)(2,1)} %pad_maximum_fusion.3), channel_id=1, source_target_pairs={{0,2},{2,0},{1,3},{3,1},{4,6},{6,4},{5,7},{7,5},{8,10},{10,8},{9,1... | collective-permute-start | bytes 2801672 | tf_op jit(solution)/shard_map/ppermute | solution.py:778
  11.1 37.2 %collective-permute-start = (bf16[512,768]{1,0:T(8,128)(2,1)}, bf16[512,768]{1,0:T(8,128)(2,1)}, u32[]{:S(2)}, u32[]{:S(2)}) collective-permute-start(bf16[512,768]{1,0:T(8,128)(2,1)} %get-tuple-element.178), channel_id=1, source_target_pairs={{0,2},{2,0},{1,3},{3,1},{4,6},{6,4},{5,7},{7,5},{8,10},{10,8},{9,1... | collective-permute-start | bytes 2359304 | tf_op jit(solution)/shard_map/ppermute | solution.py:778
  11.1 37.2 %collective-permute-start.2 = (bf16[512,768]{1,0:T(8,128)(2,1)S(1)}, bf16[512,768]{1,0:T(8,128)(2,1)}, u32[]{:S(2)}, u32[]{:S(2)}) collective-permute-start(bf16[512,768]{1,0:T(8,128)(2,1)S(1)} %get-tuple-element.177.x0.xo), channel_id=1, source_target_pairs={{0,1},{1,0},{2,3},{3,2},{4,5},{5,4},{6,7},{7,6},{8,9},{9,8},{10,11... | collective-permute-start | bytes 2359304 | tf_op jit(solution)/shard_map/ppermute | solution.py:774
  48.3 25.1 %collective-permute-start.11 = (bf16[2,768,768]{2,1,0:T(8,128)(2,1)S(1)}, bf16[2,768,768]{2,1,0:T(8,128)(2,1)}, u32[]{:S(2)}, u32[]{:S(2)}) collective-permute-start(bf16[2,768,768]{2,1,0:T(8,128)(2,1)S(1)} %pad_maximum_fusion), channel_id=1, source_target_pairs={{0,1},{1,0},{2,3},{3,2},{4,5},{5,4},{6,7},{7,6},{8,9},{9,8},{10,11... | collective-permute-start | bytes 7077896 | tf_op jit(solution)/shard_map/ppermute | solution.py:774
  48.3 5.5 %collective-permute-start.6 = (bf16[512,768]{1,0:T(8,128)(2,1)}, bf16[512,768]{1,0:T(8,128)(2,1)S(1)}, u32[]{:S(2)}, u32[]{:S(2)}) collective-permute-start(bf16[512,768]{1,0:T(8,128)(2,1)} %collective-permute-done.x1.xx), channel_id=1, source_target_pairs={{0,1},{1,0},{2,3},{3,2},{4,5},{5,4},{6,7},{7,6},{8,9},{9,8},{10,11... | collective-permute-start | bytes 2359304 | tf_op jit(solution)/shard_map/ppermute | solution.py:774
  49.4 20.9 %collective-permute-start.5 = (bf16[2,192,768]{2,1,0:T(8,128)(2,1)}, bf16[2,192,768]{2,1,0:T(8,128)(2,1)}, u32[]{:S(2)}, u32[]{:S(2)}) collective-permute-start(bf16[2,192,768]{2,1,0:T(8,128)(2,1)} %pad_maximum_fusion.10), channel_id=1, source_target_pairs={{0,2},{2,0},{1,3},{3,1},{4,6},{6,4},{5,7},{7,5},{8,10},{10,8},{9,1... | collective-permute-start | bytes 1769480 | tf_op jit(solution)/shard_map/ppermute | solution.py:778
  68.2 34.1 %collective-permute-start.13 = (bf16[768,1152]{1,0:T(8,128)(2,1)}, bf16[768,1152]{1,0:T(8,128)(2,1)}, u32[]{:S(2)}, u32[]{:S(2)}) collective-permute-start(bf16[768,1152]{1,0:T(8,128)(2,1)} %get-tuple-element.103.wm), channel_id=1, source_target_pairs={{0,1},{1,0},{2,3},{3,2},{4,5},{5,4},{6,7},{7,6},{8,9},{9,8},{10,11... | collective-permute-start | bytes 5308424 | tf_op jit(solution)/shard_map/ppermute | solution.py:774
  68.6 33.1 %collective-permute-start.10 = (bf16[896,768]{1,0:T(8,128)(2,1)}, bf16[896,768]{1,0:T(8,128)(2,1)}, u32[]{:S(2)}, u32[]{:S(2)}) collective-permute-start(bf16[896,768]{1,0:T(8,128)(2,1)} %pad_maximum_fusion.1), channel_id=1, source_target_pairs={{0,2},{2,0},{1,3},{3,1},{4,6},{6,4},{5,7},{7,5},{8,10},{10,8},{9,1... | collective-permute-start | bytes 4128776 | tf_op jit(solution)/shard_map/ppermute | solution.py:778
  70.3 30.8 %collective-permute-start.7 = (bf16[2,192,768]{2,1,0:T(8,128)(2,1)}, bf16[2,192,768]{2,1,0:T(8,128)(2,1)S(1)}, u32[]{:S(2)}, u32[]{:S(2)}) collective-permute-start(bf16[2,192,768]{2,1,0:T(8,128)(2,1)} %collective-permute-done.5.n0), channel_id=1, source_target_pairs={{0,4},{4,0},{8,12},{12,8},{16,20},{20,16},{24,28},{28,24},{1,5},{5... | collective-permute-start | bytes 1769480 | tf_op jit(solution)/shard_map/ppermute | solution.py:804
  71.8 29.4 %collective-permute-start.8 = (bf16[2,192,768]{2,1,0:T(8,128)(2,1)}, bf16[2,192,768]{2,1,0:T(8,128)(2,1)}, u32[]{:S(2)}, u32[]{:S(2)}) collective-permute-start(bf16[2,192,768]{2,1,0:T(8,128)(2,1)} %collective-permute-done.5.n0), channel_id=1, source_target_pairs={{0,8},{4,12},{8,0},{12,4},{16,24},{20,28},{24,16},{28,20},{1,9},{5... | collective-permute-start | bytes 1769480 | tf_op jit(solution)/shard_map/ppermute | solution.py:804
  73.4 28.3 %collective-permute-start.9 = (bf16[2,192,768]{2,1,0:T(8,128)(2,1)}, bf16[2,192,768]{2,1,0:T(8,128)(2,1)S(1)}, u32[]{:S(2)}, u32[]{:S(2)}) collective-permute-start(bf16[2,192,768]{2,1,0:T(8,128)(2,1)} %collective-permute-done.5.n0), channel_id=1, source_target_pairs={{0,12},{4,8},{8,4},{12,0},{16,28},{20,24},{24,20},{28,16},{1,13},{... | collective-permute-start | bytes 1769480 | tf_op jit(solution)/shard_map/ppermute | solution.py:804
  101.1 7.6 %collective-permute-start.12 = (bf16[1024,384]{1,0:T(8,128)(2,1)}, bf16[1024,384]{1,0:T(8,128)(2,1)S(1)}, u32[]{:S(2)}, u32[]{:S(2)}) collective-permute-start(bf16[1024,384]{1,0:T(8,128)(2,1)} %get-tuple-element.102.ot), channel_id=1, source_target_pairs={{0,1},{1,0},{2,3},{3,2},{4,5},{5,4},{6,7},{7,6},{8,9},{9,8},{10,11... | collective-permute-start | bytes 2359304 | tf_op jit(solution)/shard_map/ppermute | solution.py:774
  101.2 4.2 %collective-permute-start.14 = (bf16[2,192,768]{2,1,0:T(8,128)(2,1)}, bf16[2,192,768]{2,1,0:T(8,128)(2,1)S(1)}, u32[]{:S(2)}, u32[]{:S(2)}) collective-permute-start(bf16[2,192,768]{2,1,0:T(8,128)(2,1)} %collective-permute-done.5.n0), channel_id=1, source_target_pairs={{0,1},{1,0},{2,3},{3,2},{4,5},{5,4},{6,7},{7,6},{8,9},{9,8},{10,11... | collective-permute-start | bytes 1769480 | tf_op jit(solution)/shard_map/ppermute | solution.py:774
  101.7 3.7 collective-permute-start.15
  101.8 5.2 %collective-permute-start.16 = (bf16[2,192,768]{2,1,0:T(8,128)(2,1)}, bf16[2,192,768]{2,1,0:T(8,128)(2,1)S(1)}, u32[]{:S(2)}, u32[]{:S(2)}) collective-permute-start(bf16[2,192,768]{2,1,0:T(8,128)(2,1)} %collective-permute-done.8.n2), channel_id=1, source_target_pairs={{0,1},{1,0},{2,3},{3,2},{4,5},{5,4},{6,7},{7,6},{8,9},{9,8},{10,11... | collective-permute-start | bytes 1769480 | tf_op jit(solution)/shard_map/ppermute | solution.py:774
  102.3 4.8 %collective-permute-start.17 = (bf16[2,192,768]{2,1,0:T(8,128)(2,1)S(1)}, bf16[2,192,768]{2,1,0:T(8,128)(2,1)S(1)}, u32[]{:S(2)}, u32[]{:S(2)}) collective-permute-start(bf16[2,192,768]{2,1,0:T(8,128)(2,1)S(1)} %collective-permute-done.9.n3), channel_id=1, source_target_pairs={{0,1},{1,0},{2,3},{3,2},{4,5},{5,4},{6,7},{7,6},{8,9},{9,8},{10,11... | collective-permute-start | bytes 1769480 | tf_op jit(solution)/shard_map/ppermute | solution.py:774
  158.9 3.1 collective-permute-start.19
  159.1 7.1 %collective-permute-start.21 = (bf16[960,768]{1,0:T(8,128)(2,1)}, bf16[960,768]{1,0:T(8,128)(2,1)S(1)}, u32[]{:S(2)}, u32[]{:S(2)}) collective-permute-start(bf16[960,768]{1,0:T(8,128)(2,1)} %get-tuple-element.115), channel_id=1, source_target_pairs={{0,1},{1,0},{2,3},{3,2},{4,5},{5,4},{6,7},{7,6},{8,9},{9,8},{10,11... | collective-permute-start | bytes 4423688 | tf_op jit(solution)/shard_map/ppermute | solution.py:774
  159.5 9.8 %collective-permute-start.23 = (bf16[960,768]{1,0:T(8,128)(2,1)}, bf16[960,768]{1,0:T(8,128)(2,1)}, u32[]{:S(2)}, u32[]{:S(2)}) collective-permute-start(bf16[960,768]{1,0:T(8,128)(2,1)} %get-tuple-element.117), channel_id=1, source_target_pairs={{0,1},{1,0},{2,3},{3,2},{4,5},{5,4},{6,7},{7,6},{8,9},{9,8},{10,11... | collective-permute-start | bytes 4423688 | tf_op jit(solution)/shard_map/ppermute | solution.py:774
  159.6 13.7 %collective-permute-start.26 = (bf16[1024,384]{1,0:T(8,128)(2,1)}, bf16[1024,384]{1,0:T(8,128)(2,1)}, u32[]{:S(2)}, u32[]{:S(2)}) collective-permute-start(bf16[1024,384]{1,0:T(8,128)(2,1)} %get-tuple-element.122), channel_id=1, source_target_pairs={{0,1},{1,0},{2,3},{3,2},{4,5},{5,4},{6,7},{7,6},{8,9},{9,8},{10,11... | collective-permute-start | bytes 2359304 | tf_op jit(solution)/shard_map/ppermute | solution.py:774
  160.0 59.5 %collective-permute-start.18 = (bf16[768,768]{1,0:T(8,128)(2,1)}, bf16[768,768]{1,0:T(8,128)(2,1)}, u32[]{:S(2)}, u32[]{:S(2)}) collective-permute-start(bf16[768,768]{1,0:T(8,128)(2,1)} %get-tuple-element.111), channel_id=1, source_target_pairs={{0,1},{1,0},{2,3},{3,2},{4,5},{5,4},{6,7},{7,6},{8,9},{9,8},{10,11... | collective-permute-start | bytes 3538952 | tf_op jit(solution)/shard_map/ppermute | solution.py:774
  166.1 50.4 %collective-permute-start.20 = (bf16[768,768]{1,0:T(8,128)(2,1)}, bf16[768,768]{1,0:T(8,128)(2,1)}, u32[]{:S(2)}, u32[]{:S(2)}) collective-permute-start(bf16[768,768]{1,0:T(8,128)(2,1)} %add_convert_fusion), channel_id=1, source_target_pairs={{0,2},{2,0},{1,3},{3,1},{4,6},{6,4},{5,7},{7,5},{8,10},{10,8},{9,1... | collective-permute-start | bytes 3538952 | tf_op jit(solution)/shard_map/ppermute | solution.py:778
  166.2 50.3 %collective-permute-start.25 = (bf16[512,768]{1,0:T(8,128)(2,1)}, bf16[512,768]{1,0:T(8,128)(2,1)}, u32[]{:S(2)}, u32[]{:S(2)}) collective-permute-start(bf16[512,768]{1,0:T(8,128)(2,1)} %get-tuple-element.119), channel_id=1, source_target_pairs={{0,2},{2,0},{1,3},{3,1},{4,6},{6,4},{5,7},{7,5},{8,10},{10,8},{9,1... | collective-permute-start | bytes 2359304 | tf_op jit(solution)/shard_map/ppermute | solution.py:778
  169.2 47.3 %collective-permute-start.22 = (bf16[480,768]{1,0:T(8,128)(2,1)}, bf16[480,768]{1,0:T(8,128)(2,1)}, u32[]{:S(2)}, u32[]{:S(2)}) collective-permute-start(bf16[480,768]{1,0:T(8,128)(2,1)} %add_convert_fusion.3), channel_id=1, source_target_pairs={{0,4},{4,0},{8,12},{12,8},{16,20},{20,16},{24,28},{28,24},{1,5},{5... | collective-permute-start | bytes 2211848 | tf_op jit(solution)/shard_map/ppermute | solution.py:847
  173.3 43.2 %collective-permute-start.24 = (bf16[480,768]{1,0:T(8,128)(2,1)}, bf16[480,768]{1,0:T(8,128)(2,1)}, u32[]{:S(2)}, u32[]{:S(2)}) collective-permute-start(bf16[480,768]{1,0:T(8,128)(2,1)} %get-tuple-element.171), channel_id=1, source_target_pairs={{0,4},{4,0},{8,12},{12,8},{16,20},{20,16},{24,28},{28,24},{1,5},{5... | collective-permute-start | bytes 2211848 | tf_op jit(solution)/shard_map/ppermute | solution.py:847
  219.2 28.7 %collective-permute-start.28 = (bf16[480,768]{1,0:T(8,128)(2,1)}, bf16[480,768]{1,0:T(8,128)(2,1)}, u32[]{:S(2)}, u32[]{:S(2)}) collective-permute-start(bf16[480,768]{1,0:T(8,128)(2,1)} %add_convert_fusion.1), channel_id=1, source_target_pairs={{0,2},{2,0},{1,3},{3,1},{4,6},{6,4},{5,7},{7,5},{8,10},{10,8},{9,1... | collective-permute-start | bytes 2211848 | tf_op jit(solution)/shard_map/ppermute | solution.py:778
  222.3 25.5 %collective-permute-start.27 = (bf16[384,768]{1,0:T(8,128)(2,1)}, bf16[384,768]{1,0:T(8,128)(2,1)S(1)}, u32[]{:S(2)}, u32[]{:S(2)}) collective-permute-start(bf16[384,768]{1,0:T(8,128)(2,1)} %get-tuple-element.168), channel_id=1, source_target_pairs={{0,4},{4,0},{8,12},{12,8},{16,20},{20,16},{24,28},{28,24},{1,5},{5... | collective-permute-start | bytes 1769480 | tf_op jit(solution)/shard_map/ppermute | solution.py:847
  247.7 24.0 %collective-permute-start.34 = (bf16[1024,1152]{1,0:T(8,128)(2,1)}, bf16[1024,1152]{1,0:T(8,128)(2,1)}, u32[]{:S(2)}, u32[]{:S(2)}) collective-permute-start(bf16[1024,1152]{1,0:T(8,128)(2,1)} %get-tuple-element.138.dt), channel_id=1, source_target_pairs={{0,1},{1,0},{2,3},{3,2},{4,5},{5,4},{6,7},{7,6},{8,9},{9,8},{10,11... | collective-permute-start | bytes 7077896 | tf_op jit(solution)/shard_map/ppermute | solution.py:774
  251.4 17.3 %collective-permute-start.29 = (bf16[432,768]{1,0:T(8,128)(2,1)S(1)}, bf16[432,768]{1,0:T(8,128)(2,1)S(1)}, u32[]{:S(2)}, u32[]{:S(2)}) collective-permute-start(bf16[432,768]{1,0:T(8,128)(2,1)S(1)} %pad_maximum_fusion.6), channel_id=1, source_target_pairs={{0,8},{4,12},{8,0},{12,4},{16,24},{20,28},{24,16},{28,20},{1,9},{5... | collective-permute-start | bytes 1990664 | tf_op jit(solution)/shard_map/ppermute | solution.py:804
  269.0 18.4 %collective-permute-start.30 = (bf16[384,1152]{1,0:T(8,128)(2,1)}, bf16[384,1152]{1,0:T(8,128)(2,1)S(1)}, u32[]{:S(2)}, u32[]{:S(2)}) collective-permute-start(bf16[384,1152]{1,0:T(8,128)(2,1)} %get-tuple-element.145), channel_id=1, source_target_pairs={{0,1},{1,0},{2,3},{3,2},{4,5},{5,4},{6,7},{7,6},{8,9},{9,8},{10,11... | collective-permute-start | bytes 2654216 | tf_op jit(solution)/shard_map/ppermute | solution.py:774
  269.0 18.2 %collective-permute-start.33 = (bf16[216,768]{1,0:T(8,128)(2,1)S(1)}, bf16[216,768]{1,0:T(8,128)(2,1)S(1)}, u32[]{:S(2)}, u32[]{:S(2)}) collective-permute-start(bf16[216,768]{1,0:T(8,128)(2,1)S(1)} %pad_maximum_fusion.15), channel_id=1, source_target_pairs={{0,16},{4,20},{8,24},{12,28},{16,0},{20,4},{24,8},{28,12},{1,17},{... | collective-permute-start | bytes 995336 | tf_op jit(solution)/shard_map/ppermute | solution.py:804
  284.5 5.1 %collective-permute-start.36 = (f32[1,768]{1,0:T(1,128)S(1)}, f32[1,768]{1,0:T(1,128)S(1)}, u32[]{:S(2)}, u32[]{:S(2)}) collective-permute-start(f32[1,768]{1,0:T(1,128)S(1)} %collective-permute-done.35), channel_id=1, source_target_pairs={{0,2},{2,0},{1,3},{3,1},{4,6},{6,4},{5,7},{7,5},{8,10},{10,8},{9,1... | collective-permute-start | bytes 9224 | tf_op jit(solution)/shard_map/ppermute | solution.py:778
  286.1 13.3 %collective-permute-start.31 = (bf16[192,1152]{1,0:T(8,128)(2,1)}, bf16[192,1152]{1,0:T(8,128)(2,1)S(1)}, u32[]{:S(2)}, u32[]{:S(2)}) collective-permute-start(bf16[192,1152]{1,0:T(8,128)(2,1)} %get-tuple-element.146), channel_id=1, source_target_pairs={{0,2},{2,0},{1,3},{3,1},{4,6},{6,4},{5,7},{7,5},{8,10},{10,8},{9,1... | collective-permute-start | bytes 1327112 | tf_op jit(solution)/shard_map/ppermute | solution.py:778
  288.1 19.7 %collective-permute-start.32 = (bf16[192,1152]{1,0:T(8,128)(2,1)}, bf16[192,1152]{1,0:T(8,128)(2,1)S(1)}, u32[]{:S(2)}, u32[]{:S(2)}) collective-permute-start(bf16[192,1152]{1,0:T(8,128)(2,1)} %slice.133), channel_id=1, source_target_pairs={{0,2},{2,0},{1,3},{3,1},{4,6},{6,4},{5,7},{7,5},{8,10},{10,8},{9,1... | collective-permute-start | bytes 1327112 | tf_op jit(solution)/shard_map/ppermute | solution.py:778
  289.9 18.7 %collective-permute-start.40 = (bf16[216,768]{1,0:T(8,128)(2,1)S(1)}, bf16[216,768]{1,0:T(8,128)(2,1)S(1)}, u32[]{:S(2)}, u32[]{:S(2)}) collective-permute-start(bf16[216,768]{1,0:T(8,128)(2,1)S(1)} %pad_maximum_fusion.16), channel_id=1, source_target_pairs={{0,16},{4,20},{8,24},{12,28},{16,0},{20,4},{24,8},{28,12},{1,17},{... | collective-permute-start | bytes 995336 | tf_op jit(solution)/shard_map/ppermute | solution.py:804
  308.0 11.2 %collective-permute-start.37 = (bf16[192,1152]{1,0:T(8,128)(2,1)S(1)}, bf16[192,1152]{1,0:T(8,128)(2,1)S(1)}, u32[]{:S(2)}, u32[]{:S(2)}) collective-permute-start(bf16[192,1152]{1,0:T(8,128)(2,1)S(1)} %get-tuple-element.174), channel_id=1, source_target_pairs={{0,4},{4,0},{8,12},{12,8},{16,20},{20,16},{24,28},{28,24},{1,5},{5... | collective-permute-start | bytes 1327112 | tf_op jit(solution)/shard_map/ppermute | solution.py:847
  308.8 22.0 %collective-permute-start.41 = (bf16[432,768]{1,0:T(8,128)(2,1)S(1)}, bf16[432,768]{1,0:T(8,128)(2,1)S(1)}, u32[]{:S(2)}, u32[]{:S(2)}) collective-permute-start(bf16[432,768]{1,0:T(8,128)(2,1)S(1)} %pad_maximum_fusion.7), channel_id=1, source_target_pairs={{0,8},{4,12},{8,0},{12,4},{16,24},{20,28},{24,16},{28,20},{1,9},{5... | collective-permute-start | bytes 1990664 | tf_op jit(solution)/shard_map/ppermute | solution.py:804
  319.3 9.8 %collective-permute-start.38 = (bf16[96,1152]{1,0:T(8,128)(2,1)S(1)}, bf16[96,1152]{1,0:T(8,128)(2,1)S(1)}, u32[]{:S(2)}, u32[]{:S(2)}) collective-permute-start(bf16[96,1152]{1,0:T(8,128)(2,1)S(1)} %get-tuple-element.187), channel_id=1, source_target_pairs={{0,8},{4,12},{8,0},{12,4},{16,24},{20,28},{24,16},{28,20},{1,9},{5... | collective-permute-start | bytes 663560 | tf_op jit(solution)/shard_map/ppermute | solution.py:804
  321.0 46.0 %collective-permute-start.47 = (bf16[432,768]{1,0:T(8,128)(2,1)S(1)}, bf16[432,768]{1,0:T(8,128)(2,1)}, u32[]{:S(2)}, u32[]{:S(2)}) collective-permute-start(bf16[432,768]{1,0:T(8,128)(2,1)S(1)} %pad_maximum_fusion.7), channel_id=1, source_target_pairs={{0,4},{4,0},{8,12},{12,8},{16,20},{20,16},{24,28},{28,24},{1,5},{5... | collective-permute-start | bytes 1990664 | tf_op jit(solution)/shard_map/ppermute | solution.py:847
  321.5 45.4 %collective-permute-start.44 = (bf16[512,768]{1,0:T(8,128)(2,1)}, bf16[512,768]{1,0:T(8,128)(2,1)S(1)}, u32[]{:S(2)}, u32[]{:S(2)}) collective-permute-start(bf16[512,768]{1,0:T(8,128)(2,1)} %get-tuple-element.162), channel_id=1, source_target_pairs={{0,2},{2,0},{1,3},{3,1},{4,6},{6,4},{5,7},{7,5},{8,10},{10,8},{9,1... | collective-permute-start | bytes 2359304 | tf_op jit(solution)/shard_map/ppermute | solution.py:778
  329.1 11.1 %collective-permute-start.39 = (bf16[48,1152]{1,0:T(8,128)(2,1)S(1)}, bf16[48,1152]{1,0:T(8,128)(2,1)S(1)}, u32[]{:S(2)}, u32[]{:S(2)}) collective-permute-start(bf16[48,1152]{1,0:T(8,128)(2,1)S(1)} %add_convert_fusion.13), channel_id=1, source_target_pairs={{0,16},{4,20},{8,24},{12,28},{16,0},{20,4},{24,8},{28,12},{1,17},{... | collective-permute-start | bytes 331784 | tf_op jit(solution)/shard_map/ppermute | solution.py:804
  332.8 41.2 %all-to-all-start = ((f32[32,16,192]{2,1,0:T(8,128)}), f32[32,16,192]{2,1,0:T(8,128)S(1)}, u32[]{:S(2)}, u32[]{:S(2)}) async-start(f32[32,16,192]{2,1,0:T(8,128)} %bitcast.16), calls=%async_computation | async-start | bytes 1048576 | tf_op jit(solution)/shard_map/all_to_all | solution.py:977
  338.4 28.7 %collective-permute-start.46 = (bf16[432,768]{1,0:T(8,128)(2,1)}, bf16[432,768]{1,0:T(8,128)(2,1)S(1)}, u32[]{:S(2)}, u32[]{:S(2)}) collective-permute-start(bf16[432,768]{1,0:T(8,128)(2,1)} %copy-done.9), channel_id=1, source_target_pairs={{0,4},{4,0},{8,12},{12,8},{16,20},{20,16},{24,28},{28,24},{1,5},{5... | collective-permute-start | bytes 1990664 | tf_op jit(solution)/shard_map/ppermute | solution.py:847
  340.3 17.9 %collective-permute-start.42 = (bf16[48,1152]{1,0:T(8,128)(2,1)S(1)}, bf16[48,1152]{1,0:T(8,128)(2,1)S(1)}, u32[]{:S(2)}, u32[]{:S(2)}) collective-permute-start(bf16[48,1152]{1,0:T(8,128)(2,1)S(1)} %add_convert_fusion.12), channel_id=1, source_target_pairs={{0,16},{4,20},{8,24},{12,28},{16,0},{20,4},{24,8},{28,12},{1,17},{... | collective-permute-start | bytes 331784 | tf_op jit(solution)/shard_map/ppermute | solution.py:804
  358.2 7.0 %collective-permute-start.43 = (bf16[96,1152]{1,0:T(8,128)(2,1)S(1)}, bf16[96,1152]{1,0:T(8,128)(2,1)S(1)}, u32[]{:S(2)}, u32[]{:S(2)}) collective-permute-start(bf16[96,1152]{1,0:T(8,128)(2,1)S(1)} %pad_maximum_fusion.18), channel_id=1, source_target_pairs={{0,8},{4,12},{8,0},{12,4},{16,24},{20,28},{24,16},{28,20},{1,9},{5... | collective-permute-start | bytes 663560 | tf_op jit(solution)/shard_map/ppermute | solution.py:804
  365.3 11.0 %collective-permute-start.45 = (bf16[192,1152]{1,0:T(8,128)(2,1)S(1)}, bf16[192,1152]{1,0:T(8,128)(2,1)}, u32[]{:S(2)}, u32[]{:S(2)}) collective-permute-start(bf16[192,1152]{1,0:T(8,128)(2,1)S(1)} %pad_maximum_fusion.13), channel_id=1, source_target_pairs={{0,4},{4,0},{8,12},{12,8},{16,20},{20,16},{24,28},{28,24},{1,5},{5... | collective-permute-start | bytes 1327112 | tf_op jit(solution)/shard_map/ppermute | solution.py:847
  (33 other events, 225.4 us)

commit v7 on v2

--- a/solution.py
+++ b/solution.py
@@ -974,7 +974,8 @@
     small = jnp.concatenate([gt, gains, jnp.zeros((4, 5, part), f32)], axis=1)
     small = after(small, first_cat)
     small = jnp.broadcast_to(small[:, None], (4, dp, 16, part)).reshape(4 * dp, 16, part)
-    small = jnp.sum(lax.all_to_all(small, ("head", "dp"), 0, 0, tiled=True), axis=0)
+    small = lax.all_to_all(small.astype(bf16), ("head", "dp"), 0, 0, tiled=True)
+    small = jnp.sum(small.astype(f32), axis=0)
     output = order(after(out_own, g_send), out_x)
     grad_input = order(after(gi_own, ps), gi_got)
     return (

time: 371 us -> 365 us (0.984)
  waiting for transfers between devices: 97.7 us -> 83.1 us
  starting transfers between devices: 39.4 us -> 46 us
    ppermute x11, waiting for transfers between devices: 28.2 us -> 18.5 us  [swap(): return lax.ppermute(v, 'dp', flip(dp, stride))]
    ppermute x11, starting transfers between devices: 11.1 us -> 15.4 us  [swap(): return lax.ppermute(v, 'dp', flip(dp, stride))]
    ppermute x7, waiting for transfers between devices: 13.1 us -> 9.32 us  [local(): y_swap = lambda v: lax.ppermute(v, 'dp', flip(dp, 1))]
  transfers between devices with their start and end apart: 49 -> 49, of which waited for: 19 -> 18; matrix products, arithmetic and copies ran while one was open for 12% -> 12% of each run, Pallas kernels for 35% -> 35%
where the time goes in v7:
time: 365 us; the launch traced here: 364 us
  Pallas kernels  177 us (48%)
  waiting for transfers between devices  83.1 us (23%)
  starting transfers between devices  46 us (13%)
  other arithmetic  38.3 us (10%)
  local copies, waits for them, and re-layouts  17.9 us (5%)
    pallas_call x2, Pallas kernels, att_bwd_call(): pl.pallas_call(functools.partial(att_bwd_body, p0, into is not None), out...  66.2 us
    pallas_call x1, Pallas kernels, ffn_call(): pl.pallas_call(ffn_body, out_shape=[sds((2, rows, width), f32), sds((rows...  49.3 us
    ppermute x11, waiting for transfers between devices, x_swap(): return lax.ppermute(v, 'head', XNB)  44.3 us
    pallas_call x1, Pallas kernels, att_fwd_call(): pl.pallas_call(att_fwd_body, out_shape=[sds((length // 2, width), bf16),...  27.3 us
    ppermute x11, waiting for transfers between devices, swap(): return lax.ppermute(v, 'dp', flip(dp, stride))  18.5 us
    ppermute x11, starting transfers between devices, swap(): return lax.ppermute(v, 'dp', flip(dp, stride))  15.4 us
    pallas_call x1, Pallas kernels, qkv_call(): pl.pallas_call(qkv_body, out_shape=[sds((length, width), bf16), sds((leng...  13.5 us
    ppermute x11, starting transfers between devices, x_swap(): return lax.ppermute(v, 'head', XNB)  13 us
  transfers between devices with their start and end apart: 49, of which 18 were waited for; matrix products, arithmetic and copies ran while one was open for 12% of the time, Pallas kernels for 35%

profile of v7, /device:TPU:0, one launch (start us, length us, event | category | flops | bytes accessed | tf_op | source)
XLA Modules:
  0.0 363.9 jit_solution(2583992688406574366)
XLA Ops:
  6.9 3.2 collective-permute-start.4
  13.0 2.5 dynamic-slice_bitcast_fusion.1
  16.7 2.2 pad_maximum_fusion.1
  18.9 29.4 %collective-permute-done.x1.xx = bf16[512,768]{1,0:T(8,128)(2,1)} collective-permute-done((bf16[512,768]{1,0:T(8,128)(2,1)}, bf16[512,768]{1,0:T(8,128)(2,1)}, u32[]{:S(2)}, u32[]{:S(2)}) %collective-permute-start) | collective-permute-done | bytes 786464 | tf_op jit(solution)/shard_map/ppermute | solution.py:778
  49.4 1.7 collective-permute-start.5
  51.2 2.6 collective-permute-done.6.x3
  54.7 13.5 %qkv.1 = (bf16[2048,768]{1,0:T(8,128)(2,1)}, bf16[2048,1152]{1,0:T(8,128)(2,1)}, bf16[2048,1152]{1,0:T(8,128)(2,1)}, bf16[768,1152]{1,0:T(8,128)(2,1)}, f32[8,1152]{1,0:T(8,128)}) custom-call(s32[4]{0:T(128)} %pad_add_fusion.meta, bf16[512,768]{1,0:T(8,128)(2,1)} %copy-done, bf16[512,768]{1,0:T(8,128)(2,1)} %collective-permute-done.x1.xx, ...), custom_call_target="tpu_custom_call" | custom-call | flops 3623878656 | bytes 15728640 | tf_op jit(solution)/shard_map/qkv/pallas_call | solution.py:131
  68.6 1.7 collective-permute-start.10
  70.3 1.5 collective-permute-start.7
  71.8 1.6 collective-permute-start.8
  73.8 27.3 %attn_fwd.1 = (bf16[1024,384]{1,0:T(8,128)(2,1)}, bf16[1024,384]{1,0:T(8,128)(2,1)}, f32[3,2,2048]{2,1,0:T(2,128)}) custom-call(s32[4]{0:T(128)} %pad_add_fusion.meta, bf16[2048,1152]{1,0:T(8,128)(2,1)} %get-tuple-element.129.q_ref.k_ref.v_ref, bf16[2048,1152]{1,0:T(8,128)(2,1)} %get-tuple-element.129.q_ref.k_ref.v_ref, ...), custom_call_target="tpu_custom_call" | custom-call | flops 12884901888 | bytes 6291456 | tf_op jit(solution)/shard_map/attn_fwd/pallas_call | solution.py:255
  102.9 2.4 collective-permute-done.14.c0
  105.4 1.7 collective-permute-done.16.c2
  109.6 49.3 %ffn.1 = (f32[2,512,768]{2,1,0:T(8,128)}, bf16[512,768]{1,0:T(8,128)(2,1)}, bf16[1024,384]{1,0:T(8,128)(2,1)}, bf16[1024,384]{1,0:T(8,128)(2,1)}, f32[1,768]{1,0...) custom-call(s32[4]{0:T(128)} %pad_add_fusion.meta, ...), custom_call_target="tpu_custom_call" | custom-call | flops 32614907904 | bytes 31457280 | tf_op jit(solution)/shard_map/ffn/pallas_call | solution.py:623
  160.1 1.9 collective-permute-done.19
  163.0 3.1 add_convert_fusion
  166.2 2.0 collective-permute-start.25
  169.2 1.5 collective-permute-start.22
  170.8 2.6 add_convert_fusion.2
  173.8 42.7 %attn_bwd.2 = (bf16[1024,1152]{1,0:T(8,128)(2,1)}, bf16[1024,1152]{1,0:T(8,128)(2,1)}, f32[16,256]{1,0:T(8,128)}) custom-call(s32[4]{0:T(128)} %pad_add_fusion.meta, bf16[2048,1152]{1,0:T(8,128)(2,1)} %get-tuple-element.129.q_ref.k_ref.v_ref, bf16[2048,1152]{1,0:T(8,128)(2,1)} %get-tuple-element.129.q_ref.k_ref.v_ref, ...), custom_call_target="tpu_custom_call" | custom-call | flops 15032385536 | bytes 10485760 | tf_op jit(solution)/shard_map/attn_bwd/pallas_call | solution.py:407
  216.6 2.6 add_convert_fusion.1
  219.4 2.9 convert_add_fusion.1
  222.3 1.8 collective-permute-start.27
  224.1 23.6 %attn_bwd.3 = (bf16[1024,1152]{1,0:T(8,128)(2,1)}, bf16[1024,1152]{1,0:T(8,128)(2,1)}, f32[16,128]{1,0:T(8,128)}) custom-call(s32[4]{0:T(128)} %pad_add_fusion.meta, bf16[2048,1152]{1,0:T(8,128)(2,1)} %get-tuple-element.129.q_ref.k_ref.v_ref, ...), custom_call_target="tpu_custom_call", output_to_operand_aliasing={{0}: (13, {}), {1}: (14, {})} | custom-call | flops 7516192768 | bytes 5242880 | tf_op jit(solution)/shard_map/attn_bwd/pallas_call | solution.py:407
  249.8 1.5 convert_add_fusion.4
  251.4 1.6 collective-permute-start.29
  253.0 9.6 %projg.1 = (bf16[192,1152]{1,0:T(8,128)(2,1)}, bf16[192,1152]{1,0:T(8,128)(2,1)}, bf16[384,1152]{1,0:T(8,128)(2,1)}) custom-call(s32[4]{0:T(128)} %pad_add_fusion.meta, bf16[2048,768]{1,0:T(8,128)(2,1)} %get-tuple-element.136.h, bf16[1024,1152]{1,0:T(8,128)(2,1)} %get-tuple-element.137.dm, bf16[1024,1152]{1,0:T(8,128)(2,1)} %get-tuple-element.138.dt), custom_call_target="tpu_custom_call" | custom-call | flops 2048 | bytes 2048 | tf_op jit(solution)/shard_map/projg/pallas_call | solution.py:692
  262.6 6.1 %collective-permute-done.29 = bf16[432,768]{1,0:T(8,128)(2,1)S(1)} collective-permute-done((bf16[432,768]{1,0:T(8,128)(2,1)S(1)}, bf16[432,768]{1,0:T(8,128)(2,1)S(1)}, u32[]{:S(2)}, u32[]{:S(2)}) %collective-permute-start.29) | collective-permute-done | bytes 663584 | tf_op jit(solution)/shard_map/ppermute | solution.py:804
  269.1 2.7 collective-permute-start.33
  271.7 11.4 %last.1 = (f32[2,512,768]{2,1,0:T(8,128)}, bf16[512,768]{1,0:T(8,128)(2,1)}, f32[1,768]{1,0:T(1,128)}) custom-call(s32[4]{0:T(128)} %pad_add_fusion.meta, bf16[512,768]{1,0:T(8,128)(2,1)} %copy-done, bf16[512,768]{1,0:T(8,128)(2,1)} %collective-permute-done.x1.xx, bf16[1024,1152]{1,0:T(8,128)(2,1)} %get-tuple-element.137.dm, ...), custom_call_target="tpu_custom_call" | custom-call | flops 512 | bytes 512 | tf_op jit(solution)/shard_map/last/pallas_call | solution.py:750
  285.0 1.5 collective-permute-start.36
  291.0 4.3 %all-to-all-start = ((bf16[32,16,192]{2,1,0:T(8,128)(2,1)}), bf16[32,16,192]{2,1,0:T(8,128)(2,1)S(1)}, u32[]{:S(2)}, u32[]{:S(2)}) async-start(bf16[32,16,192]{2,1,0:T(8,128)(2,1)} %bitcast.16), calls=%async_computation | async-start | bytes 524288 | tf_op jit(solution)/shard_map/all_to_all | solution.py:977
  295.4 5.2 %collective-permute-done.31 = bf16[192,1152]{1,0:T(8,128)(2,1)S(1)} collective-permute-done((bf16[192,1152]{1,0:T(8,128)(2,1)}, bf16[192,1152]{1,0:T(8,128)(2,1)S(1)}, u32[]{:S(2)}, u32[]{:S(2)}) %collective-permute-start.31) | collective-permute-done | bytes 442400 | tf_op jit(solution)/shard_map/ppermute | solution.py:778
  300.5 9.7 %collective-permute-done.32 = bf16[192,1152]{1,0:T(8,128)(2,1)} collective-permute-done((bf16[192,1152]{1,0:T(8,128)(2,1)}, bf16[192,1152]{1,0:T(8,128)(2,1)}, u32[]{:S(2)}, u32[]{:S(2)}) %collective-permute-start.32) | collective-permute-done | bytes 442400 | tf_op jit(solution)/shard_map/ppermute | solution.py:778
  312.2 1.8 collective-permute-start.41
  314.0 1.5 collective-permute-start.47
  316.1 8.6 %collective-permute-done.37 = bf16[192,1152]{1,0:T(8,128)(2,1)S(1)} collective-permute-done((bf16[192,1152]{1,0:T(8,128)(2,1)S(1)}, bf16[192,1152]{1,0:T(8,128)(2,1)S(1)}, u32[]{:S(2)}, u32[]{:S(2)}) %collective-permute-start.37) | collective-permute-done | bytes 442400 | tf_op jit(solution)/shard_map/ppermute | solution.py:847
  325.5 1.7 collective-permute-start.38
  327.2 2.4 convert_dynamic-update-slice_fusion.1
  329.6 2.5 collective-permute-done.38
  334.6 1.5 collective-permute-start.46
  336.1 2.7 collective-permute-done.39
  341.3 4.2 %collective-permute-done.42 = bf16[48,1152]{1,0:T(8,128)(2,1)S(1)} collective-permute-done((bf16[48,1152]{1,0:T(8,128)(2,1)S(1)}, bf16[48,1152]{1,0:T(8,128)(2,1)S(1)}, u32[]{:S(2)}, u32[]{:S(2)}) %collective-permute-start.42) | collective-permute-done | bytes 110624 | tf_op jit(solution)/shard_map/ppermute | solution.py:804
  345.6 3.1 collective-permute-start.43
  349.7 2.8 collective-permute-done.43
  352.7 1.6 collective-permute-start.45
  357.2 1.6 fusion
  358.8 1.6 maximum_convert_fusion
  (203 shorter events, 45.9 us)
Async XLA Ops:
  3.9 2.0 collective-permute-start.3
  4.3 12.3 %collective-permute-start.1 = (bf16[192,768]{1,0:T(8,128)(2,1)}, bf16[192,768]{1,0:T(8,128)(2,1)}, u32[]{:S(2)}, u32[]{:S(2)}) collective-permute-start(bf16[192,768]{1,0:T(8,128)(2,1)} %wo_o.1), channel_id=1, source_target_pairs={{0,1},{1,0},{2,3},{3,2},{4,5},{5,4},{6,7},{7,6},{8,9},{9,8},{10,11... | collective-permute-start | bytes 884744 | tf_op jit(solution)/shard_map/ppermute | solution.py:774
  6.9 41.4 %collective-permute-start.4 = (bf16[608,768]{1,0:T(8,128)(2,1)}, bf16[608,768]{1,0:T(8,128)(2,1)}, u32[]{:S(2)}, u32[]{:S(2)}) collective-permute-start(bf16[608,768]{1,0:T(8,128)(2,1)} %pad_maximum_fusion.3), channel_id=1, source_target_pairs={{0,2},{2,0},{1,3},{3,1},{4,6},{6,4},{5,7},{7,5},{8,10},{10,8},{9,1... | collective-permute-start | bytes 2801672 | tf_op jit(solution)/shard_map/ppermute | solution.py:778
  11.1 37.2 %collective-permute-start = (bf16[512,768]{1,0:T(8,128)(2,1)}, bf16[512,768]{1,0:T(8,128)(2,1)}, u32[]{:S(2)}, u32[]{:S(2)}) collective-permute-start(bf16[512,768]{1,0:T(8,128)(2,1)} %get-tuple-element.178), channel_id=1, source_target_pairs={{0,2},{2,0},{1,3},{3,1},{4,6},{6,4},{5,7},{7,5},{8,10},{10,8},{9,1... | collective-permute-start | bytes 2359304 | tf_op jit(solution)/shard_map/ppermute | solution.py:778
  11.1 37.2 %collective-permute-start.2 = (bf16[512,768]{1,0:T(8,128)(2,1)S(1)}, bf16[512,768]{1,0:T(8,128)(2,1)}, u32[]{:S(2)}, u32[]{:S(2)}) collective-permute-start(bf16[512,768]{1,0:T(8,128)(2,1)S(1)} %get-tuple-element.177.x0.xo), channel_id=1, source_target_pairs={{0,1},{1,0},{2,3},{3,2},{4,5},{5,4},{6,7},{7,6},{8,9},{9,8},{10,11... | collective-permute-start | bytes 2359304 | tf_op jit(solution)/shard_map/ppermute | solution.py:774
  48.3 25.1 %collective-permute-start.11 = (bf16[2,768,768]{2,1,0:T(8,128)(2,1)S(1)}, bf16[2,768,768]{2,1,0:T(8,128)(2,1)}, u32[]{:S(2)}, u32[]{:S(2)}) collective-permute-start(bf16[2,768,768]{2,1,0:T(8,128)(2,1)S(1)} %pad_maximum_fusion), channel_id=1, source_target_pairs={{0,1},{1,0},{2,3},{3,2},{4,5},{5,4},{6,7},{7,6},{8,9},{9,8},{10,11... | collective-permute-start | bytes 7077896 | tf_op jit(solution)/shard_map/ppermute | solution.py:774
  48.3 5.5 %collective-permute-start.6 = (bf16[512,768]{1,0:T(8,128)(2,1)}, bf16[512,768]{1,0:T(8,128)(2,1)S(1)}, u32[]{:S(2)}, u32[]{:S(2)}) collective-permute-start(bf16[512,768]{1,0:T(8,128)(2,1)} %collective-permute-done.x1.xx), channel_id=1, source_target_pairs={{0,1},{1,0},{2,3},{3,2},{4,5},{5,4},{6,7},{7,6},{8,9},{9,8},{10,11... | collective-permute-start | bytes 2359304 | tf_op jit(solution)/shard_map/ppermute | solution.py:774
  49.4 20.9 %collective-permute-start.5 = (bf16[2,192,768]{2,1,0:T(8,128)(2,1)}, bf16[2,192,768]{2,1,0:T(8,128)(2,1)}, u32[]{:S(2)}, u32[]{:S(2)}) collective-permute-start(bf16[2,192,768]{2,1,0:T(8,128)(2,1)} %pad_maximum_fusion.10), channel_id=1, source_target_pairs={{0,2},{2,0},{1,3},{3,1},{4,6},{6,4},{5,7},{7,5},{8,10},{10,8},{9,1... | collective-permute-start | bytes 1769480 | tf_op jit(solution)/shard_map/ppermute | solution.py:778
  68.2 34.1 %collective-permute-start.13 = (bf16[768,1152]{1,0:T(8,128)(2,1)}, bf16[768,1152]{1,0:T(8,128)(2,1)}, u32[]{:S(2)}, u32[]{:S(2)}) collective-permute-start(bf16[768,1152]{1,0:T(8,128)(2,1)} %get-tuple-element.103.wm), channel_id=1, source_target_pairs={{0,1},{1,0},{2,3},{3,2},{4,5},{5,4},{6,7},{7,6},{8,9},{9,8},{10,11... | collective-permute-start | bytes 5308424 | tf_op jit(solution)/shard_map/ppermute | solution.py:774
  68.6 33.1 %collective-permute-start.10 = (bf16[896,768]{1,0:T(8,128)(2,1)}, bf16[896,768]{1,0:T(8,128)(2,1)}, u32[]{:S(2)}, u32[]{:S(2)}) collective-permute-start(bf16[896,768]{1,0:T(8,128)(2,1)} %pad_maximum_fusion.1), channel_id=1, source_target_pairs={{0,2},{2,0},{1,3},{3,1},{4,6},{6,4},{5,7},{7,5},{8,10},{10,8},{9,1... | collective-permute-start | bytes 4128776 | tf_op jit(solution)/shard_map/ppermute | solution.py:778
  70.3 30.8 %collective-permute-start.7 = (bf16[2,192,768]{2,1,0:T(8,128)(2,1)}, bf16[2,192,768]{2,1,0:T(8,128)(2,1)S(1)}, u32[]{:S(2)}, u32[]{:S(2)}) collective-permute-start(bf16[2,192,768]{2,1,0:T(8,128)(2,1)} %collective-permute-done.5.n0), channel_id=1, source_target_pairs={{0,4},{4,0},{8,12},{12,8},{16,20},{20,16},{24,28},{28,24},{1,5},{5... | collective-permute-start | bytes 1769480 | tf_op jit(solution)/shard_map/ppermute | solution.py:804
  71.8 29.4 %collective-permute-start.8 = (bf16[2,192,768]{2,1,0:T(8,128)(2,1)}, bf16[2,192,768]{2,1,0:T(8,128)(2,1)}, u32[]{:S(2)}, u32[]{:S(2)}) collective-permute-start(bf16[2,192,768]{2,1,0:T(8,128)(2,1)} %collective-permute-done.5.n0), channel_id=1, source_target_pairs={{0,8},{4,12},{8,0},{12,4},{16,24},{20,28},{24,16},{28,20},{1,9},{5... | collective-permute-start | bytes 1769480 | tf_op jit(solution)/shard_map/ppermute | solution.py:804
  73.4 28.3 %collective-permute-start.9 = (bf16[2,192,768]{2,1,0:T(8,128)(2,1)}, bf16[2,192,768]{2,1,0:T(8,128)(2,1)S(1)}, u32[]{:S(2)}, u32[]{:S(2)}) collective-permute-start(bf16[2,192,768]{2,1,0:T(8,128)(2,1)} %collective-permute-done.5.n0), channel_id=1, source_target_pairs={{0,12},{4,8},{8,4},{12,0},{16,28},{20,24},{24,20},{28,16},{1,13},{... | collective-permute-start | bytes 1769480 | tf_op jit(solution)/shard_map/ppermute | solution.py:804
  101.1 7.6 %collective-permute-start.12 = (bf16[1024,384]{1,0:T(8,128)(2,1)}, bf16[1024,384]{1,0:T(8,128)(2,1)S(1)}, u32[]{:S(2)}, u32[]{:S(2)}) collective-permute-start(bf16[1024,384]{1,0:T(8,128)(2,1)} %get-tuple-element.102.ot), channel_id=1, source_target_pairs={{0,1},{1,0},{2,3},{3,2},{4,5},{5,4},{6,7},{7,6},{8,9},{9,8},{10,11... | collective-permute-start | bytes 2359304 | tf_op jit(solution)/shard_map/ppermute | solution.py:774
  101.2 4.2 %collective-permute-start.14 = (bf16[2,192,768]{2,1,0:T(8,128)(2,1)}, bf16[2,192,768]{2,1,0:T(8,128)(2,1)S(1)}, u32[]{:S(2)}, u32[]{:S(2)}) collective-permute-start(bf16[2,192,768]{2,1,0:T(8,128)(2,1)} %collective-permute-done.5.n0), channel_id=1, source_target_pairs={{0,1},{1,0},{2,3},{3,2},{4,5},{5,4},{6,7},{7,6},{8,9},{9,8},{10,11... | collective-permute-start | bytes 1769480 | tf_op jit(solution)/shard_map/ppermute | solution.py:774
  101.7 3.7 %collective-permute-start.15 = (bf16[2,192,768]{2,1,0:T(8,128)(2,1)S(1)}, bf16[2,192,768]{2,1,0:T(8,128)(2,1)S(1)}, u32[]{:S(2)}, u32[]{:S(2)}) collective-permute-start(bf16[2,192,768]{2,1,0:T(8,128)(2,1)S(1)} %collective-permute-done.7.n1), channel_id=1, source_target_pairs={{0,1},{1,0},{2,3},{3,2},{4,5},{5,4},{6,7},{7,6},{8,9},{9,8},{10,11... | collective-permute-start | bytes 1769480 | tf_op jit(solution)/shard_map/ppermute | solution.py:774
  101.8 5.2 %collective-permute-start.16 = (bf16[2,192,768]{2,1,0:T(8,128)(2,1)}, bf16[2,192,768]{2,1,0:T(8,128)(2,1)S(1)}, u32[]{:S(2)}, u32[]{:S(2)}) collective-permute-start(bf16[2,192,768]{2,1,0:T(8,128)(2,1)} %collective-permute-done.8.n2), channel_id=1, source_target_pairs={{0,1},{1,0},{2,3},{3,2},{4,5},{5,4},{6,7},{7,6},{8,9},{9,8},{10,11... | collective-permute-start | bytes 1769480 | tf_op jit(solution)/shard_map/ppermute | solution.py:774
  102.3 4.8 %collective-permute-start.17 = (bf16[2,192,768]{2,1,0:T(8,128)(2,1)S(1)}, bf16[2,192,768]{2,1,0:T(8,128)(2,1)S(1)}, u32[]{:S(2)}, u32[]{:S(2)}) collective-permute-start(bf16[2,192,768]{2,1,0:T(8,128)(2,1)S(1)} %collective-permute-done.9.n3), channel_id=1, source_target_pairs={{0,1},{1,0},{2,3},{3,2},{4,5},{5,4},{6,7},{7,6},{8,9},{9,8},{10,11... | collective-permute-start | bytes 1769480 | tf_op jit(solution)/shard_map/ppermute | solution.py:774
  158.9 3.1 collective-permute-start.19
  159.1 7.1 %collective-permute-start.21 = (bf16[960,768]{1,0:T(8,128)(2,1)}, bf16[960,768]{1,0:T(8,128)(2,1)S(1)}, u32[]{:S(2)}, u32[]{:S(2)}) collective-permute-start(bf16[960,768]{1,0:T(8,128)(2,1)} %get-tuple-element.115), channel_id=1, source_target_pairs={{0,1},{1,0},{2,3},{3,2},{4,5},{5,4},{6,7},{7,6},{8,9},{9,8},{10,11... | collective-permute-start | bytes 4423688 | tf_op jit(solution)/shard_map/ppermute | solution.py:774
  159.4 9.8 %collective-permute-start.23 = (bf16[960,768]{1,0:T(8,128)(2,1)}, bf16[960,768]{1,0:T(8,128)(2,1)}, u32[]{:S(2)}, u32[]{:S(2)}) collective-permute-start(bf16[960,768]{1,0:T(8,128)(2,1)} %get-tuple-element.117), channel_id=1, source_target_pairs={{0,1},{1,0},{2,3},{3,2},{4,5},{5,4},{6,7},{7,6},{8,9},{9,8},{10,11... | collective-permute-start | bytes 4423688 | tf_op jit(solution)/shard_map/ppermute | solution.py:774
  159.6 13.8 %collective-permute-start.26 = (bf16[1024,384]{1,0:T(8,128)(2,1)}, bf16[1024,384]{1,0:T(8,128)(2,1)}, u32[]{:S(2)}, u32[]{:S(2)}) collective-permute-start(bf16[1024,384]{1,0:T(8,128)(2,1)} %get-tuple-element.122), channel_id=1, source_target_pairs={{0,1},{1,0},{2,3},{3,2},{4,5},{5,4},{6,7},{7,6},{8,9},{9,8},{10,11... | collective-permute-start | bytes 2359304 | tf_op jit(solution)/shard_map/ppermute | solution.py:774
  160.0 59.5 %collective-permute-start.18 = (bf16[768,768]{1,0:T(8,128)(2,1)}, bf16[768,768]{1,0:T(8,128)(2,1)}, u32[]{:S(2)}, u32[]{:S(2)}) collective-permute-start(bf16[768,768]{1,0:T(8,128)(2,1)} %get-tuple-element.111), channel_id=1, source_target_pairs={{0,1},{1,0},{2,3},{3,2},{4,5},{5,4},{6,7},{7,6},{8,9},{9,8},{10,11... | collective-permute-start | bytes 3538952 | tf_op jit(solution)/shard_map/ppermute | solution.py:774
  166.1 50.4 %collective-permute-start.20 = (bf16[768,768]{1,0:T(8,128)(2,1)}, bf16[768,768]{1,0:T(8,128)(2,1)}, u32[]{:S(2)}, u32[]{:S(2)}) collective-permute-start(bf16[768,768]{1,0:T(8,128)(2,1)} %add_convert_fusion), channel_id=1, source_target_pairs={{0,2},{2,0},{1,3},{3,1},{4,6},{6,4},{5,7},{7,5},{8,10},{10,8},{9,1... | collective-permute-start | bytes 3538952 | tf_op jit(solution)/shard_map/ppermute | solution.py:778
  166.2 50.3 %collective-permute-start.25 = (bf16[512,768]{1,0:T(8,128)(2,1)}, bf16[512,768]{1,0:T(8,128)(2,1)}, u32[]{:S(2)}, u32[]{:S(2)}) collective-permute-start(bf16[512,768]{1,0:T(8,128)(2,1)} %get-tuple-element.119), channel_id=1, source_target_pairs={{0,2},{2,0},{1,3},{3,1},{4,6},{6,4},{5,7},{7,5},{8,10},{10,8},{9,1... | collective-permute-start | bytes 2359304 | tf_op jit(solution)/shard_map/ppermute | solution.py:778
  169.2 47.3 %collective-permute-start.22 = (bf16[480,768]{1,0:T(8,128)(2,1)}, bf16[480,768]{1,0:T(8,128)(2,1)}, u32[]{:S(2)}, u32[]{:S(2)}) collective-permute-start(bf16[480,768]{1,0:T(8,128)(2,1)} %add_convert_fusion.3), channel_id=1, source_target_pairs={{0,4},{4,0},{8,12},{12,8},{16,20},{20,16},{24,28},{28,24},{1,5},{5... | collective-permute-start | bytes 2211848 | tf_op jit(solution)/shard_map/ppermute | solution.py:847
  173.3 43.2 %collective-permute-start.24 = (bf16[480,768]{1,0:T(8,128)(2,1)}, bf16[480,768]{1,0:T(8,128)(2,1)}, u32[]{:S(2)}, u32[]{:S(2)}) collective-permute-start(bf16[480,768]{1,0:T(8,128)(2,1)} %get-tuple-element.171), channel_id=1, source_target_pairs={{0,4},{4,0},{8,12},{12,8},{16,20},{20,16},{24,28},{28,24},{1,5},{5... | collective-permute-start | bytes 2211848 | tf_op jit(solution)/shard_map/ppermute | solution.py:847
  219.2 28.7 %collective-permute-start.28 = (bf16[480,768]{1,0:T(8,128)(2,1)}, bf16[480,768]{1,0:T(8,128)(2,1)}, u32[]{:S(2)}, u32[]{:S(2)}) collective-permute-start(bf16[480,768]{1,0:T(8,128)(2,1)} %add_convert_fusion.1), channel_id=1, source_target_pairs={{0,2},{2,0},{1,3},{3,1},{4,6},{6,4},{5,7},{7,5},{8,10},{10,8},{9,1... | collective-permute-start | bytes 2211848 | tf_op jit(solution)/shard_map/ppermute | solution.py:778
  222.3 25.5 %collective-permute-start.27 = (bf16[384,768]{1,0:T(8,128)(2,1)}, bf16[384,768]{1,0:T(8,128)(2,1)S(1)}, u32[]{:S(2)}, u32[]{:S(2)}) collective-permute-start(bf16[384,768]{1,0:T(8,128)(2,1)} %get-tuple-element.168), channel_id=1, source_target_pairs={{0,4},{4,0},{8,12},{12,8},{16,20},{20,16},{24,28},{28,24},{1,5},{5... | collective-permute-start | bytes 1769480 | tf_op jit(solution)/shard_map/ppermute | solution.py:847
  247.7 24.0 %collective-permute-start.34 = (bf16[1024,1152]{1,0:T(8,128)(2,1)}, bf16[1024,1152]{1,0:T(8,128)(2,1)}, u32[]{:S(2)}, u32[]{:S(2)}) collective-permute-start(bf16[1024,1152]{1,0:T(8,128)(2,1)} %get-tuple-element.138.dt), channel_id=1, source_target_pairs={{0,1},{1,0},{2,3},{3,2},{4,5},{5,4},{6,7},{7,6},{8,9},{9,8},{10,11... | collective-permute-start | bytes 7077896 | tf_op jit(solution)/shard_map/ppermute | solution.py:774
  251.4 17.3 %collective-permute-start.29 = (bf16[432,768]{1,0:T(8,128)(2,1)S(1)}, bf16[432,768]{1,0:T(8,128)(2,1)S(1)}, u32[]{:S(2)}, u32[]{:S(2)}) collective-permute-start(bf16[432,768]{1,0:T(8,128)(2,1)S(1)} %pad_maximum_fusion.6), channel_id=1, source_target_pairs={{0,8},{4,12},{8,0},{12,4},{16,24},{20,28},{24,16},{28,20},{1,9},{5... | collective-permute-start | bytes 1990664 | tf_op jit(solution)/shard_map/ppermute | solution.py:804
  269.0 18.3 %collective-permute-start.30 = (bf16[384,1152]{1,0:T(8,128)(2,1)}, bf16[384,1152]{1,0:T(8,128)(2,1)S(1)}, u32[]{:S(2)}, u32[]{:S(2)}) collective-permute-start(bf16[384,1152]{1,0:T(8,128)(2,1)} %get-tuple-element.145), channel_id=1, source_target_pairs={{0,1},{1,0},{2,3},{3,2},{4,5},{5,4},{6,7},{7,6},{8,9},{9,8},{10,11... | collective-permute-start | bytes 2654216 | tf_op jit(solution)/shard_map/ppermute | solution.py:774
  269.1 18.2 %collective-permute-start.33 = (bf16[216,768]{1,0:T(8,128)(2,1)S(1)}, bf16[216,768]{1,0:T(8,128)(2,1)S(1)}, u32[]{:S(2)}, u32[]{:S(2)}) collective-permute-start(bf16[216,768]{1,0:T(8,128)(2,1)S(1)} %pad_maximum_fusion.15), channel_id=1, source_target_pairs={{0,16},{4,20},{8,24},{12,28},{16,0},{20,4},{24,8},{28,12},{1,17},{... | collective-permute-start | bytes 995336 | tf_op jit(solution)/shard_map/ppermute | solution.py:804
  285.0 4.6 %collective-permute-start.36 = (bf16[1,768]{1,0:T(2,128)(2,1)S(1)}, bf16[1,768]{1,0:T(2,128)(2,1)S(1)}, u32[]{:S(2)}, u32[]{:S(2)}) collective-permute-start(bf16[1,768]{1,0:T(2,128)(2,1)S(1)} %collective-permute-done.35), channel_id=1, source_target_pairs={{0,2},{2,0},{1,3},{3,1},{4,6},{6,4},{5,7},{7,5},{8,10},{10,8},{9,1... | collective-permute-start | bytes 4616 | tf_op jit(solution)/shard_map/ppermute | solution.py:778
  286.5 14.0 %collective-permute-start.31 = (bf16[192,1152]{1,0:T(8,128)(2,1)}, bf16[192,1152]{1,0:T(8,128)(2,1)S(1)}, u32[]{:S(2)}, u32[]{:S(2)}) collective-permute-start(bf16[192,1152]{1,0:T(8,128)(2,1)} %get-tuple-element.146), channel_id=1, source_target_pairs={{0,2},{2,0},{1,3},{3,1},{4,6},{6,4},{5,7},{7,5},{8,10},{10,8},{9,1... | collective-permute-start | bytes 1327112 | tf_op jit(solution)/shard_map/ppermute | solution.py:778
  288.1 22.1 %collective-permute-start.32 = (bf16[192,1152]{1,0:T(8,128)(2,1)}, bf16[192,1152]{1,0:T(8,128)(2,1)}, u32[]{:S(2)}, u32[]{:S(2)}) collective-permute-start(bf16[192,1152]{1,0:T(8,128)(2,1)} %slice.133), channel_id=1, source_target_pairs={{0,2},{2,0},{1,3},{3,1},{4,6},{6,4},{5,7},{7,5},{8,10},{10,8},{9,1... | collective-permute-start | bytes 1327112 | tf_op jit(solution)/shard_map/ppermute | solution.py:778
  289.9 22.1 %collective-permute-start.40 = (bf16[216,768]{1,0:T(8,128)(2,1)S(1)}, bf16[216,768]{1,0:T(8,128)(2,1)S(1)}, u32[]{:S(2)}, u32[]{:S(2)}) collective-permute-start(bf16[216,768]{1,0:T(8,128)(2,1)S(1)} %pad_maximum_fusion.16), channel_id=1, source_target_pairs={{0,16},{4,20},{8,24},{12,28},{16,0},{20,4},{24,8},{28,12},{1,17},{... | collective-permute-start | bytes 995336 | tf_op jit(solution)/shard_map/ppermute | solution.py:804
  291.0 38.6 %all-to-all-start = ((bf16[32,16,192]{2,1,0:T(8,128)(2,1)}), bf16[32,16,192]{2,1,0:T(8,128)(2,1)S(1)}, u32[]{:S(2)}, u32[]{:S(2)}) async-start(bf16[32,16,192]{2,1,0:T(8,128)(2,1)} %bitcast.16), calls=%async_computation | async-start | bytes 524288 | tf_op jit(solution)/shard_map/all_to_all | solution.py:977
  311.5 13.2 %collective-permute-start.37 = (bf16[192,1152]{1,0:T(8,128)(2,1)S(1)}, bf16[192,1152]{1,0:T(8,128)(2,1)S(1)}, u32[]{:S(2)}, u32[]{:S(2)}) collective-permute-start(bf16[192,1152]{1,0:T(8,128)(2,1)S(1)} %get-tuple-element.174), channel_id=1, source_target_pairs={{0,4},{4,0},{8,12},{12,8},{16,20},{20,16},{24,28},{28,24},{1,5},{5... | collective-permute-start | bytes 1327112 | tf_op jit(solution)/shard_map/ppermute | solution.py:847
  312.2 22.4 %collective-permute-start.41 = (bf16[432,768]{1,0:T(8,128)(2,1)S(1)}, bf16[432,768]{1,0:T(8,128)(2,1)}, u32[]{:S(2)}, u32[]{:S(2)}) collective-permute-start(bf16[432,768]{1,0:T(8,128)(2,1)S(1)} %pad_maximum_fusion.7), channel_id=1, source_target_pairs={{0,8},{4,12},{8,0},{12,4},{16,24},{20,28},{24,16},{28,20},{1,9},{5... | collective-permute-start | bytes 1990664 | tf_op jit(solution)/shard_map/ppermute | solution.py:804
  314.0 40.4 %collective-permute-start.47 = (bf16[432,768]{1,0:T(8,128)(2,1)S(1)}, bf16[432,768]{1,0:T(8,128)(2,1)S(1)}, u32[]{:S(2)}, u32[]{:S(2)}) collective-permute-start(bf16[432,768]{1,0:T(8,128)(2,1)S(1)} %pad_maximum_fusion.7), channel_id=1, source_target_pairs={{0,4},{4,0},{8,12},{12,8},{16,20},{20,16},{24,28},{28,24},{1,5},{5... | collective-permute-start | bytes 1990664 | tf_op jit(solution)/shard_map/ppermute | solution.py:847
  315.6 38.7 %collective-permute-start.44 = (bf16[512,768]{1,0:T(8,128)(2,1)}, bf16[512,768]{1,0:T(8,128)(2,1)S(1)}, u32[]{:S(2)}, u32[]{:S(2)}) collective-permute-start(bf16[512,768]{1,0:T(8,128)(2,1)} %get-tuple-element.162), channel_id=1, source_target_pairs={{0,2},{2,0},{1,3},{3,1},{4,6},{6,4},{5,7},{7,5},{8,10},{10,8},{9,1... | collective-permute-start | bytes 2359304 | tf_op jit(solution)/shard_map/ppermute | solution.py:778
  325.5 6.7 %collective-permute-start.38 = (bf16[96,1152]{1,0:T(8,128)(2,1)}, bf16[96,1152]{1,0:T(8,128)(2,1)}, u32[]{:S(2)}, u32[]{:S(2)}) collective-permute-start(bf16[96,1152]{1,0:T(8,128)(2,1)} %get-tuple-element.187), channel_id=1, source_target_pairs={{0,8},{4,12},{8,0},{12,4},{16,24},{20,28},{24,16},{28,20},{1,9},{5... | collective-permute-start | bytes 663560 | tf_op jit(solution)/shard_map/ppermute | solution.py:804
  333.1 5.7 %collective-permute-start.39 = (bf16[48,1152]{1,0:T(8,128)(2,1)S(1)}, bf16[48,1152]{1,0:T(8,128)(2,1)S(1)}, u32[]{:S(2)}, u32[]{:S(2)}) collective-permute-start(bf16[48,1152]{1,0:T(8,128)(2,1)S(1)} %add_convert_fusion.13), channel_id=1, source_target_pairs={{0,16},{4,20},{8,24},{12,28},{16,0},{20,4},{24,8},{28,12},{1,17},{... | collective-permute-start | bytes 331784 | tf_op jit(solution)/shard_map/ppermute | solution.py:804
  334.6 19.8 %collective-permute-start.46 = (bf16[432,768]{1,0:T(8,128)(2,1)}, bf16[432,768]{1,0:T(8,128)(2,1)S(1)}, u32[]{:S(2)}, u32[]{:S(2)}) collective-permute-start(bf16[432,768]{1,0:T(8,128)(2,1)} %collective-permute-done.41), channel_id=1, source_target_pairs={{0,4},{4,0},{8,12},{12,8},{16,20},{20,16},{24,28},{28,24},{1,5},{5... | collective-permute-start | bytes 1990664 | tf_op jit(solution)/shard_map/ppermute | solution.py:847
  339.7 5.7 %collective-permute-start.42 = (bf16[48,1152]{1,0:T(8,128)(2,1)S(1)}, bf16[48,1152]{1,0:T(8,128)(2,1)S(1)}, u32[]{:S(2)}, u32[]{:S(2)}) collective-permute-start(bf16[48,1152]{1,0:T(8,128)(2,1)S(1)} %add_convert_fusion.12), channel_id=1, source_target_pairs={{0,16},{4,20},{8,24},{12,28},{16,0},{20,4},{24,8},{28,12},{1,17},{... | collective-permute-start | bytes 331784 | tf_op jit(solution)/shard_map/ppermute | solution.py:804
  345.6 7.0 %collective-permute-start.43 = (bf16[96,1152]{1,0:T(8,128)(2,1)S(1)}, bf16[96,1152]{1,0:T(8,128)(2,1)S(1)}, u32[]{:S(2)}, u32[]{:S(2)}) collective-permute-start(bf16[96,1152]{1,0:T(8,128)(2,1)S(1)} %pad_maximum_fusion.18), channel_id=1, source_target_pairs={{0,8},{4,12},{8,0},{12,4},{16,24},{20,28},{24,16},{28,20},{1,9},{5... | collective-permute-start | bytes 663560 | tf_op jit(solution)/shard_map/ppermute | solution.py:804
  352.7 8.4 %collective-permute-start.45 = (bf16[192,1152]{1,0:T(8,128)(2,1)S(1)}, bf16[192,1152]{1,0:T(8,128)(2,1)S(1)}, u32[]{:S(2)}, u32[]{:S(2)}) collective-permute-start(bf16[192,1152]{1,0:T(8,128)(2,1)S(1)} %pad_maximum_fusion.13), channel_id=1, source_target_pairs={{0,4},{4,0},{8,12},{12,8},{16,20},{20,16},{24,28},{28,24},{1,5},{5... | collective-permute-start | bytes 1327112 | tf_op jit(solution)/shard_map/ppermute | solution.py:847
  (30 other events, 200.8 us)

commit v8 on v7

--- a/solution.py
+++ b/solution.py
@@ -974,7 +974,8 @@
     small = jnp.concatenate([gt, gains, jnp.zeros((4, 5, part), f32)], axis=1)
     small = after(small, first_cat)
     small = jnp.broadcast_to(small[:, None], (4, dp, 16, part)).reshape(4 * dp, 16, part)
-    small = lax.all_to_all(small.astype(bf16), ("head", "dp"), 0, 0, tiled=True)
+    small = lax.all_to_all(small.astype(bf16).reshape(4 * dp, 8, 2 * part), ("head", "dp"), 0, 0, tiled=True)
+    small = small.reshape(4 * dp, 16, part)
     small = jnp.sum(small.astype(f32), axis=0)
     output = order(after(out_own, g_send), out_x)
     grad_input = order(after(gi_own, ps), gi_got)

time: 365 us -> 367 us (level)
  waiting for transfers between devices: 83.1 us -> 88.3 us
  starting transfers between devices: 46 us -> 41.4 us
    ppermute x11, waiting for transfers between devices: 18.5 us -> 24.6 us  [swap(): return lax.ppermute(v, 'dp', flip(dp, stride))]
where the time goes in v8:
time: 367 us; the launch traced here: 366 us
  Pallas kernels  177 us (48%)
  waiting for transfers between devices  88.3 us (24%)
  starting transfers between devices  41.4 us (11%)
  other arithmetic  39.3 us (11%)
  local copies, waits for them, and re-layouts  18.1 us (5%)
    pallas_call x2, Pallas kernels, att_bwd_call(): pl.pallas_call(functools.partial(att_bwd_body, p0, into is not None), out...  66.2 us
    pallas_call x1, Pallas kernels, ffn_call(): pl.pallas_call(ffn_body, out_shape=[sds((2, rows, width), f32), sds((rows...  49.3 us
    ppermute x11, waiting for transfers between devices, x_swap(): return lax.ppermute(v, 'head', XNB)  43.7 us
    pallas_call x1, Pallas kernels, att_fwd_call(): pl.pallas_call(att_fwd_body, out_shape=[sds((length // 2, width), bf16),...  27.3 us
    ppermute x11, waiting for transfers between devices, swap(): return lax.ppermute(v, 'dp', flip(dp, stride))  24.6 us
    pallas_call x1, Pallas kernels, qkv_call(): pl.pallas_call(qkv_body, out_shape=[sds((length, width), bf16), sds((leng...  13.5 us
    ppermute x11, starting transfers between devices, x_swap(): return lax.ppermute(v, 'head', XNB)  12.8 us
    ppermute x11, starting transfers between devices, swap(): return lax.ppermute(v, 'dp', flip(dp, stride))  12.6 us
  transfers between devices with their start and end apart: 49, of which 18 were waited for; matrix products, arithmetic and copies ran while one was open for 12% of the time, Pallas kernels for 35%

profile of v8, /device:TPU:0, one launch (start us, length us, event | category | flops | bytes accessed | tf_op | source)
XLA Modules:
  0.0 365.8 jit_solution(16432298929585718989)
XLA Ops:
  4.4 1.5 collective-permute-done.3.wb
  6.9 3.2 collective-permute-start.4
  13.0 2.5 dynamic-slice_bitcast_fusion.1
  16.7 2.2 pad_maximum_fusion.1
  18.9 29.4 %collective-permute-done.x1.xx = bf16[512,768]{1,0:T(8,128)(2,1)} collective-permute-done((bf16[512,768]{1,0:T(8,128)(2,1)}, bf16[512,768]{1,0:T(8,128)(2,1)}, u32[]{:S(2)}, u32[]{:S(2)}) %collective-permute-start) | collective-permute-done | bytes 786464 | tf_op jit(solution)/shard_map/ppermute | solution.py:778
  49.4 1.7 collective-permute-start.5
  51.2 2.6 collective-permute-done.6.x3
  54.7 13.5 %qkv.1 = (bf16[2048,768]{1,0:T(8,128)(2,1)}, bf16[2048,1152]{1,0:T(8,128)(2,1)}, bf16[2048,1152]{1,0:T(8,128)(2,1)}, bf16[768,1152]{1,0:T(8,128)(2,1)}, f32[8,1152]{1,0:T(8,128)}) custom-call(s32[4]{0:T(128)} %pad_add_fusion.meta, bf16[512,768]{1,0:T(8,128)(2,1)} %copy-done, bf16[512,768]{1,0:T(8,128)(2,1)} %collective-permute-done.x1.xx, ...), custom_call_target="tpu_custom_call" | custom-call | flops 3623878656 | bytes 15728640 | tf_op jit(solution)/shard_map/qkv/pallas_call | solution.py:131
  68.6 1.7 collective-permute-start.10
  70.3 1.5 collective-permute-start.7
  71.8 1.6 collective-permute-start.8
  73.8 27.3 %attn_fwd.1 = (bf16[1024,384]{1,0:T(8,128)(2,1)}, bf16[1024,384]{1,0:T(8,128)(2,1)}, f32[3,2,2048]{2,1,0:T(2,128)}) custom-call(s32[4]{0:T(128)} %pad_add_fusion.meta, bf16[2048,1152]{1,0:T(8,128)(2,1)} %get-tuple-element.129.q_ref.k_ref.v_ref, bf16[2048,1152]{1,0:T(8,128)(2,1)} %get-tuple-element.129.q_ref.k_ref.v_ref, ...), custom_call_target="tpu_custom_call" | custom-call | flops 12884901888 | bytes 6291456 | tf_op jit(solution)/shard_map/attn_fwd/pallas_call | solution.py:255
  102.9 2.4 collective-permute-done.14.c0
  105.4 1.7 collective-permute-done.16.c2
  109.6 49.3 %ffn.1 = (f32[2,512,768]{2,1,0:T(8,128)}, bf16[512,768]{1,0:T(8,128)(2,1)}, bf16[1024,384]{1,0:T(8,128)(2,1)}, bf16[1024,384]{1,0:T(8,128)(2,1)}, f32[1,768]{1,0...) custom-call(s32[4]{0:T(128)} %pad_add_fusion.meta, ...), custom_call_target="tpu_custom_call" | custom-call | flops 32614907904 | bytes 31457280 | tf_op jit(solution)/shard_map/ffn/pallas_call | solution.py:623
  160.1 1.9 collective-permute-done.19
  163.0 3.1 add_convert_fusion
  166.2 2.0 collective-permute-start.25
  169.2 1.5 collective-permute-start.22
  170.8 2.6 add_convert_fusion.2
  173.8 42.7 %attn_bwd.2 = (bf16[1024,1152]{1,0:T(8,128)(2,1)}, bf16[1024,1152]{1,0:T(8,128)(2,1)}, f32[16,256]{1,0:T(8,128)}) custom-call(s32[4]{0:T(128)} %pad_add_fusion.meta, bf16[2048,1152]{1,0:T(8,128)(2,1)} %get-tuple-element.129.q_ref.k_ref.v_ref, bf16[2048,1152]{1,0:T(8,128)(2,1)} %get-tuple-element.129.q_ref.k_ref.v_ref, ...), custom_call_target="tpu_custom_call" | custom-call | flops 15032385536 | bytes 10485760 | tf_op jit(solution)/shard_map/attn_bwd/pallas_call | solution.py:407
  216.6 2.6 add_convert_fusion.1
  219.4 2.9 convert_add_fusion.1
  222.3 1.8 collective-permute-start.27
  224.1 23.6 %attn_bwd.3 = (bf16[1024,1152]{1,0:T(8,128)(2,1)}, bf16[1024,1152]{1,0:T(8,128)(2,1)}, f32[16,128]{1,0:T(8,128)}) custom-call(s32[4]{0:T(128)} %pad_add_fusion.meta, bf16[2048,1152]{1,0:T(8,128)(2,1)} %get-tuple-element.129.q_ref.k_ref.v_ref, ...), custom_call_target="tpu_custom_call", output_to_operand_aliasing={{0}: (13, {}), {1}: (14, {})} | custom-call | flops 7516192768 | bytes 5242880 | tf_op jit(solution)/shard_map/attn_bwd/pallas_call | solution.py:407
  249.8 1.5 convert_add_fusion.4
  251.4 1.6 collective-permute-start.29
  253.0 9.6 %projg.1 = (bf16[192,1152]{1,0:T(8,128)(2,1)}, bf16[192,1152]{1,0:T(8,128)(2,1)}, bf16[384,1152]{1,0:T(8,128)(2,1)}) custom-call(s32[4]{0:T(128)} %pad_add_fusion.meta, bf16[2048,768]{1,0:T(8,128)(2,1)} %get-tuple-element.136.h, bf16[1024,1152]{1,0:T(8,128)(2,1)} %get-tuple-element.137.dm, bf16[1024,1152]{1,0:T(8,128)(2,1)} %get-tuple-element.138.dt), custom_call_target="tpu_custom_call" | custom-call | flops 2048 | bytes 2048 | tf_op jit(solution)/shard_map/projg/pallas_call | solution.py:692
  262.6 6.1 %collective-permute-done.29 = bf16[432,768]{1,0:T(8,128)(2,1)S(1)} collective-permute-done((bf16[432,768]{1,0:T(8,128)(2,1)S(1)}, bf16[432,768]{1,0:T(8,128)(2,1)S(1)}, u32[]{:S(2)}, u32[]{:S(2)}) %collective-permute-start.29) | collective-permute-done | bytes 663584 | tf_op jit(solution)/shard_map/ppermute | solution.py:804
  269.1 2.7 collective-permute-start.33
  271.7 11.4 %last.1 = (f32[2,512,768]{2,1,0:T(8,128)}, bf16[512,768]{1,0:T(8,128)(2,1)}, f32[1,768]{1,0:T(1,128)}) custom-call(s32[4]{0:T(128)} %pad_add_fusion.meta, bf16[512,768]{1,0:T(8,128)(2,1)} %copy-done, bf16[512,768]{1,0:T(8,128)(2,1)} %collective-permute-done.x1.xx, bf16[1024,1152]{1,0:T(8,128)(2,1)} %get-tuple-element.137.dm, ...), custom_call_target="tpu_custom_call" | custom-call | flops 512 | bytes 512 | tf_op jit(solution)/shard_map/last/pallas_call | solution.py:750
  285.0 1.5 collective-permute-start.36
  288.1 1.5 collective-permute-start.32
  291.2 4.3 %all-to-all-start = ((bf16[32,8,384]{2,1,0:T(8,128)(2,1)}), bf16[32,8,384]{2,1,0:T(8,128)(2,1)S(1)}, u32[]{:S(2)}, u32[]{:S(2)}) async-start(bf16[32,8,384]{2,1,0:T(8,128)(2,1)} %convert_element_type.267), calls=%async_computation | async-start | bytes 393216 | tf_op jit(solution)/shard_map/all_to_all | solution.py:977
  295.5 4.8 %collective-permute-done.31 = bf16[192,1152]{1,0:T(8,128)(2,1)S(1)} collective-permute-done((bf16[192,1152]{1,0:T(8,128)(2,1)}, bf16[192,1152]{1,0:T(8,128)(2,1)S(1)}, u32[]{:S(2)}, u32[]{:S(2)}) %collective-permute-start.31) | collective-permute-done | bytes 442400 | tf_op jit(solution)/shard_map/ppermute | solution.py:778
  300.3 9.4 %collective-permute-done.32 = bf16[192,1152]{1,0:T(8,128)(2,1)S(1)} collective-permute-done((bf16[192,1152]{1,0:T(8,128)(2,1)}, bf16[192,1152]{1,0:T(8,128)(2,1)S(1)}, u32[]{:S(2)}, u32[]{:S(2)}) %collective-permute-start.32) | collective-permute-done | bytes 442400 | tf_op jit(solution)/shard_map/ppermute | solution.py:778
  312.5 1.8 collective-permute-start.41
  314.3 1.6 collective-permute-start.47
  316.3 6.9 %collective-permute-done.37 = bf16[192,1152]{1,0:T(8,128)(2,1)S(1)} collective-permute-done((bf16[192,1152]{1,0:T(8,128)(2,1)S(1)}, bf16[192,1152]{1,0:T(8,128)(2,1)S(1)}, u32[]{:S(2)}, u32[]{:S(2)}) %collective-permute-start.37) | collective-permute-done | bytes 442400 | tf_op jit(solution)/shard_map/ppermute | solution.py:847
  324.0 1.8 collective-permute-start.38
  325.8 2.4 convert_dynamic-update-slice_fusion.1
  328.3 4.4 %collective-permute-done.38 = bf16[96,1152]{1,0:T(8,128)(2,1)} collective-permute-done((bf16[96,1152]{1,0:T(8,128)(2,1)}, bf16[96,1152]{1,0:T(8,128)(2,1)}, u32[]{:S(2)}, u32[]{:S(2)}) %collective-permute-start.38) | collective-permute-done | bytes 221216 | tf_op jit(solution)/shard_map/ppermute | solution.py:804
  336.5 4.0 %collective-permute-done.39 = bf16[48,1152]{1,0:T(8,128)(2,1)S(1)} collective-permute-done((bf16[48,1152]{1,0:T(8,128)(2,1)S(1)}, bf16[48,1152]{1,0:T(8,128)(2,1)S(1)}, u32[]{:S(2)}, u32[]{:S(2)}) %collective-permute-start.39) | collective-permute-done | bytes 110624 | tf_op jit(solution)/shard_map/ppermute | solution.py:804
  342.6 5.7 %collective-permute-done.42 = bf16[48,1152]{1,0:T(8,128)(2,1)S(1)} collective-permute-done((bf16[48,1152]{1,0:T(8,128)(2,1)S(1)}, bf16[48,1152]{1,0:T(8,128)(2,1)S(1)}, u32[]{:S(2)}, u32[]{:S(2)}) %collective-permute-start.42) | collective-permute-done | bytes 110624 | tf_op jit(solution)/shard_map/ppermute | solution.py:804
  350.2 4.2 %collective-permute-done.43 = bf16[96,1152]{1,0:T(8,128)(2,1)S(1)} collective-permute-done((bf16[96,1152]{1,0:T(8,128)(2,1)S(1)}, bf16[96,1152]{1,0:T(8,128)(2,1)S(1)}, u32[]{:S(2)}, u32[]{:S(2)}) %collective-permute-start.43) | collective-permute-done | bytes 221216 | tf_op jit(solution)/shard_map/ppermute | solution.py:804
  357.7 1.6 fusion
  359.3 1.6 maximum_convert_fusion
  360.9 2.1 collective-permute-done.45
  (205 shorter events, 45.0 us)
Async XLA Ops:
  3.9 2.0 collective-permute-start.3
  4.3 12.3 %collective-permute-start.1 = (bf16[192,768]{1,0:T(8,128)(2,1)}, bf16[192,768]{1,0:T(8,128)(2,1)}, u32[]{:S(2)}, u32[]{:S(2)}) collective-permute-start(bf16[192,768]{1,0:T(8,128)(2,1)} %wo_o.1), channel_id=1, source_target_pairs={{0,1},{1,0},{2,3},{3,2},{4,5},{5,4},{6,7},{7,6},{8,9},{9,8},{10,11... | collective-permute-start | bytes 884744 | tf_op jit(solution)/shard_map/ppermute | solution.py:774
  6.9 41.4 %collective-permute-start.4 = (bf16[608,768]{1,0:T(8,128)(2,1)}, bf16[608,768]{1,0:T(8,128)(2,1)}, u32[]{:S(2)}, u32[]{:S(2)}) collective-permute-start(bf16[608,768]{1,0:T(8,128)(2,1)} %pad_maximum_fusion.3), channel_id=1, source_target_pairs={{0,2},{2,0},{1,3},{3,1},{4,6},{6,4},{5,7},{7,5},{8,10},{10,8},{9,1... | collective-permute-start | bytes 2801672 | tf_op jit(solution)/shard_map/ppermute | solution.py:778
  11.1 37.2 %collective-permute-start = (bf16[512,768]{1,0:T(8,128)(2,1)}, bf16[512,768]{1,0:T(8,128)(2,1)}, u32[]{:S(2)}, u32[]{:S(2)}) collective-permute-start(bf16[512,768]{1,0:T(8,128)(2,1)} %get-tuple-element.178), channel_id=1, source_target_pairs={{0,2},{2,0},{1,3},{3,1},{4,6},{6,4},{5,7},{7,5},{8,10},{10,8},{9,1... | collective-permute-start | bytes 2359304 | tf_op jit(solution)/shard_map/ppermute | solution.py:778
  11.1 37.2 %collective-permute-start.2 = (bf16[512,768]{1,0:T(8,128)(2,1)S(1)}, bf16[512,768]{1,0:T(8,128)(2,1)}, u32[]{:S(2)}, u32[]{:S(2)}) collective-permute-start(bf16[512,768]{1,0:T(8,128)(2,1)S(1)} %get-tuple-element.177.x0.xo), channel_id=1, source_target_pairs={{0,1},{1,0},{2,3},{3,2},{4,5},{5,4},{6,7},{7,6},{8,9},{9,8},{10,11... | collective-permute-start | bytes 2359304 | tf_op jit(solution)/shard_map/ppermute | solution.py:774
  48.3 25.1 %collective-permute-start.11 = (bf16[2,768,768]{2,1,0:T(8,128)(2,1)S(1)}, bf16[2,768,768]{2,1,0:T(8,128)(2,1)}, u32[]{:S(2)}, u32[]{:S(2)}) collective-permute-start(bf16[2,768,768]{2,1,0:T(8,128)(2,1)S(1)} %pad_maximum_fusion), channel_id=1, source_target_pairs={{0,1},{1,0},{2,3},{3,2},{4,5},{5,4},{6,7},{7,6},{8,9},{9,8},{10,11... | collective-permute-start | bytes 7077896 | tf_op jit(solution)/shard_map/ppermute | solution.py:774
  48.3 5.5 %collective-permute-start.6 = (bf16[512,768]{1,0:T(8,128)(2,1)}, bf16[512,768]{1,0:T(8,128)(2,1)S(1)}, u32[]{:S(2)}, u32[]{:S(2)}) collective-permute-start(bf16[512,768]{1,0:T(8,128)(2,1)} %collective-permute-done.x1.xx), channel_id=1, source_target_pairs={{0,1},{1,0},{2,3},{3,2},{4,5},{5,4},{6,7},{7,6},{8,9},{9,8},{10,11... | collective-permute-start | bytes 2359304 | tf_op jit(solution)/shard_map/ppermute | solution.py:774
  49.4 20.9 %collective-permute-start.5 = (bf16[2,192,768]{2,1,0:T(8,128)(2,1)}, bf16[2,192,768]{2,1,0:T(8,128)(2,1)}, u32[]{:S(2)}, u32[]{:S(2)}) collective-permute-start(bf16[2,192,768]{2,1,0:T(8,128)(2,1)} %pad_maximum_fusion.10), channel_id=1, source_target_pairs={{0,2},{2,0},{1,3},{3,1},{4,6},{6,4},{5,7},{7,5},{8,10},{10,8},{9,1... | collective-permute-start | bytes 1769480 | tf_op jit(solution)/shard_map/ppermute | solution.py:778
  68.2 34.1 %collective-permute-start.13 = (bf16[768,1152]{1,0:T(8,128)(2,1)}, bf16[768,1152]{1,0:T(8,128)(2,1)}, u32[]{:S(2)}, u32[]{:S(2)}) collective-permute-start(bf16[768,1152]{1,0:T(8,128)(2,1)} %get-tuple-element.103.wm), channel_id=1, source_target_pairs={{0,1},{1,0},{2,3},{3,2},{4,5},{5,4},{6,7},{7,6},{8,9},{9,8},{10,11... | collective-permute-start | bytes 5308424 | tf_op jit(solution)/shard_map/ppermute | solution.py:774
  68.6 33.1 %collective-permute-start.10 = (bf16[896,768]{1,0:T(8,128)(2,1)}, bf16[896,768]{1,0:T(8,128)(2,1)}, u32[]{:S(2)}, u32[]{:S(2)}) collective-permute-start(bf16[896,768]{1,0:T(8,128)(2,1)} %pad_maximum_fusion.1), channel_id=1, source_target_pairs={{0,2},{2,0},{1,3},{3,1},{4,6},{6,4},{5,7},{7,5},{8,10},{10,8},{9,1... | collective-permute-start | bytes 4128776 | tf_op jit(solution)/shard_map/ppermute | solution.py:778
  70.3 30.8 %collective-permute-start.7 = (bf16[2,192,768]{2,1,0:T(8,128)(2,1)}, bf16[2,192,768]{2,1,0:T(8,128)(2,1)S(1)}, u32[]{:S(2)}, u32[]{:S(2)}) collective-permute-start(bf16[2,192,768]{2,1,0:T(8,128)(2,1)} %collective-permute-done.5.n0), channel_id=1, source_target_pairs={{0,4},{4,0},{8,12},{12,8},{16,20},{20,16},{24,28},{28,24},{1,5},{5... | collective-permute-start | bytes 1769480 | tf_op jit(solution)/shard_map/ppermute | solution.py:804
  71.8 29.4 %collective-permute-start.8 = (bf16[2,192,768]{2,1,0:T(8,128)(2,1)}, bf16[2,192,768]{2,1,0:T(8,128)(2,1)}, u32[]{:S(2)}, u32[]{:S(2)}) collective-permute-start(bf16[2,192,768]{2,1,0:T(8,128)(2,1)} %collective-permute-done.5.n0), channel_id=1, source_target_pairs={{0,8},{4,12},{8,0},{12,4},{16,24},{20,28},{24,16},{28,20},{1,9},{5... | collective-permute-start | bytes 1769480 | tf_op jit(solution)/shard_map/ppermute | solution.py:804
  73.4 28.3 %collective-permute-start.9 = (bf16[2,192,768]{2,1,0:T(8,128)(2,1)}, bf16[2,192,768]{2,1,0:T(8,128)(2,1)S(1)}, u32[]{:S(2)}, u32[]{:S(2)}) collective-permute-start(bf16[2,192,768]{2,1,0:T(8,128)(2,1)} %collective-permute-done.5.n0), channel_id=1, source_target_pairs={{0,12},{4,8},{8,4},{12,0},{16,28},{20,24},{24,20},{28,16},{1,13},{... | collective-permute-start | bytes 1769480 | tf_op jit(solution)/shard_map/ppermute | solution.py:804
  101.1 7.6 %collective-permute-start.12 = (bf16[1024,384]{1,0:T(8,128)(2,1)}, bf16[1024,384]{1,0:T(8,128)(2,1)S(1)}, u32[]{:S(2)}, u32[]{:S(2)}) collective-permute-start(bf16[1024,384]{1,0:T(8,128)(2,1)} %get-tuple-element.102.ot), channel_id=1, source_target_pairs={{0,1},{1,0},{2,3},{3,2},{4,5},{5,4},{6,7},{7,6},{8,9},{9,8},{10,11... | collective-permute-start | bytes 2359304 | tf_op jit(solution)/shard_map/ppermute | solution.py:774
  101.2 4.2 %collective-permute-start.14 = (bf16[2,192,768]{2,1,0:T(8,128)(2,1)}, bf16[2,192,768]{2,1,0:T(8,128)(2,1)S(1)}, u32[]{:S(2)}, u32[]{:S(2)}) collective-permute-start(bf16[2,192,768]{2,1,0:T(8,128)(2,1)} %collective-permute-done.5.n0), channel_id=1, source_target_pairs={{0,1},{1,0},{2,3},{3,2},{4,5},{5,4},{6,7},{7,6},{8,9},{9,8},{10,11... | collective-permute-start | bytes 1769480 | tf_op jit(solution)/shard_map/ppermute | solution.py:774
  101.7 3.7 %collective-permute-start.15 = (bf16[2,192,768]{2,1,0:T(8,128)(2,1)S(1)}, bf16[2,192,768]{2,1,0:T(8,128)(2,1)S(1)}, u32[]{:S(2)}, u32[]{:S(2)}) collective-permute-start(bf16[2,192,768]{2,1,0:T(8,128)(2,1)S(1)} %collective-permute-done.7.n1), channel_id=1, source_target_pairs={{0,1},{1,0},{2,3},{3,2},{4,5},{5,4},{6,7},{7,6},{8,9},{9,8},{10,11... | collective-permute-start | bytes 1769480 | tf_op jit(solution)/shard_map/ppermute | solution.py:774
  101.8 5.2 %collective-permute-start.16 = (bf16[2,192,768]{2,1,0:T(8,128)(2,1)}, bf16[2,192,768]{2,1,0:T(8,128)(2,1)S(1)}, u32[]{:S(2)}, u32[]{:S(2)}) collective-permute-start(bf16[2,192,768]{2,1,0:T(8,128)(2,1)} %collective-permute-done.8.n2), channel_id=1, source_target_pairs={{0,1},{1,0},{2,3},{3,2},{4,5},{5,4},{6,7},{7,6},{8,9},{9,8},{10,11... | collective-permute-start | bytes 1769480 | tf_op jit(solution)/shard_map/ppermute | solution.py:774
  102.3 4.8 %collective-permute-start.17 = (bf16[2,192,768]{2,1,0:T(8,128)(2,1)S(1)}, bf16[2,192,768]{2,1,0:T(8,128)(2,1)S(1)}, u32[]{:S(2)}, u32[]{:S(2)}) collective-permute-start(bf16[2,192,768]{2,1,0:T(8,128)(2,1)S(1)} %collective-permute-done.9.n3), channel_id=1, source_target_pairs={{0,1},{1,0},{2,3},{3,2},{4,5},{5,4},{6,7},{7,6},{8,9},{9,8},{10,11... | collective-permute-start | bytes 1769480 | tf_op jit(solution)/shard_map/ppermute | solution.py:774
  158.9 3.1 collective-permute-start.19
  159.1 7.1 %collective-permute-start.21 = (bf16[960,768]{1,0:T(8,128)(2,1)}, bf16[960,768]{1,0:T(8,128)(2,1)S(1)}, u32[]{:S(2)}, u32[]{:S(2)}) collective-permute-start(bf16[960,768]{1,0:T(8,128)(2,1)} %get-tuple-element.115), channel_id=1, source_target_pairs={{0,1},{1,0},{2,3},{3,2},{4,5},{5,4},{6,7},{7,6},{8,9},{9,8},{10,11... | collective-permute-start | bytes 4423688 | tf_op jit(solution)/shard_map/ppermute | solution.py:774
  159.4 9.8 %collective-permute-start.23 = (bf16[960,768]{1,0:T(8,128)(2,1)}, bf16[960,768]{1,0:T(8,128)(2,1)}, u32[]{:S(2)}, u32[]{:S(2)}) collective-permute-start(bf16[960,768]{1,0:T(8,128)(2,1)} %get-tuple-element.117), channel_id=1, source_target_pairs={{0,1},{1,0},{2,3},{3,2},{4,5},{5,4},{6,7},{7,6},{8,9},{9,8},{10,11... | collective-permute-start | bytes 4423688 | tf_op jit(solution)/shard_map/ppermute | solution.py:774
  159.6 13.8 %collective-permute-start.26 = (bf16[1024,384]{1,0:T(8,128)(2,1)}, bf16[1024,384]{1,0:T(8,128)(2,1)}, u32[]{:S(2)}, u32[]{:S(2)}) collective-permute-start(bf16[1024,384]{1,0:T(8,128)(2,1)} %get-tuple-element.122), channel_id=1, source_target_pairs={{0,1},{1,0},{2,3},{3,2},{4,5},{5,4},{6,7},{7,6},{8,9},{9,8},{10,11... | collective-permute-start | bytes 2359304 | tf_op jit(solution)/shard_map/ppermute | solution.py:774
  160.0 59.5 %collective-permute-start.18 = (bf16[768,768]{1,0:T(8,128)(2,1)}, bf16[768,768]{1,0:T(8,128)(2,1)}, u32[]{:S(2)}, u32[]{:S(2)}) collective-permute-start(bf16[768,768]{1,0:T(8,128)(2,1)} %get-tuple-element.111), channel_id=1, source_target_pairs={{0,1},{1,0},{2,3},{3,2},{4,5},{5,4},{6,7},{7,6},{8,9},{9,8},{10,11... | collective-permute-start | bytes 3538952 | tf_op jit(solution)/shard_map/ppermute | solution.py:774
  166.1 50.4 %collective-permute-start.20 = (bf16[768,768]{1,0:T(8,128)(2,1)}, bf16[768,768]{1,0:T(8,128)(2,1)}, u32[]{:S(2)}, u32[]{:S(2)}) collective-permute-start(bf16[768,768]{1,0:T(8,128)(2,1)} %add_convert_fusion), channel_id=1, source_target_pairs={{0,2},{2,0},{1,3},{3,1},{4,6},{6,4},{5,7},{7,5},{8,10},{10,8},{9,1... | collective-permute-start | bytes 3538952 | tf_op jit(solution)/shard_map/ppermute | solution.py:778
  166.2 50.3 %collective-permute-start.25 = (bf16[512,768]{1,0:T(8,128)(2,1)}, bf16[512,768]{1,0:T(8,128)(2,1)}, u32[]{:S(2)}, u32[]{:S(2)}) collective-permute-start(bf16[512,768]{1,0:T(8,128)(2,1)} %get-tuple-element.119), channel_id=1, source_target_pairs={{0,2},{2,0},{1,3},{3,1},{4,6},{6,4},{5,7},{7,5},{8,10},{10,8},{9,1... | collective-permute-start | bytes 2359304 | tf_op jit(solution)/shard_map/ppermute | solution.py:778
  169.2 47.3 %collective-permute-start.22 = (bf16[480,768]{1,0:T(8,128)(2,1)}, bf16[480,768]{1,0:T(8,128)(2,1)}, u32[]{:S(2)}, u32[]{:S(2)}) collective-permute-start(bf16[480,768]{1,0:T(8,128)(2,1)} %add_convert_fusion.3), channel_id=1, source_target_pairs={{0,4},{4,0},{8,12},{12,8},{16,20},{20,16},{24,28},{28,24},{1,5},{5... | collective-permute-start | bytes 2211848 | tf_op jit(solution)/shard_map/ppermute | solution.py:847
  173.3 43.2 %collective-permute-start.24 = (bf16[480,768]{1,0:T(8,128)(2,1)}, bf16[480,768]{1,0:T(8,128)(2,1)}, u32[]{:S(2)}, u32[]{:S(2)}) collective-permute-start(bf16[480,768]{1,0:T(8,128)(2,1)} %get-tuple-element.171), channel_id=1, source_target_pairs={{0,4},{4,0},{8,12},{12,8},{16,20},{20,16},{24,28},{28,24},{1,5},{5... | collective-permute-start | bytes 2211848 | tf_op jit(solution)/shard_map/ppermute | solution.py:847
  219.2 28.7 %collective-permute-start.28 = (bf16[480,768]{1,0:T(8,128)(2,1)}, bf16[480,768]{1,0:T(8,128)(2,1)}, u32[]{:S(2)}, u32[]{:S(2)}) collective-permute-start(bf16[480,768]{1,0:T(8,128)(2,1)} %add_convert_fusion.1), channel_id=1, source_target_pairs={{0,2},{2,0},{1,3},{3,1},{4,6},{6,4},{5,7},{7,5},{8,10},{10,8},{9,1... | collective-permute-start | bytes 2211848 | tf_op jit(solution)/shard_map/ppermute | solution.py:778
  222.3 25.5 %collective-permute-start.27 = (bf16[384,768]{1,0:T(8,128)(2,1)}, bf16[384,768]{1,0:T(8,128)(2,1)S(1)}, u32[]{:S(2)}, u32[]{:S(2)}) collective-permute-start(bf16[384,768]{1,0:T(8,128)(2,1)} %get-tuple-element.168), channel_id=1, source_target_pairs={{0,4},{4,0},{8,12},{12,8},{16,20},{20,16},{24,28},{28,24},{1,5},{5... | collective-permute-start | bytes 1769480 | tf_op jit(solution)/shard_map/ppermute | solution.py:847
  247.7 24.0 %collective-permute-start.34 = (bf16[1024,1152]{1,0:T(8,128)(2,1)}, bf16[1024,1152]{1,0:T(8,128)(2,1)}, u32[]{:S(2)}, u32[]{:S(2)}) collective-permute-start(bf16[1024,1152]{1,0:T(8,128)(2,1)} %get-tuple-element.138.dt), channel_id=1, source_target_pairs={{0,1},{1,0},{2,3},{3,2},{4,5},{5,4},{6,7},{7,6},{8,9},{9,8},{10,11... | collective-permute-start | bytes 7077896 | tf_op jit(solution)/shard_map/ppermute | solution.py:774
  251.4 17.3 %collective-permute-start.29 = (bf16[432,768]{1,0:T(8,128)(2,1)S(1)}, bf16[432,768]{1,0:T(8,128)(2,1)S(1)}, u32[]{:S(2)}, u32[]{:S(2)}) collective-permute-start(bf16[432,768]{1,0:T(8,128)(2,1)S(1)} %pad_maximum_fusion.6), channel_id=1, source_target_pairs={{0,8},{4,12},{8,0},{12,4},{16,24},{20,28},{24,16},{28,20},{1,9},{5... | collective-permute-start | bytes 1990664 | tf_op jit(solution)/shard_map/ppermute | solution.py:804
  269.0 18.3 %collective-permute-start.30 = (bf16[384,1152]{1,0:T(8,128)(2,1)}, bf16[384,1152]{1,0:T(8,128)(2,1)S(1)}, u32[]{:S(2)}, u32[]{:S(2)}) collective-permute-start(bf16[384,1152]{1,0:T(8,128)(2,1)} %get-tuple-element.145), channel_id=1, source_target_pairs={{0,1},{1,0},{2,3},{3,2},{4,5},{5,4},{6,7},{7,6},{8,9},{9,8},{10,11... | collective-permute-start | bytes 2654216 | tf_op jit(solution)/shard_map/ppermute | solution.py:774
  269.1 18.2 %collective-permute-start.33 = (bf16[216,768]{1,0:T(8,128)(2,1)S(1)}, bf16[216,768]{1,0:T(8,128)(2,1)S(1)}, u32[]{:S(2)}, u32[]{:S(2)}) collective-permute-start(bf16[216,768]{1,0:T(8,128)(2,1)S(1)} %pad_maximum_fusion.15), channel_id=1, source_target_pairs={{0,16},{4,20},{8,24},{12,28},{16,0},{20,4},{24,8},{28,12},{1,17},{... | collective-permute-start | bytes 995336 | tf_op jit(solution)/shard_map/ppermute | solution.py:804
  285.0 4.6 %collective-permute-start.36 = (bf16[1,768]{1,0:T(2,128)(2,1)S(1)}, bf16[1,768]{1,0:T(2,128)(2,1)S(1)}, u32[]{:S(2)}, u32[]{:S(2)}) collective-permute-start(bf16[1,768]{1,0:T(2,128)(2,1)S(1)} %collective-permute-done.35), channel_id=1, source_target_pairs={{0,2},{2,0},{1,3},{3,1},{4,6},{6,4},{5,7},{7,5},{8,10},{10,8},{9,1... | collective-permute-start | bytes 4616 | tf_op jit(solution)/shard_map/ppermute | solution.py:778
  286.5 13.9 %collective-permute-start.31 = (bf16[192,1152]{1,0:T(8,128)(2,1)}, bf16[192,1152]{1,0:T(8,128)(2,1)S(1)}, u32[]{:S(2)}, u32[]{:S(2)}) collective-permute-start(bf16[192,1152]{1,0:T(8,128)(2,1)} %get-tuple-element.146), channel_id=1, source_target_pairs={{0,2},{2,0},{1,3},{3,1},{4,6},{6,4},{5,7},{7,5},{8,10},{10,8},{9,1... | collective-permute-start | bytes 1327112 | tf_op jit(solution)/shard_map/ppermute | solution.py:778
  288.1 21.6 %collective-permute-start.32 = (bf16[192,1152]{1,0:T(8,128)(2,1)}, bf16[192,1152]{1,0:T(8,128)(2,1)S(1)}, u32[]{:S(2)}, u32[]{:S(2)}) collective-permute-start(bf16[192,1152]{1,0:T(8,128)(2,1)} %slice.133), channel_id=1, source_target_pairs={{0,2},{2,0},{1,3},{3,1},{4,6},{6,4},{5,7},{7,5},{8,10},{10,8},{9,1... | collective-permute-start | bytes 1327112 | tf_op jit(solution)/shard_map/ppermute | solution.py:778
  290.0 20.6 %collective-permute-start.40 = (bf16[216,768]{1,0:T(8,128)(2,1)S(1)}, bf16[216,768]{1,0:T(8,128)(2,1)}, u32[]{:S(2)}, u32[]{:S(2)}) collective-permute-start(bf16[216,768]{1,0:T(8,128)(2,1)S(1)} %pad_maximum_fusion.16), channel_id=1, source_target_pairs={{0,16},{4,20},{8,24},{12,28},{16,0},{20,4},{24,8},{28,12},{1,17},{... | collective-permute-start | bytes 995336 | tf_op jit(solution)/shard_map/ppermute | solution.py:804
  291.2 36.9 %all-to-all-start = ((bf16[32,8,384]{2,1,0:T(8,128)(2,1)}), bf16[32,8,384]{2,1,0:T(8,128)(2,1)S(1)}, u32[]{:S(2)}, u32[]{:S(2)}) async-start(bf16[32,8,384]{2,1,0:T(8,128)(2,1)} %convert_element_type.267), calls=%async_computation | async-start | bytes 393216 | tf_op jit(solution)/shard_map/all_to_all | solution.py:977
  310.0 13.2 %collective-permute-start.37 = (bf16[192,1152]{1,0:T(8,128)(2,1)S(1)}, bf16[192,1152]{1,0:T(8,128)(2,1)S(1)}, u32[]{:S(2)}, u32[]{:S(2)}) collective-permute-start(bf16[192,1152]{1,0:T(8,128)(2,1)S(1)} %get-tuple-element.174), channel_id=1, source_target_pairs={{0,4},{4,0},{8,12},{12,8},{16,20},{20,16},{24,28},{28,24},{1,5},{5... | collective-permute-start | bytes 1327112 | tf_op jit(solution)/shard_map/ppermute | solution.py:847
  312.5 22.7 %collective-permute-start.41 = (bf16[432,768]{1,0:T(8,128)(2,1)S(1)}, bf16[432,768]{1,0:T(8,128)(2,1)}, u32[]{:S(2)}, u32[]{:S(2)}) collective-permute-start(bf16[432,768]{1,0:T(8,128)(2,1)S(1)} %pad_maximum_fusion.7), channel_id=1, source_target_pairs={{0,8},{4,12},{8,0},{12,4},{16,24},{20,28},{24,16},{28,20},{1,9},{5... | collective-permute-start | bytes 1990664 | tf_op jit(solution)/shard_map/ppermute | solution.py:804
  314.3 40.6 %collective-permute-start.47 = (bf16[432,768]{1,0:T(8,128)(2,1)S(1)}, bf16[432,768]{1,0:T(8,128)(2,1)S(1)}, u32[]{:S(2)}, u32[]{:S(2)}) collective-permute-start(bf16[432,768]{1,0:T(8,128)(2,1)S(1)} %pad_maximum_fusion.7), channel_id=1, source_target_pairs={{0,4},{4,0},{8,12},{12,8},{16,20},{20,16},{24,28},{28,24},{1,5},{5... | collective-permute-start | bytes 1990664 | tf_op jit(solution)/shard_map/ppermute | solution.py:847
  315.9 38.9 %collective-permute-start.44 = (bf16[512,768]{1,0:T(8,128)(2,1)}, bf16[512,768]{1,0:T(8,128)(2,1)S(1)}, u32[]{:S(2)}, u32[]{:S(2)}) collective-permute-start(bf16[512,768]{1,0:T(8,128)(2,1)} %get-tuple-element.162), channel_id=1, source_target_pairs={{0,2},{2,0},{1,3},{3,1},{4,6},{6,4},{5,7},{7,5},{8,10},{10,8},{9,1... | collective-permute-start | bytes 2359304 | tf_op jit(solution)/shard_map/ppermute | solution.py:778
  324.0 8.7 %collective-permute-start.38 = (bf16[96,1152]{1,0:T(8,128)(2,1)}, bf16[96,1152]{1,0:T(8,128)(2,1)}, u32[]{:S(2)}, u32[]{:S(2)}) collective-permute-start(bf16[96,1152]{1,0:T(8,128)(2,1)} %get-tuple-element.187), channel_id=1, source_target_pairs={{0,8},{4,12},{8,0},{12,4},{16,24},{20,28},{24,16},{28,20},{1,9},{5... | collective-permute-start | bytes 663560 | tf_op jit(solution)/shard_map/ppermute | solution.py:804
  333.6 6.9 %collective-permute-start.39 = (bf16[48,1152]{1,0:T(8,128)(2,1)S(1)}, bf16[48,1152]{1,0:T(8,128)(2,1)S(1)}, u32[]{:S(2)}, u32[]{:S(2)}) collective-permute-start(bf16[48,1152]{1,0:T(8,128)(2,1)S(1)} %add_convert_fusion.13), channel_id=1, source_target_pairs={{0,16},{4,20},{8,24},{12,28},{16,0},{20,4},{24,8},{28,12},{1,17},{... | collective-permute-start | bytes 331784 | tf_op jit(solution)/shard_map/ppermute | solution.py:804
  335.2 19.7 %collective-permute-start.46 = (bf16[432,768]{1,0:T(8,128)(2,1)}, bf16[432,768]{1,0:T(8,128)(2,1)S(1)}, u32[]{:S(2)}, u32[]{:S(2)}) collective-permute-start(bf16[432,768]{1,0:T(8,128)(2,1)} %collective-permute-done.41), channel_id=1, source_target_pairs={{0,4},{4,0},{8,12},{12,8},{16,20},{20,16},{24,28},{28,24},{1,5},{5... | collective-permute-start | bytes 1990664 | tf_op jit(solution)/shard_map/ppermute | solution.py:847
  341.4 6.9 %collective-permute-start.42 = (bf16[48,1152]{1,0:T(8,128)(2,1)S(1)}, bf16[48,1152]{1,0:T(8,128)(2,1)S(1)}, u32[]{:S(2)}, u32[]{:S(2)}) collective-permute-start(bf16[48,1152]{1,0:T(8,128)(2,1)S(1)} %add_convert_fusion.12), channel_id=1, source_target_pairs={{0,16},{4,20},{8,24},{12,28},{16,0},{20,4},{24,8},{28,12},{1,17},{... | collective-permute-start | bytes 331784 | tf_op jit(solution)/shard_map/ppermute | solution.py:804
  348.4 6.0 %collective-permute-start.43 = (bf16[96,1152]{1,0:T(8,128)(2,1)S(1)}, bf16[96,1152]{1,0:T(8,128)(2,1)S(1)}, u32[]{:S(2)}, u32[]{:S(2)}) collective-permute-start(bf16[96,1152]{1,0:T(8,128)(2,1)S(1)} %pad_maximum_fusion.18), channel_id=1, source_target_pairs={{0,8},{4,12},{8,0},{12,4},{16,24},{20,28},{24,16},{28,20},{1,9},{5... | collective-permute-start | bytes 663560 | tf_op jit(solution)/shard_map/ppermute | solution.py:804
  354.6 8.4 %collective-permute-start.45 = (bf16[192,1152]{1,0:T(8,128)(2,1)S(1)}, bf16[192,1152]{1,0:T(8,128)(2,1)S(1)}, u32[]{:S(2)}, u32[]{:S(2)}) collective-permute-start(bf16[192,1152]{1,0:T(8,128)(2,1)S(1)} %pad_maximum_fusion.13), channel_id=1, source_target_pairs={{0,4},{4,0},{8,12},{12,8},{16,20},{20,16},{24,28},{28,24},{1,5},{5... | collective-permute-start | bytes 1327112 | tf_op jit(solution)/shard_map/ppermute | solution.py:847
  (30 other events, 197.9 us)
